TPU v7x, 128 devices: a whole 4x4x4 slice. The times are simulated.
128 devices in a mesh: row: 8 (over y_lo, z), col: 16 (over y_hi, x, core).
Axes of the slice: x: 4, y: 4 (y_hi: 2, y_lo: 2; y = y_hi * 2 + y_lo), z: 4, core: 2. Of those that a mesh axis runs over, the one named last changes fastest.
Arguments:
- features: bfloat16 [24576, 512], P(('col', 'row')), may hold values from -6 to 6
- out_grad: bfloat16 [24576, 512], P(('row', 'col')), may hold values from -6 to 6
- weight: bfloat16 [512, 512], replicated, may hold values from -0.25 to 0.25
- block_values: bfloat16 [8, 16, 288, 4096], P('row', 'col'), may hold values from -0.125 to 0.125
- block_coords: int32 [8, 16, 2, 288], P('row', 'col'), may hold values from 0 to 47, as said below
- block_counts: int32 [8, 16], P('row', 'col'), may hold values from 1 to 288, as said below
Outputs:
- activations: bfloat16 [24576, 512], P(('row', 'col'))
- weight_grad: float32 [512, 512], replicated
- feature_grad: bfloat16 [24576, 512], P(('col', 'row'))
Inputs may be any that keep to these rules, and one draw needn't show every extreme that they name: `block_coords`: entry 0 of a slot is a block row below 48, entry 1 a block column below 24; the 288 slots of a tile name distinct blocks. `block_counts`: slots from the count onward are padding: their coordinates and values are ignored. Some tile has exactly 288 live slots.
All inputs are finite; a program needn't handle non-finite values.
Results may differ from a plain program's by a relative error of at most 0.025.
Values may be sent and summed in bfloat16 or wider, within the bound.
No kernel may reach another device: no remote copies, remote signals or barrier semaphores. Data moves between devices by JAX's collectives and lax.ppermute only.
A program may use at most 128 MiB of HBM per device.

v0:
```python
import math

import jax
import jax.numpy as jnp
from jax import lax
from jax.sharding import PartitionSpec as P


def settle(term):
    return lax.optimization_barrier(term.astype(jnp.bfloat16)).astype(jnp.float32)


def per_device(features, out_grad, weight, block_values, block_coords, block_counts):
    row_devices = lax.axis_size("row")
    col_devices = lax.axis_size("col")
    node_count = features.shape[0]
    side = 64
    slot_total = block_values.shape[2]
    block_rows = node_count * col_devices // side
    block_cols = node_count * row_devices // side
    live_count = block_counts[0, 0]
    row_ids = block_coords[0, 0, 0]
    col_ids = block_coords[0, 0, 1]
    slot_vals = block_values.reshape(slot_total, side, side)
    live = jnp.arange(slot_total, dtype=jnp.int32) < live_count
    slot_vals = jnp.where(live[:, None, None], slot_vals, jnp.zeros_like(slot_vals))
    panel = lax.all_gather(features, "row", axis=0, tiled=True)
    dense_tile = jnp.zeros((block_rows, side, block_cols, side), jnp.bfloat16)
    dense_tile = dense_tile.at[row_ids, :, col_ids, :].add(slot_vals)
    dense_tile = dense_tile.reshape(block_rows * side, block_cols * side)
    partial_agg = settle(jnp.dot(dense_tile, panel, preferred_element_type=jnp.float32))
    aggregated = lax.psum_scatter(
        partial_agg.astype(jnp.bfloat16), "col", scatter_dimension=0, tiled=True
    )
    pre_act = jnp.dot(aggregated, weight, preferred_element_type=jnp.float32)
    sigmoid_pre = jax.nn.sigmoid(pre_act)
    activations = (pre_act * sigmoid_pre).astype(jnp.bfloat16)
    grad_pre = (
        out_grad.astype(jnp.float32) * sigmoid_pre * (1.0 + pre_act * (1.0 - sigmoid_pre))
    ).astype(jnp.bfloat16)
    activations, grad_pre = (activations, grad_pre)
    grad_agg = lax.dot_general(
        grad_pre, weight, (((1,), (1,)), ((), ())), preferred_element_type=jnp.float32
    ).astype(jnp.bfloat16)
    grad_rows = lax.all_gather(grad_agg, "col", axis=0, tiled=True)
    local_wgrad = lax.dot_general(
        aggregated, grad_pre, (((0,), (0,)), ((), ())), preferred_element_type=jnp.float32
    )
    total_nodes = node_count * row_devices * col_devices
    weight_grad = lax.psum(local_wgrad, ("row", "col")) * jnp.float32(1.0 / math.sqrt(total_nodes))
    partial_grad = settle(
        lax.dot_general(
            dense_tile, grad_rows, (((0,), (0,)), ((), ())), preferred_element_type=jnp.float32
        )
    )
    feature_grad = lax.psum_scatter(
        partial_grad.astype(jnp.bfloat16), "row", scatter_dimension=0, tiled=True
    )
    return (activations, weight_grad, feature_grad)


def solution(mesh):
    return jax.shard_map(
        per_device,
        mesh=mesh,
        in_specs=(
            P(("col", "row"), None),
            P(("row", "col"), None),
            P(),
            P("row", "col", None, None),
            P("row", "col", None, None),
            P("row", "col"),
        ),
        out_specs=(P(("row", "col"), None), P(), P(("col", "row"), None)),
        check_vma=False,
    )
```

profile of v0, /device:TPU:0, one launch (start us, length us, event | category | flops | bytes accessed | tf_op | source)
XLA Modules:
  0.0 468.8 jit_solution(1539356239016432633)
XLA Ops:
  7.2 0.0 copy-start
  7.2 0.0 all-gather.3.cloned.1.call-start
  7.2 0.7 all-gather.3.cloned.1.call-update
  7.9 0.0 reduce-scatter.3.cloned.1.call-start
  8.0 4.5 copy.9
  13.1 3.9 broadcast_select_fusion
  17.0 9.9 %copy.10 = bf16[288,64,64]{2,1,0:T(8,128)(2,1)} copy(bf16[288,64,64]{0,2,1:T(8,128)(2,1)} %broadcast_select_fusion) | data formatting | bytes 4718592 | tf_op jit(solution)/shard_map/jit(_where)/select_n | solution.py:26
  26.9 0.0 copy-done.1
  26.9 7.1 %broadcast_in_dim.17 = bf16[48,64,24,64]{3,1,2,0:T(8,128)(2,1)} broadcast(bf16[]{:T(256)} %constant.6.clone.1), dimensions={} | broadcast | bytes 9437186 | tf_op jit(solution)/shard_map/broadcast_in_dim | solution.py:28
  34.0 45.5 %scatter_fusion = bf16[48,64,24,64]{3,1,2,0:T(8,128)(2,1)} fusion(bf16[48,64,24,64]{3,1,2,0:T(8,128)(2,1)} %broadcast_in_dim.17, s32[288]{0:T(512)S(1)} %fusion.1, bf16[288,64,64]{2,1,0:T(8,128)(2,1)} %copy.10), kind=kCustom, calls=%fused_computation | custom fusion | flops 1179648 | bytes 7080192 | tf_op jit(solution)/shard_map/scatter-add | solution.py:29
  79.6 22.7 %copy.11 = bf16[48,64,24,64]{3,2,1,0:T(8,128)(2,1)} copy(bf16[48,64,24,64]{3,1,2,0:T(8,128)(2,1)} %scatter_fusion) | data formatting | bytes 18874368 | tf_op jit(solution)/shard_map/scatter-add | solution.py:29
  102.2 24.6 %reshape.73 = bf16[3072,1536]{1,0:T(8,128)(2,1)} reshape(bf16[48,64,24,64]{3,2,1,0:T(8,128)(2,1)} %copy.11) | data formatting | bytes 18874368 | tf_op jit(solution)/shard_map/reshape | solution.py:30
  126.8 9.2 %convolution_convert_fusion = bf16[3072,512]{1,0:T(8,128)(2,1)} fusion(bf16[3072,1536]{1,0:T(8,128)(2,1)} %reshape.73, bf16[1536,512]{1,0:T(8,128)(2,1)} %all-gather.3.cloned.1.call-done), kind=kOutput, calls=%fused_computation.1 | convolution fusion | flops 4833411072 | bytes 14155776 | tf_op jit(solution)/shard_map/dot_general | solution.py:31
  136.1 0.0 reduce-scatter.3.cloned.1.call-update
  136.1 0.0 all-gather.5.cloned.1.call-start
  136.1 77.7 %reduce-scatter.3.cloned.1.call-done = bf16[192,512]{1,0:T(8,128)(2,1)} async-done(((bf16[3072,512]{1,0:T(8,128)(2,1)}), bf16[192,512]{1,0:T(8,128)(2,1)}) %reduce-scatter.3.cloned.1.call-update) | async-done | bytes 196624 | tf_op jit(solution)/shard_map/reduce_scatter | solution.py:32
  213.9 0.0 copy-done
  213.9 2.0 multiply_convert_fusion.1
  215.9 0.0 copy-done.2
  215.9 1.0 convolution_convert_fusion.2
  216.9 0.0 all-gather.5.cloned.1.call-update
  216.9 0.0 all-reduce.2.cloned.1.call-start
  217.0 0.0 copy-done.3
  217.0 1.4 fusion.2
  218.4 0.0 all-reduce.2.cloned.1.call-update
  218.4 0.2 reduce-scatter.5.cloned.1.call-start
  218.7 49.5 %all-gather.5.cloned.1.call-done = bf16[3072,512]{1,0:T(8,128)(2,1)} async-done(((bf16[192,512]{1,0:T(8,128)(2,1)}), bf16[3072,512]{1,0:T(8,128)(2,1)}) %all-gather.5.cloned.1.call-update) | async-done | bytes 3145744 | tf_op jit(solution)/shard_map/all_gather | solution.py:45
  268.2 10.4 %convolution_convert_fusion.1 = bf16[1536,512]{1,0:T(8,128)(2,1)} fusion(bf16[3072,1536]{1,0:T(8,128)(2,1)} %reshape.73, bf16[3072,512]{1,0:T(8,128)(2,1)} %all-gather.5.cloned.1.call-done), kind=kOutput, calls=%fused_computation.3 | convolution fusion | flops 4832624640 | bytes 14155776 | tf_op jit(solution)/shard_map/dot_general | solution.py:52
  278.6 0.0 reduce-scatter.5.cloned.1.call-update
  278.6 140.3 %all-reduce.2.cloned.1.call-done = f32[512,512]{1,0:T(8,128)} async-done(((f32[512,512]{1,0:T(8,128)}), f32[512,512]{1,0:T(8,128)}) %all-reduce.2.cloned.1.call-update) | async-done | bytes 1048592 | tf_op jit(solution)/shard_map/psum | solution.py:50
  418.9 2.3 broadcast_multiply_fusion
  421.2 41.0 %reduce-scatter.5.cloned.1.call-done = bf16[192,512]{1,0:T(8,128)(2,1)} async-done(((bf16[1536,512]{1,0:T(8,128)(2,1)}), bf16[192,512]{1,0:T(8,128)(2,1)}) %reduce-scatter.5.cloned.1.call-update) | async-done | bytes 196624 | tf_op jit(solution)/shard_map/reduce_scatter | solution.py:56
  (6 shorter events, 0.0 us)
Async XLA Ops:
  7.2 206.7 %copy-start = (bf16[512,512]{1,0:T(8,128)(2,1)S(1)}, bf16[512,512]{1,0:T(8,128)(2,1)}, u32[]{:S(2)}) copy-start(bf16[512,512]{1,0:T(8,128)(2,1)} %param.8) | copy-start | bytes 1572868
  7.2 119.6 %all-gather.3.cloned.1.call-start = ((), (), s32[]{:S(2)}) async-start(), calls=%async_computation.2 | async-start | bytes 1769472 | tf_op jit(solution)/shard_map/all_gather | solution.py:27
  7.9 206.0 %reduce-scatter.3.cloned.1.call-start = ((), (), s32[]{:S(2)}) async-start(), calls=%async_computation.3 | async-start | bytes 3342336 | tf_op jit(solution)/shard_map/reduce_scatter | solution.py:32
  17.0 10.0 %copy-start.1 = (s32[1,1,2,288]{3,2,1,0:T(2,128)S(1)}, s32[1,1,2,288]{3,2,1,0:T(2,128)}, u32[]{:S(2)}) copy-start(s32[1,1,2,288]{3,2,1,0:T(2,128)} %param.10) | copy-start | bytes 6916
  136.1 79.8 %copy-start.2 = (bf16[192,512]{1,0:T(8,128)(2,1)S(1)}, bf16[192,512]{1,0:T(8,128)(2,1)}, u32[]{:S(2)}) copy-start(bf16[192,512]{1,0:T(8,128)(2,1)} %param.7) | copy-start | bytes 589828
  136.1 132.1 %all-gather.5.cloned.1.call-start = ((), (), s32[]{:S(2)}) async-start(), calls=%async_computation.5 | async-start | bytes 3342336 | tf_op jit(solution)/shard_map/all_gather | solution.py:45
  213.9 3.1 copy-start.3
  216.9 202.0 %all-reduce.2.cloned.1.call-start = ((), (), s32[]{:S(2)}) async-start(), calls=%async_computation.4 | async-start | bytes 2097152 | tf_op jit(solution)/shard_map/psum | solution.py:50
  218.4 243.8 %reduce-scatter.5.cloned.1.call-start = ((), (), s32[]{:S(2)}) async-start(), calls=%async_computation.6 | async-start | bytes 1769472 | tf_op jit(solution)/shard_map/reduce_scatter | solution.py:56
Sparse Core Ops, SparseCore 0:
  9.7 43.1 all-gather.2
  136.2 77.6 reduce-scatter.2
  217.1 51.0 all-gather.4
  273.4 145.4 all-reduce.1
  421.9 40.3 reduce-scatter.4
where the time goes:
time: 471 us; the launch traced here: 469 us
  waiting for transfers between devices  309 us (66%)
  local copies, waits for them, and re-layouts  68.8 us (15%)
  other arithmetic  51.7 us (11%)
  matrix products  24.1 us (5%)
  between operations  14.5 us (3%)
    psum x1, waiting for transfers between devices, per_device(): lax.psum(local_wgrad, ('row', 'col'))  140 us
    reduce_scatter x1, waiting for transfers between devices, per_device(): lax.psum_scatter(partial_agg.astype(jnp.bfloat16), 'col', scatter_dimensi...  77.7 us
    all_gather x1, waiting for transfers between devices, per_device(): grad_rows = lax.all_gather(grad_agg, 'col', axis=0, tiled=True)  49.5 us
    scatter-add x1, other arithmetic, per_device(): dense_tile = dense_tile.at[row_ids, :, col_ids, :].add(slot_vals)  45.5 us
    reduce_scatter x1, waiting for transfers between devices, per_device(): lax.psum_scatter(partial_grad.astype(jnp.bfloat16), 'row', scatter_dimens...  41 us
    reshape x1, local copies, waits for them, and re-layouts, per_device(): dense_tile = dense_tile.reshape(block_rows * side, block_cols * side)  24.6 us
    scatter-add x1, local copies, waits for them, and re-layouts, per_device(): dense_tile = dense_tile.at[row_ids, :, col_ids, :].add(slot_vals)  22.7 us
    dot_general x1, matrix products, per_device(): lax.dot_general(dense_tile, grad_rows, (((0,), (0,)), ((), ())), preferre...  10.4 us
  transfers between devices with their start and end apart: 5, of which 4 were waited for; matrix products, arithmetic and copies ran while one was open for 28% of the time, Pallas kernels for 0%

commit v1 on v0

v1 whole, which is shorter than its diff:
```python
import math

import jax
import jax.numpy as jnp
from jax import lax
from jax.experimental import pallas as pl
from jax.experimental.pallas import tpu as pltpu
from jax.sharding import Mesh, PartitionSpec as P

AXES = ("y_lo", "z", "y_hi", "x", "core")
SIZES = (2, 4, 2, 4, 2)
ROW = ("y_lo", "z")
CHIP = ("y_hi", "x")
COL = ("y_hi", "x", "core")
SIDE = 64
PEERS = 8
OWN = 192
WIDTH = 512


def shift(array, axes, count, step):
    return lax.ppermute(array, axes, [(i, (i + step) % count) for i in range(count)])


def build_kernel(coords, counts, values, dense):
    rows, cols = dense.shape
    per_owner = OWN // SIDE
    me_row = lax.axis_index(ROW)
    me_chip = lax.axis_index(CHIP)
    me_core = lax.axis_index("core")

    @pl.loop(0, rows // SIDE)
    def _(r):
        dense[pl.ds(pl.multiple_of(r * SIDE, SIDE), SIDE), :] = jnp.zeros((SIDE, cols), dense.dtype)

    count = counts[0, 0]
    lane = lax.broadcasted_iota(jnp.int32, (SIDE, 2 * SIDE), 1)

    @pl.loop(0, (count + 15) // 16)
    def _(g):
        group = values[0, 0, pl.ds(pl.multiple_of(g * 16, 16), 16), :]
        pairs = group.astype(jnp.float32).reshape(16, SIDE // 2, 2 * SIDE)
        for k in range(16):
            slot = g * 16 + k
            live = slot < count
            block_row = jnp.where(live, coords[0, 0, 0, slot], 0)
            block_col = jnp.where(live, coords[0, 0, 1, slot], 0)
            owner = block_row // per_owner
            side = (owner + me_core) & 1
            chip = ((owner >> 1) - me_chip) & (PEERS - 1)
            at_row = (side * PEERS + chip) * per_owner + block_row % per_owner
            source = (me_row - block_col // per_owner) & (PEERS - 1)
            at_col = source * per_owner + block_col % per_owner
            odd = (at_col & 1) == 1
            plain = pairs[k]
            turned = pltpu.roll(plain, SIDE, 1)
            block = jnp.concatenate(
                [jnp.where(odd, turned, plain), jnp.where(odd, plain, turned)], axis=0
            ).astype(dense.dtype)
            first = jnp.where(live, (at_col & 1) * SIDE, 4 * SIDE)
            mask = (lane >= first) & (lane < first + SIDE)
            place = dense.at[
                pl.ds(pl.multiple_of(at_row * SIDE, SIDE), SIDE),
                pl.ds(pl.multiple_of((at_col >> 1) * 2 * SIDE, 2 * SIDE), 2 * SIDE),
            ]
            place[...] = jnp.where(mask, block, place[...])


def build(coords, counts, values):
    return pl.pallas_call(
        build_kernel,
        out_shape=jax.ShapeDtypeStruct((2 * PEERS * OWN, PEERS * OWN), jnp.bfloat16),
        in_specs=[pl.BlockSpec(memory_space=pltpu.SMEM)] * 2 + [pl.BlockSpec(memory_space=pltpu.VMEM)],
        out_specs=pl.BlockSpec(memory_space=pltpu.VMEM),
        compiler_params=pltpu.CompilerParams(vmem_limit_bytes=24 << 20),
        cost_estimate=pl.CostEstimate(flops=0, bytes_accessed=30 << 20, transcendentals=0),
        name="build",
    )(coords, counts, values)


def middle_kernel(*refs):
    parts = refs[:PEERS]
    out_grad, weight, activations, grad_agg, local_wgrad = refs[PEERS:]
    total = parts[0][...].astype(jnp.float32)
    for part in parts[1:]:
        total = total + part[...].astype(jnp.float32)
    aggregated = total.astype(jnp.bfloat16)
    at = lax.broadcasted_iota(jnp.int32, (OWN, OWN), 0)
    to = lax.broadcasted_iota(jnp.int32, (OWN, OWN), 1)
    half = SIDE // 2
    turn = jnp.where(
        (at // SIDE == to // SIDE) & (to % SIDE == 2 * (at % half) + (at % SIDE) // half), 1.0, 0.0
    ).astype(jnp.bfloat16)
    w = weight[...]
    pre_act = jnp.dot(aggregated, w, preferred_element_type=jnp.float32)
    sig = jax.nn.sigmoid(pre_act)
    act = (pre_act * sig).astype(jnp.bfloat16)
    activations[...] = lax.dot_general(
        turn, act, (((0,), (0,)), ((), ())), preferred_element_type=jnp.float32
    ).astype(jnp.bfloat16)
    cotangent = jnp.dot(turn, out_grad[...], preferred_element_type=jnp.float32)
    grad_pre = (cotangent * sig * (1.0 + pre_act * (1.0 - sig))).astype(jnp.bfloat16)
    grad_agg[...] = lax.dot_general(
        grad_pre, w, (((1,), (1,)), ((), ())), preferred_element_type=jnp.float32
    ).astype(jnp.bfloat16)
    local_wgrad[...] = lax.dot_general(
        aggregated, grad_pre, (((0,), (0,)), ((), ())), preferred_element_type=jnp.float32
    ).astype(local_wgrad.dtype)


def middle(parts, out_grad, weight):
    vmem = pl.BlockSpec(memory_space=pltpu.VMEM)
    return pl.pallas_call(
        middle_kernel,
        out_shape=(
            jax.ShapeDtypeStruct((OWN, WIDTH), jnp.bfloat16),
            jax.ShapeDtypeStruct((OWN, WIDTH), jnp.bfloat16),
            jax.ShapeDtypeStruct((WIDTH, WIDTH), jnp.bfloat16),
        ),
        in_specs=[vmem] * (PEERS + 2),
        out_specs=(vmem,) * 3,
        compiler_params=pltpu.CompilerParams(vmem_limit_bytes=24 << 20),
        cost_estimate=pl.CostEstimate(flops=2 * 3 * OWN * WIDTH * WIDTH, bytes_accessed=4 << 20, transcendentals=0),
        name="middle",
    )(*parts, out_grad, weight)


def fsum(parts):
    total = parts[0].astype(jnp.float32)
    for part in parts[1:]:
        total = total + part.astype(jnp.float32)
    return total


def per_device(features, out_grad, weight, block_values, block_coords, block_counts):
    panel = [features] + [shift(features, ROW, PEERS, k) for k in range(1, PEERS)]
    dense = build(block_coords, block_counts, block_values)
    panel = jnp.concatenate(panel, axis=0)

    half = PEERS * OWN
    partial_agg = jnp.dot(dense, panel, preferred_element_type=jnp.float32).astype(jnp.bfloat16)
    other = lax.ppermute(partial_agg[half:], "core", [(0, 1), (1, 0)])
    parts = []
    for k in range(PEERS):
        rows = slice(k * OWN, (k + 1) * OWN)
        both = (partial_agg[rows].astype(jnp.float32) + other[rows].astype(jnp.float32)).astype(jnp.bfloat16)
        parts.append(shift(both, CHIP, PEERS, k) if k else both)

    activations, grad_agg, local_wgrad = middle(parts, out_grad, weight)

    mine = [grad_agg] + [shift(grad_agg, CHIP, PEERS, PEERS - p) for p in range(1, PEERS)]
    mine = jnp.concatenate(mine, axis=0)
    theirs = lax.ppermute(mine, "core", [(0, 1), (1, 0)])
    grad_rows = jnp.concatenate([mine, theirs], axis=0)
    partial_grad = lax.dot_general(
        dense, grad_rows, (((0,), (0,)), ((), ())), preferred_element_type=jnp.float32
    ).astype(jnp.bfloat16)
    pieces = []
    for p in range(PEERS):
        piece = partial_grad[p * OWN : (p + 1) * OWN]
        pieces.append(shift(piece, ROW, PEERS, PEERS - p) if p else piece)
    feature_grad = fsum(pieces).astype(jnp.bfloat16)

    slices = lax.all_to_all(local_wgrad.reshape(16, 32, WIDTH), COL, 0, 0)
    summed = fsum([slices[k] for k in range(16)]).astype(jnp.bfloat16)
    rows_sum = [summed] + [shift(summed, ROW, PEERS, k) for k in range(1, PEERS)]
    summed = fsum(rows_sum).astype(jnp.bfloat16)
    weight_grad = lax.all_to_all(jnp.broadcast_to(summed[None], (16, 32, WIDTH)), COL, 0, 0)
    total_nodes = OWN * 128
    weight_grad = weight_grad.reshape(WIDTH, WIDTH).astype(jnp.float32) * jnp.float32(1.0 / math.sqrt(total_nodes))
    return (activations, weight_grad, feature_grad)


def solution(mesh):
    fine = Mesh(mesh.devices.reshape(SIZES), AXES)
    return jax.shard_map(
        per_device,
        mesh=fine,
        in_specs=(
            P(COL + ROW, None),
            P(ROW + COL, None),
            P(),
            P(ROW, COL, None, None),
            P(ROW, COL, None, None),
            P(ROW, COL),
        ),
        out_specs=(P(ROW + COL, None), P(), P(COL + ROW, None)),
        check_vma=False,
    )
```

time: 471 us -> 180 us (0.38)
  waiting for transfers between devices: 309 us -> 45.7 us
  starting transfers between devices: 0.38 us -> 82.7 us
  local copies, waits for them, and re-layouts: 68.8 us -> 13.1 us
  other arithmetic: 51.7 us -> 2.68 us
  blocking collectives: 0 us -> 15 us
  between operations: 14.5 us -> 1.54 us
  matrix products: 24.1 us -> 14.8 us
    psum x1 -> x0, waiting for transfers between devices: 140 us -> none  [per_device(): lax.psum(local_wgrad, ('row', 'col'))]
    reduce_scatter x2 -> x0, waiting for transfers between devices: 119 us -> none  [the longest x1 77.7 us: per_device(): lax.psum_scatter(partial_agg.astype(jnp.bfloat16), 'col', scatter_dimensi...]
    ppermute x0 -> x37, starting transfers between devices: none -> 79.1 us  [the longest x35 79 us: shift(): lax.ppermute(array, axes, [(i, (i + step) % count) for i in range(count)])]
    all_gather x2 -> x0, waiting for transfers between devices: 49.5 us -> none  [the longest x1 49.5 us: per_device(): grad_rows = lax.all_gather(grad_agg, 'col', axis=0, tiled=True)]
    ppermute x0 -> x37, waiting for transfers between devices: none -> 45.7 us  [the longest x35 42.3 us: shift(): lax.ppermute(array, axes, [(i, (i + step) % count) for i in range(count)])]
    scatter-add x1 -> x0, other arithmetic: 45.5 us -> none  [per_device(): dense_tile = dense_tile.at[row_ids, :, col_ids, :].add(slot_vals)]
    reshape x1 -> x0, local copies, waits for them, and re-layouts: 24.6 us -> none  [per_device(): dense_tile = dense_tile.reshape(block_rows * side, block_cols * side)]
    scatter-add x1 -> x0, local copies, waits for them, and re-layouts: 22.7 us -> none  [per_device(): dense_tile = dense_tile.at[row_ids, :, col_ids, :].add(slot_vals)]
  transfers between devices with their start and end apart: 5 -> 38, of which waited for: 4 -> 14; matrix products, arithmetic and copies ran while one was open for 28% -> 11% of each run, Pallas kernels for 0% -> 2%
where the time goes in v1:
time: 180 us; the launch traced here: 179 us
  starting transfers between devices  82.7 us (46%)
  waiting for transfers between devices  45.7 us (25%)
  blocking collectives  15 us (8%)
  matrix products  14.8 us (8%)
  local copies, waits for them, and re-layouts  13.1 us (7%)
  Pallas kernels  4.04 us (2%)
  other arithmetic  2.68 us (1%)
    ppermute x35, starting transfers between devices, shift(): lax.ppermute(array, axes, [(i, (i + step) % count) for i in range(count)])  79 us
    ppermute x35, waiting for transfers between devices, shift(): lax.ppermute(array, axes, [(i, (i + step) % count) for i in range(count)])  42.3 us
    all_to_all x1, blocking collectives, per_device(): slices = lax.all_to_all(local_wgrad.reshape(16, 32, WIDTH), COL, 0, 0)  15 us
    dot_general x1, matrix products, per_device(): lax.dot_general(dense, grad_rows, (((0,), (0,)), ((), ())), preferred_ele...  9.52 us
    unnamed x28, local copies, waits for them, and re-layouts  9.17 us
    dot_general x1, matrix products, per_device(): jnp.dot(dense, panel, preferred_element_type=jnp.float32)  5.25 us
  transfers between devices with their start and end apart: 38, of which 14 were waited for; matrix products, arithmetic and copies ran while one was open for 11% of the time, Pallas kernels for 2%

profile of v1, /device:TPU:0, one launch (start us, length us, event | category | flops | bytes accessed | tf_op | source)
XLA Modules:
  0.0 179.5 jit_solution(13327187068501897041)
XLA Ops:
  0.6 2.1 %collective-permute-start = (bf16[192,512]{1,0:T(8,128)(2,1)}, bf16[192,512]{1,0:T(8,128)(2,1)S(1)}, u32[]{:S(2)}, u32[]{:S(2)}) collective-permute-start(bf16[192,512]{1,0:T(8,128)(2,1)} %param.6), channel_id=1, source_target_pairs={{0,16},{16,32},{32,48},{48,64},{64,80},{80,96},{96,112},{112,0},{1... | collective-permute-start | bytes 589832 | tf_op jit(solution)/shard_map/ppermute | solution.py:22
  2.7 3.6 %collective-permute-start.1 = (bf16[192,512]{1,0:T(8,128)(2,1)}, bf16[192,512]{1,0:T(8,128)(2,1)S(1)}, u32[]{:S(2)}, u32[]{:S(2)}) collective-permute-start(bf16[192,512]{1,0:T(8,128)(2,1)} %param.6), channel_id=1, source_target_pairs={{0,32},{16,48},{32,64},{48,80},{64,96},{80,112},{96,0},{112,16},{1... | collective-permute-start | bytes 589832 | tf_op jit(solution)/shard_map/ppermute | solution.py:22
  6.3 2.0 %collective-permute-start.2 = (bf16[192,512]{1,0:T(8,128)(2,1)}, bf16[192,512]{1,0:T(8,128)(2,1)S(1)}, u32[]{:S(2)}, u32[]{:S(2)}) collective-permute-start(bf16[192,512]{1,0:T(8,128)(2,1)} %param.6), channel_id=1, source_target_pairs={{0,48},{16,64},{32,80},{48,96},{64,112},{80,0},{96,16},{112,32},{1... | collective-permute-start | bytes 589832 | tf_op jit(solution)/shard_map/ppermute | solution.py:22
  8.8 2.0 %collective-permute-start.4 = (bf16[192,512]{1,0:T(8,128)(2,1)}, bf16[192,512]{1,0:T(8,128)(2,1)S(1)}, u32[]{:S(2)}, u32[]{:S(2)}) collective-permute-start(bf16[192,512]{1,0:T(8,128)(2,1)} %param.6), channel_id=1, source_target_pairs={{0,80},{16,96},{32,112},{48,0},{64,16},{80,32},{96,48},{112,64},{1... | collective-permute-start | bytes 589832 | tf_op jit(solution)/shard_map/ppermute | solution.py:22
  13.8 2.8 %build.1 = bf16[3072,1536]{1,0:T(8,128)(2,1)S(1)} custom-call(s32[1,1,2,288]{3,2,1,0:T(2,128)S(1)} %copy-done.4, s32[1,1]{1,0:T(1,128)S(6)} %copy.31.counts, bf16[1,1,288,4096]{3,2,1,0:T(8,128)(2,1)S(1)} %copy-done.1), custom_call_target="tpu_custom_call" | custom-call | bytes 31457280 | tf_op jit(solution)/shard_map/build/pallas_call | solution.py:70
  16.9 4.7 %collective-permute-start.6 = (bf16[192,512]{1,0:T(8,128)(2,1)S(1)}, bf16[192,512]{1,0:T(8,128)(2,1)S(1)}, u32[]{:S(2)}, u32[]{:S(2)}) collective-permute-start(bf16[192,512]{1,0:T(8,128)(2,1)S(1)} %copy-done.5), channel_id=1, source_target_pairs={{0,112},{16,0},{32,16},{48,32},{64,48},{80,64},{96,80},{112,96},{1... | collective-permute-start | bytes 589832 | tf_op jit(solution)/shard_map/ppermute | solution.py:22
  21.7 8.2 %collective-permute-done.5 = bf16[192,512]{1,0:T(8,128)(2,1)S(1)} collective-permute-done((bf16[192,512]{1,0:T(8,128)(2,1)S(1)}, bf16[192,512]{1,0:T(8,128)(2,1)S(1)}, u32[]{:S(2)}, u32[]{:S(2)}) %collective-permute-start.5) | collective-permute-done | bytes 196640 | tf_op jit(solution)/shard_map/ppermute | solution.py:22
  30.3 5.3 %convolution_convert_fusion = bf16[3072,512]{1,0:T(8,128)(2,1)S(1)} fusion(bf16[3072,1536]{1,0:T(8,128)(2,1)S(1)} %build.1, bf16[1536,512]{1,0:T(8,128)(2,1)S(1)} %constant_dynamic-update-slice_fusion), kind=kOutput, calls=%fused_computation | convolution fusion | flops 4833411072 | bytes 14155776 | tf_op jit(solution)/shard_map/dot_general | solution.py:141
  35.8 3.4 %collective-permute-done.7 = bf16[1536,512]{1,0:T(8,128)(2,1)S(1)} collective-permute-done((bf16[1536,512]{1,0:T(8,128)(2,1)S(1)}, bf16[1536,512]{1,0:T(8,128)(2,1)S(1)}, u32[]{:S(2)}, u32[]{:S(2)}) %collective-permute-start.7) | collective-permute-done | bytes 1572896 | tf_op jit(solution)/shard_map/ppermute | solution.py:142
  39.7 2.1 %collective-permute-start.10 = (bf16[192,512]{1,0:T(8,128)(2,1)S(1)}, bf16[192,512]{1,0:T(8,128)(2,1)S(1)}, u32[]{:S(2)}, u32[]{:S(2)}) collective-permute-start(bf16[192,512]{1,0:T(8,128)(2,1)S(1)} %get-tuple-element.13), channel_id=1, source_target_pairs={{0,6},{2,8},{4,10},{6,12},{8,14},{10,0},{12,2},{14,4},{1,7},{3,9},... | collective-permute-start | bytes 589832 | tf_op jit(solution)/shard_map/ppermute | solution.py:22
  41.8 3.6 %collective-permute-start.11 = (bf16[192,512]{1,0:T(8,128)(2,1)S(1)}, bf16[192,512]{1,0:T(8,128)(2,1)S(1)}, u32[]{:S(2)}, u32[]{:S(2)}) collective-permute-start(bf16[192,512]{1,0:T(8,128)(2,1)S(1)} %get-tuple-element.12), channel_id=1, source_target_pairs={{0,8},{2,10},{4,12},{6,14},{8,0},{10,2},{12,4},{14,6},{1,9},{3,11}... | collective-permute-start | bytes 589832 | tf_op jit(solution)/shard_map/ppermute | solution.py:22
  45.6 3.7 %collective-permute-start.13 = (bf16[192,512]{1,0:T(8,128)(2,1)S(1)}, bf16[192,512]{1,0:T(8,128)(2,1)S(1)}, u32[]{:S(2)}, u32[]{:S(2)}) collective-permute-start(bf16[192,512]{1,0:T(8,128)(2,1)S(1)} %get-tuple-element.10), channel_id=1, source_target_pairs={{0,12},{2,14},{4,0},{6,2},{8,4},{10,6},{12,8},{14,10},{1,13},{3,15... | collective-permute-start | bytes 589832 | tf_op jit(solution)/shard_map/ppermute | solution.py:22
  49.3 2.8 %collective-permute-start.14 = (bf16[192,512]{1,0:T(8,128)(2,1)S(1)}, bf16[192,512]{1,0:T(8,128)(2,1)S(1)}, u32[]{:S(2)}, u32[]{:S(2)}) collective-permute-start(bf16[192,512]{1,0:T(8,128)(2,1)S(1)} %get-tuple-element.9), channel_id=1, source_target_pairs={{0,14},{2,0},{4,2},{6,4},{8,6},{10,8},{12,10},{14,12},{1,15},{3,1}... | collective-permute-start | bytes 589832 | tf_op jit(solution)/shard_map/ppermute | solution.py:22
  53.6 10.4 %collective-permute-start.9 = (bf16[192,512]{1,0:T(8,128)(2,1)S(1)}, bf16[192,512]{1,0:T(8,128)(2,1)S(1)}, u32[]{:S(2)}, u32[]{:S(2)}) collective-permute-start(bf16[192,512]{1,0:T(8,128)(2,1)S(1)} %get-tuple-element.14), channel_id=1, source_target_pairs={{0,4},{2,6},{4,8},{6,10},{8,12},{10,14},{12,0},{14,2},{1,5},{3,7},... | collective-permute-start | bytes 589832 | tf_op jit(solution)/shard_map/ppermute | solution.py:22
  64.1 7.8 %collective-permute-done.9.refs_2_ = bf16[192,512]{1,0:T(8,128)(2,1)S(1)} collective-permute-done((bf16[192,512]{1,0:T(8,128)(2,1)S(1)}, bf16[192,512]{1,0:T(8,128)(2,1)S(1)}, u32[]{:S(2)}, u32[]{:S(2)}) %collective-permute-start.9) | collective-permute-done | bytes 196640 | tf_op jit(solution)/shard_map/ppermute | solution.py:22
  74.3 2.5 %collective-permute-start.23 = (bf16[192,512]{1,0:T(8,128)(2,1)S(1)}, bf16[192,512]{1,0:T(8,128)(2,1)S(1)}, u32[]{:S(2)}, u32[]{:S(2)}) collective-permute-start(bf16[192,512]{1,0:T(8,128)(2,1)S(1)} %get-tuple-element.8), channel_id=1, source_target_pairs={{0,12},{2,14},{4,0},{6,2},{8,4},{10,6},{12,8},{14,10},{1,13},{3,15... | collective-permute-start | bytes 589832 | tf_op jit(solution)/shard_map/ppermute | solution.py:22
  78.0 2.7 %collective-permute-start.25 = (bf16[192,512]{1,0:T(8,128)(2,1)S(1)}, bf16[192,512]{1,0:T(8,128)(2,1)S(1)}, u32[]{:S(2)}, u32[]{:S(2)}) collective-permute-start(bf16[192,512]{1,0:T(8,128)(2,1)S(1)} %get-tuple-element.8), channel_id=1, source_target_pairs={{0,8},{2,10},{4,12},{6,14},{8,0},{10,2},{12,4},{14,6},{1,9},{3,11}... | collective-permute-start | bytes 589832 | tf_op jit(solution)/shard_map/ppermute | solution.py:22
  81.7 4.7 %collective-permute-start.27 = (bf16[192,512]{1,0:T(8,128)(2,1)S(1)}, bf16[192,512]{1,0:T(8,128)(2,1)S(1)}, u32[]{:S(2)}, u32[]{:S(2)}) collective-permute-start(bf16[192,512]{1,0:T(8,128)(2,1)S(1)} %get-tuple-element.8), channel_id=1, source_target_pairs={{0,4},{2,6},{4,8},{6,10},{8,12},{10,14},{12,0},{14,2},{1,5},{3,7},... | collective-permute-start | bytes 589832 | tf_op jit(solution)/shard_map/ppermute | solution.py:22
  87.1 6.9 %collective-permute-start.28 = (bf16[192,512]{1,0:T(8,128)(2,1)S(1)}, bf16[192,512]{1,0:T(8,128)(2,1)S(1)}, u32[]{:S(2)}, u32[]{:S(2)}) collective-permute-start(bf16[192,512]{1,0:T(8,128)(2,1)S(1)} %get-tuple-element.8), channel_id=1, source_target_pairs={{0,2},{2,4},{4,6},{6,8},{8,10},{10,12},{12,14},{14,0},{1,3},{3,5},... | collective-permute-start | bytes 589832 | tf_op jit(solution)/shard_map/ppermute | solution.py:22
  95.4 2.4 %collective-permute-done.25 = bf16[192,512]{1,0:T(8,128)(2,1)S(1)} collective-permute-done((bf16[192,512]{1,0:T(8,128)(2,1)S(1)}, bf16[192,512]{1,0:T(8,128)(2,1)S(1)}, u32[]{:S(2)}, u32[]{:S(2)}) %collective-permute-start.25) | collective-permute-done | bytes 196640 | tf_op jit(solution)/shard_map/ppermute | solution.py:22
  102.5 15.0 %all_to_all.10 = bf16[16,32,512]{2,1,0:T(8,128)(2,1)S(1)} all-to-all(bf16[16,32,512]{2,1,0:T(8,128)(2,1)S(1)} %bitcast.17), channel_id=1, replica_groups=mesh['y_lo'=2,'z'=4,'y_hi'=2,'x'=4,'core'=2] {'y_hi','x','core'}, dimensions={0} | all-to-all | bytes 1048576 | tf_op jit(solution)/shard_map/all_to_all | solution.py:164
  118.9 3.0 %collective-permute-start.16 = (bf16[32,512]{1,0:T(8,128)(2,1)S(1)}, bf16[32,512]{1,0:T(8,128)(2,1)S(1)}, u32[]{:S(2)}, u32[]{:S(2)}) collective-permute-start(bf16[32,512]{1,0:T(8,128)(2,1)S(1)} %fusion), channel_id=1, source_target_pairs={{0,32},{16,48},{32,64},{48,80},{64,96},{80,112},{96,0},{112,16},{1... | collective-permute-start | bytes 98312 | tf_op jit(solution)/shard_map/ppermute | solution.py:22
  123.7 2.1 %collective-permute-start.19 = (bf16[32,512]{1,0:T(8,128)(2,1)S(1)}, bf16[32,512]{1,0:T(8,128)(2,1)S(1)}, u32[]{:S(2)}, u32[]{:S(2)}) collective-permute-start(bf16[32,512]{1,0:T(8,128)(2,1)S(1)} %fusion), channel_id=1, source_target_pairs={{0,80},{16,96},{32,112},{48,0},{64,16},{80,32},{96,48},{112,64},{1... | collective-permute-start | bytes 98312 | tf_op jit(solution)/shard_map/ppermute | solution.py:22
  127.8 2.0 %collective-permute-start.21 = (bf16[32,512]{1,0:T(8,128)(2,1)S(1)}, bf16[32,512]{1,0:T(8,128)(2,1)S(1)}, u32[]{:S(2)}, u32[]{:S(2)}) collective-permute-start(bf16[32,512]{1,0:T(8,128)(2,1)S(1)} %fusion), channel_id=1, source_target_pairs={{0,112},{16,0},{32,16},{48,32},{64,48},{80,64},{96,80},{112,96},{1... | collective-permute-start | bytes 98312 | tf_op jit(solution)/shard_map/ppermute | solution.py:22
  132.6 3.6 %all-to-all-start.1 = ((bf16[16,32,512]{2,1,0:T(8,128)(2,1)}), bf16[16,32,512]{2,1,0:T(8,128)(2,1)S(1)}, u32[]{:S(2)}, u32[]{:S(2)}) async-start(bf16[16,32,512]{2,1,0:T(8,128)(2,1)} %broadcast_in_dim.2), calls=%async_computation.1 | async-start | bytes 1048576 | tf_op jit(solution)/shard_map/all_to_all | solution.py:168
  137.6 9.5 %convolution_convert_fusion.1 = bf16[1536,512]{1,0:T(8,128)(2,1)S(1)} fusion(bf16[3072,1536]{1,0:T(8,128)(2,1)} %copy-done, bf16[3072,512]{1,0:T(8,128)(2,1)} %constant_dynamic-update-slice_fusion.16), kind=kOutput, calls=%fused_computation.1 | convolution fusion | flops 4832624640 | bytes 14155776 | tf_op jit(solution)/shard_map/dot_general | solution.py:155
  148.1 4.1 %collective-permute-start.30 = (bf16[192,512]{1,0:T(8,128)(2,1)S(1)}, bf16[192,512]{1,0:T(8,128)(2,1)S(1)}, u32[]{:S(2)}, u32[]{:S(2)}) collective-permute-start(bf16[192,512]{1,0:T(8,128)(2,1)S(1)} %get-tuple-element.17), channel_id=1, source_target_pairs={{0,112},{16,0},{32,16},{48,32},{64,48},{80,64},{96,80},{112,96},{1... | collective-permute-start | bytes 589832 | tf_op jit(solution)/shard_map/ppermute | solution.py:22
  156.3 4.0 %collective-permute-done.30 = bf16[192,512]{1,0:T(8,128)(2,1)S(1)} collective-permute-done((bf16[192,512]{1,0:T(8,128)(2,1)S(1)}, bf16[192,512]{1,0:T(8,128)(2,1)S(1)}, u32[]{:S(2)}, u32[]{:S(2)}) %collective-permute-start.30) | collective-permute-done | bytes 196640 | tf_op jit(solution)/shard_map/ppermute | solution.py:22
  160.3 6.7 %collective-permute-done.31 = bf16[192,512]{1,0:T(8,128)(2,1)S(1)} collective-permute-done((bf16[192,512]{1,0:T(8,128)(2,1)S(1)}, bf16[192,512]{1,0:T(8,128)(2,1)S(1)}, u32[]{:S(2)}, u32[]{:S(2)}) %collective-permute-start.31) | collective-permute-done | bytes 196640 | tf_op jit(solution)/shard_map/ppermute | solution.py:22
  168.2 3.2 %collective-permute-done.32 = bf16[192,512]{1,0:T(8,128)(2,1)S(1)} collective-permute-done((bf16[192,512]{1,0:T(8,128)(2,1)}, bf16[192,512]{1,0:T(8,128)(2,1)S(1)}, u32[]{:S(2)}, u32[]{:S(2)}) %collective-permute-start.32) | collective-permute-done | bytes 196640 | tf_op jit(solution)/shard_map/ppermute | solution.py:22
  171.4 4.3 %collective-permute-done.33 = bf16[192,512]{1,0:T(8,128)(2,1)S(1)} collective-permute-done((bf16[192,512]{1,0:T(8,128)(2,1)}, bf16[192,512]{1,0:T(8,128)(2,1)S(1)}, u32[]{:S(2)}, u32[]{:S(2)}) %collective-permute-start.33) | collective-permute-done | bytes 196640 | tf_op jit(solution)/shard_map/ppermute | solution.py:22
  176.1 2.6 %collective-permute-done.36 = bf16[192,512]{1,0:T(8,128)(2,1)S(1)} collective-permute-done((bf16[192,512]{1,0:T(8,128)(2,1)}, bf16[192,512]{1,0:T(8,128)(2,1)S(1)}, u32[]{:S(2)}, u32[]{:S(2)}) %collective-permute-start.36) | collective-permute-done | bytes 196640 | tf_op jit(solution)/shard_map/ppermute | solution.py:22
  (88 shorter events, 34.3 us)
Async XLA Ops:
  0.6 16.0 %collective-permute-start = (bf16[192,512]{1,0:T(8,128)(2,1)}, bf16[192,512]{1,0:T(8,128)(2,1)S(1)}, u32[]{:S(2)}, u32[]{:S(2)}) collective-permute-start(bf16[192,512]{1,0:T(8,128)(2,1)} %param.6), channel_id=1, source_target_pairs={{0,16},{16,32},{32,48},{48,64},{64,80},{80,96},{96,112},{112,0},{1... | collective-permute-start | bytes 589832 | tf_op jit(solution)/shard_map/ppermute | solution.py:22
  2.7 14.2 %collective-permute-start.1 = (bf16[192,512]{1,0:T(8,128)(2,1)}, bf16[192,512]{1,0:T(8,128)(2,1)S(1)}, u32[]{:S(2)}, u32[]{:S(2)}) collective-permute-start(bf16[192,512]{1,0:T(8,128)(2,1)} %param.6), channel_id=1, source_target_pairs={{0,32},{16,48},{32,64},{48,80},{64,96},{80,112},{96,0},{112,16},{1... | collective-permute-start | bytes 589832 | tf_op jit(solution)/shard_map/ppermute | solution.py:22
  6.3 15.3 %collective-permute-start.2 = (bf16[192,512]{1,0:T(8,128)(2,1)}, bf16[192,512]{1,0:T(8,128)(2,1)S(1)}, u32[]{:S(2)}, u32[]{:S(2)}) collective-permute-start(bf16[192,512]{1,0:T(8,128)(2,1)} %param.6), channel_id=1, source_target_pairs={{0,48},{16,64},{32,80},{48,96},{64,112},{80,0},{96,16},{112,32},{1... | collective-permute-start | bytes 589832 | tf_op jit(solution)/shard_map/ppermute | solution.py:22
  8.3 13.3 %collective-permute-start.3 = (bf16[192,512]{1,0:T(8,128)(2,1)}, bf16[192,512]{1,0:T(8,128)(2,1)S(1)}, u32[]{:S(2)}, u32[]{:S(2)}) collective-permute-start(bf16[192,512]{1,0:T(8,128)(2,1)} %param.6), channel_id=1, source_target_pairs={{0,64},{16,80},{32,96},{48,112},{64,0},{80,16},{96,32},{112,48},{1... | collective-permute-start | bytes 589832 | tf_op jit(solution)/shard_map/ppermute | solution.py:22
  8.8 12.9 %collective-permute-start.4 = (bf16[192,512]{1,0:T(8,128)(2,1)}, bf16[192,512]{1,0:T(8,128)(2,1)S(1)}, u32[]{:S(2)}, u32[]{:S(2)}) collective-permute-start(bf16[192,512]{1,0:T(8,128)(2,1)} %param.6), channel_id=1, source_target_pairs={{0,80},{16,96},{32,112},{48,0},{64,16},{80,32},{96,48},{112,64},{1... | collective-permute-start | bytes 589832 | tf_op jit(solution)/shard_map/ppermute | solution.py:22
  16.7 13.2 %collective-permute-start.5 = (bf16[192,512]{1,0:T(8,128)(2,1)S(1)}, bf16[192,512]{1,0:T(8,128)(2,1)S(1)}, u32[]{:S(2)}, u32[]{:S(2)}) collective-permute-start(bf16[192,512]{1,0:T(8,128)(2,1)S(1)} %copy-done.5), channel_id=1, source_target_pairs={{0,96},{16,112},{32,0},{48,16},{64,32},{80,48},{96,64},{112,80},{1... | collective-permute-start | bytes 589832 | tf_op jit(solution)/shard_map/ppermute | solution.py:22
  16.9 13.4 %collective-permute-start.6 = (bf16[192,512]{1,0:T(8,128)(2,1)S(1)}, bf16[192,512]{1,0:T(8,128)(2,1)S(1)}, u32[]{:S(2)}, u32[]{:S(2)}) collective-permute-start(bf16[192,512]{1,0:T(8,128)(2,1)S(1)} %copy-done.5), channel_id=1, source_target_pairs={{0,112},{16,0},{32,16},{48,32},{64,48},{80,64},{96,80},{112,96},{1... | collective-permute-start | bytes 589832 | tf_op jit(solution)/shard_map/ppermute | solution.py:22
  39.7 12.4 %collective-permute-start.10 = (bf16[192,512]{1,0:T(8,128)(2,1)S(1)}, bf16[192,512]{1,0:T(8,128)(2,1)S(1)}, u32[]{:S(2)}, u32[]{:S(2)}) collective-permute-start(bf16[192,512]{1,0:T(8,128)(2,1)S(1)} %get-tuple-element.13), channel_id=1, source_target_pairs={{0,6},{2,8},{4,10},{6,12},{8,14},{10,0},{12,2},{14,4},{1,7},{3,9},... | collective-permute-start | bytes 589832 | tf_op jit(solution)/shard_map/ppermute | solution.py:22
  41.8 11.8 %collective-permute-start.11 = (bf16[192,512]{1,0:T(8,128)(2,1)S(1)}, bf16[192,512]{1,0:T(8,128)(2,1)S(1)}, u32[]{:S(2)}, u32[]{:S(2)}) collective-permute-start(bf16[192,512]{1,0:T(8,128)(2,1)S(1)} %get-tuple-element.12), channel_id=1, source_target_pairs={{0,8},{2,10},{4,12},{6,14},{8,0},{10,2},{12,4},{14,6},{1,9},{3,11}... | collective-permute-start | bytes 589832 | tf_op jit(solution)/shard_map/ppermute | solution.py:22
  45.3 18.7 %collective-permute-start.12 = (bf16[192,512]{1,0:T(8,128)(2,1)S(1)}, bf16[192,512]{1,0:T(8,128)(2,1)S(1)}, u32[]{:S(2)}, u32[]{:S(2)}) collective-permute-start(bf16[192,512]{1,0:T(8,128)(2,1)S(1)} %get-tuple-element.11), channel_id=1, source_target_pairs={{0,10},{2,12},{4,14},{6,0},{8,2},{10,4},{12,6},{14,8},{1,11},{3,13... | collective-permute-start | bytes 589832 | tf_op jit(solution)/shard_map/ppermute | solution.py:22
  45.6 18.5 %collective-permute-start.13 = (bf16[192,512]{1,0:T(8,128)(2,1)S(1)}, bf16[192,512]{1,0:T(8,128)(2,1)S(1)}, u32[]{:S(2)}, u32[]{:S(2)}) collective-permute-start(bf16[192,512]{1,0:T(8,128)(2,1)S(1)} %get-tuple-element.10), channel_id=1, source_target_pairs={{0,12},{2,14},{4,0},{6,2},{8,4},{10,6},{12,8},{14,10},{1,13},{3,15... | collective-permute-start | bytes 589832 | tf_op jit(solution)/shard_map/ppermute | solution.py:22
  49.3 14.8 %collective-permute-start.14 = (bf16[192,512]{1,0:T(8,128)(2,1)S(1)}, bf16[192,512]{1,0:T(8,128)(2,1)S(1)}, u32[]{:S(2)}, u32[]{:S(2)}) collective-permute-start(bf16[192,512]{1,0:T(8,128)(2,1)S(1)} %get-tuple-element.9), channel_id=1, source_target_pairs={{0,14},{2,0},{4,2},{6,4},{8,6},{10,8},{12,10},{14,12},{1,15},{3,1}... | collective-permute-start | bytes 589832 | tf_op jit(solution)/shard_map/ppermute | solution.py:22
  52.1 11.9 %collective-permute-start.8 = (bf16[192,512]{1,0:T(8,128)(2,1)S(1)}, bf16[192,512]{1,0:T(8,128)(2,1)S(1)}, u32[]{:S(2)}, u32[]{:S(2)}) collective-permute-start(bf16[192,512]{1,0:T(8,128)(2,1)S(1)} %get-tuple-element.15), channel_id=1, source_target_pairs={{0,2},{2,4},{4,6},{6,8},{8,10},{10,12},{12,14},{14,0},{1,3},{3,5},... | collective-permute-start | bytes 589832 | tf_op jit(solution)/shard_map/ppermute | solution.py:22
  53.6 18.3 %collective-permute-start.9 = (bf16[192,512]{1,0:T(8,128)(2,1)S(1)}, bf16[192,512]{1,0:T(8,128)(2,1)S(1)}, u32[]{:S(2)}, u32[]{:S(2)}) collective-permute-start(bf16[192,512]{1,0:T(8,128)(2,1)S(1)} %get-tuple-element.14), channel_id=1, source_target_pairs={{0,4},{2,6},{4,8},{6,10},{8,12},{10,14},{12,0},{14,2},{1,5},{3,7},... | collective-permute-start | bytes 589832 | tf_op jit(solution)/shard_map/ppermute | solution.py:22
  73.1 8.6 %collective-permute-start.22 = (bf16[192,512]{1,0:T(8,128)(2,1)S(1)}, bf16[192,512]{1,0:T(8,128)(2,1)S(1)}, u32[]{:S(2)}, u32[]{:S(2)}) collective-permute-start(bf16[192,512]{1,0:T(8,128)(2,1)S(1)} %get-tuple-element.8), channel_id=1, source_target_pairs={{0,14},{2,0},{4,2},{6,4},{8,6},{10,8},{12,10},{14,12},{1,15},{3,1}... | collective-permute-start | bytes 589832 | tf_op jit(solution)/shard_map/ppermute | solution.py:22
  74.3 12.8 %collective-permute-start.23 = (bf16[192,512]{1,0:T(8,128)(2,1)S(1)}, bf16[192,512]{1,0:T(8,128)(2,1)S(1)}, u32[]{:S(2)}, u32[]{:S(2)}) collective-permute-start(bf16[192,512]{1,0:T(8,128)(2,1)S(1)} %get-tuple-element.8), channel_id=1, source_target_pairs={{0,12},{2,14},{4,0},{6,2},{8,4},{10,6},{12,8},{14,10},{1,13},{3,15... | collective-permute-start | bytes 589832 | tf_op jit(solution)/shard_map/ppermute | solution.py:22
  76.9 17.9 %collective-permute-start.24 = (bf16[192,512]{1,0:T(8,128)(2,1)S(1)}, bf16[192,512]{1,0:T(8,128)(2,1)S(1)}, u32[]{:S(2)}, u32[]{:S(2)}) collective-permute-start(bf16[192,512]{1,0:T(8,128)(2,1)S(1)} %get-tuple-element.8), channel_id=1, source_target_pairs={{0,10},{2,12},{4,14},{6,0},{8,2},{10,4},{12,6},{14,8},{1,11},{3,13... | collective-permute-start | bytes 589832 | tf_op jit(solution)/shard_map/ppermute | solution.py:22
  78.0 19.8 %collective-permute-start.25 = (bf16[192,512]{1,0:T(8,128)(2,1)S(1)}, bf16[192,512]{1,0:T(8,128)(2,1)S(1)}, u32[]{:S(2)}, u32[]{:S(2)}) collective-permute-start(bf16[192,512]{1,0:T(8,128)(2,1)S(1)} %get-tuple-element.8), channel_id=1, source_target_pairs={{0,8},{2,10},{4,12},{6,14},{8,0},{10,2},{12,4},{14,6},{1,9},{3,11}... | collective-permute-start | bytes 589832 | tf_op jit(solution)/shard_map/ppermute | solution.py:22
  80.7 17.8 %collective-permute-start.26 = (bf16[192,512]{1,0:T(8,128)(2,1)S(1)}, bf16[192,512]{1,0:T(8,128)(2,1)S(1)}, u32[]{:S(2)}, u32[]{:S(2)}) collective-permute-start(bf16[192,512]{1,0:T(8,128)(2,1)S(1)} %get-tuple-element.8), channel_id=1, source_target_pairs={{0,6},{2,8},{4,10},{6,12},{8,14},{10,0},{12,2},{14,4},{1,7},{3,9},... | collective-permute-start | bytes 589832 | tf_op jit(solution)/shard_map/ppermute | solution.py:22
  81.7 17.6 %collective-permute-start.27 = (bf16[192,512]{1,0:T(8,128)(2,1)S(1)}, bf16[192,512]{1,0:T(8,128)(2,1)S(1)}, u32[]{:S(2)}, u32[]{:S(2)}) collective-permute-start(bf16[192,512]{1,0:T(8,128)(2,1)S(1)} %get-tuple-element.8), channel_id=1, source_target_pairs={{0,4},{2,6},{4,8},{6,10},{8,12},{10,14},{12,0},{14,2},{1,5},{3,7},... | collective-permute-start | bytes 589832 | tf_op jit(solution)/shard_map/ppermute | solution.py:22
  87.1 12.9 %collective-permute-start.28 = (bf16[192,512]{1,0:T(8,128)(2,1)S(1)}, bf16[192,512]{1,0:T(8,128)(2,1)S(1)}, u32[]{:S(2)}, u32[]{:S(2)}) collective-permute-start(bf16[192,512]{1,0:T(8,128)(2,1)S(1)} %get-tuple-element.8), channel_id=1, source_target_pairs={{0,2},{2,4},{4,6},{6,8},{8,10},{10,12},{12,14},{14,0},{1,3},{3,5},... | collective-permute-start | bytes 589832 | tf_op jit(solution)/shard_map/ppermute | solution.py:22
  100.7 35.5 %collective-permute-start.29 = (bf16[1536,512]{1,0:T(8,128)(2,1)}, bf16[1536,512]{1,0:T(8,128)(2,1)S(1)}, u32[]{:S(2)}, u32[]{:S(2)}) collective-permute-start(bf16[1536,512]{1,0:T(8,128)(2,1)} %get-tuple-element.24), channel_id=1, source_target_pairs={{0,1},{1,0},{2,3},{3,2},{4,5},{5,4},{6,7},{7,6},{8,9},{9,8},{10,11... | collective-permute-start | bytes 4718600 | tf_op jit(solution)/shard_map/ppermute | solution.py:153
  118.9 6.9 %collective-permute-start.16 = (bf16[32,512]{1,0:T(8,128)(2,1)S(1)}, bf16[32,512]{1,0:T(8,128)(2,1)S(1)}, u32[]{:S(2)}, u32[]{:S(2)}) collective-permute-start(bf16[32,512]{1,0:T(8,128)(2,1)S(1)} %fusion), channel_id=1, source_target_pairs={{0,32},{16,48},{32,64},{48,80},{64,96},{80,112},{96,0},{112,16},{1... | collective-permute-start | bytes 98312 | tf_op jit(solution)/shard_map/ppermute | solution.py:22
  121.9 7.9 %collective-permute-start.18 = (bf16[32,512]{1,0:T(8,128)(2,1)S(1)}, bf16[32,512]{1,0:T(8,128)(2,1)S(1)}, u32[]{:S(2)}, u32[]{:S(2)}) collective-permute-start(bf16[32,512]{1,0:T(8,128)(2,1)S(1)} %fusion), channel_id=1, source_target_pairs={{0,64},{16,80},{32,96},{48,112},{64,0},{80,16},{96,32},{112,48},{1... | collective-permute-start | bytes 98312 | tf_op jit(solution)/shard_map/ppermute | solution.py:22
  132.6 34.4 %all-to-all-start.1 = ((bf16[16,32,512]{2,1,0:T(8,128)(2,1)}), bf16[16,32,512]{2,1,0:T(8,128)(2,1)S(1)}, u32[]{:S(2)}, u32[]{:S(2)}) async-start(bf16[16,32,512]{2,1,0:T(8,128)(2,1)} %broadcast_in_dim.2), calls=%async_computation.1 | async-start | bytes 1048576 | tf_op jit(solution)/shard_map/all_to_all | solution.py:168
  148.1 12.2 %collective-permute-start.30 = (bf16[192,512]{1,0:T(8,128)(2,1)S(1)}, bf16[192,512]{1,0:T(8,128)(2,1)S(1)}, u32[]{:S(2)}, u32[]{:S(2)}) collective-permute-start(bf16[192,512]{1,0:T(8,128)(2,1)S(1)} %get-tuple-element.17), channel_id=1, source_target_pairs={{0,112},{16,0},{32,16},{48,32},{64,48},{80,64},{96,80},{112,96},{1... | collective-permute-start | bytes 589832 | tf_op jit(solution)/shard_map/ppermute | solution.py:22
  152.2 14.8 %collective-permute-start.31 = (bf16[192,512]{1,0:T(8,128)(2,1)S(1)}, bf16[192,512]{1,0:T(8,128)(2,1)S(1)}, u32[]{:S(2)}, u32[]{:S(2)}) collective-permute-start(bf16[192,512]{1,0:T(8,128)(2,1)S(1)} %get-tuple-element.23), channel_id=1, source_target_pairs={{0,96},{16,112},{32,0},{48,16},{64,32},{80,48},{96,64},{112,80},{1... | collective-permute-start | bytes 589832 | tf_op jit(solution)/shard_map/ppermute | solution.py:22
  152.2 19.1 %collective-permute-start.32 = (bf16[192,512]{1,0:T(8,128)(2,1)}, bf16[192,512]{1,0:T(8,128)(2,1)S(1)}, u32[]{:S(2)}, u32[]{:S(2)}) collective-permute-start(bf16[192,512]{1,0:T(8,128)(2,1)} %get-tuple-element.22), channel_id=1, source_target_pairs={{0,80},{16,96},{32,112},{48,0},{64,16},{80,32},{96,48},{112,64},{1... | collective-permute-start | bytes 589832 | tf_op jit(solution)/shard_map/ppermute | solution.py:22
  152.9 22.7 %collective-permute-start.33 = (bf16[192,512]{1,0:T(8,128)(2,1)}, bf16[192,512]{1,0:T(8,128)(2,1)S(1)}, u32[]{:S(2)}, u32[]{:S(2)}) collective-permute-start(bf16[192,512]{1,0:T(8,128)(2,1)} %get-tuple-element.21), channel_id=1, source_target_pairs={{0,64},{16,80},{32,96},{48,112},{64,0},{80,16},{96,32},{112,48},{1... | collective-permute-start | bytes 589832 | tf_op jit(solution)/shard_map/ppermute | solution.py:22
  154.5 21.1 %collective-permute-start.34 = (bf16[192,512]{1,0:T(8,128)(2,1)}, bf16[192,512]{1,0:T(8,128)(2,1)S(1)}, u32[]{:S(2)}, u32[]{:S(2)}) collective-permute-start(bf16[192,512]{1,0:T(8,128)(2,1)} %get-tuple-element.20), channel_id=1, source_target_pairs={{0,48},{16,64},{32,80},{48,96},{64,112},{80,0},{96,16},{112,32},{1... | collective-permute-start | bytes 589832 | tf_op jit(solution)/shard_map/ppermute | solution.py:22
  160.3 15.8 %collective-permute-start.35 = (bf16[192,512]{1,0:T(8,128)(2,1)}, bf16[192,512]{1,0:T(8,128)(2,1)S(1)}, u32[]{:S(2)}, u32[]{:S(2)}) collective-permute-start(bf16[192,512]{1,0:T(8,128)(2,1)} %get-tuple-element.19), channel_id=1, source_target_pairs={{0,32},{16,48},{32,64},{48,80},{64,96},{80,112},{96,0},{112,16},{1... | collective-permute-start | bytes 589832 | tf_op jit(solution)/shard_map/ppermute | solution.py:22
  167.0 11.6 %collective-permute-start.36 = (bf16[192,512]{1,0:T(8,128)(2,1)}, bf16[192,512]{1,0:T(8,128)(2,1)S(1)}, u32[]{:S(2)}, u32[]{:S(2)}) collective-permute-start(bf16[192,512]{1,0:T(8,128)(2,1)} %get-tuple-element.18), channel_id=1, source_target_pairs={{0,16},{16,32},{32,48},{48,64},{64,80},{80,96},{96,112},{112,0},{1... | collective-permute-start | bytes 589832 | tf_op jit(solution)/shard_map/ppermute | solution.py:22
  (13 other events, 129.3 us)

commit v2 on v1

v2 whole, which is shorter than its diff:
```python
import math

import jax
import jax.numpy as jnp
from jax import lax
from jax.experimental import pallas as pl
from jax.experimental.pallas import tpu as pltpu
from jax.sharding import Mesh, PartitionSpec as P

AXES = ("y_lo", "z", "y_hi", "x", "core")
SIZES = (2, 4, 2, 4, 2)
ROW = ("y_lo", "z")
CHIP = ("y_hi", "x")
COL = ("y_hi", "x", "core")
SIDE = 64
PEERS = 8
OWN = 192
WIDTH = 512


def build_kernel(coords, counts, values, near, far):
    rows, cols = near.shape
    per_owner = OWN // SIDE
    me_core = lax.axis_index("core")

    @pl.loop(0, rows // SIDE)
    def _(r):
        at = pl.ds(pl.multiple_of(r * SIDE, SIDE), SIDE)
        near[at, :] = jnp.zeros((SIDE, cols), near.dtype)
        far[at, :] = jnp.zeros((SIDE, cols), far.dtype)

    count = counts[0, 0]
    lane = lax.broadcasted_iota(jnp.int32, (SIDE, 2 * SIDE), 1)

    @pl.loop(0, (count + 15) // 16)
    def _(g):
        group = values[0, 0, pl.ds(pl.multiple_of(g * 16, 16), 16), :]
        pairs = group.astype(jnp.float32).reshape(16, SIDE // 2, 2 * SIDE)
        for k in range(16):
            slot = g * 16 + k
            live = slot < count
            block_row = jnp.where(live, coords[0, 0, 0, slot], 0)
            block_col = jnp.where(live, coords[0, 0, 1, slot], 0)
            owner = block_row // per_owner
            is_far = ((owner + me_core) & 1) == 1
            at_row = (owner >> 1) * per_owner + block_row % per_owner
            odd = (block_col & 1) == 1
            plain = pairs[k]
            turned = pltpu.roll(plain, SIDE, 1)
            block = jnp.concatenate(
                [jnp.where(odd, turned, plain), jnp.where(odd, plain, turned)], axis=0
            ).astype(near.dtype)
            first = jnp.where(live, (block_col & 1) * SIDE, 4 * SIDE)
            mask = (lane >= first) & (lane < first + SIDE)
            place = (
                pl.ds(pl.multiple_of(at_row * SIDE, SIDE), SIDE),
                pl.ds(pl.multiple_of((block_col >> 1) * 2 * SIDE, 2 * SIDE), 2 * SIDE),
            )

            @pl.when(is_far)
            def _():
                far[place] = jnp.where(mask, block, far[place])

            @pl.when(jnp.logical_not(is_far))
            def _():
                near[place] = jnp.where(mask, block, near[place])


def build(coords, counts, values):
    tile = jax.ShapeDtypeStruct((PEERS * OWN, PEERS * OWN), jnp.bfloat16)
    return pl.pallas_call(
        build_kernel,
        out_shape=(tile, tile),
        in_specs=[pl.BlockSpec(memory_space=pltpu.SMEM)] * 2 + [pl.BlockSpec(memory_space=pltpu.VMEM)],
        out_specs=(pl.BlockSpec(memory_space=pltpu.VMEM),) * 2,
        compiler_params=pltpu.CompilerParams(vmem_limit_bytes=24 << 20),
        cost_estimate=pl.CostEstimate(flops=0, bytes_accessed=30 << 20, transcendentals=0),
        name="build",
    )(coords, counts, values)


def middle_kernel(parts, out_grad, weight, activations, send, wgrad_near, wgrad_far):
    total = parts[0].astype(jnp.float32)
    for k in range(1, PEERS):
        total = total + parts[k].astype(jnp.float32)
    aggregated = total.astype(jnp.bfloat16)
    at = lax.broadcasted_iota(jnp.int32, (OWN, OWN), 0)
    to = lax.broadcasted_iota(jnp.int32, (OWN, OWN), 1)
    half = SIDE // 2
    turn = jnp.where(
        (at // SIDE == to // SIDE) & (to % SIDE == 2 * (at % half) + (at % SIDE) // half), 1.0, 0.0
    ).astype(jnp.bfloat16)
    w = weight[...]
    pre_act = jnp.dot(aggregated, w, preferred_element_type=jnp.float32)
    sig = jax.nn.sigmoid(pre_act)
    act = (pre_act * sig).astype(jnp.bfloat16)
    activations[...] = lax.dot_general(
        turn, act, (((0,), (0,)), ((), ())), preferred_element_type=jnp.float32
    ).astype(jnp.bfloat16)
    cotangent = jnp.dot(turn, out_grad[...], preferred_element_type=jnp.float32)
    grad_pre = (cotangent * sig * (1.0 + pre_act * (1.0 - sig))).astype(jnp.bfloat16)
    grad_agg = lax.dot_general(
        grad_pre, w, (((1,), (1,)), ((), ())), preferred_element_type=jnp.float32
    ).astype(jnp.bfloat16)
    for k in range(PEERS):
        send[k] = grad_agg
    local = lax.dot_general(
        aggregated, grad_pre, (((0,), (0,)), ((), ())), preferred_element_type=jnp.float32
    ).astype(jnp.bfloat16)
    first, last = local[: WIDTH // 2], local[WIDTH // 2 :]
    core = lax.axis_index("core")
    wgrad_near[...] = jnp.where(core == 0, first, last)
    wgrad_far[...] = jnp.where(core == 0, last, first)


def middle(parts, out_grad, weight):
    vmem = pl.BlockSpec(memory_space=pltpu.VMEM)
    wgrad = jax.ShapeDtypeStruct((WIDTH // 2, WIDTH), jnp.bfloat16)
    return pl.pallas_call(
        middle_kernel,
        out_shape=(
            jax.ShapeDtypeStruct((OWN, WIDTH), jnp.bfloat16),
            jax.ShapeDtypeStruct((PEERS, OWN, WIDTH), jnp.bfloat16),
            wgrad,
            wgrad,
        ),
        in_specs=[vmem] * 3,
        out_specs=(vmem,) * 4,
        compiler_params=pltpu.CompilerParams(vmem_limit_bytes=24 << 20),
        cost_estimate=pl.CostEstimate(flops=2 * 3 * OWN * WIDTH * WIDTH, bytes_accessed=4 << 20, transcendentals=0),
        name="middle",
    )(parts, out_grad, weight)


def fsum(parts):
    total = parts[0].astype(jnp.float32)
    for k in range(1, parts.shape[0]):
        total = total + parts[k].astype(jnp.float32)
    return total


def exchange(parts, axes):
    return lax.all_to_all(parts, axes, 0, 0)


def trade(array, axis, bit=1):
    return lax.ppermute(array, axis, [(i, i ^ bit) for i in range(lax.axis_size(axis))])


def add(a, b):
    return (a.astype(jnp.float32) + b.astype(jnp.float32)).astype(jnp.bfloat16)


def sum_wgrad(near, far):
    total = add(near, trade(far, "core"))
    steps = (("x", 1), ("y_hi", 1), ("x", 2))
    high = [(lax.axis_index(axis) & bit) != 0 for axis, bit in steps]
    for (axis, bit), up in zip(steps, high):
        few = total.shape[0] // 2
        low_part, high_part = total[:few], total[few:]
        sent = jnp.where(up, low_part, high_part)
        kept = jnp.where(up, high_part, low_part)
        total = add(kept, trade(sent, axis, bit))
    for axis, bit in (("z", 1), ("z", 2), ("y_lo", 1)):
        total = add(total, trade(total, axis, bit))
    return total, steps, high


def gather_wgrad(total, steps, high):
    for (axis, bit), up in reversed(list(zip(steps, high))):
        other = trade(total, axis, bit)
        total = jnp.concatenate([jnp.where(up, other, total), jnp.where(up, total, other)], axis=0)
    other = trade(total, "core")
    up = lax.axis_index("core") != 0
    return jnp.concatenate([jnp.where(up, other, total), jnp.where(up, total, other)], axis=0)


def per_device(features, out_grad, weight, block_values, block_coords, block_counts):
    rows = PEERS * OWN
    panel = exchange(jnp.broadcast_to(features[None], (PEERS, OWN, WIDTH)), ROW).reshape(rows, WIDTH)
    near, far = build(block_coords, block_counts, block_values)

    other = jnp.dot(far, panel, preferred_element_type=jnp.float32).astype(jnp.bfloat16)
    other = trade(other, "core")
    own = jnp.dot(near, panel, preferred_element_type=jnp.float32)
    both = (own + other.astype(jnp.float32)).astype(jnp.bfloat16)
    parts = exchange(both.reshape(PEERS, OWN, WIDTH), CHIP)

    activations, send, wgrad_near, wgrad_far = middle(parts, out_grad, weight)

    mine = exchange(send, CHIP).reshape(rows, WIDTH)
    theirs = trade(mine, "core")
    down = (((0,), (0,)), ((), ()))
    partial_grad = lax.dot_general(near, mine, down, preferred_element_type=jnp.float32)
    partial_grad = partial_grad + lax.dot_general(far, theirs, down, preferred_element_type=jnp.float32)
    received = exchange(partial_grad.astype(jnp.bfloat16).reshape(PEERS, OWN, WIDTH), ROW)
    feature_grad = fsum(received).astype(jnp.bfloat16)

    weight_grad = gather_wgrad(*sum_wgrad(wgrad_near, wgrad_far))
    total_nodes = OWN * PEERS * 2 * PEERS
    weight_grad = weight_grad.astype(jnp.float32) * jnp.float32(1.0 / math.sqrt(total_nodes))
    return (activations, weight_grad, feature_grad)


def solution(mesh):
    fine = Mesh(mesh.devices.reshape(SIZES), AXES)
    return jax.shard_map(
        per_device,
        mesh=fine,
        in_specs=(
            P(COL + ROW, None),
            P(ROW + COL, None),
            P(),
            P(ROW, COL, None, None),
            P(ROW, COL, None, None),
            P(ROW, COL),
        ),
        out_specs=(P(ROW + COL, None), P(), P(COL + ROW, None)),
        check_vma=False,
    )
```

time: 180 us -> 166 us (0.922)
  starting transfers between devices: 82.7 us -> 43.8 us
  Pallas kernels: 4.04 us -> 22.4 us
  blocking collectives: 15 us -> 26 us
  local copies, waits for them, and re-layouts: 13.1 us -> 6.61 us
  matrix products: 14.8 us -> 18.4 us
  waiting for transfers between devices: 45.7 us -> 43.3 us
    ppermute x37 -> x13, starting transfers between devices: 79.1 us -> 27.6 us  [trade(): lax.ppermute(array, axis, [(i, i ^ bit) for i in range(lax.axis_size(axis...]
    pallas_call x1, Pallas kernels: 2.81 us -> 20.3 us  [build(): pl.pallas_call(build_kernel, out_shape=(tile, tile), in_specs=[pl.BlockSp...]
    all_to_all x1 -> x3, starting transfers between devices: 3.57 us -> 16.2 us  [exchange(): return lax.all_to_all(parts, axes, 0, 0)]
    all_to_all x1, blocking collectives: 15 us -> 26 us  [exchange(): return lax.all_to_all(parts, axes, 0, 0)]
    ppermute x37 -> x13, waiting for transfers between devices: 45.7 us -> 36.2 us  [trade(): lax.ppermute(array, axis, [(i, i ^ bit) for i in range(lax.axis_size(axis...]
    all_to_all x1 -> x3, waiting for transfers between devices: 0.01 us -> 7.08 us  [exchange(): return lax.all_to_all(parts, axes, 0, 0)]
    unnamed x28 -> x18, local copies, waits for them, and re-layouts: 9.17 us -> 4.35 us
    dot_general x2 -> x4, matrix products: 14.8 us -> 18.4 us  [the longest x1 5.59 us: per_device(): jnp.dot(far, panel, preferred_element_type=jnp.float32).astype(jnp.bfloat16)]
  transfers between devices with their start and end apart: 38 -> 16, of which waited for: 14 -> 12; matrix products, arithmetic and copies ran while one was open for 11% -> 6% of each run, Pallas kernels for 2% -> 12%
where the time goes in v2:
time: 166 us; the launch traced here: 164 us
  starting transfers between devices  43.8 us (26%)
  waiting for transfers between devices  43.3 us (26%)
  blocking collectives  26 us (16%)
  Pallas kernels  22.4 us (13%)
  matrix products  18.4 us (11%)
  local copies, waits for them, and re-layouts  6.61 us (4%)
  other arithmetic  2.43 us (1%)
    ppermute x13, waiting for transfers between devices, trade(): lax.ppermute(array, axis, [(i, i ^ bit) for i in range(lax.axis_size(axis...  36.2 us
    ppermute x13, starting transfers between devices, trade(): lax.ppermute(array, axis, [(i, i ^ bit) for i in range(lax.axis_size(axis...  27.6 us
    all_to_all x1, blocking collectives, exchange(): return lax.all_to_all(parts, axes, 0, 0)  26 us
    pallas_call x1, Pallas kernels, build(): pl.pallas_call(build_kernel, out_shape=(tile, tile), in_specs=[pl.BlockSp...  20.3 us
    all_to_all x3, starting transfers between devices, exchange(): return lax.all_to_all(parts, axes, 0, 0)  16.2 us
    all_to_all x3, waiting for transfers between devices, exchange(): return lax.all_to_all(parts, axes, 0, 0)  7.08 us
    dot_general x1, matrix products, per_device(): jnp.dot(far, panel, preferred_element_type=jnp.float32).astype(jnp.bfloat16)  5.59 us
    dot_general x1, matrix products, per_device(): lax.dot_general(near, mine, down, preferred_element_type=jnp.float32)  4.87 us
  transfers between devices with their start and end apart: 16, of which 12 were waited for; matrix products, arithmetic and copies ran while one was open for 6% of the time, Pallas kernels for 12%

profile of v2, /device:TPU:0, one launch (start us, length us, event | category | flops | bytes accessed | tf_op | source)
XLA Modules:
  0.0 164.4 jit_solution(12300769329018213218)
XLA Ops:
  0.6 2.3 %broadcast_in_dim.2 = bf16[8,192,512]{2,1,0:T(8,128)(2,1)} broadcast(bf16[192,512]{1,0:T(8,128)(2,1)} %param.6), dimensions={1,2} | broadcast | bytes 1769472 | tf_op jit(solution)/shard_map/broadcast_in_dim | solution.py:180
  2.9 6.5 %all-to-all-start = ((bf16[8,192,512]{2,1,0:T(8,128)(2,1)}), bf16[8,192,512]{2,1,0:T(8,128)(2,1)}, u32[]{:S(2)}, u32[]{:S(2)}) async-start(bf16[8,192,512]{2,1,0:T(8,128)(2,1)} %broadcast_in_dim.2), calls=%async_computation | async-start | bytes 3145728 | tf_op jit(solution)/shard_map/all_to_all | solution.py:143
  10.1 20.3 %build.1 = (bf16[1536,1536]{1,0:T(8,128)(2,1)S(1)}, bf16[1536,1536]{1,0:T(8,128)(2,1)S(1)}) custom-call(s32[1,1,2,288]{3,2,1,0:T(2,128)S(1)} %copy-done.3, s32[1,1]{1,0:T(1,128)S(6)} %copy.9.counts, bf16[1,1,288,4096]{3,2,1,0:T(8,128)(2,1)S(1)} %copy-done), custom_call_target="tpu_custom_call" | custom-call | bytes 31457280 | tf_op jit(solution)/shard_map/build/pallas_call | solution.py:71
  30.4 2.1 %copy-done.4 = bf16[1536,1536]{1,0:T(8,128)(2,1)} copy-done((bf16[1536,1536]{1,0:T(8,128)(2,1)}, bf16[1536,1536]{1,0:T(8,128)(2,1)S(1)}, u32[]{:S(2)}) %copy-start.4) | copy-done | bytes 4718616
  32.6 2.2 %copy-done.5 = bf16[1536,1536]{1,0:T(8,128)(2,1)} copy-done((bf16[1536,1536]{1,0:T(8,128)(2,1)}, bf16[1536,1536]{1,0:T(8,128)(2,1)S(1)}, u32[]{:S(2)}) %copy-start.5) | copy-done | bytes 4718616
  34.8 5.6 %convolution_convert_fusion = bf16[1536,512]{1,0:T(8,128)(2,1)S(1)} fusion(bf16[1536,1536]{1,0:T(8,128)(2,1)} %copy-done.4, bf16[1536,512]{1,0:T(8,128)(2,1)} %bitcast), kind=kOutput, calls=%fused_computation.3 | convolution fusion | flops 2416705536 | bytes 7864320 | tf_op jit(solution)/shard_map/dot_general | solution.py:183
  40.5 3.4 %collective-permute-done = bf16[1536,512]{1,0:T(8,128)(2,1)S(1)} collective-permute-done((bf16[1536,512]{1,0:T(8,128)(2,1)S(1)}, bf16[1536,512]{1,0:T(8,128)(2,1)S(1)}, u32[]{:S(2)}, u32[]{:S(2)}) %collective-permute-start) | collective-permute-done | bytes 1572896 | tf_op jit(solution)/shard_map/ppermute | solution.py:147
  43.9 4.2 %add_convert_fusion = bf16[1536,512]{1,0:T(8,128)(2,1)S(1)} fusion(bf16[1536,512]{1,0:T(8,128)(2,1)S(1)} %collective-permute-done, bf16[1536,1536]{1,0:T(8,128)(2,1)S(1)} %copy-done.6, bf16[1536,512]{1,0:T(8,128)(2,1)} %bitcast), kind=kOutput, calls=%fused_computation.1 | convolution fusion | flops 2418278400 | bytes 9437184 | tf_op jit(solution)/shard_map/dot_general | solution.py:185
  48.1 26.0 %all_to_all.20.parts = bf16[8,192,512]{2,1,0:T(8,128)(2,1)S(1)} all-to-all(bf16[8,192,512]{2,1,0:T(8,128)(2,1)S(1)} %bitcast.18), channel_id=1, replica_groups=mesh['y_lo'=2,'z'=4,'y_hi'=2,'x'=4,'core'=2] {'y_hi','x'}, dimensions={0} | all-to-all | bytes 3145728 | tf_op jit(solution)/shard_map/all_to_all | solution.py:143
  74.0 2.0 %middle.1 = (bf16[192,512]{1,0:T(8,128)(2,1)}, bf16[8,192,512]{2,1,0:T(8,128)(2,1)}, bf16[256,512]{1,0:T(8,128)(2,1)S(1)}, bf16[256,512]{1,0:T(8,128)(2,1)S(1)}) custom-call(bf16[8,192,512]{2,1,0:T(8,128)(2,1)S(1)} %all_to_all.20.parts, bf16[192,512]{1,0:T(8,128)(2,1)S(1)} %copy-done.2, bf16[512,512]{1,0:T(8,128)(2,1)S(1)} %copy-done.1), custom_call_target="tpu_custom_call" | custom-call | flops 301989888 | bytes 4194304 | tf_op jit(solution)/shard_map/middle/pallas_call | solution.py:119
  76.1 1.5 collective-permute-done.1
  78.7 3.6 %all-to-all-start.2 = ((bf16[8,192,512]{2,1,0:T(8,128)(2,1)}), bf16[8,192,512]{2,1,0:T(8,128)(2,1)S(1)}, u32[]{:S(2)}, u32[]{:S(2)}) async-start(bf16[8,192,512]{2,1,0:T(8,128)(2,1)} %get-tuple-element.14), calls=%async_computation.2 | async-start | bytes 3145728 | tf_op jit(solution)/shard_map/all_to_all | solution.py:143
  82.2 1.1 collective-permute-done.2
  83.4 2.4 %collective-permute-start.3 = (bf16[64,512]{1,0:T(8,128)(2,1)S(1)}, bf16[64,512]{1,0:T(8,128)(2,1)S(1)}, u32[]{:S(2)}, u32[]{:S(2)}) collective-permute-start(bf16[64,512]{1,0:T(8,128)(2,1)S(1)} %broadcast_select_fusion.7), channel_id=1, source_target_pairs={{0,8},{8,0},{1,9},{9,1},{2,10},{10,2},{3,11},{11,3},{4,12},{12,4},... | collective-permute-start | bytes 196616 | tf_op jit(solution)/shard_map/ppermute | solution.py:147
  85.8 14.5 %collective-permute-done.3 = bf16[64,512]{1,0:T(8,128)(2,1)S(1)} collective-permute-done((bf16[64,512]{1,0:T(8,128)(2,1)S(1)}, bf16[64,512]{1,0:T(8,128)(2,1)S(1)}, u32[]{:S(2)}, u32[]{:S(2)}) %collective-permute-start.3) | collective-permute-done | bytes 65568 | tf_op jit(solution)/shard_map/ppermute | solution.py:147
  100.4 7.3 %collective-permute-start.4 = (bf16[32,512]{1,0:T(8,128)(2,1)S(1)}, bf16[32,512]{1,0:T(8,128)(2,1)S(1)}, u32[]{:S(2)}, u32[]{:S(2)}) collective-permute-start(bf16[32,512]{1,0:T(8,128)(2,1)S(1)} %broadcast_select_fusion.10), channel_id=1, source_target_pairs={{0,4},{2,6},{4,0},{6,2},{1,5},{3,7},{5,1},{7,3},{8,12},{10,14},{12... | collective-permute-start | bytes 98312 | tf_op jit(solution)/shard_map/ppermute | solution.py:147
  107.7 1.9 %collective-permute-done.4 = bf16[32,512]{1,0:T(8,128)(2,1)S(1)} collective-permute-done((bf16[32,512]{1,0:T(8,128)(2,1)S(1)}, bf16[32,512]{1,0:T(8,128)(2,1)S(1)}, u32[]{:S(2)}, u32[]{:S(2)}) %collective-permute-start.4) | collective-permute-done | bytes 32800 | tf_op jit(solution)/shard_map/ppermute | solution.py:147
  109.6 5.8 %collective-permute-start.5 = (bf16[32,512]{1,0:T(8,128)(2,1)S(1)}, bf16[32,512]{1,0:T(8,128)(2,1)S(1)}, u32[]{:S(2)}, u32[]{:S(2)}) collective-permute-start(bf16[32,512]{1,0:T(8,128)(2,1)S(1)} %add_convert_fusion.8), channel_id=1, source_target_pairs={{0,16},{16,0},{32,48},{48,32},{1,17},{17,1},{33,49},{49,33},{2,18}... | collective-permute-start | bytes 98312 | tf_op jit(solution)/shard_map/ppermute | solution.py:147
  115.4 1.9 %collective-permute-done.5 = bf16[32,512]{1,0:T(8,128)(2,1)S(1)} collective-permute-done((bf16[32,512]{1,0:T(8,128)(2,1)S(1)}, bf16[32,512]{1,0:T(8,128)(2,1)S(1)}, u32[]{:S(2)}, u32[]{:S(2)}) %collective-permute-start.5) | collective-permute-done | bytes 32800 | tf_op jit(solution)/shard_map/ppermute | solution.py:147
  117.3 3.4 %collective-permute-start.6 = (bf16[32,512]{1,0:T(8,128)(2,1)S(1)}, bf16[32,512]{1,0:T(8,128)(2,1)S(1)}, u32[]{:S(2)}, u32[]{:S(2)}) collective-permute-start(bf16[32,512]{1,0:T(8,128)(2,1)S(1)} %add_convert_fusion.7), channel_id=1, source_target_pairs={{0,32},{16,48},{32,0},{48,16},{1,33},{17,49},{33,1},{49,17},{2,34}... | collective-permute-start | bytes 98312 | tf_op jit(solution)/shard_map/ppermute | solution.py:147
  120.7 2.1 %collective-permute-done.6 = bf16[32,512]{1,0:T(8,128)(2,1)S(1)} collective-permute-done((bf16[32,512]{1,0:T(8,128)(2,1)S(1)}, bf16[32,512]{1,0:T(8,128)(2,1)S(1)}, u32[]{:S(2)}, u32[]{:S(2)}) %collective-permute-start.6) | collective-permute-done | bytes 32800 | tf_op jit(solution)/shard_map/ppermute | solution.py:147
  122.8 2.4 %collective-permute-start.7 = (bf16[32,512]{1,0:T(8,128)(2,1)S(1)}, bf16[32,512]{1,0:T(8,128)(2,1)S(1)}, u32[]{:S(2)}, u32[]{:S(2)}) collective-permute-start(bf16[32,512]{1,0:T(8,128)(2,1)S(1)} %add_convert_fusion.6), channel_id=1, source_target_pairs={{0,64},{64,0},{1,65},{65,1},{2,66},{66,2},{3,67},{67,3},{4,68},{68... | collective-permute-start | bytes 98312 | tf_op jit(solution)/shard_map/ppermute | solution.py:147
  125.2 1.9 %collective-permute-done.7 = bf16[32,512]{1,0:T(8,128)(2,1)S(1)} collective-permute-done((bf16[32,512]{1,0:T(8,128)(2,1)S(1)}, bf16[32,512]{1,0:T(8,128)(2,1)S(1)}, u32[]{:S(2)}, u32[]{:S(2)}) %collective-permute-start.7) | collective-permute-done | bytes 32800 | tf_op jit(solution)/shard_map/ppermute | solution.py:147
  127.1 3.6 %collective-permute-start.8 = (bf16[32,512]{1,0:T(8,128)(2,1)S(1)}, bf16[32,512]{1,0:T(8,128)(2,1)S(1)}, u32[]{:S(2)}, u32[]{:S(2)}) collective-permute-start(bf16[32,512]{1,0:T(8,128)(2,1)S(1)} %add_convert_fusion.5), channel_id=1, source_target_pairs={{0,4},{2,6},{4,0},{6,2},{1,5},{3,7},{5,1},{7,3},{8,12},{10,14},{12... | collective-permute-start | bytes 98312 | tf_op jit(solution)/shard_map/ppermute | solution.py:147
  130.7 1.9 %collective-permute-done.8 = bf16[32,512]{1,0:T(8,128)(2,1)S(1)} collective-permute-done((bf16[32,512]{1,0:T(8,128)(2,1)S(1)}, bf16[32,512]{1,0:T(8,128)(2,1)S(1)}, u32[]{:S(2)}, u32[]{:S(2)}) %collective-permute-start.8) | collective-permute-done | bytes 32800 | tf_op jit(solution)/shard_map/ppermute | solution.py:147
  133.7 4.9 %fusion.2 = f32[1536,512]{1,0:T(8,128)S(1)} fusion(bf16[1536,1536]{1,0:T(8,128)(2,1)} %copy-done.5, bf16[1536,512]{1,0:T(8,128)(2,1)S(1)} %bitcast.17), kind=kOutput, calls=%fused_computation.28 | convolution fusion | flops 2415919104 | bytes 9437184 | tf_op jit(solution)/shard_map/dot_general | solution.py:194
  138.6 3.8 %fusion = bf16[1536,512]{1,0:T(8,128)(2,1)} fusion(f32[1536,512]{1,0:T(8,128)S(1)} %fusion.2, bf16[1536,1536]{1,0:T(8,128)(2,1)S(1)} %bitcast.15, bf16[1536,512]{1,0:T(8,128)(2,1)S(1)} %collective-permute-done.12), kind=kOutput, calls=%fused_computation.2 | convolution fusion | flops 2417491968 | bytes 11010048 | tf_op jit(solution)/shard_map/dot_general | solution.py:195
  142.4 6.1 %all-to-all-start.3 = ((bf16[8,192,512]{2,1,0:T(8,128)(2,1)}), bf16[8,192,512]{2,1,0:T(8,128)(2,1)S(1)}, u32[]{:S(2)}, u32[]{:S(2)}) async-start(bf16[8,192,512]{2,1,0:T(8,128)(2,1)} %bitcast.3), calls=%async_computation.3 | async-start | bytes 3145728 | tf_op jit(solution)/shard_map/all_to_all | solution.py:143
  149.1 4.4 %collective-permute-done.10 = bf16[128,512]{1,0:T(8,128)(2,1)S(1)} collective-permute-done((bf16[128,512]{1,0:T(8,128)(2,1)S(1)}, bf16[128,512]{1,0:T(8,128)(2,1)S(1)}, u32[]{:S(2)}, u32[]{:S(2)}) %collective-permute-start.10) | collective-permute-done | bytes 131104 | tf_op jit(solution)/shard_map/ppermute | solution.py:147
  153.7 1.5 collective-permute-done.11
  155.3 1.1 convert_multiply_fusion
  156.5 7.1 %all-to-all-done.3 = bf16[8,192,512]{2,1,0:T(8,128)(2,1)S(1)} async-done(((bf16[8,192,512]{2,1,0:T(8,128)(2,1)}), bf16[8,192,512]{2,1,0:T(8,128)(2,1)S(1)}, u32[]{:S(2)}, u32[]{:S(2)}) %all-to-all-start.3) | async-done | bytes 1572896 | tf_op jit(solution)/shard_map/all_to_all | solution.py:143
  (46 shorter events, 4.1 us)
Async XLA Ops:
  2.9 7.2 %copy-start = (bf16[1,1,288,4096]{3,2,1,0:T(8,128)(2,1)S(1)}, bf16[1,1,288,4096]{3,2,1,0:T(8,128)(2,1)}, u32[]{:S(2)}) copy-start(bf16[1,1,288,4096]{3,2,1,0:T(8,128)(2,1)} %values.1) | copy-start | bytes 7077892
  2.9 7.2 %copy-start.3 = (s32[1,1,2,288]{3,2,1,0:T(2,128)S(1)}, s32[1,1,2,288]{3,2,1,0:T(2,128)}, u32[]{:S(2)}) copy-start(s32[1,1,2,288]{3,2,1,0:T(2,128)} %coords.1) | copy-start | bytes 6916
  2.9 31.9 %all-to-all-start = ((bf16[8,192,512]{2,1,0:T(8,128)(2,1)}), bf16[8,192,512]{2,1,0:T(8,128)(2,1)}, u32[]{:S(2)}, u32[]{:S(2)}) async-start(bf16[8,192,512]{2,1,0:T(8,128)(2,1)} %broadcast_in_dim.2), calls=%async_computation | async-start | bytes 3145728 | tf_op jit(solution)/shard_map/all_to_all | solution.py:143
  30.4 2.1 %copy-start.4 = (bf16[1536,1536]{1,0:T(8,128)(2,1)}, bf16[1536,1536]{1,0:T(8,128)(2,1)S(1)}, u32[]{:S(2)}) copy-start(bf16[1536,1536]{1,0:T(8,128)(2,1)S(1)} %get-tuple-element.10) | copy-start | bytes 14155780
  32.6 2.2 %copy-start.5 = (bf16[1536,1536]{1,0:T(8,128)(2,1)}, bf16[1536,1536]{1,0:T(8,128)(2,1)S(1)}, u32[]{:S(2)}) copy-start(bf16[1536,1536]{1,0:T(8,128)(2,1)S(1)} %get-tuple-element.9) | copy-start | bytes 14155780
  34.8 9.1 %copy-start.6 = (bf16[1536,1536]{1,0:T(8,128)(2,1)S(1)}, bf16[1536,1536]{1,0:T(8,128)(2,1)}, u32[]{:S(2)}) copy-start(bf16[1536,1536]{1,0:T(8,128)(2,1)} %copy-done.5) | copy-start | bytes 14155780
  40.4 3.5 %collective-permute-start = (bf16[1536,512]{1,0:T(8,128)(2,1)S(1)}, bf16[1536,512]{1,0:T(8,128)(2,1)S(1)}, u32[]{:S(2)}, u32[]{:S(2)}) collective-permute-start(bf16[1536,512]{1,0:T(8,128)(2,1)S(1)} %convolution_convert_fusion), channel_id=1, source_target_pairs={{0,1},{1,0},{2,3},{3,2},{4,5},{5,4},{6,7},{7,6},{8,9},{9,8},{10,11... | collective-permute-start | bytes 4718600 | tf_op jit(solution)/shard_map/ppermute | solution.py:147
  48.0 26.0 %copy-start.1 = (bf16[512,512]{1,0:T(8,128)(2,1)S(1)}, bf16[512,512]{1,0:T(8,128)(2,1)}, u32[]{:S(2)}) copy-start(bf16[512,512]{1,0:T(8,128)(2,1)} %weight.1) | copy-start | bytes 1572868
  48.0 26.0 %copy-start.2 = (bf16[192,512]{1,0:T(8,128)(2,1)S(1)}, bf16[192,512]{1,0:T(8,128)(2,1)}, u32[]{:S(2)}) copy-start(bf16[192,512]{1,0:T(8,128)(2,1)} %out_grad.1) | copy-start | bytes 589828
  76.1 1.5 collective-permute-start.1
  77.7 5.6 %collective-permute-start.2 = (bf16[128,512]{1,0:T(8,128)(2,1)S(1)}, bf16[128,512]{1,0:T(8,128)(2,1)S(1)}, u32[]{:S(2)}, u32[]{:S(2)}) collective-permute-start(bf16[128,512]{1,0:T(8,128)(2,1)S(1)} %broadcast_select_fusion.4), channel_id=1, source_target_pairs={{0,2},{2,0},{4,6},{6,4},{1,3},{3,1},{5,7},{7,5},{8,10},{10,8},{12,... | collective-permute-start | bytes 393224 | tf_op jit(solution)/shard_map/ppermute | solution.py:147
  78.7 42.0 %all-to-all-start.2 = ((bf16[8,192,512]{2,1,0:T(8,128)(2,1)}), bf16[8,192,512]{2,1,0:T(8,128)(2,1)S(1)}, u32[]{:S(2)}, u32[]{:S(2)}) async-start(bf16[8,192,512]{2,1,0:T(8,128)(2,1)} %get-tuple-element.14), calls=%async_computation.2 | async-start | bytes 3145728 | tf_op jit(solution)/shard_map/all_to_all | solution.py:143
  83.4 17.0 %collective-permute-start.3 = (bf16[64,512]{1,0:T(8,128)(2,1)S(1)}, bf16[64,512]{1,0:T(8,128)(2,1)S(1)}, u32[]{:S(2)}, u32[]{:S(2)}) collective-permute-start(bf16[64,512]{1,0:T(8,128)(2,1)S(1)} %broadcast_select_fusion.7), channel_id=1, source_target_pairs={{0,8},{8,0},{1,9},{9,1},{2,10},{10,2},{3,11},{11,3},{4,12},{12,4},... | collective-permute-start | bytes 196616 | tf_op jit(solution)/shard_map/ppermute | solution.py:147
  100.4 9.2 %collective-permute-start.4 = (bf16[32,512]{1,0:T(8,128)(2,1)S(1)}, bf16[32,512]{1,0:T(8,128)(2,1)S(1)}, u32[]{:S(2)}, u32[]{:S(2)}) collective-permute-start(bf16[32,512]{1,0:T(8,128)(2,1)S(1)} %broadcast_select_fusion.10), channel_id=1, source_target_pairs={{0,4},{2,6},{4,0},{6,2},{1,5},{3,7},{5,1},{7,3},{8,12},{10,14},{12... | collective-permute-start | bytes 98312 | tf_op jit(solution)/shard_map/ppermute | solution.py:147
  109.6 7.7 %collective-permute-start.5 = (bf16[32,512]{1,0:T(8,128)(2,1)S(1)}, bf16[32,512]{1,0:T(8,128)(2,1)S(1)}, u32[]{:S(2)}, u32[]{:S(2)}) collective-permute-start(bf16[32,512]{1,0:T(8,128)(2,1)S(1)} %add_convert_fusion.8), channel_id=1, source_target_pairs={{0,16},{16,0},{32,48},{48,32},{1,17},{17,1},{33,49},{49,33},{2,18}... | collective-permute-start | bytes 98312 | tf_op jit(solution)/shard_map/ppermute | solution.py:147
  117.3 5.5 %collective-permute-start.6 = (bf16[32,512]{1,0:T(8,128)(2,1)S(1)}, bf16[32,512]{1,0:T(8,128)(2,1)S(1)}, u32[]{:S(2)}, u32[]{:S(2)}) collective-permute-start(bf16[32,512]{1,0:T(8,128)(2,1)S(1)} %add_convert_fusion.7), channel_id=1, source_target_pairs={{0,32},{16,48},{32,0},{48,16},{1,33},{17,49},{33,1},{49,17},{2,34}... | collective-permute-start | bytes 98312 | tf_op jit(solution)/shard_map/ppermute | solution.py:147
  120.7 17.9 %collective-permute-start.12 = (bf16[1536,512]{1,0:T(8,128)(2,1)S(1)}, bf16[1536,512]{1,0:T(8,128)(2,1)S(1)}, u32[]{:S(2)}, u32[]{:S(2)}) collective-permute-start(bf16[1536,512]{1,0:T(8,128)(2,1)S(1)} %bitcast.16), channel_id=1, source_target_pairs={{0,1},{1,0},{2,3},{3,2},{4,5},{5,4},{6,7},{7,6},{8,9},{9,8},{10,11... | collective-permute-start | bytes 4718600 | tf_op jit(solution)/shard_map/ppermute | solution.py:147
  122.8 4.3 %collective-permute-start.7 = (bf16[32,512]{1,0:T(8,128)(2,1)S(1)}, bf16[32,512]{1,0:T(8,128)(2,1)S(1)}, u32[]{:S(2)}, u32[]{:S(2)}) collective-permute-start(bf16[32,512]{1,0:T(8,128)(2,1)S(1)} %add_convert_fusion.6), channel_id=1, source_target_pairs={{0,64},{64,0},{1,65},{65,1},{2,66},{66,2},{3,67},{67,3},{4,68},{68... | collective-permute-start | bytes 98312 | tf_op jit(solution)/shard_map/ppermute | solution.py:147
  127.1 5.5 %collective-permute-start.8 = (bf16[32,512]{1,0:T(8,128)(2,1)S(1)}, bf16[32,512]{1,0:T(8,128)(2,1)S(1)}, u32[]{:S(2)}, u32[]{:S(2)}) collective-permute-start(bf16[32,512]{1,0:T(8,128)(2,1)S(1)} %add_convert_fusion.5), channel_id=1, source_target_pairs={{0,4},{2,6},{4,0},{6,2},{1,5},{3,7},{5,1},{7,3},{8,12},{10,14},{12... | collective-permute-start | bytes 98312 | tf_op jit(solution)/shard_map/ppermute | solution.py:147
  132.6 5.9 %slice-start = ((s8[4718592]{0:T(1024)(128)(4,1)}), s8[4194304]{0:T(1024)(128)(4,1)S(1)}, s32[]{:S(2)}) async-start(s8[4718592]{0:T(1024)(128)(4,1)} %bitcast.14), calls=%async_computation.4 | async-start | bytes 8388608
  132.7 5.9 %slice-start.1 = ((s8[4718592]{0:T(1024)(128)(4,1)}), s8[524288]{0:T(1024)(128)(4,1)S(1)}, s32[]{:S(2)}) async-start(s8[4718592]{0:T(1024)(128)(4,1)} %bitcast.14), calls=%async_computation.5 | async-start | bytes 1048576
  132.7 15.8 %collective-permute-start.9 = (bf16[64,512]{1,0:T(8,128)(2,1)S(1)}, bf16[64,512]{1,0:T(8,128)(2,1)S(1)}, u32[]{:S(2)}, u32[]{:S(2)}) collective-permute-start(bf16[64,512]{1,0:T(8,128)(2,1)S(1)} %pad_maximum_fusion.2), channel_id=1, source_target_pairs={{0,8},{8,0},{1,9},{9,1},{2,10},{10,2},{3,11},{11,3},{4,12},{12,4},... | collective-permute-start | bytes 196616 | tf_op jit(solution)/shard_map/ppermute | solution.py:147
  142.4 21.1 %all-to-all-start.3 = ((bf16[8,192,512]{2,1,0:T(8,128)(2,1)}), bf16[8,192,512]{2,1,0:T(8,128)(2,1)S(1)}, u32[]{:S(2)}, u32[]{:S(2)}) async-start(bf16[8,192,512]{2,1,0:T(8,128)(2,1)} %bitcast.3), calls=%async_computation.3 | async-start | bytes 3145728 | tf_op jit(solution)/shard_map/all_to_all | solution.py:143
  148.5 5.0 %collective-permute-start.10 = (bf16[128,512]{1,0:T(8,128)(2,1)S(1)}, bf16[128,512]{1,0:T(8,128)(2,1)S(1)}, u32[]{:S(2)}, u32[]{:S(2)}) collective-permute-start(bf16[128,512]{1,0:T(8,128)(2,1)S(1)} %pad_maximum_fusion.1), channel_id=1, source_target_pairs={{0,2},{2,0},{4,6},{6,4},{1,3},{3,1},{5,7},{7,5},{8,10},{10,8},{12,... | collective-permute-start | bytes 393224 | tf_op jit(solution)/shard_map/ppermute | solution.py:147
  153.6 1.6 collective-permute-start.11

commit v3 on v1

v3 whole, which is shorter than its diff:
```python
import math

import jax
import jax.numpy as jnp
from jax import lax
from jax.experimental import pallas as pl
from jax.experimental.pallas import tpu as pltpu
from jax.sharding import Mesh, PartitionSpec as P

AXES = ("y_lo", "z", "y_hi", "x", "core")
SIZES = (2, 4, 2, 4, 2)
ROW = ("y_lo", "z")
CHIP = ("y_hi", "x")
COL = ("y_hi", "x", "core")
SIDE = 64
PEERS = 8
OWN = 192
WIDTH = 512
ROWS = PEERS * OWN
STEP = 256
RING = 4
PIECE = WIDTH // 2 // RING
LANES = WIDTH // RING


def vmem_call(kernel, outs, name, scratch=(), flops=0, moved=1 << 20, limit=16 << 20):
    vmem = pl.BlockSpec(memory_space=pltpu.VMEM)

    def call(*args):
        return pl.pallas_call(
            kernel,
            out_shape=outs,
            in_specs=[vmem] * len(args),
            out_specs=jax.tree.map(lambda _: vmem, outs),
            scratch_shapes=scratch,
            compiler_params=pltpu.CompilerParams(vmem_limit_bytes=limit),
            cost_estimate=pl.CostEstimate(flops=flops, bytes_accessed=moved, transcendentals=0),
            name=name,
        )(*args)

    return call


def bf16(*shape):
    return jax.ShapeDtypeStruct(shape, jnp.bfloat16)


def build_kernel(coords, counts, values, dense):
    rows, cols = dense.shape
    per_owner = OWN // SIDE
    me_core = lax.axis_index("core")

    @pl.loop(0, rows // SIDE)
    def _(r):
        dense[pl.ds(pl.multiple_of(r * SIDE, SIDE), SIDE), :] = jnp.zeros((SIDE, cols), dense.dtype)

    count = counts[0, 0]
    lane = lax.broadcasted_iota(jnp.int32, (SIDE, 2 * SIDE), 1)

    @pl.loop(0, (count + 15) // 16)
    def _(g):
        group = values[0, 0, pl.ds(pl.multiple_of(g * 16, 16), 16), :]
        pairs = group.astype(jnp.float32).reshape(16, SIDE // 2, 2 * SIDE)
        for k in range(16):
            slot = g * 16 + k
            live = slot < count
            block_row = jnp.where(live, coords[0, 0, 0, slot], 0)
            block_col = jnp.where(live, coords[0, 0, 1, slot], 0)
            owner = block_row // per_owner
            far = (owner + me_core) & 1
            at_row = (far * PEERS + (owner >> 1)) * per_owner + block_row % per_owner
            odd = (block_col & 1) == 1
            plain = pairs[k]
            turned = pltpu.roll(plain, SIDE, 1)
            block = jnp.concatenate(
                [jnp.where(odd, turned, plain), jnp.where(odd, plain, turned)], axis=0
            ).astype(dense.dtype)
            first = jnp.where(live, (block_col & 1) * SIDE, 4 * SIDE)
            mask = (lane >= first) & (lane < first + SIDE)
            place = dense.at[
                pl.ds(pl.multiple_of(at_row * SIDE, SIDE), SIDE),
                pl.ds(pl.multiple_of((block_col >> 1) * 2 * SIDE, 2 * SIDE), 2 * SIDE),
            ]
            place[...] = jnp.where(mask, block, place[...])


def build(coords, counts, values):
    return pl.pallas_call(
        build_kernel,
        out_shape=bf16(2 * ROWS, ROWS),
        in_specs=[pl.BlockSpec(memory_space=pltpu.SMEM)] * 2 + [pl.BlockSpec(memory_space=pltpu.VMEM)],
        out_specs=pl.BlockSpec(memory_space=pltpu.VMEM),
        compiler_params=pltpu.CompilerParams(vmem_limit_bytes=16 << 20),
        cost_estimate=pl.CostEstimate(flops=0, bytes_accessed=30 << 20, transcendentals=0),
        name="build",
    )(coords, counts, values)


def over_rows(a, b):
    return lax.dot_general(a, b, (((0,), (0,)), ((), ())), preferred_element_type=jnp.float32)


def down_kernel(dense, panel, out):
    out[...] = jnp.dot(dense[...], panel[...], preferred_element_type=jnp.float32).astype(out.dtype)


def down_add_kernel(dense, panel, other, *rest):
    out = rest[-1]
    own = jnp.dot(dense[...], panel[...], preferred_element_type=jnp.float32)
    out[...] = (own + other[...].astype(jnp.float32)).astype(out.dtype)


def up_kernel(dense, rows, out):
    out[...] = over_rows(dense[...], rows[...]).astype(out.dtype)


def up_add_kernel(dense, rows, other, out):
    out[...] = (over_rows(dense[...], rows[...]) + other[...]).astype(out.dtype)


def product(kernel, name, steps, dense_spec, extra_specs, out_spec, out_shape, *args, aliases={}):
    return pl.pallas_call(
        kernel,
        grid=(steps,),
        out_shape=out_shape,
        in_specs=[dense_spec, pl.BlockSpec((ROWS, WIDTH), lambda r: (0, 0))] + extra_specs,
        out_specs=out_spec,
        input_output_aliases=aliases,
        compiler_params=pltpu.CompilerParams(vmem_limit_bytes=56 << 20),
        cost_estimate=pl.CostEstimate(
            flops=2 * STEP * steps * ROWS * WIDTH, bytes_accessed=8 << 20, transcendentals=0
        ),
        name=name,
    )(*args)


def strip(first=0):
    return pl.BlockSpec((STEP, WIDTH), lambda r: (first + r, 0))


def down_both(dense, panel):
    all_steps = ROWS // STEP
    runs = ((0, all_steps // 2), (all_steps // 2, all_steps - all_steps // 2))

    def tile(first):
        return pl.BlockSpec((STEP, ROWS), lambda r: (first + r, 0))

    others = []
    for n, (first, steps) in enumerate(runs):
        far = product(
            down_kernel, f"down_far_{n}", steps, tile(all_steps + first), [], strip(),
            bf16(steps * STEP, WIDTH), dense, panel,
        )
        others.append(trade(far, "core"))
    out = []
    for n, (first, steps) in enumerate(runs):
        out = product(
            down_add_kernel, f"down_near_{n}", steps, tile(first),
            [strip()] + [pl.BlockSpec(memory_space=pl.ANY)] * (n > 0), strip(first),
            bf16(ROWS, WIDTH), dense, panel, others[n], *([out] if n else []),
            aliases={3: 0} if n else {},
        )
    return out


def up_both(dense, mine, theirs):
    def tile(half):
        return pl.BlockSpec((ROWS, STEP), lambda r: (half, r))

    steps = ROWS // STEP
    near = product(
        up_kernel, "up_near", steps, tile(0), [], strip(),
        jax.ShapeDtypeStruct((ROWS, WIDTH), jnp.float32), dense, mine,
    )
    return product(up_add_kernel, "up_far", steps, tile(1), [strip()], strip(), bf16(ROWS, WIDTH), dense, theirs, near)


def middle_kernel(parts, out_grad, weight, activations, send, wgrad_near, wgrad_far, local):
    total = parts[0].astype(jnp.float32)
    for k in range(1, PEERS):
        total = total + parts[k].astype(jnp.float32)
    aggregated = total.astype(jnp.bfloat16)
    at = lax.broadcasted_iota(jnp.int32, (OWN, OWN), 0)
    to = lax.broadcasted_iota(jnp.int32, (OWN, OWN), 1)
    half = SIDE // 2
    turn = jnp.where(
        (at // SIDE == to // SIDE) & (to % SIDE == 2 * (at % half) + (at % SIDE) // half), 1.0, 0.0
    ).astype(jnp.bfloat16)
    w = weight[...]
    pre_act = jnp.dot(aggregated, w, preferred_element_type=jnp.float32)
    sig = jax.nn.sigmoid(pre_act)
    act = (pre_act * sig).astype(jnp.bfloat16)
    activations[...] = over_rows(turn, act).astype(jnp.bfloat16)
    cotangent = jnp.dot(turn, out_grad[...], preferred_element_type=jnp.float32)
    grad_pre = (cotangent * sig * (1.0 + pre_act * (1.0 - sig))).astype(jnp.bfloat16)
    grad_agg = lax.dot_general(
        grad_pre, w, (((1,), (1,)), ((), ())), preferred_element_type=jnp.float32
    ).astype(jnp.bfloat16)
    for k in range(PEERS):
        send[k] = grad_agg
    local[...] = over_rows(aggregated, grad_pre).astype(jnp.bfloat16)
    core = lax.axis_index("core")
    for k in range(RING):
        for g in range(RING):
            for out, half_of in ((wgrad_near, core), (wgrad_far, 1 - core)):
                rows, cols = wgrad_place(half_of, k, g)
                out[k * PIECE : (k + 1) * PIECE, g * LANES : (g + 1) * LANES] = local[rows, cols]


def wgrad_place(half_of, k, g):
    row = half_of * (WIDTH // 2) + ((lax.axis_index("z") + k) & (RING - 1)) * PIECE
    col = ((lax.axis_index("x") + g) & (RING - 1)) * LANES
    return pl.ds(pl.multiple_of(row, PIECE), PIECE), pl.ds(pl.multiple_of(col, LANES), LANES)


def add(a, b):
    return (a.astype(jnp.float32) + b.astype(jnp.float32)).astype(jnp.bfloat16)


def pair_kernel(near, other, *outs):
    for k, out in enumerate(outs):
        rows = slice(k * PIECE, (k + 1) * PIECE)
        out[...] = add(near[rows], other[rows])


def sum_kernel(*refs):
    *parts, out = refs
    total = parts[0][...].astype(jnp.float32)
    for part in parts[1:]:
        total = total + part[...].astype(jnp.float32)
    out[...] = total.astype(out.dtype)


def square_kernel(a, b, c, d, out):
    first = a[...].astype(jnp.float32) + b[...].astype(jnp.float32)
    out[...] = (first + (c[...].astype(jnp.float32) + d[...].astype(jnp.float32))).astype(out.dtype)


def turn_kernel(*refs):
    pieces, outs = refs[:RING], refs[RING:]
    for g, out in enumerate(outs):
        for k, piece in enumerate(pieces):
            out[k * PIECE : (k + 1) * PIECE] = piece[:, g * LANES : (g + 1) * LANES]


def join_kernel(*refs):
    *parts, out = refs
    for g, part in enumerate(parts):
        out[:, g * LANES : (g + 1) * LANES] = part[...]


def place_kernel(mine, theirs, out):
    core = lax.axis_index("core")
    scale = 1.0 / math.sqrt(OWN * PEERS * 2 * PEERS)
    for k in range(RING):
        for g in range(RING):
            for part, half_of in ((mine, core), (theirs, 1 - core)):
                value = part[k * PIECE : (k + 1) * PIECE, g * LANES : (g + 1) * LANES].astype(jnp.float32)
                rows, cols = wgrad_place(half_of, k, g)
                out[rows, cols] = value * jnp.float32(scale)


def spread_kernel(array, out, sems):
    copies = [pltpu.make_async_copy(array, out.at[k], sems.at[k]) for k in range(PEERS)]
    for copy in copies:
        copy.start()
    for copy in copies:
        copy.wait()


def spread(array):
    anywhere = pl.BlockSpec(memory_space=pl.ANY)
    return pl.pallas_call(
        spread_kernel,
        out_shape=jax.ShapeDtypeStruct((PEERS,) + array.shape, array.dtype),
        in_specs=[anywhere],
        out_specs=anywhere,
        scratch_shapes=[pltpu.SemaphoreType.DMA((PEERS,))],
        cost_estimate=pl.CostEstimate(flops=0, bytes_accessed=2 << 20, transcendentals=0),
        name="spread",
    )(array)


def exchange(parts, axes):
    return lax.all_to_all(parts, axes, 0, 0)


def trade(array, axes, bits=1):
    return lax.ppermute(array, axes, [(i, i ^ bits) for i in range(lax.axis_size(axes))])


def scatter_ring(pieces, axis, name):
    arrived = [pieces[0]]
    for k in range(1, RING):
        arrived.append(lax.ppermute(pieces[k], axis, [(i, (i + k) % RING) for i in range(RING)]))
    return vmem_call(sum_kernel, bf16(*pieces[0].shape), name)(*arrived)


def gather_ring(piece, axis):
    pieces = [piece]
    for k in range(1, RING):
        pieces.append(lax.ppermute(piece, axis, [(i, (i - k) % RING) for i in range(RING)]))
    return pieces


def per_device(features, out_grad, weight, block_values, block_coords, block_counts):
    panel = exchange(spread(features), ROW).reshape(ROWS, WIDTH)
    dense = build(block_coords, block_counts, block_values)

    parts = exchange(down_both(dense, panel).reshape(PEERS, OWN, WIDTH), CHIP)

    half = bf16(WIDTH // 2, WIDTH)
    activations, send, wgrad_near, wgrad_far = vmem_call(
        middle_kernel,
        (bf16(OWN, WIDTH), bf16(PEERS, OWN, WIDTH), half, half),
        "middle",
        scratch=[pltpu.VMEM((WIDTH, WIDTH), jnp.bfloat16)],
        flops=2 * 3 * OWN * WIDTH * WIDTH,
    )(parts, out_grad, weight)

    mine = exchange(send, CHIP).reshape(ROWS, WIDTH)

    piece = bf16(PIECE, WIDTH)
    pieces = vmem_call(pair_kernel, (piece,) * RING, "pair")(wgrad_near, trade(wgrad_far, "core"))
    summed = scatter_ring(pieces, "z", "sum_z")
    ys = ("y_lo", "y_hi")
    summed = vmem_call(square_kernel, piece, "sum_y")(
        summed, trade(summed, ys, 1), trade(summed, ys, 2), trade(summed, ys, 3)
    )
    summed, mine = lax.optimization_barrier((summed, mine))
    pieces = gather_ring(summed, "z")
    theirs = trade(mine, "core")
    partial_grad = up_both(dense, mine, theirs)
    partial_grad, *pieces = lax.optimization_barrier((partial_grad, *pieces))
    received = exchange(partial_grad.reshape(PEERS, OWN, WIDTH), ROW)

    column = bf16(WIDTH // 2, LANES)
    columns = vmem_call(turn_kernel, (column,) * RING, "turn")(*pieces)
    summed = scatter_ring(columns, "x", "sum_x")
    columns = gather_ring(summed, "x")
    own_half = vmem_call(join_kernel, half, "join")(*columns)
    weight_grad = vmem_call(place_kernel, jax.ShapeDtypeStruct((WIDTH, WIDTH), jnp.float32), "place")(
        own_half, trade(own_half, "core")
    )

    total = received[0].astype(jnp.float32)
    for k in range(1, PEERS):
        total = total + received[k].astype(jnp.float32)
    feature_grad = total.astype(jnp.bfloat16)
    return (activations, weight_grad, feature_grad)


def solution(mesh):
    fine = Mesh(mesh.devices.reshape(SIZES), AXES)
    return jax.shard_map(
        per_device,
        mesh=fine,
        in_specs=(
            P(COL + ROW, None),
            P(ROW + COL, None),
            P(),
            P(ROW, COL, None, None),
            P(ROW, COL, None, None),
            P(ROW, COL),
        ),
        out_specs=(P(ROW + COL, None), P(), P(COL + ROW, None)),
        check_vma=False,
    )
```

time: 180 us -> 204 us (1.13)
  Pallas kernels: 4.04 us -> 90.2 us
  starting transfers between devices: 82.7 us -> 36.6 us
  matrix products: 14.8 us -> 0 us
  blocking collectives: 15 us -> 29.8 us
  waiting for transfers between devices: 45.7 us -> 36.9 us
  local copies, waits for them, and re-layouts: 13.1 us -> 6.61 us
    pallas_call x2 -> x16, Pallas kernels: 4.04 us -> 90.2 us  [the longest x1 48.8 us: spread(): pl.pallas_call(spread_kernel, out_shape=jax.ShapeDtypeStruct((PEERS,) + a...]
    ppermute x37 -> x20, starting transfers between devices: 79.1 us -> 22 us  [the longest x6 10.1 us: scatter_ring(): lax.ppermute(pieces[k], axis, [(i, (i + k) % RING) for i in range(RING)])]
    ppermute x37 -> x20, waiting for transfers between devices: 45.7 us -> 23.6 us  [the longest x8 12.2 us: trade(): lax.ppermute(array, axes, [(i, i ^ bits) for i in range(lax.axis_size(axe...]
    all_to_all x1, blocking collectives: 15 us -> 29.8 us  [exchange(): return lax.all_to_all(parts, axes, 0, 0)]
    dot_general x2 -> x0, matrix products: 14.8 us -> none  [the longest x1 9.52 us: per_device(): lax.dot_general(dense, grad_rows, (((0,), (0,)), ((), ())), preferred_ele...]
    all_to_all x1 -> x3, waiting for transfers between devices: 0.01 us -> 13.3 us  [exchange(): return lax.all_to_all(parts, axes, 0, 0)]
    all_to_all x1 -> x3, starting transfers between devices: 3.57 us -> 14.6 us  [exchange(): return lax.all_to_all(parts, axes, 0, 0)]
    unnamed x28 -> x18, local copies, waits for them, and re-layouts: 9.17 us -> 6.61 us
  transfers between devices with their start and end apart: 38 -> 23, of which waited for: 14 -> 15; matrix products, arithmetic and copies ran while one was open for 11% -> 0% of each run, Pallas kernels for 2% -> 15%
where the time goes in v3:
time: 204 us; the launch traced here: 203 us
  Pallas kernels  90.2 us (44%)
  waiting for transfers between devices  36.9 us (18%)
  starting transfers between devices  36.6 us (18%)
  blocking collectives  29.8 us (15%)
  local copies, waits for them, and re-layouts  6.61 us (3%)
    pallas_call x1, Pallas kernels, spread(): pl.pallas_call(spread_kernel, out_shape=jax.ShapeDtypeStruct((PEERS,) + a...  48.8 us
    pallas_call x6, Pallas kernels, product(): pl.pallas_call(kernel, grid=(steps,), out_shape=out_shape, in_specs=[dens...  35.1 us
    all_to_all x1, blocking collectives, exchange(): return lax.all_to_all(parts, axes, 0, 0)  29.8 us
    all_to_all x3, starting transfers between devices, exchange(): return lax.all_to_all(parts, axes, 0, 0)  14.6 us
    all_to_all x3, waiting for transfers between devices, exchange(): return lax.all_to_all(parts, axes, 0, 0)  13.3 us
    ppermute x8, waiting for transfers between devices, trade(): lax.ppermute(array, axes, [(i, i ^ bits) for i in range(lax.axis_size(axe...  12.2 us
    ppermute x6, starting transfers between devices, scatter_ring(): lax.ppermute(pieces[k], axis, [(i, (i + k) % RING) for i in range(RING)])  10.1 us
    ppermute x6, starting transfers between devices, gather_ring(): lax.ppermute(piece, axis, [(i, (i - k) % RING) for i in range(RING)])  7.04 us
  transfers between devices with their start and end apart: 23, of which 15 were waited for; matrix products, arithmetic and copies ran while one was open for 0% of the time, Pallas kernels for 15%

profile of v3, /device:TPU:0, one launch (start us, length us, event | category | flops | bytes accessed | tf_op | source)
XLA Modules:
  0.0 202.5 jit_solution(9732135135480643334)
XLA Ops:
  0.6 48.8 %spread.1 = bf16[8,192,512]{2,1,0:T(8,128)(2,1)} custom-call(bf16[192,512]{1,0:T(8,128)(2,1)} %array.1), custom_call_target="tpu_custom_call" | custom-call | bytes 2097152 | tf_op jit(solution)/shard_map/spread/pallas_call | solution.py:273
  49.5 6.6 %all-to-all-start = ((bf16[8,192,512]{2,1,0:T(8,128)(2,1)}), bf16[8,192,512]{2,1,0:T(8,128)(2,1)}, u32[]{:S(2)}, u32[]{:S(2)}) async-start(bf16[8,192,512]{2,1,0:T(8,128)(2,1)} %spread.1), calls=%async_computation | async-start | bytes 3145728 | tf_op jit(solution)/shard_map/all_to_all | solution.py:285
  56.7 2.8 %build.1.dense = bf16[3072,1536]{1,0:T(8,128)(2,1)S(1)} custom-call(s32[1,1,2,288]{3,2,1,0:T(2,128)S(1)} %copy-done.4, s32[1,1]{1,0:T(1,128)S(6)} %copy.11.counts, bf16[1,1,288,4096]{3,2,1,0:T(8,128)(2,1)S(1)} %copy-done.1), custom_call_target="tpu_custom_call" | custom-call | bytes 31457280 | tf_op jit(solution)/shard_map/build/pallas_call | solution.py:88
  59.6 3.6 %copy-done = bf16[3072,1536]{1,0:T(8,128)(2,1)} copy-done((bf16[3072,1536]{1,0:T(8,128)(2,1)}, bf16[3072,1536]{1,0:T(8,128)(2,1)S(1)}, u32[]{:S(2)}) %copy-start) | copy-done | bytes 9437208
  63.2 13.3 %all-to-all-done = bf16[8,192,512]{2,1,0:T(8,128)(2,1)} async-done(((bf16[8,192,512]{2,1,0:T(8,128)(2,1)}), bf16[8,192,512]{2,1,0:T(8,128)(2,1)}, u32[]{:S(2)}, u32[]{:S(2)}) %all-to-all-start) | async-done | bytes 1572896 | tf_op jit(solution)/shard_map/all_to_all | solution.py:285
  76.6 4.7 %down_far_0.1 = bf16[768,512]{1,0:T(8,128)(2,1)} custom-call(bf16[3072,1536]{1,0:T(8,128)(2,1)} %copy-done, bf16[1536,512]{1,0:T(8,128)(2,1)} %bitcast.panel), custom_call_target="tpu_custom_call" | custom-call | flops 1207959552 | bytes 8388608 | tf_op jit(solution)/shard_map/down_far_0/pallas_call | solution.py:122
  81.3 4.8 %down_far_1.1 = bf16[768,512]{1,0:T(8,128)(2,1)} custom-call(bf16[3072,1536]{1,0:T(8,128)(2,1)} %copy-done, bf16[1536,512]{1,0:T(8,128)(2,1)} %bitcast.panel), custom_call_target="tpu_custom_call" | custom-call | flops 1207959552 | bytes 8388608 | tf_op jit(solution)/shard_map/down_far_1/pallas_call | solution.py:122
  87.5 5.1 %down_near_0.1.rest_0_ = bf16[1536,512]{1,0:T(8,128)(2,1)} custom-call(bf16[3072,1536]{1,0:T(8,128)(2,1)} %copy-done, bf16[1536,512]{1,0:T(8,128)(2,1)} %bitcast.panel, bf16[768,512]{1,0:T(8,128)(2,1)} %copy-done.8), custom_call_target="tpu_custom_call" | custom-call | flops 1207959552 | bytes 8388608 | tf_op jit(solution)/shard_map/down_near_0/pallas_call | solution.py:122
  93.5 4.9 %down_near_1.1 = bf16[1536,512]{1,0:T(8,128)(2,1)} custom-call(bf16[3072,1536]{1,0:T(8,128)(2,1)} %copy-done, bf16[1536,512]{1,0:T(8,128)(2,1)} %bitcast.panel, bf16[768,512]{1,0:T(8,128)(2,1)} %copy-done.7, bf16[1536,512]{1,0:T(8,128)(2,1)} %down_near_0.1.rest_0_), custom_call_target="tpu_custom_call", output_to_operand_aliasing={{}: (3, {})} | custom-call | flops 1207959552 | bytes 8388608 | tf_op jit(solution)/shard_map/down_near_1/pallas_call | solution.py:122
  98.4 29.8 %all_to_all.20.parts = bf16[8,192,512]{2,1,0:T(8,128)(2,1)S(1)} all-to-all(bf16[8,192,512]{2,1,0:T(8,128)(2,1)} %bitcast.6), channel_id=1, replica_groups=mesh['y_lo'=2,'z'=4,'y_hi'=2,'x'=4,'core'=2] {'y_hi','x'}, dimensions={0} | all-to-all | bytes 3145728 | tf_op jit(solution)/shard_map/all_to_all | solution.py:285
  128.2 2.0 %middle.1 = (bf16[192,512]{1,0:T(8,128)(2,1)}, bf16[8,192,512]{2,1,0:T(8,128)(2,1)}, bf16[256,512]{1,0:T(8,128)(2,1)S(1)}, bf16[256,512]{1,0:T(8,128)(2,1)S(1)}) custom-call(bf16[8,192,512]{2,1,0:T(8,128)(2,1)S(1)} %all_to_all.20.parts, bf16[192,512]{1,0:T(8,128)(2,1)S(1)} %copy-done.3, bf16[512,512]{1,0:T(8,128)(2,1)S(1)} %copy-done.2), custom_call_target="tpu_custom_call" | custom-call | flops 301989888 | bytes 1048576 | tf_op jit(solution)/shard_map/middle/pallas_call | solution.py:30
  130.2 3.6 %all-to-all-start.2 = ((bf16[8,192,512]{2,1,0:T(8,128)(2,1)}), bf16[8,192,512]{2,1,0:T(8,128)(2,1)S(1)}, u32[]{:S(2)}, u32[]{:S(2)}) async-start(bf16[8,192,512]{2,1,0:T(8,128)(2,1)} %get-tuple-element.29), calls=%async_computation.2 | async-start | bytes 3145728 | tf_op jit(solution)/shard_map/all_to_all | solution.py:285
  133.9 1.5 collective-permute-done.2.other
  136.4 2.5 %collective-permute-start.4 = (bf16[64,512]{1,0:T(8,128)(2,1)S(1)}, bf16[64,512]{1,0:T(8,128)(2,1)S(1)}, u32[]{:S(2)}, u32[]{:S(2)}) collective-permute-start(bf16[64,512]{1,0:T(8,128)(2,1)S(1)} %get-tuple-element.27), channel_id=1, source_target_pairs={{0,32},{16,48},{32,0},{48,16},{1,33},{17,49},{33,1},{49,17},{2,34}... | collective-permute-start | bytes 196616 | tf_op jit(solution)/shard_map/ppermute | solution.py:295
  140.0 1.7 collective-permute-done.3.refs_1_
  143.2 3.4 %collective-permute-start.6 = (bf16[64,512]{1,0:T(8,128)(2,1)S(1)}, bf16[64,512]{1,0:T(8,128)(2,1)S(1)}, u32[]{:S(2)}, u32[]{:S(2)}) collective-permute-start(bf16[64,512]{1,0:T(8,128)(2,1)S(1)} %sum_z.1.a), channel_id=1, source_target_pairs={{0,8},{8,0},{64,72},{72,64},{1,9},{9,1},{65,73},{73,65},{2,10},{10... | collective-permute-start | bytes 196616 | tf_op jit(solution)/shard_map/ppermute | solution.py:289
  147.4 5.3 %collective-permute-done.6.b = bf16[64,512]{1,0:T(8,128)(2,1)S(1)} collective-permute-done((bf16[64,512]{1,0:T(8,128)(2,1)S(1)}, bf16[64,512]{1,0:T(8,128)(2,1)S(1)}, u32[]{:S(2)}, u32[]{:S(2)}) %collective-permute-start.6) | collective-permute-done | bytes 65568 | tf_op jit(solution)/shard_map/ppermute | solution.py:289
  152.7 2.0 collective-permute-done.7.c
  154.6 1.9 collective-permute-done.8.d
  156.7 2.1 %collective-permute-start.10 = (bf16[64,512]{1,0:T(8,128)(2,1)S(1)}, bf16[64,512]{1,0:T(8,128)(2,1)S(1)}, u32[]{:S(2)}, u32[]{:S(2)}) collective-permute-start(bf16[64,512]{1,0:T(8,128)(2,1)S(1)} %sum_y.1.refs_0_), channel_id=1, source_target_pairs={{0,48},{16,0},{32,16},{48,32},{1,49},{17,1},{33,17},{49,33},{2,50}... | collective-permute-start | bytes 196616 | tf_op jit(solution)/shard_map/ppermute | solution.py:302
  160.0 7.7 %up_near.1.other = f32[1536,512]{1,0:T(8,128)} custom-call(bf16[3072,1536]{1,0:T(8,128)(2,1)} %copy-done, bf16[1536,512]{1,0:T(8,128)(2,1)} %bitcast.8), custom_call_target="tpu_custom_call" | custom-call | flops 2415919104 | bytes 8388608 | tf_op jit(solution)/shard_map/up_near/pallas_call | solution.py:122
  167.7 1.1 copy-done.6
  168.9 7.9 %up_far.1 = bf16[1536,512]{1,0:T(8,128)(2,1)} custom-call(bf16[3072,1536]{1,0:T(8,128)(2,1)} %copy-done, bf16[1536,512]{1,0:T(8,128)(2,1)} %copy-done.6, f32[1536,512]{1,0:T(8,128)} %up_near.1.other), custom_call_target="tpu_custom_call" | custom-call | flops 2415919104 | bytes 8388608 | tf_op jit(solution)/shard_map/up_far/pallas_call | solution.py:122
  176.8 4.5 %all-to-all-start.3 = ((bf16[8,192,512]{2,1,0:T(8,128)(2,1)}), bf16[8,192,512]{2,1,0:T(8,128)(2,1)S(1)}, u32[]{:S(2)}, u32[]{:S(2)}) async-start(bf16[8,192,512]{2,1,0:T(8,128)(2,1)} %bitcast.9), calls=%async_computation.3 | async-start | bytes 3145728 | tf_op jit(solution)/shard_map/all_to_all | solution.py:285
  181.3 1.8 collective-permute-start.13
  183.1 2.3 %collective-permute-start.14 = (bf16[256,128]{1,0:T(8,128)(2,1)S(1)}, bf16[256,128]{1,0:T(8,128)(2,1)S(1)}, u32[]{:S(2)}, u32[]{:S(2)}) collective-permute-start(bf16[256,128]{1,0:T(8,128)(2,1)S(1)} %get-tuple-element.38), channel_id=1, source_target_pairs={{0,4},{2,6},{4,0},{6,2},{1,5},{3,7},{5,1},{7,3},{8,12},{10,14},{12... | collective-permute-start | bytes 196616 | tf_op jit(solution)/shard_map/ppermute | solution.py:295
  185.4 1.5 collective-permute-start.15
  187.6 1.3 collective-permute-done.14.refs_2_
  189.7 2.7 %collective-permute-start.16 = (bf16[256,128]{1,0:T(8,128)(2,1)S(1)}, bf16[256,128]{1,0:T(8,128)(2,1)S(1)}, u32[]{:S(2)}, u32[]{:S(2)}) collective-permute-start(bf16[256,128]{1,0:T(8,128)(2,1)S(1)} %sum_x.1.refs_0_), channel_id=1, source_target_pairs={{0,6},{2,0},{4,2},{6,4},{1,7},{3,1},{5,3},{7,5},{8,14},{10,8},{12,... | collective-permute-start | bytes 196616 | tf_op jit(solution)/shard_map/ppermute | solution.py:302
  193.4 1.6 collective-permute-done.16.refs_1_
  195.0 3.4 %collective-permute-done.17.refs_2_ = bf16[256,128]{1,0:T(8,128)(2,1)S(1)} collective-permute-done((bf16[256,128]{1,0:T(8,128)(2,1)S(1)}, bf16[256,128]{1,0:T(8,128)(2,1)S(1)}, u32[]{:S(2)}, u32[]{:S(2)}) %collective-permute-start.17) | collective-permute-done | bytes 65568 | tf_op jit(solution)/shard_map/ppermute | solution.py:302
  199.0 1.5 collective-permute-done.19.theirs
  (50 shorter events, 13.3 us)
Async XLA Ops:
  49.5 7.2 %copy-start.1 = (bf16[1,1,288,4096]{3,2,1,0:T(8,128)(2,1)S(1)}, bf16[1,1,288,4096]{3,2,1,0:T(8,128)(2,1)}, u32[]{:S(2)}) copy-start(bf16[1,1,288,4096]{3,2,1,0:T(8,128)(2,1)} %values.1) | copy-start | bytes 7077892
  49.5 7.2 %copy-start.4 = (s32[1,1,2,288]{3,2,1,0:T(2,128)S(1)}, s32[1,1,2,288]{3,2,1,0:T(2,128)}, u32[]{:S(2)}) copy-start(s32[1,1,2,288]{3,2,1,0:T(2,128)} %coords.1) | copy-start | bytes 6916
  49.5 27.1 %all-to-all-start = ((bf16[8,192,512]{2,1,0:T(8,128)(2,1)}), bf16[8,192,512]{2,1,0:T(8,128)(2,1)}, u32[]{:S(2)}, u32[]{:S(2)}) async-start(bf16[8,192,512]{2,1,0:T(8,128)(2,1)} %spread.1), calls=%async_computation | async-start | bytes 3145728 | tf_op jit(solution)/shard_map/all_to_all | solution.py:285
  59.6 3.7 %copy-start = (bf16[3072,1536]{1,0:T(8,128)(2,1)}, bf16[3072,1536]{1,0:T(8,128)(2,1)S(1)}, u32[]{:S(2)}) copy-start(bf16[3072,1536]{1,0:T(8,128)(2,1)S(1)} %build.1.dense) | copy-start | bytes 28311556
  81.3 5.3 %collective-permute-start.1 = (bf16[768,512]{1,0:T(8,128)(2,1)}, bf16[768,512]{1,0:T(8,128)(2,1)S(1)}, u32[]{:S(2)}, u32[]{:S(2)}) collective-permute-start(bf16[768,512]{1,0:T(8,128)(2,1)} %down_far_0.1), channel_id=1, source_target_pairs={{0,1},{1,0},{2,3},{3,2},{4,5},{5,4},{6,7},{7,6},{8,9},{9,8},{10,11... | collective-permute-start | bytes 2359304 | tf_op jit(solution)/shard_map/ppermute | solution.py:289
  86.1 6.5 %collective-permute-start = (bf16[768,512]{1,0:T(8,128)(2,1)}, bf16[768,512]{1,0:T(8,128)(2,1)S(1)}, u32[]{:S(2)}, u32[]{:S(2)}) collective-permute-start(bf16[768,512]{1,0:T(8,128)(2,1)} %down_far_1.1), channel_id=1, source_target_pairs={{0,1},{1,0},{2,3},{3,2},{4,5},{5,4},{6,7},{7,6},{8,9},{9,8},{10,11... | collective-permute-start | bytes 2359304 | tf_op jit(solution)/shard_map/ppermute | solution.py:289
  86.6 0.9 copy-start.8
  92.6 0.9 copy-start.7
  98.4 29.8 %copy-start.2 = (bf16[512,512]{1,0:T(8,128)(2,1)S(1)}, bf16[512,512]{1,0:T(8,128)(2,1)}, u32[]{:S(2)}) copy-start(bf16[512,512]{1,0:T(8,128)(2,1)} %weight.1) | copy-start | bytes 1572868
  98.4 29.8 %copy-start.3 = (bf16[192,512]{1,0:T(8,128)(2,1)S(1)}, bf16[192,512]{1,0:T(8,128)(2,1)}, u32[]{:S(2)}) copy-start(bf16[192,512]{1,0:T(8,128)(2,1)} %out_grad.1) | copy-start | bytes 589828
  130.2 26.4 %all-to-all-start.2 = ((bf16[8,192,512]{2,1,0:T(8,128)(2,1)}), bf16[8,192,512]{2,1,0:T(8,128)(2,1)S(1)}, u32[]{:S(2)}, u32[]{:S(2)}) async-start(bf16[8,192,512]{2,1,0:T(8,128)(2,1)} %get-tuple-element.29), calls=%async_computation.2 | async-start | bytes 3145728 | tf_op jit(solution)/shard_map/all_to_all | solution.py:285
  133.8 1.6 collective-permute-start.2
  135.5 6.2 %collective-permute-start.3 = (bf16[64,512]{1,0:T(8,128)(2,1)S(1)}, bf16[64,512]{1,0:T(8,128)(2,1)S(1)}, u32[]{:S(2)}, u32[]{:S(2)}) collective-permute-start(bf16[64,512]{1,0:T(8,128)(2,1)S(1)} %get-tuple-element.26), channel_id=1, source_target_pairs={{0,16},{16,32},{32,48},{48,0},{1,17},{17,33},{33,49},{49,1},{2,18}... | collective-permute-start | bytes 196616 | tf_op jit(solution)/shard_map/ppermute | solution.py:295
  136.4 6.1 %collective-permute-start.4 = (bf16[64,512]{1,0:T(8,128)(2,1)S(1)}, bf16[64,512]{1,0:T(8,128)(2,1)S(1)}, u32[]{:S(2)}, u32[]{:S(2)}) collective-permute-start(bf16[64,512]{1,0:T(8,128)(2,1)S(1)} %get-tuple-element.27), channel_id=1, source_target_pairs={{0,32},{16,48},{32,0},{48,16},{1,33},{17,49},{33,1},{49,17},{2,34}... | collective-permute-start | bytes 196616 | tf_op jit(solution)/shard_map/ppermute | solution.py:295
  138.9 4.3 %collective-permute-start.5 = (bf16[64,512]{1,0:T(8,128)(2,1)S(1)}, bf16[64,512]{1,0:T(8,128)(2,1)S(1)}, u32[]{:S(2)}, u32[]{:S(2)}) collective-permute-start(bf16[64,512]{1,0:T(8,128)(2,1)S(1)} %get-tuple-element.28), channel_id=1, source_target_pairs={{0,48},{16,0},{32,16},{48,32},{1,49},{17,1},{33,17},{49,33},{2,50}... | collective-permute-start | bytes 196616 | tf_op jit(solution)/shard_map/ppermute | solution.py:295
  143.2 9.4 %collective-permute-start.6 = (bf16[64,512]{1,0:T(8,128)(2,1)S(1)}, bf16[64,512]{1,0:T(8,128)(2,1)S(1)}, u32[]{:S(2)}, u32[]{:S(2)}) collective-permute-start(bf16[64,512]{1,0:T(8,128)(2,1)S(1)} %sum_z.1.a), channel_id=1, source_target_pairs={{0,8},{8,0},{64,72},{72,64},{1,9},{9,1},{65,73},{73,65},{2,10},{10... | collective-permute-start | bytes 196616 | tf_op jit(solution)/shard_map/ppermute | solution.py:289
  146.7 7.9 %collective-permute-start.7 = (bf16[64,512]{1,0:T(8,128)(2,1)S(1)}, bf16[64,512]{1,0:T(8,128)(2,1)S(1)}, u32[]{:S(2)}, u32[]{:S(2)}) collective-permute-start(bf16[64,512]{1,0:T(8,128)(2,1)S(1)} %sum_z.1.a), channel_id=1, source_target_pairs={{0,64},{8,72},{64,0},{72,8},{1,65},{9,73},{65,1},{73,9},{2,66},{10... | collective-permute-start | bytes 196616 | tf_op jit(solution)/shard_map/ppermute | solution.py:289
  147.2 9.3 %collective-permute-start.8 = (bf16[64,512]{1,0:T(8,128)(2,1)S(1)}, bf16[64,512]{1,0:T(8,128)(2,1)S(1)}, u32[]{:S(2)}, u32[]{:S(2)}) collective-permute-start(bf16[64,512]{1,0:T(8,128)(2,1)S(1)} %sum_z.1.a), channel_id=1, source_target_pairs={{0,72},{8,64},{64,8},{72,0},{1,73},{9,65},{65,9},{73,1},{2,74},{10... | collective-permute-start | bytes 196616 | tf_op jit(solution)/shard_map/ppermute | solution.py:289
  156.6 3.5 %copy-start.5 = (bf16[8,192,512]{2,1,0:T(8,128)(2,1)}, bf16[8,192,512]{2,1,0:T(8,128)(2,1)S(1)}, u32[]{:S(2)}) copy-start(bf16[8,192,512]{2,1,0:T(8,128)(2,1)S(1)} %all-to-all-done.2) | copy-start | bytes 4718596
  156.6 11.1 %collective-permute-start.9 = (bf16[1536,512]{1,0:T(8,128)(2,1)S(1)}, bf16[1536,512]{1,0:T(8,128)(2,1)S(1)}, u32[]{:S(2)}, u32[]{:S(2)}) collective-permute-start(bf16[1536,512]{1,0:T(8,128)(2,1)S(1)} %bitcast.7), channel_id=1, source_target_pairs={{0,1},{1,0},{2,3},{3,2},{4,5},{5,4},{6,7},{7,6},{8,9},{9,8},{10,11... | collective-permute-start | bytes 4718600 | tf_op jit(solution)/shard_map/ppermute | solution.py:289
  156.7 20.1 %collective-permute-start.10 = (bf16[64,512]{1,0:T(8,128)(2,1)S(1)}, bf16[64,512]{1,0:T(8,128)(2,1)S(1)}, u32[]{:S(2)}, u32[]{:S(2)}) collective-permute-start(bf16[64,512]{1,0:T(8,128)(2,1)S(1)} %sum_y.1.refs_0_), channel_id=1, source_target_pairs={{0,48},{16,0},{32,16},{48,32},{1,49},{17,1},{33,17},{49,33},{2,50}... | collective-permute-start | bytes 196616 | tf_op jit(solution)/shard_map/ppermute | solution.py:302
  158.8 18.0 %collective-permute-start.11 = (bf16[64,512]{1,0:T(8,128)(2,1)S(1)}, bf16[64,512]{1,0:T(8,128)(2,1)S(1)}, u32[]{:S(2)}, u32[]{:S(2)}) collective-permute-start(bf16[64,512]{1,0:T(8,128)(2,1)S(1)} %sum_y.1.refs_0_), channel_id=1, source_target_pairs={{0,32},{16,48},{32,0},{48,16},{1,33},{17,49},{33,1},{49,17},{2,34}... | collective-permute-start | bytes 196616 | tf_op jit(solution)/shard_map/ppermute | solution.py:302
  159.7 17.1 %collective-permute-start.12 = (bf16[64,512]{1,0:T(8,128)(2,1)S(1)}, bf16[64,512]{1,0:T(8,128)(2,1)S(1)}, u32[]{:S(2)}, u32[]{:S(2)}) collective-permute-start(bf16[64,512]{1,0:T(8,128)(2,1)S(1)} %sum_y.1.refs_0_), channel_id=1, source_target_pairs={{0,16},{16,32},{32,48},{48,0},{1,17},{17,33},{33,49},{49,1},{2,18}... | collective-permute-start | bytes 196616 | tf_op jit(solution)/shard_map/ppermute | solution.py:302
  167.7 1.1 copy-start.6
  176.8 24.8 %all-to-all-start.3 = ((bf16[8,192,512]{2,1,0:T(8,128)(2,1)}), bf16[8,192,512]{2,1,0:T(8,128)(2,1)S(1)}, u32[]{:S(2)}, u32[]{:S(2)}) async-start(bf16[8,192,512]{2,1,0:T(8,128)(2,1)} %bitcast.9), calls=%async_computation.3 | async-start | bytes 3145728 | tf_op jit(solution)/shard_map/all_to_all | solution.py:285
  181.3 6.2 %collective-permute-start.13 = (bf16[256,128]{1,0:T(8,128)(2,1)S(1)}, bf16[256,128]{1,0:T(8,128)(2,1)S(1)}, u32[]{:S(2)}, u32[]{:S(2)}) collective-permute-start(bf16[256,128]{1,0:T(8,128)(2,1)S(1)} %get-tuple-element.37), channel_id=1, source_target_pairs={{0,2},{2,4},{4,6},{6,0},{1,3},{3,5},{5,7},{7,1},{8,10},{10,12},{12... | collective-permute-start | bytes 196616 | tf_op jit(solution)/shard_map/ppermute | solution.py:295
  183.1 5.8 %collective-permute-start.14 = (bf16[256,128]{1,0:T(8,128)(2,1)S(1)}, bf16[256,128]{1,0:T(8,128)(2,1)S(1)}, u32[]{:S(2)}, u32[]{:S(2)}) collective-permute-start(bf16[256,128]{1,0:T(8,128)(2,1)S(1)} %get-tuple-element.38), channel_id=1, source_target_pairs={{0,4},{2,6},{4,0},{6,2},{1,5},{3,7},{5,1},{7,3},{8,12},{10,14},{12... | collective-permute-start | bytes 196616 | tf_op jit(solution)/shard_map/ppermute | solution.py:295
  185.4 4.3 %collective-permute-start.15 = (bf16[256,128]{1,0:T(8,128)(2,1)S(1)}, bf16[256,128]{1,0:T(8,128)(2,1)S(1)}, u32[]{:S(2)}, u32[]{:S(2)}) collective-permute-start(bf16[256,128]{1,0:T(8,128)(2,1)S(1)} %get-tuple-element.39), channel_id=1, source_target_pairs={{0,6},{2,0},{4,2},{6,4},{1,7},{3,1},{5,3},{7,5},{8,14},{10,8},{12,... | collective-permute-start | bytes 196616 | tf_op jit(solution)/shard_map/ppermute | solution.py:295
  189.7 5.3 %collective-permute-start.16 = (bf16[256,128]{1,0:T(8,128)(2,1)S(1)}, bf16[256,128]{1,0:T(8,128)(2,1)S(1)}, u32[]{:S(2)}, u32[]{:S(2)}) collective-permute-start(bf16[256,128]{1,0:T(8,128)(2,1)S(1)} %sum_x.1.refs_0_), channel_id=1, source_target_pairs={{0,6},{2,0},{4,2},{6,4},{1,7},{3,1},{5,3},{7,5},{8,14},{10,8},{12,... | collective-permute-start | bytes 196616 | tf_op jit(solution)/shard_map/ppermute | solution.py:302
  192.4 5.9 %collective-permute-start.17 = (bf16[256,128]{1,0:T(8,128)(2,1)S(1)}, bf16[256,128]{1,0:T(8,128)(2,1)S(1)}, u32[]{:S(2)}, u32[]{:S(2)}) collective-permute-start(bf16[256,128]{1,0:T(8,128)(2,1)S(1)} %sum_x.1.refs_0_), channel_id=1, source_target_pairs={{0,4},{2,6},{4,0},{6,2},{1,5},{3,7},{5,1},{7,3},{8,12},{10,14},{12... | collective-permute-start | bytes 196616 | tf_op jit(solution)/shard_map/ppermute | solution.py:302
  192.7 6.2 %collective-permute-start.18 = (bf16[256,128]{1,0:T(8,128)(2,1)S(1)}, bf16[256,128]{1,0:T(8,128)(2,1)S(1)}, u32[]{:S(2)}, u32[]{:S(2)}) collective-permute-start(bf16[256,128]{1,0:T(8,128)(2,1)S(1)} %sum_x.1.refs_0_), channel_id=1, source_target_pairs={{0,2},{2,4},{4,6},{6,0},{1,3},{3,5},{5,7},{7,1},{8,10},{10,12},{12... | collective-permute-start | bytes 196616 | tf_op jit(solution)/shard_map/ppermute | solution.py:302
  198.9 1.6 collective-permute-start.19

commit v4 on v3

--- a/solution.py
+++ b/solution.py
@@ -1,3 +1,4 @@
+import functools
 import math
 
 import jax
@@ -23,7 +24,7 @@
 LANES = WIDTH // RING
 
 
-def vmem_call(kernel, outs, name, scratch=(), flops=0, moved=1 << 20, limit=16 << 20):
+def vmem_call(kernel, outs, name, scratch=(), flops=0, moved=1 << 20, limit=16 << 20, aliases={}):
     vmem = pl.BlockSpec(memory_space=pltpu.VMEM)
 
     def call(*args):
@@ -33,6 +34,7 @@
             in_specs=[vmem] * len(args),
             out_specs=jax.tree.map(lambda _: vmem, outs),
             scratch_shapes=scratch,
+            input_output_aliases=aliases,
             compiler_params=pltpu.CompilerParams(vmem_limit_bytes=limit),
             cost_estimate=pl.CostEstimate(flops=flops, bytes_accessed=moved, transcendentals=0),
             name=name,
@@ -45,7 +47,7 @@
     return jax.ShapeDtypeStruct(shape, jnp.bfloat16)
 
 
-def build_kernel(coords, counts, values, dense):
+def build_kernel(coords, counts, values, near, far, dense, sems):
     rows, cols = dense.shape
     per_owner = OWN // SIDE
     me_core = lax.axis_index("core")
@@ -67,8 +69,8 @@
             block_row = jnp.where(live, coords[0, 0, 0, slot], 0)
             block_col = jnp.where(live, coords[0, 0, 1, slot], 0)
             owner = block_row // per_owner
-            far = (owner + me_core) & 1
-            at_row = (far * PEERS + (owner >> 1)) * per_owner + block_row % per_owner
+            half = (owner + me_core) & 1
+            at_row = (half * PEERS + (owner >> 1)) * per_owner + block_row % per_owner
             odd = (block_col & 1) == 1
             plain = pairs[k]
             turned = pltpu.roll(plain, SIDE, 1)
@@ -83,14 +85,25 @@
             ]
             place[...] = jnp.where(mask, block, place[...])
 
+    copies = [
+        pltpu.make_async_copy(dense.at[pl.ds(0, ROWS)], near, sems.at[0]),
+        pltpu.make_async_copy(dense.at[pl.ds(ROWS, ROWS)], far, sems.at[1]),
+    ]
+    for copy in copies:
+        copy.start()
+    for copy in copies:
+        copy.wait()
+
 
 def build(coords, counts, values):
+    anywhere = pl.BlockSpec(memory_space=pltpu.HBM)
     return pl.pallas_call(
         build_kernel,
-        out_shape=bf16(2 * ROWS, ROWS),
+        out_shape=(bf16(ROWS, ROWS),) * 2,
         in_specs=[pl.BlockSpec(memory_space=pltpu.SMEM)] * 2 + [pl.BlockSpec(memory_space=pltpu.VMEM)],
-        out_specs=pl.BlockSpec(memory_space=pltpu.VMEM),
-        compiler_params=pltpu.CompilerParams(vmem_limit_bytes=16 << 20),
+        out_specs=(anywhere,) * 2,
+        scratch_shapes=[pltpu.VMEM((2 * ROWS, ROWS), jnp.bfloat16), pltpu.SemaphoreType.DMA((2,))],
+        compiler_params=pltpu.CompilerParams(vmem_limit_bytes=24 << 20),
         cost_estimate=pl.CostEstimate(flops=0, bytes_accessed=30 << 20, transcendentals=0),
         name="build",
     )(coords, counts, values)
@@ -100,79 +113,51 @@
     return lax.dot_general(a, b, (((0,), (0,)), ((), ())), preferred_element_type=jnp.float32)
 
 
-def down_kernel(dense, panel, out):
-    out[...] = jnp.dot(dense[...], panel[...], preferred_element_type=jnp.float32).astype(out.dtype)
-
-
-def down_add_kernel(dense, panel, other, *rest):
+def down_kernel(first, count, tile, panel, out):
+    for r in range(0, count, STEP):
+        rows = slice(first + r, first + r + STEP)
+        out[r : r + STEP] = jnp.dot(tile[rows], panel[...], preferred_element_type=jnp.float32).astype(out.dtype)
+
+
+def down_add_kernel(first, count, tile, panel, other, *rest):
     out = rest[-1]
-    own = jnp.dot(dense[...], panel[...], preferred_element_type=jnp.float32)
-    out[...] = (own + other[...].astype(jnp.float32)).astype(out.dtype)
-
-
-def up_kernel(dense, rows, out):
-    out[...] = over_rows(dense[...], rows[...]).astype(out.dtype)
-
-
-def up_add_kernel(dense, rows, other, out):
-    out[...] = (over_rows(dense[...], rows[...]) + other[...]).astype(out.dtype)
-
-
-def product(kernel, name, steps, dense_spec, extra_specs, out_spec, out_shape, *args, aliases={}):
-    return pl.pallas_call(
-        kernel,
-        grid=(steps,),
-        out_shape=out_shape,
-        in_specs=[dense_spec, pl.BlockSpec((ROWS, WIDTH), lambda r: (0, 0))] + extra_specs,
-        out_specs=out_spec,
-        input_output_aliases=aliases,
-        compiler_params=pltpu.CompilerParams(vmem_limit_bytes=56 << 20),
-        cost_estimate=pl.CostEstimate(
-            flops=2 * STEP * steps * ROWS * WIDTH, bytes_accessed=8 << 20, transcendentals=0
-        ),
-        name=name,
-    )(*args)
-
-
-def strip(first=0):
-    return pl.BlockSpec((STEP, WIDTH), lambda r: (first + r, 0))
-
-
-def down_both(dense, panel):
-    all_steps = ROWS // STEP
-    runs = ((0, all_steps // 2), (all_steps // 2, all_steps - all_steps // 2))
-
-    def tile(first):
-        return pl.BlockSpec((STEP, ROWS), lambda r: (first + r, 0))
-
+    for r in range(0, count, STEP):
+        rows = slice(first + r, first + r + STEP)
+        own = jnp.dot(tile[rows], panel[...], preferred_element_type=jnp.float32)
+        out[rows] = (own + other[r : r + STEP].astype(jnp.float32)).astype(out.dtype)
+
+
+def up_kernel(tile, rows, out):
+    for r in range(0, ROWS, STEP):
+        out[r : r + STEP] = over_rows(tile[:, r : r + STEP], rows[...])
+
+
+def up_add_kernel(tile, rows, other, out):
+    for r in range(0, ROWS, STEP):
+        total = over_rows(tile[:, r : r + STEP], rows[...]) + other[r : r + STEP]
+        out[r : r + STEP] = total.astype(out.dtype)
+
+
+def down_both(near, far, panel):
+    count = ROWS // 2
+    work = 2 * count * ROWS * WIDTH
     others = []
-    for n, (first, steps) in enumerate(runs):
-        far = product(
-            down_kernel, f"down_far_{n}", steps, tile(all_steps + first), [], strip(),
-            bf16(steps * STEP, WIDTH), dense, panel,
-        )
-        others.append(trade(far, "core"))
+    for n in range(2):
+        kernel = functools.partial(down_kernel, n * count, count)
+        others.append(trade(vmem_call(kernel, bf16(count, WIDTH), f"down_far_{n}", flops=work)(far, panel), "core"))
     out = []
-    for n, (first, steps) in enumerate(runs):
-        out = product(
-            down_add_kernel, f"down_near_{n}", steps, tile(first),
-            [strip()] + [pl.BlockSpec(memory_space=pl.ANY)] * (n > 0), strip(first),
-            bf16(ROWS, WIDTH), dense, panel, others[n], *([out] if n else []),
-            aliases={3: 0} if n else {},
-        )
+    for n in range(2):
+        kernel = functools.partial(down_add_kernel, n * count, count)
+        out = vmem_call(
+            kernel, bf16(ROWS, WIDTH), f"down_near_{n}", flops=work, aliases={3: 0} if n else {}
+        )(near, panel, others[n], *([out] if n else []))
     return out
 
 
-def up_both(dense, mine, theirs):
-    def tile(half):
-        return pl.BlockSpec((ROWS, STEP), lambda r: (half, r))
-
-    steps = ROWS // STEP
-    near = product(
-        up_kernel, "up_near", steps, tile(0), [], strip(),
-        jax.ShapeDtypeStruct((ROWS, WIDTH), jnp.float32), dense, mine,
-    )
-    return product(up_add_kernel, "up_far", steps, tile(1), [strip()], strip(), bf16(ROWS, WIDTH), dense, theirs, near)
+def up_both(near, far, mine, theirs):
+    work = 2 * ROWS * ROWS * WIDTH
+    own = vmem_call(up_kernel, jax.ShapeDtypeStruct((ROWS, WIDTH), jnp.float32), "up_near", flops=work)(near, mine)
+    return vmem_call(up_add_kernel, bf16(ROWS, WIDTH), "up_far", flops=work)(far, theirs, own)
 
 
 def middle_kernel(parts, out_grad, weight, activations, send, wgrad_near, wgrad_far, local):
@@ -260,27 +245,6 @@
                 out[rows, cols] = value * jnp.float32(scale)
 
 
-def spread_kernel(array, out, sems):
-    copies = [pltpu.make_async_copy(array, out.at[k], sems.at[k]) for k in range(PEERS)]
-    for copy in copies:
-        copy.start()
-    for copy in copies:
-        copy.wait()
-
-
-def spread(array):
-    anywhere = pl.BlockSpec(memory_space=pl.ANY)
-    return pl.pallas_call(
-        spread_kernel,
-        out_shape=jax.ShapeDtypeStruct((PEERS,) + array.shape, array.dtype),
-        in_specs=[anywhere],
-        out_specs=anywhere,
-        scratch_shapes=[pltpu.SemaphoreType.DMA((PEERS,))],
-        cost_estimate=pl.CostEstimate(flops=0, bytes_accessed=2 << 20, transcendentals=0),
-        name="spread",
-    )(array)
-
-
 def exchange(parts, axes):
     return lax.all_to_all(parts, axes, 0, 0)
 
@@ -304,10 +268,10 @@
 
 
 def per_device(features, out_grad, weight, block_values, block_coords, block_counts):
-    panel = exchange(spread(features), ROW).reshape(ROWS, WIDTH)
-    dense = build(block_coords, block_counts, block_values)
-
-    parts = exchange(down_both(dense, panel).reshape(PEERS, OWN, WIDTH), CHIP)
+    panel = exchange(jnp.broadcast_to(features[None], (PEERS, OWN, WIDTH)), ROW).reshape(ROWS, WIDTH)
+    near, far = build(block_coords, block_counts, block_values)
+
+    parts = exchange(down_both(near, far, panel).reshape(PEERS, OWN, WIDTH), CHIP)
 
     half = bf16(WIDTH // 2, WIDTH)
     activations, send, wgrad_near, wgrad_far = vmem_call(
@@ -330,7 +294,7 @@
     summed, mine = lax.optimization_barrier((summed, mine))
     pieces = gather_ring(summed, "z")
     theirs = trade(mine, "core")
-    partial_grad = up_both(dense, mine, theirs)
+    partial_grad = up_both(near, far, mine, theirs)
     partial_grad, *pieces = lax.optimization_barrier((partial_grad, *pieces))
     received = exchange(partial_grad.reshape(PEERS, OWN, WIDTH), ROW)
 

time: 204 us -> 140 us (0.69)
  Pallas kernels: 90.2 us -> 18.2 us
  local copies, waits for them, and re-layouts: 6.61 us -> 15.3 us
    pallas_call x8 -> x1, Pallas kernels: 86.8 us -> 2.8 us  [build(): pl.pallas_call(build_kernel, out_shape=(bf16(ROWS, ROWS),) * 2, in_specs=...]
    pallas_call x8 -> x14, Pallas kernels: 3.43 us -> 15.4 us  [call(): pl.pallas_call(kernel, out_shape=outs, in_specs=[vmem] * len(args), out_s...]
    unnamed x18 -> x20, local copies, waits for them, and re-layouts: 6.61 us -> 13.1 us
    broadcast_in_dim x0 -> x1, local copies, waits for them, and re-layouts: none -> 2.21 us  [per_device(): jnp.broadcast_to(features[None], (PEERS, OWN, WIDTH))]
  transfers between devices with their start and end apart: 23 -> 23, of which waited for: 15 -> 18; matrix products, arithmetic and copies ran while one was open for 0% -> 0% of each run, Pallas kernels for 15% -> 10%
where the time goes in v4:
time: 140 us; the launch traced here: 139 us
  starting transfers between devices  38.2 us (27%)
  waiting for transfers between devices  35.2 us (25%)
  blocking collectives  29.9 us (21%)
  Pallas kernels  18.2 us (13%)
  local copies, waits for them, and re-layouts  15.3 us (11%)
  between operations  1.49 us (1%)
    all_to_all x1, blocking collectives, exchange(): return lax.all_to_all(parts, axes, 0, 0)  29.9 us
    pallas_call x14, Pallas kernels, call(): pl.pallas_call(kernel, out_shape=outs, in_specs=[vmem] * len(args), out_s...  15.4 us
    all_to_all x3, starting transfers between devices, exchange(): return lax.all_to_all(parts, axes, 0, 0)  13.7 us
    ppermute x8, waiting for transfers between devices, trade(): lax.ppermute(array, axes, [(i, i ^ bits) for i in range(lax.axis_size(axe...  13.3 us
    unnamed x20, local copies, waits for them, and re-layouts  13.1 us
    all_to_all x3, waiting for transfers between devices, exchange(): return lax.all_to_all(parts, axes, 0, 0)  11.9 us
    ppermute x6, starting transfers between devices, scatter_ring(): lax.ppermute(pieces[k], axis, [(i, (i + k) % RING) for i in range(RING)])  9.82 us
    ppermute x6, starting transfers between devices, gather_ring(): lax.ppermute(piece, axis, [(i, (i - k) % RING) for i in range(RING)])  8.98 us
  transfers between devices with their start and end apart: 23, of which 18 were waited for; matrix products, arithmetic and copies ran while one was open for 0% of the time, Pallas kernels for 10%

profile of v4, /device:TPU:0, one launch (start us, length us, event | category | flops | bytes accessed | tf_op | source)
XLA Modules:
  0.0 139.2 jit_solution(3755191209288133845)
XLA Ops:
  0.6 2.2 %broadcast_in_dim.2 = bf16[8,192,512]{2,1,0:T(8,128)(2,1)} broadcast(bf16[192,512]{1,0:T(8,128)(2,1)} %param.6), dimensions={1,2} | broadcast | bytes 1769472 | tf_op jit(solution)/shard_map/broadcast_in_dim | solution.py:271
  2.8 6.5 %all-to-all-start = ((bf16[8,192,512]{2,1,0:T(8,128)(2,1)}), bf16[8,192,512]{2,1,0:T(8,128)(2,1)S(1)}, u32[]{:S(2)}, u32[]{:S(2)}) async-start(bf16[8,192,512]{2,1,0:T(8,128)(2,1)} %broadcast_in_dim.2), calls=%async_computation | async-start | bytes 3145728 | tf_op jit(solution)/shard_map/all_to_all | solution.py:249
  10.1 1.7 %copy-done.6 = bf16[1,1,288,4096]{3,2,1,0:T(8,128)(2,1)S(1)} copy-done((bf16[1,1,288,4096]{3,2,1,0:T(8,128)(2,1)S(1)}, bf16[1,1,288,4096]{3,2,1,0:T(8,128)(2,1)}, u32[]{:S(2)}) %copy-start.6) | copy-done | bytes 2359320
  11.7 2.8 %build.1 = (bf16[1536,1536]{1,0:T(8,128)(2,1)S(1)}, bf16[1536,1536]{1,0:T(8,128)(2,1)S(1)}) custom-call(s32[1,1,2,288]{3,2,1,0:T(2,128)S(1)} %copy-done.9, s32[1,1]{1,0:T(1,128)S(6)} %copy.11.counts, bf16[1,1,288,4096]{3,2,1,0:T(8,128)(2,1)S(1)} %copy-done.6), custom_call_target="tpu_custom_call" | custom-call | bytes 31457280 | tf_op jit(solution)/shard_map/build/pallas_call | solution.py:100
  14.5 2.1 %copy-done = bf16[1536,1536]{1,0:T(8,128)(2,1)} copy-done((bf16[1536,1536]{1,0:T(8,128)(2,1)}, bf16[1536,1536]{1,0:T(8,128)(2,1)S(1)}, u32[]{:S(2)}) %copy-start) | copy-done | bytes 4718616
  16.7 2.2 %copy-done.3 = bf16[1536,1536]{1,0:T(8,128)(2,1)} copy-done((bf16[1536,1536]{1,0:T(8,128)(2,1)}, bf16[1536,1536]{1,0:T(8,128)(2,1)S(1)}, u32[]{:S(2)}) %copy-start.3) | copy-done | bytes 4718616
  18.8 11.0 %all-to-all-done = bf16[8,192,512]{2,1,0:T(8,128)(2,1)S(1)} async-done(((bf16[8,192,512]{2,1,0:T(8,128)(2,1)}), bf16[8,192,512]{2,1,0:T(8,128)(2,1)S(1)}, u32[]{:S(2)}, u32[]{:S(2)}) %all-to-all-start) | async-done | bytes 1572896 | tf_op jit(solution)/shard_map/all_to_all | solution.py:249
  29.8 2.3 %copy-done.4 = bf16[1536,1536]{1,0:T(8,128)(2,1)S(1)} copy-done((bf16[1536,1536]{1,0:T(8,128)(2,1)S(1)}, bf16[1536,1536]{1,0:T(8,128)(2,1)}, u32[]{:S(2)}) %copy-start.4) | copy-done | bytes 4718616
  36.0 1.4 down_near_0.1.rest_0_
  37.5 1.4 down_near_1.1
  38.9 29.9 %all_to_all.20.parts = bf16[8,192,512]{2,1,0:T(8,128)(2,1)S(1)} all-to-all(bf16[8,192,512]{2,1,0:T(8,128)(2,1)S(1)} %bitcast.10), channel_id=1, replica_groups=mesh['y_lo'=2,'z'=4,'y_hi'=2,'x'=4,'core'=2] {'y_hi','x'}, dimensions={0} | all-to-all | bytes 3145728 | tf_op jit(solution)/shard_map/all_to_all | solution.py:249
  68.8 2.1 %middle.1 = (bf16[192,512]{1,0:T(8,128)(2,1)}, bf16[8,192,512]{2,1,0:T(8,128)(2,1)}, bf16[256,512]{1,0:T(8,128)(2,1)S(1)}, bf16[256,512]{1,0:T(8,128)(2,1)S(1)}) custom-call(bf16[8,192,512]{2,1,0:T(8,128)(2,1)S(1)} %all_to_all.20.parts, bf16[192,512]{1,0:T(8,128)(2,1)S(1)} %copy-done.8, bf16[512,512]{1,0:T(8,128)(2,1)S(1)} %copy-done.7), custom_call_target="tpu_custom_call" | custom-call | flops 301989888 | bytes 1048576 | tf_op jit(solution)/shard_map/middle/pallas_call | solution.py:31
  70.9 3.6 %all-to-all-start.2 = ((bf16[8,192,512]{2,1,0:T(8,128)(2,1)}), bf16[8,192,512]{2,1,0:T(8,128)(2,1)S(1)}, u32[]{:S(2)}, u32[]{:S(2)}) async-start(bf16[8,192,512]{2,1,0:T(8,128)(2,1)} %get-tuple-element.33), calls=%async_computation.2 | async-start | bytes 3145728 | tf_op jit(solution)/shard_map/all_to_all | solution.py:249
  74.6 1.5 %collective-permute-done.2.other = bf16[256,512]{1,0:T(8,128)(2,1)S(1)} collective-permute-done((bf16[256,512]{1,0:T(8,128)(2,1)S(1)}, bf16[256,512]{1,0:T(8,128)(2,1)S(1)}, u32[]{:S(2)}, u32[]{:S(2)}) %collective-permute-start.2) | collective-permute-done | bytes 262176 | tf_op jit(solution)/shard_map/ppermute | solution.py:253
  77.1 2.5 %collective-permute-start.4 = (bf16[64,512]{1,0:T(8,128)(2,1)S(1)}, bf16[64,512]{1,0:T(8,128)(2,1)S(1)}, u32[]{:S(2)}, u32[]{:S(2)}) collective-permute-start(bf16[64,512]{1,0:T(8,128)(2,1)S(1)} %get-tuple-element.31), channel_id=1, source_target_pairs={{0,32},{16,48},{32,0},{48,16},{1,33},{17,49},{33,1},{49,17},{2,34}... | collective-permute-start | bytes 196616 | tf_op jit(solution)/shard_map/ppermute | solution.py:259
  80.7 1.7 %collective-permute-done.3.refs_1_ = bf16[64,512]{1,0:T(8,128)(2,1)S(1)} collective-permute-done((bf16[64,512]{1,0:T(8,128)(2,1)S(1)}, bf16[64,512]{1,0:T(8,128)(2,1)S(1)}, u32[]{:S(2)}, u32[]{:S(2)}) %collective-permute-start.3) | collective-permute-done | bytes 65568 | tf_op jit(solution)/shard_map/ppermute | solution.py:259
  83.9 3.1 %collective-permute-start.8 = (bf16[64,512]{1,0:T(8,128)(2,1)S(1)}, bf16[64,512]{1,0:T(8,128)(2,1)S(1)}, u32[]{:S(2)}, u32[]{:S(2)}) collective-permute-start(bf16[64,512]{1,0:T(8,128)(2,1)S(1)} %sum_z.1.a), channel_id=1, source_target_pairs={{0,72},{8,64},{64,8},{72,0},{1,73},{9,65},{65,9},{73,1},{2,74},{10... | collective-permute-start | bytes 196616 | tf_op jit(solution)/shard_map/ppermute | solution.py:253
  88.7 6.0 %collective-permute-done.8.d = bf16[64,512]{1,0:T(8,128)(2,1)S(1)} collective-permute-done((bf16[64,512]{1,0:T(8,128)(2,1)S(1)}, bf16[64,512]{1,0:T(8,128)(2,1)S(1)}, u32[]{:S(2)}, u32[]{:S(2)}) %collective-permute-start.8) | collective-permute-done | bytes 65568 | tf_op jit(solution)/shard_map/ppermute | solution.py:253
  95.7 2.8 %collective-permute-done.6.b = bf16[64,512]{1,0:T(8,128)(2,1)S(1)} collective-permute-done((bf16[64,512]{1,0:T(8,128)(2,1)S(1)}, bf16[64,512]{1,0:T(8,128)(2,1)S(1)}, u32[]{:S(2)}, u32[]{:S(2)}) %collective-permute-start.6) | collective-permute-done | bytes 65568 | tf_op jit(solution)/shard_map/ppermute | solution.py:253
  99.6 2.5 %collective-permute-start.11 = (bf16[64,512]{1,0:T(8,128)(2,1)S(1)}, bf16[64,512]{1,0:T(8,128)(2,1)S(1)}, u32[]{:S(2)}, u32[]{:S(2)}) collective-permute-start(bf16[64,512]{1,0:T(8,128)(2,1)S(1)} %sum_y.1.refs_0_), channel_id=1, source_target_pairs={{0,32},{16,48},{32,0},{48,16},{1,33},{17,49},{33,1},{49,17},{2,34}... | collective-permute-start | bytes 196616 | tf_op jit(solution)/shard_map/ppermute | solution.py:266
  103.2 2.3 %copy-done.2 = bf16[1536,1536]{1,0:T(8,128)(2,1)S(1)} copy-done((bf16[1536,1536]{1,0:T(8,128)(2,1)S(1)}, bf16[1536,1536]{1,0:T(8,128)(2,1)}, u32[]{:S(2)}) %copy-start.2) | copy-done | bytes 4718616
  105.5 2.6 %up_near.1.other = f32[1536,512]{1,0:T(8,128)S(1)} custom-call(bf16[1536,1536]{1,0:T(8,128)(2,1)S(1)} %copy-done.2, bf16[1536,512]{1,0:T(8,128)(2,1)S(1)} %bitcast.12), custom_call_target="tpu_custom_call" | custom-call | flops 2415919104 | bytes 1048576 | tf_op jit(solution)/shard_map/up_near/pallas_call | solution.py:31
  108.2 2.3 %copy-done.5 = bf16[1536,1536]{1,0:T(8,128)(2,1)S(1)} copy-done((bf16[1536,1536]{1,0:T(8,128)(2,1)S(1)}, bf16[1536,1536]{1,0:T(8,128)(2,1)}, u32[]{:S(2)}) %copy-start.5) | copy-done | bytes 4718616
  110.5 3.8 %up_far.1 = bf16[1536,512]{1,0:T(8,128)(2,1)} custom-call(bf16[1536,1536]{1,0:T(8,128)(2,1)S(1)} %copy-done.5, bf16[1536,512]{1,0:T(8,128)(2,1)S(1)} %collective-permute-done.9.rows, f32[1536,512]{1,0:T(8,128)S(1)} %up_near.1.other), custom_call_target="tpu_custom_call" | custom-call | flops 2415919104 | bytes 1048576 | tf_op jit(solution)/shard_map/up_far/pallas_call | solution.py:31
  114.3 3.6 %all-to-all-start.3 = ((bf16[8,192,512]{2,1,0:T(8,128)(2,1)}), bf16[8,192,512]{2,1,0:T(8,128)(2,1)S(1)}, u32[]{:S(2)}, u32[]{:S(2)}) async-start(bf16[8,192,512]{2,1,0:T(8,128)(2,1)} %bitcast.3), calls=%async_computation.3 | async-start | bytes 3145728 | tf_op jit(solution)/shard_map/all_to_all | solution.py:249
  118.0 2.0 %collective-permute-start.13 = (bf16[256,128]{1,0:T(8,128)(2,1)S(1)}, bf16[256,128]{1,0:T(8,128)(2,1)S(1)}, u32[]{:S(2)}, u32[]{:S(2)}) collective-permute-start(bf16[256,128]{1,0:T(8,128)(2,1)S(1)} %get-tuple-element.41), channel_id=1, source_target_pairs={{0,2},{2,4},{4,6},{6,0},{1,3},{3,5},{5,7},{7,1},{8,10},{10,12},{12... | collective-permute-start | bytes 196616 | tf_op jit(solution)/shard_map/ppermute | solution.py:259
  120.0 1.8 %collective-permute-start.14 = (bf16[256,128]{1,0:T(8,128)(2,1)S(1)}, bf16[256,128]{1,0:T(8,128)(2,1)S(1)}, u32[]{:S(2)}, u32[]{:S(2)}) collective-permute-start(bf16[256,128]{1,0:T(8,128)(2,1)S(1)} %get-tuple-element.42), channel_id=1, source_target_pairs={{0,4},{2,6},{4,0},{6,2},{1,5},{3,7},{5,1},{7,3},{8,12},{10,14},{12... | collective-permute-start | bytes 196616 | tf_op jit(solution)/shard_map/ppermute | solution.py:259
  121.8 1.5 %collective-permute-start.15 = (bf16[256,128]{1,0:T(8,128)(2,1)S(1)}, bf16[256,128]{1,0:T(8,128)(2,1)S(1)}, u32[]{:S(2)}, u32[]{:S(2)}) collective-permute-start(bf16[256,128]{1,0:T(8,128)(2,1)S(1)} %get-tuple-element.43), channel_id=1, source_target_pairs={{0,6},{2,0},{4,2},{6,4},{1,7},{3,1},{5,3},{7,5},{8,14},{10,8},{12,... | collective-permute-start | bytes 196616 | tf_op jit(solution)/shard_map/ppermute | solution.py:259
  123.7 2.1 %collective-permute-done.14.refs_2_ = bf16[256,128]{1,0:T(8,128)(2,1)S(1)} collective-permute-done((bf16[256,128]{1,0:T(8,128)(2,1)S(1)}, bf16[256,128]{1,0:T(8,128)(2,1)S(1)}, u32[]{:S(2)}, u32[]{:S(2)}) %collective-permute-start.14) | collective-permute-done | bytes 65568 | tf_op jit(solution)/shard_map/ppermute | solution.py:259
  127.2 3.1 %collective-permute-start.17 = (bf16[256,128]{1,0:T(8,128)(2,1)S(1)}, bf16[256,128]{1,0:T(8,128)(2,1)S(1)}, u32[]{:S(2)}, u32[]{:S(2)}) collective-permute-start(bf16[256,128]{1,0:T(8,128)(2,1)S(1)} %sum_x.1.refs_0_), channel_id=1, source_target_pairs={{0,4},{2,6},{4,0},{6,2},{1,5},{3,7},{5,1},{7,3},{8,12},{10,14},{12... | collective-permute-start | bytes 196616 | tf_op jit(solution)/shard_map/ppermute | solution.py:266
  131.7 1.6 %collective-permute-done.17.refs_2_ = bf16[256,128]{1,0:T(8,128)(2,1)S(1)} collective-permute-done((bf16[256,128]{1,0:T(8,128)(2,1)S(1)}, bf16[256,128]{1,0:T(8,128)(2,1)S(1)}, u32[]{:S(2)}, u32[]{:S(2)}) %collective-permute-start.17) | collective-permute-done | bytes 65568 | tf_op jit(solution)/shard_map/ppermute | solution.py:266
  134.7 1.5 %collective-permute-done.19.theirs = bf16[256,512]{1,0:T(8,128)(2,1)S(1)} collective-permute-done((bf16[256,512]{1,0:T(8,128)(2,1)S(1)}, bf16[256,512]{1,0:T(8,128)(2,1)S(1)}, u32[]{:S(2)}, u32[]{:S(2)}) %collective-permute-start.19) | collective-permute-done | bytes 262176 | tf_op jit(solution)/shard_map/ppermute | solution.py:253
  (52 shorter events, 20.0 us)
Async XLA Ops:
  2.8 7.2 %copy-start.9 = (s32[1,1,2,288]{3,2,1,0:T(2,128)S(1)}, s32[1,1,2,288]{3,2,1,0:T(2,128)}, u32[]{:S(2)}) copy-start(s32[1,1,2,288]{3,2,1,0:T(2,128)} %coords.1) | copy-start | bytes 6916
  2.8 27.0 %all-to-all-start = ((bf16[8,192,512]{2,1,0:T(8,128)(2,1)}), bf16[8,192,512]{2,1,0:T(8,128)(2,1)S(1)}, u32[]{:S(2)}, u32[]{:S(2)}) async-start(bf16[8,192,512]{2,1,0:T(8,128)(2,1)} %broadcast_in_dim.2), calls=%async_computation | async-start | bytes 3145728 | tf_op jit(solution)/shard_map/all_to_all | solution.py:249
  14.5 2.1 %copy-start = (bf16[1536,1536]{1,0:T(8,128)(2,1)}, bf16[1536,1536]{1,0:T(8,128)(2,1)S(1)}, u32[]{:S(2)}) copy-start(bf16[1536,1536]{1,0:T(8,128)(2,1)S(1)} %get-tuple-element.24.tile) | copy-start | bytes 14155780
  16.7 2.2 %copy-start.3 = (bf16[1536,1536]{1,0:T(8,128)(2,1)}, bf16[1536,1536]{1,0:T(8,128)(2,1)S(1)}, u32[]{:S(2)}) copy-start(bf16[1536,1536]{1,0:T(8,128)(2,1)S(1)} %get-tuple-element.25.tile) | copy-start | bytes 14155780
  29.8 2.3 %copy-start.4 = (bf16[1536,1536]{1,0:T(8,128)(2,1)S(1)}, bf16[1536,1536]{1,0:T(8,128)(2,1)}, u32[]{:S(2)}) copy-start(bf16[1536,1536]{1,0:T(8,128)(2,1)} %copy-done.3) | copy-start | bytes 14155780
  33.5 2.4 %collective-permute-start.1 = (bf16[768,512]{1,0:T(8,128)(2,1)S(1)}, bf16[768,512]{1,0:T(8,128)(2,1)S(1)}, u32[]{:S(2)}, u32[]{:S(2)}) collective-permute-start(bf16[768,512]{1,0:T(8,128)(2,1)S(1)} %down_far_0.1), channel_id=1, source_target_pairs={{0,1},{1,0},{2,3},{3,2},{4,5},{5,4},{6,7},{7,6},{8,9},{9,8},{10,11... | collective-permute-start | bytes 2359304 | tf_op jit(solution)/shard_map/ppermute | solution.py:253
  33.6 2.3 %copy-start.1 = (bf16[1536,1536]{1,0:T(8,128)(2,1)S(1)}, bf16[1536,1536]{1,0:T(8,128)(2,1)}, u32[]{:S(2)}) copy-start(bf16[1536,1536]{1,0:T(8,128)(2,1)} %copy-done) | copy-start | bytes 14155780
  35.0 2.5 %collective-permute-start = (bf16[768,512]{1,0:T(8,128)(2,1)S(1)}, bf16[768,512]{1,0:T(8,128)(2,1)S(1)}, u32[]{:S(2)}, u32[]{:S(2)}) collective-permute-start(bf16[768,512]{1,0:T(8,128)(2,1)S(1)} %down_far_1.1), channel_id=1, source_target_pairs={{0,1},{1,0},{2,3},{3,2},{4,5},{5,4},{6,7},{7,6},{8,9},{9,8},{10,11... | collective-permute-start | bytes 2359304 | tf_op jit(solution)/shard_map/ppermute | solution.py:253
  38.9 30.0 %copy-start.7 = (bf16[512,512]{1,0:T(8,128)(2,1)S(1)}, bf16[512,512]{1,0:T(8,128)(2,1)}, u32[]{:S(2)}) copy-start(bf16[512,512]{1,0:T(8,128)(2,1)} %weight.1) | copy-start | bytes 1572868
  38.9 29.9 %copy-start.8 = (bf16[192,512]{1,0:T(8,128)(2,1)S(1)}, bf16[192,512]{1,0:T(8,128)(2,1)}, u32[]{:S(2)}) copy-start(bf16[192,512]{1,0:T(8,128)(2,1)} %out_grad.1) | copy-start | bytes 589828
  70.9 27.7 %all-to-all-start.2 = ((bf16[8,192,512]{2,1,0:T(8,128)(2,1)}), bf16[8,192,512]{2,1,0:T(8,128)(2,1)S(1)}, u32[]{:S(2)}, u32[]{:S(2)}) async-start(bf16[8,192,512]{2,1,0:T(8,128)(2,1)} %get-tuple-element.33), calls=%async_computation.2 | async-start | bytes 3145728 | tf_op jit(solution)/shard_map/all_to_all | solution.py:249
  74.5 1.6 %collective-permute-start.2 = (bf16[256,512]{1,0:T(8,128)(2,1)S(1)}, bf16[256,512]{1,0:T(8,128)(2,1)S(1)}, u32[]{:S(2)}, u32[]{:S(2)}) collective-permute-start(bf16[256,512]{1,0:T(8,128)(2,1)S(1)} %get-tuple-element.28), channel_id=1, source_target_pairs={{0,1},{1,0},{2,3},{3,2},{4,5},{5,4},{6,7},{7,6},{8,9},{9,8},{10,11... | collective-permute-start | bytes 786440 | tf_op jit(solution)/shard_map/ppermute | solution.py:253
  76.2 6.2 %collective-permute-start.3 = (bf16[64,512]{1,0:T(8,128)(2,1)S(1)}, bf16[64,512]{1,0:T(8,128)(2,1)S(1)}, u32[]{:S(2)}, u32[]{:S(2)}) collective-permute-start(bf16[64,512]{1,0:T(8,128)(2,1)S(1)} %get-tuple-element.30), channel_id=1, source_target_pairs={{0,16},{16,32},{32,48},{48,0},{1,17},{17,33},{33,49},{49,1},{2,18}... | collective-permute-start | bytes 196616 | tf_op jit(solution)/shard_map/ppermute | solution.py:259
  77.1 6.1 %collective-permute-start.4 = (bf16[64,512]{1,0:T(8,128)(2,1)S(1)}, bf16[64,512]{1,0:T(8,128)(2,1)S(1)}, u32[]{:S(2)}, u32[]{:S(2)}) collective-permute-start(bf16[64,512]{1,0:T(8,128)(2,1)S(1)} %get-tuple-element.31), channel_id=1, source_target_pairs={{0,32},{16,48},{32,0},{48,16},{1,33},{17,49},{33,1},{49,17},{2,34}... | collective-permute-start | bytes 196616 | tf_op jit(solution)/shard_map/ppermute | solution.py:259
  79.6 4.3 %collective-permute-start.5 = (bf16[64,512]{1,0:T(8,128)(2,1)S(1)}, bf16[64,512]{1,0:T(8,128)(2,1)S(1)}, u32[]{:S(2)}, u32[]{:S(2)}) collective-permute-start(bf16[64,512]{1,0:T(8,128)(2,1)S(1)} %get-tuple-element.32), channel_id=1, source_target_pairs={{0,48},{16,0},{32,16},{48,32},{1,49},{17,1},{33,17},{49,33},{2,50}... | collective-permute-start | bytes 196616 | tf_op jit(solution)/shard_map/ppermute | solution.py:259
  83.9 10.8 %collective-permute-start.8 = (bf16[64,512]{1,0:T(8,128)(2,1)S(1)}, bf16[64,512]{1,0:T(8,128)(2,1)S(1)}, u32[]{:S(2)}, u32[]{:S(2)}) collective-permute-start(bf16[64,512]{1,0:T(8,128)(2,1)S(1)} %sum_z.1.a), channel_id=1, source_target_pairs={{0,72},{8,64},{64,8},{72,0},{1,73},{9,65},{65,9},{73,1},{2,74},{10... | collective-permute-start | bytes 196616 | tf_op jit(solution)/shard_map/ppermute | solution.py:253
  87.0 8.6 %collective-permute-start.7 = (bf16[64,512]{1,0:T(8,128)(2,1)S(1)}, bf16[64,512]{1,0:T(8,128)(2,1)S(1)}, u32[]{:S(2)}, u32[]{:S(2)}) collective-permute-start(bf16[64,512]{1,0:T(8,128)(2,1)S(1)} %sum_z.1.a), channel_id=1, source_target_pairs={{0,64},{8,72},{64,0},{72,8},{1,65},{9,73},{65,1},{73,9},{2,66},{10... | collective-permute-start | bytes 196616 | tf_op jit(solution)/shard_map/ppermute | solution.py:253
  87.3 11.2 %collective-permute-start.6 = (bf16[64,512]{1,0:T(8,128)(2,1)S(1)}, bf16[64,512]{1,0:T(8,128)(2,1)S(1)}, u32[]{:S(2)}, u32[]{:S(2)}) collective-permute-start(bf16[64,512]{1,0:T(8,128)(2,1)S(1)} %sum_z.1.a), channel_id=1, source_target_pairs={{0,8},{8,0},{64,72},{72,64},{1,9},{9,1},{65,73},{73,65},{2,10},{10... | collective-permute-start | bytes 196616 | tf_op jit(solution)/shard_map/ppermute | solution.py:253
  98.5 9.6 %collective-permute-start.9 = (bf16[1536,512]{1,0:T(8,128)(2,1)S(1)}, bf16[1536,512]{1,0:T(8,128)(2,1)S(1)}, u32[]{:S(2)}, u32[]{:S(2)}) collective-permute-start(bf16[1536,512]{1,0:T(8,128)(2,1)S(1)} %bitcast.11), channel_id=1, source_target_pairs={{0,1},{1,0},{2,3},{3,2},{4,5},{5,4},{6,7},{7,6},{8,9},{9,8},{10,11... | collective-permute-start | bytes 4718600 | tf_op jit(solution)/shard_map/ppermute | solution.py:253
  98.6 15.7 %collective-permute-start.12 = (bf16[64,512]{1,0:T(8,128)(2,1)S(1)}, bf16[64,512]{1,0:T(8,128)(2,1)S(1)}, u32[]{:S(2)}, u32[]{:S(2)}) collective-permute-start(bf16[64,512]{1,0:T(8,128)(2,1)S(1)} %sum_y.1.refs_0_), channel_id=1, source_target_pairs={{0,16},{16,32},{32,48},{48,0},{1,17},{17,33},{33,49},{49,1},{2,18}... | collective-permute-start | bytes 196616 | tf_op jit(solution)/shard_map/ppermute | solution.py:266
  99.6 14.8 %collective-permute-start.11 = (bf16[64,512]{1,0:T(8,128)(2,1)S(1)}, bf16[64,512]{1,0:T(8,128)(2,1)S(1)}, u32[]{:S(2)}, u32[]{:S(2)}) collective-permute-start(bf16[64,512]{1,0:T(8,128)(2,1)S(1)} %sum_y.1.refs_0_), channel_id=1, source_target_pairs={{0,32},{16,48},{32,0},{48,16},{1,33},{17,49},{33,1},{49,17},{2,34}... | collective-permute-start | bytes 196616 | tf_op jit(solution)/shard_map/ppermute | solution.py:266
  102.1 12.3 %collective-permute-start.10 = (bf16[64,512]{1,0:T(8,128)(2,1)S(1)}, bf16[64,512]{1,0:T(8,128)(2,1)S(1)}, u32[]{:S(2)}, u32[]{:S(2)}) collective-permute-start(bf16[64,512]{1,0:T(8,128)(2,1)S(1)} %sum_y.1.refs_0_), channel_id=1, source_target_pairs={{0,48},{16,0},{32,16},{48,32},{1,49},{17,1},{33,17},{49,33},{2,50}... | collective-permute-start | bytes 196616 | tf_op jit(solution)/shard_map/ppermute | solution.py:266
  103.2 2.3 %copy-start.2 = (bf16[1536,1536]{1,0:T(8,128)(2,1)S(1)}, bf16[1536,1536]{1,0:T(8,128)(2,1)}, u32[]{:S(2)}) copy-start(bf16[1536,1536]{1,0:T(8,128)(2,1)} %copy-done) | copy-start | bytes 14155780
  108.2 2.3 %copy-start.5 = (bf16[1536,1536]{1,0:T(8,128)(2,1)S(1)}, bf16[1536,1536]{1,0:T(8,128)(2,1)}, u32[]{:S(2)}) copy-start(bf16[1536,1536]{1,0:T(8,128)(2,1)} %copy-done.3) | copy-start | bytes 14155780
  114.3 24.0 %all-to-all-start.3 = ((bf16[8,192,512]{2,1,0:T(8,128)(2,1)}), bf16[8,192,512]{2,1,0:T(8,128)(2,1)S(1)}, u32[]{:S(2)}, u32[]{:S(2)}) async-start(bf16[8,192,512]{2,1,0:T(8,128)(2,1)} %bitcast.3), calls=%async_computation.3 | async-start | bytes 3145728 | tf_op jit(solution)/shard_map/all_to_all | solution.py:249
  118.0 5.7 %collective-permute-start.13 = (bf16[256,128]{1,0:T(8,128)(2,1)S(1)}, bf16[256,128]{1,0:T(8,128)(2,1)S(1)}, u32[]{:S(2)}, u32[]{:S(2)}) collective-permute-start(bf16[256,128]{1,0:T(8,128)(2,1)S(1)} %get-tuple-element.41), channel_id=1, source_target_pairs={{0,2},{2,4},{4,6},{6,0},{1,3},{3,5},{5,7},{7,1},{8,10},{10,12},{12... | collective-permute-start | bytes 196616 | tf_op jit(solution)/shard_map/ppermute | solution.py:259
  120.0 5.8 %collective-permute-start.14 = (bf16[256,128]{1,0:T(8,128)(2,1)S(1)}, bf16[256,128]{1,0:T(8,128)(2,1)S(1)}, u32[]{:S(2)}, u32[]{:S(2)}) collective-permute-start(bf16[256,128]{1,0:T(8,128)(2,1)S(1)} %get-tuple-element.42), channel_id=1, source_target_pairs={{0,4},{2,6},{4,0},{6,2},{1,5},{3,7},{5,1},{7,3},{8,12},{10,14},{12... | collective-permute-start | bytes 196616 | tf_op jit(solution)/shard_map/ppermute | solution.py:259
  121.8 4.3 %collective-permute-start.15 = (bf16[256,128]{1,0:T(8,128)(2,1)S(1)}, bf16[256,128]{1,0:T(8,128)(2,1)S(1)}, u32[]{:S(2)}, u32[]{:S(2)}) collective-permute-start(bf16[256,128]{1,0:T(8,128)(2,1)S(1)} %get-tuple-element.43), channel_id=1, source_target_pairs={{0,6},{2,0},{4,2},{6,4},{1,7},{3,1},{5,3},{7,5},{8,14},{10,8},{12,... | collective-permute-start | bytes 196616 | tf_op jit(solution)/shard_map/ppermute | solution.py:259
  126.1 5.5 %collective-permute-start.18 = (bf16[256,128]{1,0:T(8,128)(2,1)S(1)}, bf16[256,128]{1,0:T(8,128)(2,1)S(1)}, u32[]{:S(2)}, u32[]{:S(2)}) collective-permute-start(bf16[256,128]{1,0:T(8,128)(2,1)S(1)} %sum_x.1.refs_0_), channel_id=1, source_target_pairs={{0,2},{2,4},{4,6},{6,0},{1,3},{3,5},{5,7},{7,1},{8,10},{10,12},{12... | collective-permute-start | bytes 196616 | tf_op jit(solution)/shard_map/ppermute | solution.py:266
  127.2 6.1 %collective-permute-start.17 = (bf16[256,128]{1,0:T(8,128)(2,1)S(1)}, bf16[256,128]{1,0:T(8,128)(2,1)S(1)}, u32[]{:S(2)}, u32[]{:S(2)}) collective-permute-start(bf16[256,128]{1,0:T(8,128)(2,1)S(1)} %sum_x.1.refs_0_), channel_id=1, source_target_pairs={{0,4},{2,6},{4,0},{6,2},{1,5},{3,7},{5,1},{7,3},{8,12},{10,14},{12... | collective-permute-start | bytes 196616 | tf_op jit(solution)/shard_map/ppermute | solution.py:266
  130.3 4.3 %collective-permute-start.16 = (bf16[256,128]{1,0:T(8,128)(2,1)S(1)}, bf16[256,128]{1,0:T(8,128)(2,1)S(1)}, u32[]{:S(2)}, u32[]{:S(2)}) collective-permute-start(bf16[256,128]{1,0:T(8,128)(2,1)S(1)} %sum_x.1.refs_0_), channel_id=1, source_target_pairs={{0,6},{2,0},{4,2},{6,4},{1,7},{3,1},{5,3},{7,5},{8,14},{10,8},{12,... | collective-permute-start | bytes 196616 | tf_op jit(solution)/shard_map/ppermute | solution.py:266
  134.6 1.6 %collective-permute-start.19 = (bf16[256,512]{1,0:T(8,128)(2,1)S(1)}, bf16[256,512]{1,0:T(8,128)(2,1)S(1)}, u32[]{:S(2)}, u32[]{:S(2)}) collective-permute-start(bf16[256,512]{1,0:T(8,128)(2,1)S(1)} %join.1.mine), channel_id=1, source_target_pairs={{0,1},{1,0},{2,3},{3,2},{4,5},{5,4},{6,7},{7,6},{8,9},{9,8},{10,11... | collective-permute-start | bytes 786440 | tf_op jit(solution)/shard_map/ppermute | solution.py:253
  (1 other events, 1.7 us)

commit v5 on v4

--- a/solution.py
+++ b/solution.py
@@ -47,7 +47,18 @@
     return jax.ShapeDtypeStruct(shape, jnp.bfloat16)
 
 
-def build_kernel(coords, counts, values, near, far, dense, sems):
+def relative(owner, slow, fast):
+    apart = (owner >> 2) ^ lax.axis_index(slow)
+    ahead = ((owner & (RING - 1)) - lax.axis_index(fast)) & (RING - 1)
+    return apart * RING + ahead
+
+
+def absolute(place, slow, fast):
+    apart, ahead = divmod(place, RING)
+    return (lax.axis_index(slow) ^ apart) * RING + ((lax.axis_index(fast) + ahead) & (RING - 1))
+
+
+def build_kernel(coords, counts, values, dense):
     rows, cols = dense.shape
     per_owner = OWN // SIDE
     me_core = lax.axis_index("core")
@@ -70,40 +81,30 @@
             block_col = jnp.where(live, coords[0, 0, 1, slot], 0)
             owner = block_row // per_owner
             half = (owner + me_core) & 1
-            at_row = (half * PEERS + (owner >> 1)) * per_owner + block_row % per_owner
-            odd = (block_col & 1) == 1
+            at_row = (half * PEERS + relative(owner >> 1, *CHIP)) * per_owner + block_row % per_owner
+            at_col = relative(block_col // per_owner, *ROW) * per_owner + block_col % per_owner
+            odd = (at_col & 1) == 1
             plain = pairs[k]
             turned = pltpu.roll(plain, SIDE, 1)
             block = jnp.concatenate(
                 [jnp.where(odd, turned, plain), jnp.where(odd, plain, turned)], axis=0
             ).astype(dense.dtype)
-            first = jnp.where(live, (block_col & 1) * SIDE, 4 * SIDE)
+            first = jnp.where(live, (at_col & 1) * SIDE, 4 * SIDE)
             mask = (lane >= first) & (lane < first + SIDE)
             place = dense.at[
                 pl.ds(pl.multiple_of(at_row * SIDE, SIDE), SIDE),
-                pl.ds(pl.multiple_of((block_col >> 1) * 2 * SIDE, 2 * SIDE), 2 * SIDE),
+                pl.ds(pl.multiple_of((at_col >> 1) * 2 * SIDE, 2 * SIDE), 2 * SIDE),
             ]
             place[...] = jnp.where(mask, block, place[...])
 
-    copies = [
-        pltpu.make_async_copy(dense.at[pl.ds(0, ROWS)], near, sems.at[0]),
-        pltpu.make_async_copy(dense.at[pl.ds(ROWS, ROWS)], far, sems.at[1]),
-    ]
-    for copy in copies:
-        copy.start()
-    for copy in copies:
-        copy.wait()
-
 
 def build(coords, counts, values):
-    anywhere = pl.BlockSpec(memory_space=pltpu.HBM)
     return pl.pallas_call(
         build_kernel,
-        out_shape=(bf16(ROWS, ROWS),) * 2,
+        out_shape=bf16(2 * ROWS, ROWS),
         in_specs=[pl.BlockSpec(memory_space=pltpu.SMEM)] * 2 + [pl.BlockSpec(memory_space=pltpu.VMEM)],
-        out_specs=(anywhere,) * 2,
-        scratch_shapes=[pltpu.VMEM((2 * ROWS, ROWS), jnp.bfloat16), pltpu.SemaphoreType.DMA((2,))],
-        compiler_params=pltpu.CompilerParams(vmem_limit_bytes=24 << 20),
+        out_specs=pl.BlockSpec(memory_space=pltpu.VMEM),
+        compiler_params=pltpu.CompilerParams(vmem_limit_bytes=16 << 20),
         cost_estimate=pl.CostEstimate(flops=0, bytes_accessed=30 << 20, transcendentals=0),
         name="build",
     )(coords, counts, values)
@@ -113,51 +114,54 @@
     return lax.dot_general(a, b, (((0,), (0,)), ((), ())), preferred_element_type=jnp.float32)
 
 
-def down_kernel(first, count, tile, panel, out):
+def down_kernel(first, count, dense, panel, out):
     for r in range(0, count, STEP):
-        rows = slice(first + r, first + r + STEP)
-        out[r : r + STEP] = jnp.dot(tile[rows], panel[...], preferred_element_type=jnp.float32).astype(out.dtype)
-
-
-def down_add_kernel(first, count, tile, panel, other, *rest):
-    out = rest[-1]
-    for r in range(0, count, STEP):
-        rows = slice(first + r, first + r + STEP)
-        own = jnp.dot(tile[rows], panel[...], preferred_element_type=jnp.float32)
-        out[rows] = (own + other[r : r + STEP].astype(jnp.float32)).astype(out.dtype)
-
-
-def up_kernel(tile, rows, out):
+        rows = slice(ROWS + first + r, ROWS + first + r + STEP)
+        out[r : r + STEP] = jnp.dot(dense[rows], panel[...], preferred_element_type=jnp.float32).astype(out.dtype)
+
+
+def store(out, place, axes, value):
+    for k in range(2):
+        out[absolute(place + k, *axes)] = value[k * OWN : (k + 1) * OWN].astype(out.dtype)
+
+
+def down_add_kernel(first, count, dense, panel, other, *rest):
+    for r in range(0, count, 2 * OWN):
+        own = jnp.dot(dense[first + r : first + r + 2 * OWN], panel[...], preferred_element_type=jnp.float32)
+        store(rest[-1], (first + r) // OWN, CHIP, own + other[r : r + 2 * OWN].astype(jnp.float32))
+
+
+def up_kernel(dense, rows, out):
     for r in range(0, ROWS, STEP):
-        out[r : r + STEP] = over_rows(tile[:, r : r + STEP], rows[...])
-
-
-def up_add_kernel(tile, rows, other, out):
-    for r in range(0, ROWS, STEP):
-        total = over_rows(tile[:, r : r + STEP], rows[...]) + other[r : r + STEP]
-        out[r : r + STEP] = total.astype(out.dtype)
-
-
-def down_both(near, far, panel):
+        out[r : r + STEP] = over_rows(dense[:ROWS, r : r + STEP], rows[...])
+
+
+def up_add_kernel(dense, rows, other, out):
+    for r in range(0, ROWS, 2 * OWN):
+        total = over_rows(dense[ROWS:, r : r + 2 * OWN], rows[...]) + other[r : r + 2 * OWN]
+        store(out, r // OWN, ROW, total)
+
+
+def down_both(dense, panel):
     count = ROWS // 2
     work = 2 * count * ROWS * WIDTH
     others = []
     for n in range(2):
         kernel = functools.partial(down_kernel, n * count, count)
-        others.append(trade(vmem_call(kernel, bf16(count, WIDTH), f"down_far_{n}", flops=work)(far, panel), "core"))
+        others.append(trade(vmem_call(kernel, bf16(count, WIDTH), f"down_far_{n}", flops=work)(dense, panel), "core"))
     out = []
     for n in range(2):
         kernel = functools.partial(down_add_kernel, n * count, count)
         out = vmem_call(
-            kernel, bf16(ROWS, WIDTH), f"down_near_{n}", flops=work, aliases={3: 0} if n else {}
-        )(near, panel, others[n], *([out] if n else []))
+            kernel, bf16(PEERS, OWN, WIDTH), f"down_near_{n}", flops=work, aliases={3: 0} if n else {}
+        )(dense, panel, others[n], *([out] if n else []))
     return out
 
 
-def up_both(near, far, mine, theirs):
+def up_both(dense, mine, theirs):
     work = 2 * ROWS * ROWS * WIDTH
-    own = vmem_call(up_kernel, jax.ShapeDtypeStruct((ROWS, WIDTH), jnp.float32), "up_near", flops=work)(near, mine)
-    return vmem_call(up_add_kernel, bf16(ROWS, WIDTH), "up_far", flops=work)(far, theirs, own)
+    own = vmem_call(up_kernel, jax.ShapeDtypeStruct((ROWS, WIDTH), jnp.float32), "up_near", flops=work)(dense, mine)
+    return vmem_call(up_add_kernel, bf16(PEERS, OWN, WIDTH), "up_far", flops=work)(dense, theirs, own)
 
 
 def middle_kernel(parts, out_grad, weight, activations, send, wgrad_near, wgrad_far, local):
@@ -181,8 +185,7 @@
     grad_agg = lax.dot_general(
         grad_pre, w, (((1,), (1,)), ((), ())), preferred_element_type=jnp.float32
     ).astype(jnp.bfloat16)
-    for k in range(PEERS):
-        send[k] = grad_agg
+    send[...] = grad_agg
     local[...] = over_rows(aggregated, grad_pre).astype(jnp.bfloat16)
     core = lax.axis_index("core")
     for k in range(RING):
@@ -253,6 +256,26 @@
     return lax.ppermute(array, axes, [(i, i ^ bits) for i in range(lax.axis_size(axes))])
 
 
+def stack_kernel(*refs):
+    *parts, out = refs
+    for k, part in enumerate(parts):
+        out[k * OWN : (k + 1) * OWN] = part[...]
+
+
+def gather(block, slow, fast):
+    def ahead(array, step):
+        return lax.ppermute(array, fast, [(i, (i - step) % RING) for i in range(RING)])
+
+    across = trade(block, slow)
+    before, after = ahead(block, -1), ahead(block, 1)
+    across_before = trade(before, slow)
+    across_after = ahead(across, 1)
+    beyond = ahead(before, -1)
+    across_beyond = ahead(across_after, 1)
+    blocks = (block, after, beyond, before, across, across_after, across_beyond, across_before)
+    return vmem_call(stack_kernel, bf16(ROWS, WIDTH), "stack_" + fast)(*blocks)
+
+
 def scatter_ring(pieces, axis, name):
     arrived = [pieces[0]]
     for k in range(1, RING):
@@ -268,21 +291,20 @@
 
 
 def per_device(features, out_grad, weight, block_values, block_coords, block_counts):
-    panel = exchange(jnp.broadcast_to(features[None], (PEERS, OWN, WIDTH)), ROW).reshape(ROWS, WIDTH)
-    near, far = build(block_coords, block_counts, block_values)
-
-    parts = exchange(down_both(near, far, panel).reshape(PEERS, OWN, WIDTH), CHIP)
+    dense = build(block_coords, block_counts, block_values)
+    panel = gather(features, *ROW)
+    parts = exchange(down_both(dense, panel), CHIP)
 
     half = bf16(WIDTH // 2, WIDTH)
     activations, send, wgrad_near, wgrad_far = vmem_call(
         middle_kernel,
-        (bf16(OWN, WIDTH), bf16(PEERS, OWN, WIDTH), half, half),
+        (bf16(OWN, WIDTH), bf16(OWN, WIDTH), half, half),
         "middle",
         scratch=[pltpu.VMEM((WIDTH, WIDTH), jnp.bfloat16)],
         flops=2 * 3 * OWN * WIDTH * WIDTH,
     )(parts, out_grad, weight)
 
-    mine = exchange(send, CHIP).reshape(ROWS, WIDTH)
+    mine = gather(send, *CHIP)
 
     piece = bf16(PIECE, WIDTH)
     pieces = vmem_call(pair_kernel, (piece,) * RING, "pair")(wgrad_near, trade(wgrad_far, "core"))
@@ -294,9 +316,9 @@
     summed, mine = lax.optimization_barrier((summed, mine))
     pieces = gather_ring(summed, "z")
     theirs = trade(mine, "core")
-    partial_grad = up_both(near, far, mine, theirs)
+    partial_grad = up_both(dense, mine, theirs)
     partial_grad, *pieces = lax.optimization_barrier((partial_grad, *pieces))
-    received = exchange(partial_grad.reshape(PEERS, OWN, WIDTH), ROW)
+    received = exchange(partial_grad, ROW)
 
     column = bf16(WIDTH // 2, LANES)
     columns = vmem_call(turn_kernel, (column,) * RING, "turn")(*pieces)

time: 140 us -> 138 us (0.986)
  local copies, waits for them, and re-layouts: 15.3 us -> 2.36 us
  starting transfers between devices: 38.2 us -> 46.7 us
  blocking collectives: 29.9 us -> 34.5 us
    ppermute x0 -> x10, starting transfers between devices: none -> 17 us  [ahead(): lax.ppermute(array, fast, [(i, (i - step) % RING) for i in range(RING)])]
    all_to_all x3 -> x1, waiting for transfers between devices: 11.9 us -> 0.74 us  [exchange(): return lax.all_to_all(parts, axes, 0, 0)]
    unnamed x20 -> x10, local copies, waits for them, and re-layouts: 13.1 us -> 2.36 us
    all_to_all x3 -> x1, starting transfers between devices: 13.7 us -> 4.52 us  [exchange(): return lax.all_to_all(parts, axes, 0, 0)]
    ppermute x8 -> x12, waiting for transfers between devices: 13.3 us -> 19.9 us  [trade(): lax.ppermute(array, axes, [(i, i ^ bits) for i in range(lax.axis_size(axe...]
    all_to_all x1, blocking collectives: 29.9 us -> 34.5 us  [exchange(): return lax.all_to_all(parts, axes, 0, 0)]
    ppermute x8 -> x12, starting transfers between devices: 5.7 us -> 9.97 us  [trade(): lax.ppermute(array, axes, [(i, i ^ bits) for i in range(lax.axis_size(axe...]
    broadcast_in_dim x1 -> x0, local copies, waits for them, and re-layouts: 2.21 us -> none  [per_device(): jnp.broadcast_to(features[None], (PEERS, OWN, WIDTH))]
  transfers between devices with their start and end apart: 23 -> 35, of which waited for: 18 -> 17; matrix products, arithmetic and copies ran while one was open for 0% -> 0% of each run, Pallas kernels for 10% -> 10%
where the time goes in v5:
time: 138 us
  starting transfers between devices  46.7 us (34%)
  blocking collectives  34.5 us (25%)
  waiting for transfers between devices  34.3 us (25%)
  Pallas kernels  18.1 us (13%)
  local copies, waits for them, and re-layouts  2.36 us (2%)
  between operations  1.54 us (1%)
    all_to_all x1, blocking collectives, exchange(): return lax.all_to_all(parts, axes, 0, 0)  34.5 us
    ppermute x12, waiting for transfers between devices, trade(): lax.ppermute(array, axes, [(i, i ^ bits) for i in range(lax.axis_size(axe...  19.9 us
    ppermute x10, starting transfers between devices, ahead(): lax.ppermute(array, fast, [(i, (i - step) % RING) for i in range(RING)])  17 us
    pallas_call x16, Pallas kernels, call(): pl.pallas_call(kernel, out_shape=outs, in_specs=[vmem] * len(args), out_s...  15.1 us
    ppermute x12, starting transfers between devices, trade(): lax.ppermute(array, axes, [(i, i ^ bits) for i in range(lax.axis_size(axe...  9.97 us
    ppermute x6, starting transfers between devices, scatter_ring(): lax.ppermute(pieces[k], axis, [(i, (i + k) % RING) for i in range(RING)])  7.83 us
    ppermute x6, starting transfers between devices, gather_ring(): lax.ppermute(piece, axis, [(i, (i - k) % RING) for i in range(RING)])  7.39 us
    ppermute x6, waiting for transfers between devices, scatter_ring(): lax.ppermute(pieces[k], axis, [(i, (i + k) % RING) for i in range(RING)])  6.36 us
  transfers between devices with their start and end apart: 35, of which 17 were waited for; matrix products, arithmetic and copies ran while one was open for 0% of the time, Pallas kernels for 10%

profile of v5, /device:TPU:0, one launch (start us, length us, event | category | flops | bytes accessed | tf_op | source)
XLA Modules:
  0.0 138.5 jit_solution(5005932044807595628)
XLA Ops:
  0.6 1.7 %collective-permute-start.3 = (bf16[192,512]{1,0:T(8,128)(2,1)}, bf16[192,512]{1,0:T(8,128)(2,1)S(1)}, u32[]{:S(2)}, u32[]{:S(2)}) collective-permute-start(bf16[192,512]{1,0:T(8,128)(2,1)} %refs_0_.1), channel_id=1, source_target_pairs={{0,64},{64,0},{1,65},{65,1},{2,66},{66,2},{3,67},{67,3},{4,68},{68... | collective-permute-start | bytes 589832 | tf_op jit(solution)/shard_map/ppermute | solution.py:256
  2.4 1.9 %collective-permute-start.1 = (bf16[192,512]{1,0:T(8,128)(2,1)}, bf16[192,512]{1,0:T(8,128)(2,1)S(1)}, u32[]{:S(2)}, u32[]{:S(2)}) collective-permute-start(bf16[192,512]{1,0:T(8,128)(2,1)} %refs_0_.1), channel_id=1, source_target_pairs={{0,16},{16,32},{32,48},{48,0},{1,17},{17,33},{33,49},{49,1},{2,18}... | collective-permute-start | bytes 589832 | tf_op jit(solution)/shard_map/ppermute | solution.py:267
  4.3 3.2 %collective-permute-done.3.refs_4_ = bf16[192,512]{1,0:T(8,128)(2,1)S(1)} collective-permute-done((bf16[192,512]{1,0:T(8,128)(2,1)}, bf16[192,512]{1,0:T(8,128)(2,1)S(1)}, u32[]{:S(2)}, u32[]{:S(2)}) %collective-permute-start.3) | collective-permute-done | bytes 196640 | tf_op jit(solution)/shard_map/ppermute | solution.py:256
  7.5 4.2 %collective-permute-start.4 = (bf16[192,512]{1,0:T(8,128)(2,1)S(1)}, bf16[192,512]{1,0:T(8,128)(2,1)S(1)}, u32[]{:S(2)}, u32[]{:S(2)}) collective-permute-start(bf16[192,512]{1,0:T(8,128)(2,1)S(1)} %collective-permute-done.3.refs_4_), channel_id=1, source_target_pairs={{0,48},{16,0},{32,16},{48,32},{1,49},{17,1},{33,17},{49,33},{2,50}... | collective-permute-start | bytes 589832 | tf_op jit(solution)/shard_map/ppermute | solution.py:267
  12.1 1.6 %collective-permute-start.2 = (bf16[192,512]{1,0:T(8,128)(2,1)S(1)}, bf16[192,512]{1,0:T(8,128)(2,1)S(1)}, u32[]{:S(2)}, u32[]{:S(2)}) collective-permute-start(bf16[192,512]{1,0:T(8,128)(2,1)S(1)} %collective-permute-done.1.refs_3_), channel_id=1, source_target_pairs={{0,16},{16,32},{32,48},{48,0},{1,17},{17,33},{33,49},{49,1},{2,18}... | collective-permute-start | bytes 589832 | tf_op jit(solution)/shard_map/ppermute | solution.py:267
  13.7 1.6 %collective-permute-start.6 = (bf16[192,512]{1,0:T(8,128)(2,1)S(1)}, bf16[192,512]{1,0:T(8,128)(2,1)S(1)}, u32[]{:S(2)}, u32[]{:S(2)}) collective-permute-start(bf16[192,512]{1,0:T(8,128)(2,1)S(1)} %collective-permute-done.1.refs_3_), channel_id=1, source_target_pairs={{0,64},{64,0},{1,65},{65,1},{2,66},{66,2},{3,67},{67,3},{4,68},{68... | collective-permute-start | bytes 589832 | tf_op jit(solution)/shard_map/ppermute | solution.py:256
  15.3 1.7 %collective-permute-done.4.refs_5_ = bf16[192,512]{1,0:T(8,128)(2,1)S(1)} collective-permute-done((bf16[192,512]{1,0:T(8,128)(2,1)S(1)}, bf16[192,512]{1,0:T(8,128)(2,1)S(1)}, u32[]{:S(2)}, u32[]{:S(2)}) %collective-permute-start.4) | collective-permute-done | bytes 196640 | tf_op jit(solution)/shard_map/ppermute | solution.py:267
  17.0 3.7 %collective-permute-start.5 = (bf16[192,512]{1,0:T(8,128)(2,1)S(1)}, bf16[192,512]{1,0:T(8,128)(2,1)S(1)}, u32[]{:S(2)}, u32[]{:S(2)}) collective-permute-start(bf16[192,512]{1,0:T(8,128)(2,1)S(1)} %collective-permute-done.4.refs_5_), channel_id=1, source_target_pairs={{0,48},{16,0},{32,16},{48,32},{1,49},{17,1},{33,17},{49,33},{2,50}... | collective-permute-start | bytes 589832 | tf_op jit(solution)/shard_map/ppermute | solution.py:267
  21.4 1.7 %copy-done = bf16[1,1,288,4096]{3,2,1,0:T(8,128)(2,1)S(1)} copy-done((bf16[1,1,288,4096]{3,2,1,0:T(8,128)(2,1)S(1)}, bf16[1,1,288,4096]{3,2,1,0:T(8,128)(2,1)}, u32[]{:S(2)}) %copy-start) | copy-done | bytes 2359320
  23.7 3.0 %build.1.dense = bf16[3072,1536]{1,0:T(8,128)(2,1)S(1)} custom-call(s32[1,1,2,288]{3,2,1,0:T(2,128)S(1)} %copy-done.4, s32[1,1]{1,0:T(1,128)S(6)} %copy.11.counts, bf16[1,1,288,4096]{3,2,1,0:T(8,128)(2,1)S(1)} %copy-done), custom_call_target="tpu_custom_call" | custom-call | bytes 31457280 | tf_op jit(solution)/shard_map/build/pallas_call | solution.py:102
  26.9 1.4 down_far_0.1
  28.4 1.4 down_far_1.1
  33.7 34.5 %all_to_all.10.parts = bf16[8,192,512]{2,1,0:T(8,128)(2,1)S(1)} all-to-all(bf16[8,192,512]{2,1,0:T(8,128)(2,1)S(1)} %down_near_1.1), channel_id=1, replica_groups=mesh['y_lo'=2,'z'=4,'y_hi'=2,'x'=4,'core'=2] {'y_hi','x'}, dimensions={0} | all-to-all | bytes 3145728 | tf_op jit(solution)/shard_map/all_to_all | solution.py:252
  68.2 1.6 %middle.1 = (bf16[192,512]{1,0:T(8,128)(2,1)}, bf16[192,512]{1,0:T(8,128)(2,1)S(1)}, bf16[256,512]{1,0:T(8,128)(2,1)S(1)}, bf16[256,512]{1,0:T(8,128)(2,1)S(1)}) custom-call(bf16[8,192,512]{2,1,0:T(8,128)(2,1)S(1)} %all_to_all.10.parts, bf16[192,512]{1,0:T(8,128)(2,1)S(1)} %copy-done.3, bf16[512,512]{1,0:T(8,128)(2,1)S(1)} %copy-done.1), custom_call_target="tpu_custom_call" | custom-call | flops 301989888 | bytes 1048576 | tf_op jit(solution)/shard_map/middle/pallas_call | solution.py:31
  71.2 6.6 %collective-permute-done.19.refs_4_ = bf16[192,512]{1,0:T(8,128)(2,1)S(1)} collective-permute-done((bf16[192,512]{1,0:T(8,128)(2,1)S(1)}, bf16[192,512]{1,0:T(8,128)(2,1)S(1)}, u32[]{:S(2)}, u32[]{:S(2)}) %collective-permute-start.19) | collective-permute-done | bytes 196640 | tf_op jit(solution)/shard_map/ppermute | solution.py:256
  78.3 3.1 %collective-permute-start.12 = (bf16[64,512]{1,0:T(8,128)(2,1)S(1)}, bf16[64,512]{1,0:T(8,128)(2,1)S(1)}, u32[]{:S(2)}, u32[]{:S(2)}) collective-permute-start(bf16[64,512]{1,0:T(8,128)(2,1)S(1)} %get-tuple-element.28), channel_id=1, source_target_pairs={{0,48},{16,0},{32,16},{48,32},{1,49},{17,1},{33,17},{49,33},{2,50}... | collective-permute-start | bytes 196616 | tf_op jit(solution)/shard_map/ppermute | solution.py:282
  81.5 2.9 %collective-permute-done.10.refs_1_ = bf16[64,512]{1,0:T(8,128)(2,1)S(1)} collective-permute-done((bf16[64,512]{1,0:T(8,128)(2,1)S(1)}, bf16[64,512]{1,0:T(8,128)(2,1)S(1)}, u32[]{:S(2)}, u32[]{:S(2)}) %collective-permute-start.10) | collective-permute-done | bytes 65568 | tf_op jit(solution)/shard_map/ppermute | solution.py:282
  87.3 1.4 %collective-permute-start.18 = (bf16[192,512]{1,0:T(8,128)(2,1)S(1)}, bf16[192,512]{1,0:T(8,128)(2,1)S(1)}, u32[]{:S(2)}, u32[]{:S(2)}) collective-permute-start(bf16[192,512]{1,0:T(8,128)(2,1)S(1)} %collective-permute-done.17.refs_3_), channel_id=1, source_target_pairs={{0,2},{2,4},{4,6},{6,0},{1,3},{3,5},{5,7},{7,1},{8,10},{10,12},{12... | collective-permute-start | bytes 589832 | tf_op jit(solution)/shard_map/ppermute | solution.py:267
  88.7 2.2 %collective-permute-start.22 = (bf16[192,512]{1,0:T(8,128)(2,1)S(1)}, bf16[192,512]{1,0:T(8,128)(2,1)S(1)}, u32[]{:S(2)}, u32[]{:S(2)}) collective-permute-start(bf16[192,512]{1,0:T(8,128)(2,1)S(1)} %collective-permute-done.17.refs_3_), channel_id=1, source_target_pairs={{0,8},{8,0},{1,9},{9,1},{2,10},{10,2},{3,11},{11,3},{4,12},{12,4},... | collective-permute-start | bytes 589832 | tf_op jit(solution)/shard_map/ppermute | solution.py:256
  90.9 2.0 %collective-permute-start.21 = (bf16[192,512]{1,0:T(8,128)(2,1)S(1)}, bf16[192,512]{1,0:T(8,128)(2,1)S(1)}, u32[]{:S(2)}, u32[]{:S(2)}) collective-permute-start(bf16[192,512]{1,0:T(8,128)(2,1)S(1)} %collective-permute-done.20.refs_5_), channel_id=1, source_target_pairs={{0,6},{2,0},{4,2},{6,4},{1,7},{3,1},{5,3},{7,5},{8,14},{10,8},{12,... | collective-permute-start | bytes 589832 | tf_op jit(solution)/shard_map/ppermute | solution.py:267
  93.6 3.6 %collective-permute-done.14.c = bf16[64,512]{1,0:T(8,128)(2,1)S(1)} collective-permute-done((bf16[64,512]{1,0:T(8,128)(2,1)S(1)}, bf16[64,512]{1,0:T(8,128)(2,1)S(1)}, u32[]{:S(2)}, u32[]{:S(2)}) %collective-permute-start.14) | collective-permute-done | bytes 65568 | tf_op jit(solution)/shard_map/ppermute | solution.py:256
  98.2 4.5 %collective-permute-done.15.d = bf16[64,512]{1,0:T(8,128)(2,1)S(1)} collective-permute-done((bf16[64,512]{1,0:T(8,128)(2,1)S(1)}, bf16[64,512]{1,0:T(8,128)(2,1)S(1)}, u32[]{:S(2)}, u32[]{:S(2)}) %collective-permute-start.15) | collective-permute-done | bytes 65568 | tf_op jit(solution)/shard_map/ppermute | solution.py:256
  103.0 2.5 %collective-permute-start.24 = (bf16[64,512]{1,0:T(8,128)(2,1)S(1)}, bf16[64,512]{1,0:T(8,128)(2,1)S(1)}, u32[]{:S(2)}, u32[]{:S(2)}) collective-permute-start(bf16[64,512]{1,0:T(8,128)(2,1)S(1)} %sum_y.1.refs_0_), channel_id=1, source_target_pairs={{0,48},{16,0},{32,16},{48,32},{1,49},{17,1},{33,17},{49,33},{2,50}... | collective-permute-start | bytes 196616 | tf_op jit(solution)/shard_map/ppermute | solution.py:289
  106.4 2.6 %up_near.1.other = f32[1536,512]{1,0:T(8,128)S(1)} custom-call(bf16[3072,1536]{1,0:T(8,128)(2,1)S(1)} %build.1.dense, bf16[1536,512]{1,0:T(8,128)(2,1)S(1)} %stack_x.1.rows), custom_call_target="tpu_custom_call" | custom-call | flops 2415919104 | bytes 1048576 | tf_op jit(solution)/shard_map/up_near/pallas_call | solution.py:31
  109.1 3.8 %up_far.1 = bf16[8,192,512]{2,1,0:T(8,128)(2,1)} custom-call(bf16[3072,1536]{1,0:T(8,128)(2,1)S(1)} %build.1.dense, bf16[1536,512]{1,0:T(8,128)(2,1)S(1)} %collective-permute-done.23.rows, f32[1536,512]{1,0:T(8,128)S(1)} %up_near.1.other), custom_call_target="tpu_custom_call" | custom-call | flops 2415919104 | bytes 1048576 | tf_op jit(solution)/shard_map/up_far/pallas_call | solution.py:31
  112.9 4.5 %all-to-all-start.1 = ((bf16[8,192,512]{2,1,0:T(8,128)(2,1)}), bf16[8,192,512]{2,1,0:T(8,128)(2,1)S(1)}, u32[]{:S(2)}, u32[]{:S(2)}) async-start(bf16[8,192,512]{2,1,0:T(8,128)(2,1)} %up_far.1), calls=%async_computation.1 | async-start | bytes 3145728 | tf_op jit(solution)/shard_map/all_to_all | solution.py:252
  118.1 1.7 %collective-permute-start.28 = (bf16[256,128]{1,0:T(8,128)(2,1)S(1)}, bf16[256,128]{1,0:T(8,128)(2,1)S(1)}, u32[]{:S(2)}, u32[]{:S(2)}) collective-permute-start(bf16[256,128]{1,0:T(8,128)(2,1)S(1)} %get-tuple-element.38), channel_id=1, source_target_pairs={{0,4},{2,6},{4,0},{6,2},{1,5},{3,7},{5,1},{7,3},{8,12},{10,14},{12... | collective-permute-start | bytes 196616 | tf_op jit(solution)/shard_map/ppermute | solution.py:282
  119.7 2.3 %collective-permute-start.29 = (bf16[256,128]{1,0:T(8,128)(2,1)S(1)}, bf16[256,128]{1,0:T(8,128)(2,1)S(1)}, u32[]{:S(2)}, u32[]{:S(2)}) collective-permute-start(bf16[256,128]{1,0:T(8,128)(2,1)S(1)} %get-tuple-element.39), channel_id=1, source_target_pairs={{0,6},{2,0},{4,2},{6,4},{1,7},{3,1},{5,3},{7,5},{8,14},{10,8},{12,... | collective-permute-start | bytes 196616 | tf_op jit(solution)/shard_map/ppermute | solution.py:282
  124.6 3.0 %collective-permute-start.30 = (bf16[256,128]{1,0:T(8,128)(2,1)S(1)}, bf16[256,128]{1,0:T(8,128)(2,1)S(1)}, u32[]{:S(2)}, u32[]{:S(2)}) collective-permute-start(bf16[256,128]{1,0:T(8,128)(2,1)S(1)} %sum_x.1.refs_0_), channel_id=1, source_target_pairs={{0,6},{2,0},{4,2},{6,4},{1,7},{3,1},{5,3},{7,5},{8,14},{10,8},{12,... | collective-permute-start | bytes 196616 | tf_op jit(solution)/shard_map/ppermute | solution.py:289
  128.5 1.6 %collective-permute-done.30.refs_1_ = bf16[256,128]{1,0:T(8,128)(2,1)S(1)} collective-permute-done((bf16[256,128]{1,0:T(8,128)(2,1)S(1)}, bf16[256,128]{1,0:T(8,128)(2,1)S(1)}, u32[]{:S(2)}, u32[]{:S(2)}) %collective-permute-start.30) | collective-permute-done | bytes 65568 | tf_op jit(solution)/shard_map/ppermute | solution.py:289
  130.1 3.3 %collective-permute-done.31.refs_2_ = bf16[256,128]{1,0:T(8,128)(2,1)S(1)} collective-permute-done((bf16[256,128]{1,0:T(8,128)(2,1)S(1)}, bf16[256,128]{1,0:T(8,128)(2,1)S(1)}, u32[]{:S(2)}, u32[]{:S(2)}) %collective-permute-start.31) | collective-permute-done | bytes 65568 | tf_op jit(solution)/shard_map/ppermute | solution.py:289
  134.2 1.5 %collective-permute-done.33.theirs = bf16[256,512]{1,0:T(8,128)(2,1)S(1)} collective-permute-done((bf16[256,512]{1,0:T(8,128)(2,1)S(1)}, bf16[256,512]{1,0:T(8,128)(2,1)S(1)}, u32[]{:S(2)}, u32[]{:S(2)}) %collective-permute-start.33) | collective-permute-done | bytes 262176 | tf_op jit(solution)/shard_map/ppermute | solution.py:256
  (67 shorter events, 20.7 us)
Async XLA Ops:
  0.6 6.9 %collective-permute-start.3 = (bf16[192,512]{1,0:T(8,128)(2,1)}, bf16[192,512]{1,0:T(8,128)(2,1)S(1)}, u32[]{:S(2)}, u32[]{:S(2)}) collective-permute-start(bf16[192,512]{1,0:T(8,128)(2,1)} %refs_0_.1), channel_id=1, source_target_pairs={{0,64},{64,0},{1,65},{65,1},{2,66},{66,2},{3,67},{67,3},{4,68},{68... | collective-permute-start | bytes 589832 | tf_op jit(solution)/shard_map/ppermute | solution.py:256
  2.4 9.7 %collective-permute-start.1 = (bf16[192,512]{1,0:T(8,128)(2,1)}, bf16[192,512]{1,0:T(8,128)(2,1)S(1)}, u32[]{:S(2)}, u32[]{:S(2)}) collective-permute-start(bf16[192,512]{1,0:T(8,128)(2,1)} %refs_0_.1), channel_id=1, source_target_pairs={{0,16},{16,32},{32,48},{48,0},{1,17},{17,33},{33,49},{49,1},{2,18}... | collective-permute-start | bytes 589832 | tf_op jit(solution)/shard_map/ppermute | solution.py:267
  7.5 9.6 %collective-permute-start.4 = (bf16[192,512]{1,0:T(8,128)(2,1)S(1)}, bf16[192,512]{1,0:T(8,128)(2,1)S(1)}, u32[]{:S(2)}, u32[]{:S(2)}) collective-permute-start(bf16[192,512]{1,0:T(8,128)(2,1)S(1)} %collective-permute-done.3.refs_4_), channel_id=1, source_target_pairs={{0,48},{16,0},{32,16},{48,32},{1,49},{17,1},{33,17},{49,33},{2,50}... | collective-permute-start | bytes 589832 | tf_op jit(solution)/shard_map/ppermute | solution.py:267
  11.7 15.1 %collective-permute-start = (bf16[192,512]{1,0:T(8,128)(2,1)}, bf16[192,512]{1,0:T(8,128)(2,1)S(1)}, u32[]{:S(2)}, u32[]{:S(2)}) collective-permute-start(bf16[192,512]{1,0:T(8,128)(2,1)} %refs_0_.1), channel_id=1, source_target_pairs={{0,48},{16,0},{32,16},{48,32},{1,49},{17,1},{33,17},{49,33},{2,50}... | collective-permute-start | bytes 589832 | tf_op jit(solution)/shard_map/ppermute | solution.py:267
  12.1 14.7 %collective-permute-start.2 = (bf16[192,512]{1,0:T(8,128)(2,1)S(1)}, bf16[192,512]{1,0:T(8,128)(2,1)S(1)}, u32[]{:S(2)}, u32[]{:S(2)}) collective-permute-start(bf16[192,512]{1,0:T(8,128)(2,1)S(1)} %collective-permute-done.1.refs_3_), channel_id=1, source_target_pairs={{0,16},{16,32},{32,48},{48,0},{1,17},{17,33},{33,49},{49,1},{2,18}... | collective-permute-start | bytes 589832 | tf_op jit(solution)/shard_map/ppermute | solution.py:267
  13.7 13.1 %collective-permute-start.6 = (bf16[192,512]{1,0:T(8,128)(2,1)S(1)}, bf16[192,512]{1,0:T(8,128)(2,1)S(1)}, u32[]{:S(2)}, u32[]{:S(2)}) collective-permute-start(bf16[192,512]{1,0:T(8,128)(2,1)S(1)} %collective-permute-done.1.refs_3_), channel_id=1, source_target_pairs={{0,64},{64,0},{1,65},{65,1},{2,66},{66,2},{3,67},{67,3},{4,68},{68... | collective-permute-start | bytes 589832 | tf_op jit(solution)/shard_map/ppermute | solution.py:256
  17.0 9.8 %collective-permute-start.5 = (bf16[192,512]{1,0:T(8,128)(2,1)S(1)}, bf16[192,512]{1,0:T(8,128)(2,1)S(1)}, u32[]{:S(2)}, u32[]{:S(2)}) collective-permute-start(bf16[192,512]{1,0:T(8,128)(2,1)S(1)} %collective-permute-done.4.refs_5_), channel_id=1, source_target_pairs={{0,48},{16,0},{32,16},{48,32},{1,49},{17,1},{33,17},{49,33},{2,50}... | collective-permute-start | bytes 589832 | tf_op jit(solution)/shard_map/ppermute | solution.py:267
  69.8 8.0 %collective-permute-start.19 = (bf16[192,512]{1,0:T(8,128)(2,1)S(1)}, bf16[192,512]{1,0:T(8,128)(2,1)S(1)}, u32[]{:S(2)}, u32[]{:S(2)}) collective-permute-start(bf16[192,512]{1,0:T(8,128)(2,1)S(1)} %get-tuple-element.29.refs_0_), channel_id=1, source_target_pairs={{0,8},{8,0},{1,9},{9,1},{2,10},{10,2},{3,11},{11,3},{4,12},{12,4},... | collective-permute-start | bytes 589832 | tf_op jit(solution)/shard_map/ppermute | solution.py:256
  70.4 7.7 %collective-permute-start.9 = (bf16[256,512]{1,0:T(8,128)(2,1)S(1)}, bf16[256,512]{1,0:T(8,128)(2,1)S(1)}, u32[]{:S(2)}, u32[]{:S(2)}) collective-permute-start(bf16[256,512]{1,0:T(8,128)(2,1)S(1)} %get-tuple-element.24), channel_id=1, source_target_pairs={{0,1},{1,0},{2,3},{3,2},{4,5},{5,4},{6,7},{7,6},{8,9},{9,8},{10,11... | collective-permute-start | bytes 786440 | tf_op jit(solution)/shard_map/ppermute | solution.py:256
  70.4 16.9 %collective-permute-start.17 = (bf16[192,512]{1,0:T(8,128)(2,1)S(1)}, bf16[192,512]{1,0:T(8,128)(2,1)S(1)}, u32[]{:S(2)}, u32[]{:S(2)}) collective-permute-start(bf16[192,512]{1,0:T(8,128)(2,1)S(1)} %get-tuple-element.29.refs_0_), channel_id=1, source_target_pairs={{0,2},{2,4},{4,6},{6,0},{1,3},{3,5},{5,7},{7,1},{8,10},{10,12},{12... | collective-permute-start | bytes 589832 | tf_op jit(solution)/shard_map/ppermute | solution.py:267
  77.8 13.1 %collective-permute-start.20 = (bf16[192,512]{1,0:T(8,128)(2,1)S(1)}, bf16[192,512]{1,0:T(8,128)(2,1)S(1)}, u32[]{:S(2)}, u32[]{:S(2)}) collective-permute-start(bf16[192,512]{1,0:T(8,128)(2,1)S(1)} %collective-permute-done.19.refs_4_), channel_id=1, source_target_pairs={{0,6},{2,0},{4,2},{6,4},{1,7},{3,1},{5,3},{7,5},{8,14},{10,8},{12,... | collective-permute-start | bytes 589832 | tf_op jit(solution)/shard_map/ppermute | solution.py:267
  78.2 6.2 %collective-permute-start.10 = (bf16[64,512]{1,0:T(8,128)(2,1)S(1)}, bf16[64,512]{1,0:T(8,128)(2,1)S(1)}, u32[]{:S(2)}, u32[]{:S(2)}) collective-permute-start(bf16[64,512]{1,0:T(8,128)(2,1)S(1)} %get-tuple-element.26), channel_id=1, source_target_pairs={{0,16},{16,32},{32,48},{48,0},{1,17},{17,33},{33,49},{49,1},{2,18}... | collective-permute-start | bytes 196616 | tf_op jit(solution)/shard_map/ppermute | solution.py:282
  78.2 6.2 %collective-permute-start.11 = (bf16[64,512]{1,0:T(8,128)(2,1)S(1)}, bf16[64,512]{1,0:T(8,128)(2,1)S(1)}, u32[]{:S(2)}, u32[]{:S(2)}) collective-permute-start(bf16[64,512]{1,0:T(8,128)(2,1)S(1)} %get-tuple-element.27), channel_id=1, source_target_pairs={{0,32},{16,48},{32,0},{48,16},{1,33},{17,49},{33,1},{49,17},{2,34}... | collective-permute-start | bytes 196616 | tf_op jit(solution)/shard_map/ppermute | solution.py:282
  78.3 6.9 %collective-permute-start.12 = (bf16[64,512]{1,0:T(8,128)(2,1)S(1)}, bf16[64,512]{1,0:T(8,128)(2,1)S(1)}, u32[]{:S(2)}, u32[]{:S(2)}) collective-permute-start(bf16[64,512]{1,0:T(8,128)(2,1)S(1)} %get-tuple-element.28), channel_id=1, source_target_pairs={{0,48},{16,0},{32,16},{48,32},{1,49},{17,1},{33,17},{49,33},{2,50}... | collective-permute-start | bytes 196616 | tf_op jit(solution)/shard_map/ppermute | solution.py:282
  85.3 7.6 %collective-permute-start.13 = (bf16[64,512]{1,0:T(8,128)(2,1)S(1)}, bf16[64,512]{1,0:T(8,128)(2,1)S(1)}, u32[]{:S(2)}, u32[]{:S(2)}) collective-permute-start(bf16[64,512]{1,0:T(8,128)(2,1)S(1)} %sum_z.1.a), channel_id=1, source_target_pairs={{0,8},{8,0},{64,72},{72,64},{1,9},{9,1},{65,73},{73,65},{2,10},{10... | collective-permute-start | bytes 196616 | tf_op jit(solution)/shard_map/ppermute | solution.py:256
  86.7 16.1 %collective-permute-start.16 = (bf16[192,512]{1,0:T(8,128)(2,1)S(1)}, bf16[192,512]{1,0:T(8,128)(2,1)S(1)}, u32[]{:S(2)}, u32[]{:S(2)}) collective-permute-start(bf16[192,512]{1,0:T(8,128)(2,1)S(1)} %get-tuple-element.29.refs_0_), channel_id=1, source_target_pairs={{0,6},{2,0},{4,2},{6,4},{1,7},{3,1},{5,3},{7,5},{8,14},{10,8},{12,... | collective-permute-start | bytes 589832 | tf_op jit(solution)/shard_map/ppermute | solution.py:267
  87.3 15.4 %collective-permute-start.18 = (bf16[192,512]{1,0:T(8,128)(2,1)S(1)}, bf16[192,512]{1,0:T(8,128)(2,1)S(1)}, u32[]{:S(2)}, u32[]{:S(2)}) collective-permute-start(bf16[192,512]{1,0:T(8,128)(2,1)S(1)} %collective-permute-done.17.refs_3_), channel_id=1, source_target_pairs={{0,2},{2,4},{4,6},{6,0},{1,3},{3,5},{5,7},{7,1},{8,10},{10,12},{12... | collective-permute-start | bytes 589832 | tf_op jit(solution)/shard_map/ppermute | solution.py:267
  88.7 14.0 %collective-permute-start.22 = (bf16[192,512]{1,0:T(8,128)(2,1)S(1)}, bf16[192,512]{1,0:T(8,128)(2,1)S(1)}, u32[]{:S(2)}, u32[]{:S(2)}) collective-permute-start(bf16[192,512]{1,0:T(8,128)(2,1)S(1)} %collective-permute-done.17.refs_3_), channel_id=1, source_target_pairs={{0,8},{8,0},{1,9},{9,1},{2,10},{10,2},{3,11},{11,3},{4,12},{12,4},... | collective-permute-start | bytes 589832 | tf_op jit(solution)/shard_map/ppermute | solution.py:256
  90.9 11.8 %collective-permute-start.21 = (bf16[192,512]{1,0:T(8,128)(2,1)S(1)}, bf16[192,512]{1,0:T(8,128)(2,1)S(1)}, u32[]{:S(2)}, u32[]{:S(2)}) collective-permute-start(bf16[192,512]{1,0:T(8,128)(2,1)S(1)} %collective-permute-done.20.refs_5_), channel_id=1, source_target_pairs={{0,6},{2,0},{4,2},{6,4},{1,7},{3,1},{5,3},{7,5},{8,14},{10,8},{12,... | collective-permute-start | bytes 589832 | tf_op jit(solution)/shard_map/ppermute | solution.py:267
  92.9 4.3 %collective-permute-start.14 = (bf16[64,512]{1,0:T(8,128)(2,1)S(1)}, bf16[64,512]{1,0:T(8,128)(2,1)S(1)}, u32[]{:S(2)}, u32[]{:S(2)}) collective-permute-start(bf16[64,512]{1,0:T(8,128)(2,1)S(1)} %sum_z.1.a), channel_id=1, source_target_pairs={{0,64},{8,72},{64,0},{72,8},{1,65},{9,73},{65,1},{73,9},{2,66},{10... | collective-permute-start | bytes 196616 | tf_op jit(solution)/shard_map/ppermute | solution.py:256
  97.2 5.5 %collective-permute-start.15 = (bf16[64,512]{1,0:T(8,128)(2,1)S(1)}, bf16[64,512]{1,0:T(8,128)(2,1)S(1)}, u32[]{:S(2)}, u32[]{:S(2)}) collective-permute-start(bf16[64,512]{1,0:T(8,128)(2,1)S(1)} %sum_z.1.a), channel_id=1, source_target_pairs={{0,72},{8,64},{64,8},{72,0},{1,73},{9,65},{65,9},{73,1},{2,74},{10... | collective-permute-start | bytes 196616 | tf_op jit(solution)/shard_map/ppermute | solution.py:256
  102.9 6.2 %collective-permute-start.23 = (bf16[1536,512]{1,0:T(8,128)(2,1)S(1)}, bf16[1536,512]{1,0:T(8,128)(2,1)S(1)}, u32[]{:S(2)}, u32[]{:S(2)}) collective-permute-start(bf16[1536,512]{1,0:T(8,128)(2,1)S(1)} %stack_x.1.rows), channel_id=1, source_target_pairs={{0,1},{1,0},{2,3},{3,2},{4,5},{5,4},{6,7},{7,6},{8,9},{9,8},{10,11... | collective-permute-start | bytes 4718600 | tf_op jit(solution)/shard_map/ppermute | solution.py:256
  103.0 9.9 %collective-permute-start.24 = (bf16[64,512]{1,0:T(8,128)(2,1)S(1)}, bf16[64,512]{1,0:T(8,128)(2,1)S(1)}, u32[]{:S(2)}, u32[]{:S(2)}) collective-permute-start(bf16[64,512]{1,0:T(8,128)(2,1)S(1)} %sum_y.1.refs_0_), channel_id=1, source_target_pairs={{0,48},{16,0},{32,16},{48,32},{1,49},{17,1},{33,17},{49,33},{2,50}... | collective-permute-start | bytes 196616 | tf_op jit(solution)/shard_map/ppermute | solution.py:289
  105.4 7.5 %collective-permute-start.25 = (bf16[64,512]{1,0:T(8,128)(2,1)S(1)}, bf16[64,512]{1,0:T(8,128)(2,1)S(1)}, u32[]{:S(2)}, u32[]{:S(2)}) collective-permute-start(bf16[64,512]{1,0:T(8,128)(2,1)S(1)} %sum_y.1.refs_0_), channel_id=1, source_target_pairs={{0,32},{16,48},{32,0},{48,16},{1,33},{17,49},{33,1},{49,17},{2,34}... | collective-permute-start | bytes 196616 | tf_op jit(solution)/shard_map/ppermute | solution.py:289
  106.4 6.4 %collective-permute-start.26 = (bf16[64,512]{1,0:T(8,128)(2,1)S(1)}, bf16[64,512]{1,0:T(8,128)(2,1)S(1)}, u32[]{:S(2)}, u32[]{:S(2)}) collective-permute-start(bf16[64,512]{1,0:T(8,128)(2,1)S(1)} %sum_y.1.refs_0_), channel_id=1, source_target_pairs={{0,16},{16,32},{32,48},{48,0},{1,17},{17,33},{33,49},{49,1},{2,18}... | collective-permute-start | bytes 196616 | tf_op jit(solution)/shard_map/ppermute | solution.py:289
  112.9 24.7 %all-to-all-start.1 = ((bf16[8,192,512]{2,1,0:T(8,128)(2,1)}), bf16[8,192,512]{2,1,0:T(8,128)(2,1)S(1)}, u32[]{:S(2)}, u32[]{:S(2)}) async-start(bf16[8,192,512]{2,1,0:T(8,128)(2,1)} %up_far.1), calls=%async_computation.1 | async-start | bytes 3145728 | tf_op jit(solution)/shard_map/all_to_all | solution.py:252
  117.5 5.7 %collective-permute-start.27 = (bf16[256,128]{1,0:T(8,128)(2,1)S(1)}, bf16[256,128]{1,0:T(8,128)(2,1)S(1)}, u32[]{:S(2)}, u32[]{:S(2)}) collective-permute-start(bf16[256,128]{1,0:T(8,128)(2,1)S(1)} %get-tuple-element.37), channel_id=1, source_target_pairs={{0,2},{2,4},{4,6},{6,0},{1,3},{3,5},{5,7},{7,1},{8,10},{10,12},{12... | collective-permute-start | bytes 196616 | tf_op jit(solution)/shard_map/ppermute | solution.py:282
  118.1 5.8 %collective-permute-start.28 = (bf16[256,128]{1,0:T(8,128)(2,1)S(1)}, bf16[256,128]{1,0:T(8,128)(2,1)S(1)}, u32[]{:S(2)}, u32[]{:S(2)}) collective-permute-start(bf16[256,128]{1,0:T(8,128)(2,1)S(1)} %get-tuple-element.38), channel_id=1, source_target_pairs={{0,4},{2,6},{4,0},{6,2},{1,5},{3,7},{5,1},{7,3},{8,12},{10,14},{12... | collective-permute-start | bytes 196616 | tf_op jit(solution)/shard_map/ppermute | solution.py:282
  119.7 4.8 %collective-permute-start.29 = (bf16[256,128]{1,0:T(8,128)(2,1)S(1)}, bf16[256,128]{1,0:T(8,128)(2,1)S(1)}, u32[]{:S(2)}, u32[]{:S(2)}) collective-permute-start(bf16[256,128]{1,0:T(8,128)(2,1)S(1)} %get-tuple-element.39), channel_id=1, source_target_pairs={{0,6},{2,0},{4,2},{6,4},{1,7},{3,1},{5,3},{7,5},{8,14},{10,8},{12,... | collective-permute-start | bytes 196616 | tf_op jit(solution)/shard_map/ppermute | solution.py:282
  124.6 5.5 %collective-permute-start.30 = (bf16[256,128]{1,0:T(8,128)(2,1)S(1)}, bf16[256,128]{1,0:T(8,128)(2,1)S(1)}, u32[]{:S(2)}, u32[]{:S(2)}) collective-permute-start(bf16[256,128]{1,0:T(8,128)(2,1)S(1)} %sum_x.1.refs_0_), channel_id=1, source_target_pairs={{0,6},{2,0},{4,2},{6,4},{1,7},{3,1},{5,3},{7,5},{8,14},{10,8},{12,... | collective-permute-start | bytes 196616 | tf_op jit(solution)/shard_map/ppermute | solution.py:289
  127.6 5.8 %collective-permute-start.31 = (bf16[256,128]{1,0:T(8,128)(2,1)S(1)}, bf16[256,128]{1,0:T(8,128)(2,1)S(1)}, u32[]{:S(2)}, u32[]{:S(2)}) collective-permute-start(bf16[256,128]{1,0:T(8,128)(2,1)S(1)} %sum_x.1.refs_0_), channel_id=1, source_target_pairs={{0,4},{2,6},{4,0},{6,2},{1,5},{3,7},{5,1},{7,3},{8,12},{10,14},{12... | collective-permute-start | bytes 196616 | tf_op jit(solution)/shard_map/ppermute | solution.py:289
  128.1 6.0 %collective-permute-start.32 = (bf16[256,128]{1,0:T(8,128)(2,1)S(1)}, bf16[256,128]{1,0:T(8,128)(2,1)S(1)}, u32[]{:S(2)}, u32[]{:S(2)}) collective-permute-start(bf16[256,128]{1,0:T(8,128)(2,1)S(1)} %sum_x.1.refs_0_), channel_id=1, source_target_pairs={{0,2},{2,4},{4,6},{6,0},{1,3},{3,5},{5,7},{7,1},{8,10},{10,12},{12... | collective-permute-start | bytes 196616 | tf_op jit(solution)/shard_map/ppermute | solution.py:289
  (8 other events, 81.0 us)

commit v6 on v5

--- a/solution.py
+++ b/solution.py
@@ -20,6 +20,7 @@
 ROWS = PEERS * OWN
 STEP = 256
 RING = 4
+PARTS = 3
 PIECE = WIDTH // 2 // RING
 LANES = WIDTH // RING
 
@@ -58,19 +59,24 @@
     return (lax.axis_index(slow) ^ apart) * RING + ((lax.axis_index(fast) + ahead) & (RING - 1))
 
 
-def build_kernel(coords, counts, values, dense):
+def build_kernel(part, coords, counts, values, *rest):
+    dense = rest[-1]
     rows, cols = dense.shape
     per_owner = OWN // SIDE
     me_core = lax.axis_index("core")
 
-    @pl.loop(0, rows // SIDE)
-    def _(r):
-        dense[pl.ds(pl.multiple_of(r * SIDE, SIDE), SIDE), :] = jnp.zeros((SIDE, cols), dense.dtype)
+    if part == 0:
+
+        @pl.loop(0, rows // SIDE)
+        def _(r):
+            dense[pl.ds(pl.multiple_of(r * SIDE, SIDE), SIDE), :] = jnp.zeros((SIDE, cols), dense.dtype)
 
     count = counts[0, 0]
     lane = lax.broadcasted_iota(jnp.int32, (SIDE, 2 * SIDE), 1)
 
-    @pl.loop(0, (count + 15) // 16)
+    groups = (count + 15) >> 4
+
+    @pl.loop((groups * part) // PARTS, (groups * (part + 1)) // PARTS)
     def _(g):
         group = values[0, 0, pl.ds(pl.multiple_of(g * 16, 16), 16), :]
         pairs = group.astype(jnp.float32).reshape(16, SIDE // 2, 2 * SIDE)
@@ -98,16 +104,18 @@
             place[...] = jnp.where(mask, block, place[...])
 
 
-def build(coords, counts, values):
+def build(part, coords, counts, values, *dense):
+    vmem = pl.BlockSpec(memory_space=pltpu.VMEM)
     return pl.pallas_call(
-        build_kernel,
+        functools.partial(build_kernel, part),
         out_shape=bf16(2 * ROWS, ROWS),
-        in_specs=[pl.BlockSpec(memory_space=pltpu.SMEM)] * 2 + [pl.BlockSpec(memory_space=pltpu.VMEM)],
-        out_specs=pl.BlockSpec(memory_space=pltpu.VMEM),
+        in_specs=[pl.BlockSpec(memory_space=pltpu.SMEM)] * 2 + [vmem] * (1 + len(dense)),
+        out_specs=vmem,
+        input_output_aliases={3: 0} if dense else {},
         compiler_params=pltpu.CompilerParams(vmem_limit_bytes=16 << 20),
-        cost_estimate=pl.CostEstimate(flops=0, bytes_accessed=30 << 20, transcendentals=0),
-        name="build",
-    )(coords, counts, values)
+        cost_estimate=pl.CostEstimate(flops=0, bytes_accessed=8 << 20, transcendentals=0),
+        name=f"build_{part}",
+    )(coords, counts, values, *dense)
 
 
 def over_rows(a, b):
@@ -262,18 +270,23 @@
         out[k * OWN : (k + 1) * OWN] = part[...]
 
 
-def gather(block, slow, fast):
+def gather(block, slow, fast, tasks, state):
     def ahead(array, step):
         return lax.ppermute(array, fast, [(i, (i - step) % RING) for i in range(RING)])
 
     across = trade(block, slow)
     before, after = ahead(block, -1), ahead(block, 1)
+    across, before, after, state = lax.optimization_barrier((across, before, after, tasks[0](state)))
     across_before = trade(before, slow)
     across_after = ahead(across, 1)
     beyond = ahead(before, -1)
+    across_before, across_after, beyond, state = lax.optimization_barrier(
+        (across_before, across_after, beyond, tasks[1](state))
+    )
     across_beyond = ahead(across_after, 1)
+    across_beyond, state = lax.optimization_barrier((across_beyond, tasks[2](state)))
     blocks = (block, after, beyond, before, across, across_after, across_beyond, across_before)
-    return vmem_call(stack_kernel, bf16(ROWS, WIDTH), "stack_" + fast)(*blocks)
+    return vmem_call(stack_kernel, bf16(ROWS, WIDTH), "stack_" + fast)(*blocks), state
 
 
 def scatter_ring(pieces, axis, name):
@@ -291,8 +304,10 @@
 
 
 def per_device(features, out_grad, weight, block_values, block_coords, block_counts):
-    dense = build(block_coords, block_counts, block_values)
-    panel = gather(features, *ROW)
+    raw = (block_coords, block_counts, block_values)
+    tasks = [lambda dense, part=part: build(part, *raw, *dense) for part in range(PARTS)]
+    tasks = [lambda dense, task=task: (task(dense),) for task in tasks]
+    panel, (dense,) = gather(features, *ROW, tasks, ())
     parts = exchange(down_both(dense, panel), CHIP)
 
     half = bf16(WIDTH // 2, WIDTH)
@@ -304,16 +319,21 @@
         flops=2 * 3 * OWN * WIDTH * WIDTH,
     )(parts, out_grad, weight)
 
-    mine = gather(send, *CHIP)
-
     piece = bf16(PIECE, WIDTH)
-    pieces = vmem_call(pair_kernel, (piece,) * RING, "pair")(wgrad_near, trade(wgrad_far, "core"))
-    summed = scatter_ring(pieces, "z", "sum_z")
     ys = ("y_lo", "y_hi")
-    summed = vmem_call(square_kernel, piece, "sum_y")(
-        summed, trade(summed, ys, 1), trade(summed, ys, 2), trade(summed, ys, 3)
-    )
-    summed, mine = lax.optimization_barrier((summed, mine))
+
+    def over_core(terms):
+        return vmem_call(pair_kernel, (piece,) * RING, "pair")(terms[0], trade(terms[1], "core"))
+
+    def over_z(pieces):
+        return scatter_ring(pieces, "z", "sum_z")
+
+    def over_y(summed):
+        return vmem_call(square_kernel, piece, "sum_y")(
+            summed, trade(summed, ys, 1), trade(summed, ys, 2), trade(summed, ys, 3)
+        )
+
+    mine, summed = gather(send, *CHIP, (over_core, over_z, over_y), (wgrad_near, wgrad_far))
     pieces = gather_ring(summed, "z")
     theirs = trade(mine, "core")
     partial_grad = up_both(dense, mine, theirs)

time: 138 us -> 138 us (level); the launches traced: 138 us -> 137 us
  blocking collectives: 34.5 us -> 29.9 us
  starting transfers between devices: 46.7 us -> 48.1 us
    ppermute x12, waiting for transfers between devices: 19.9 us -> 6.64 us  [trade(): lax.ppermute(array, axes, [(i, i ^ bits) for i in range(lax.axis_size(axe...]
    ppermute x10, waiting for transfers between devices: 1.77 us -> 14.3 us  [ahead(): lax.ppermute(array, fast, [(i, (i - step) % RING) for i in range(RING)])]
    all_to_all x1, blocking collectives: 34.5 us -> 29.9 us  [exchange(): return lax.all_to_all(parts, axes, 0, 0)]
    ppermute x6, starting transfers between devices: 7.83 us -> 9.6 us  [scatter_ring(): lax.ppermute(pieces[k], axis, [(i, (i + k) % RING) for i in range(RING)])]
    ppermute x6, waiting for transfers between devices: 5.53 us -> 4.03 us  [gather_ring(): lax.ppermute(piece, axis, [(i, (i - k) % RING) for i in range(RING)])]
    ppermute x6, starting transfers between devices: 7.39 us -> 8.77 us  [gather_ring(): lax.ppermute(piece, axis, [(i, (i - k) % RING) for i in range(RING)])]
    pallas_call x1 -> x3, Pallas kernels: 3.02 us -> 4.25 us  [build(): pl.pallas_call(functools.partial(build_kernel, part), out_shape=bf16(2 *...]
  transfers between devices with their start and end apart: 35 -> 35, of which waited for: 17 -> 21; matrix products, arithmetic and copies ran while one was open for 0% -> 0% of each run, Pallas kernels for 10% -> 11%
where the time goes in v6:
time: 138 us; the launch traced here: 137 us
  starting transfers between devices  48.1 us (35%)
  waiting for transfers between devices  34.6 us (25%)
  blocking collectives  29.9 us (22%)
  Pallas kernels  19.3 us (14%)
  local copies, waits for them, and re-layouts  2.36 us (2%)
  between operations  1.55 us (1%)
    all_to_all x1, blocking collectives, exchange(): return lax.all_to_all(parts, axes, 0, 0)  29.9 us
    ppermute x10, starting transfers between devices, ahead(): lax.ppermute(array, fast, [(i, (i - step) % RING) for i in range(RING)])  16.6 us
    pallas_call x16, Pallas kernels, call(): pl.pallas_call(kernel, out_shape=outs, in_specs=[vmem] * len(args), out_s...  15.1 us
    ppermute x10, waiting for transfers between devices, ahead(): lax.ppermute(array, fast, [(i, (i - step) % RING) for i in range(RING)])  14.3 us
    ppermute x6, starting transfers between devices, scatter_ring(): lax.ppermute(pieces[k], axis, [(i, (i + k) % RING) for i in range(RING)])  9.6 us
    ppermute x12, starting transfers between devices, trade(): lax.ppermute(array, axes, [(i, i ^ bits) for i in range(lax.axis_size(axe...  9.03 us
    ppermute x6, starting transfers between devices, gather_ring(): lax.ppermute(piece, axis, [(i, (i - k) % RING) for i in range(RING)])  8.77 us
    ppermute x6, waiting for transfers between devices, scatter_ring(): lax.ppermute(pieces[k], axis, [(i, (i + k) % RING) for i in range(RING)])  7.66 us
  transfers between devices with their start and end apart: 35, of which 21 were waited for; matrix products, arithmetic and copies ran while one was open for 0% of the time, Pallas kernels for 11%

profile of v6, /device:TPU:0, one launch (start us, length us, event | category | flops | bytes accessed | tf_op | source)
XLA Modules:
  0.0 136.8 jit_solution(15908988418808934717)
XLA Ops:
  0.6 2.1 %collective-permute-start.1 = (bf16[192,512]{1,0:T(8,128)(2,1)}, bf16[192,512]{1,0:T(8,128)(2,1)S(1)}, u32[]{:S(2)}, u32[]{:S(2)}) collective-permute-start(bf16[192,512]{1,0:T(8,128)(2,1)} %refs_0_.1), channel_id=1, source_target_pairs={{0,16},{16,32},{32,48},{48,0},{1,17},{17,33},{33,49},{49,1},{2,18}... | collective-permute-start | bytes 589832 | tf_op jit(solution)/shard_map/ppermute | solution.py:275
  2.7 1.6 %collective-permute-start = (bf16[192,512]{1,0:T(8,128)(2,1)}, bf16[192,512]{1,0:T(8,128)(2,1)S(1)}, u32[]{:S(2)}, u32[]{:S(2)}) collective-permute-start(bf16[192,512]{1,0:T(8,128)(2,1)} %refs_0_.1), channel_id=1, source_target_pairs={{0,64},{64,0},{1,65},{65,1},{2,66},{66,2},{3,67},{67,3},{4,68},{68... | collective-permute-start | bytes 589832 | tf_op jit(solution)/shard_map/ppermute | solution.py:264
  4.3 2.2 %collective-permute-start.2 = (bf16[192,512]{1,0:T(8,128)(2,1)}, bf16[192,512]{1,0:T(8,128)(2,1)S(1)}, u32[]{:S(2)}, u32[]{:S(2)}) collective-permute-start(bf16[192,512]{1,0:T(8,128)(2,1)} %refs_0_.1), channel_id=1, source_target_pairs={{0,48},{16,0},{32,16},{48,32},{1,49},{17,1},{33,17},{49,33},{2,50}... | collective-permute-start | bytes 589832 | tf_op jit(solution)/shard_map/ppermute | solution.py:275
  7.2 1.7 %copy-done = bf16[1,1,288,4096]{3,2,1,0:T(8,128)(2,1)S(1)} copy-done((bf16[1,1,288,4096]{3,2,1,0:T(8,128)(2,1)S(1)}, bf16[1,1,288,4096]{3,2,1,0:T(8,128)(2,1)}, u32[]{:S(2)}) %copy-start) | copy-done | bytes 2359320
  9.5 1.8 %build_0.1.rest_0_ = bf16[3072,1536]{1,0:T(8,128)(2,1)S(1)} custom-call(s32[1,1,2,288]{3,2,1,0:T(2,128)S(1)} %copy-done.4, s32[1,1]{1,0:T(1,128)S(6)} %copy.15.counts, bf16[1,1,288,4096]{3,2,1,0:T(8,128)(2,1)S(1)} %copy-done), custom_call_target="tpu_custom_call" | custom-call | bytes 8388608 | tf_op jit(solution)/shard_map/build_0/pallas_call | solution.py:109
  11.3 3.0 %collective-permute-start.4 = (bf16[192,512]{1,0:T(8,128)(2,1)S(1)}, bf16[192,512]{1,0:T(8,128)(2,1)S(1)}, u32[]{:S(2)}, u32[]{:S(2)}) collective-permute-start(bf16[192,512]{1,0:T(8,128)(2,1)S(1)} %collective-permute-done.refs_4_), channel_id=1, source_target_pairs={{0,48},{16,0},{32,16},{48,32},{1,49},{17,1},{33,17},{49,33},{2,50}... | collective-permute-start | bytes 589832 | tf_op jit(solution)/shard_map/ppermute | solution.py:275
  15.8 2.1 %collective-permute-done.4.refs_5_ = bf16[192,512]{1,0:T(8,128)(2,1)S(1)} collective-permute-done((bf16[192,512]{1,0:T(8,128)(2,1)S(1)}, bf16[192,512]{1,0:T(8,128)(2,1)S(1)}, u32[]{:S(2)}, u32[]{:S(2)}) %collective-permute-start.4) | collective-permute-done | bytes 196640 | tf_op jit(solution)/shard_map/ppermute | solution.py:275
  17.9 3.3 %collective-permute-done.5.refs_2_ = bf16[192,512]{1,0:T(8,128)(2,1)S(1)} collective-permute-done((bf16[192,512]{1,0:T(8,128)(2,1)S(1)}, bf16[192,512]{1,0:T(8,128)(2,1)S(1)}, u32[]{:S(2)}, u32[]{:S(2)}) %collective-permute-start.5) | collective-permute-done | bytes 196640 | tf_op jit(solution)/shard_map/ppermute | solution.py:275
  21.2 2.0 %collective-permute-start.6 = (bf16[192,512]{1,0:T(8,128)(2,1)S(1)}, bf16[192,512]{1,0:T(8,128)(2,1)S(1)}, u32[]{:S(2)}, u32[]{:S(2)}) collective-permute-start(bf16[192,512]{1,0:T(8,128)(2,1)S(1)} %collective-permute-done.4.refs_5_), channel_id=1, source_target_pairs={{0,48},{16,0},{32,16},{48,32},{1,49},{17,1},{33,17},{49,33},{2,50}... | collective-permute-start | bytes 589832 | tf_op jit(solution)/shard_map/ppermute | solution.py:275
  24.6 2.2 %collective-permute-done.6.refs_6_ = bf16[192,512]{1,0:T(8,128)(2,1)S(1)} collective-permute-done((bf16[192,512]{1,0:T(8,128)(2,1)S(1)}, bf16[192,512]{1,0:T(8,128)(2,1)S(1)}, u32[]{:S(2)}, u32[]{:S(2)}) %collective-permute-start.6) | collective-permute-done | bytes 196640 | tf_op jit(solution)/shard_map/ppermute | solution.py:275
  33.7 29.9 %all_to_all.10.parts = bf16[8,192,512]{2,1,0:T(8,128)(2,1)S(1)} all-to-all(bf16[8,192,512]{2,1,0:T(8,128)(2,1)S(1)} %down_near_1.1), channel_id=1, replica_groups=mesh['y_lo'=2,'z'=4,'y_hi'=2,'x'=4,'core'=2] {'y_hi','x'}, dimensions={0} | all-to-all | bytes 3145728 | tf_op jit(solution)/shard_map/all_to_all | solution.py:260
  63.6 1.6 %middle.1 = (bf16[192,512]{1,0:T(8,128)(2,1)}, bf16[192,512]{1,0:T(8,128)(2,1)S(1)}, bf16[256,512]{1,0:T(8,128)(2,1)S(1)}, bf16[256,512]{1,0:T(8,128)(2,1)S(1)}) custom-call(bf16[8,192,512]{2,1,0:T(8,128)(2,1)S(1)} %all_to_all.10.parts, bf16[192,512]{1,0:T(8,128)(2,1)S(1)} %copy-done.3, bf16[512,512]{1,0:T(8,128)(2,1)S(1)} %copy-done.1), custom_call_target="tpu_custom_call" | custom-call | flops 301989888 | bytes 1048576 | tf_op jit(solution)/shard_map/middle/pallas_call | solution.py:32
  67.8 4.7 %collective-permute-done.11.refs_1_ = bf16[192,512]{1,0:T(8,128)(2,1)S(1)} collective-permute-done((bf16[192,512]{1,0:T(8,128)(2,1)S(1)}, bf16[192,512]{1,0:T(8,128)(2,1)S(1)}, u32[]{:S(2)}, u32[]{:S(2)}) %collective-permute-start.11) | collective-permute-done | bytes 196640 | tf_op jit(solution)/shard_map/ppermute | solution.py:275
  72.5 2.0 %collective-permute-done.10.refs_3_ = bf16[192,512]{1,0:T(8,128)(2,1)S(1)} collective-permute-done((bf16[192,512]{1,0:T(8,128)(2,1)S(1)}, bf16[192,512]{1,0:T(8,128)(2,1)S(1)}, u32[]{:S(2)}, u32[]{:S(2)}) %collective-permute-start.10) | collective-permute-done | bytes 196640 | tf_op jit(solution)/shard_map/ppermute | solution.py:275
  75.5 2.3 %collective-permute-start.14 = (bf16[192,512]{1,0:T(8,128)(2,1)S(1)}, bf16[192,512]{1,0:T(8,128)(2,1)S(1)}, u32[]{:S(2)}, u32[]{:S(2)}) collective-permute-start(bf16[192,512]{1,0:T(8,128)(2,1)S(1)} %collective-permute-done.9.refs_4_), channel_id=1, source_target_pairs={{0,6},{2,0},{4,2},{6,4},{1,7},{3,1},{5,3},{7,5},{8,14},{10,8},{12,... | collective-permute-start | bytes 589832 | tf_op jit(solution)/shard_map/ppermute | solution.py:275
  78.7 4.7 %collective-permute-start.17 = (bf16[64,512]{1,0:T(8,128)(2,1)S(1)}, bf16[64,512]{1,0:T(8,128)(2,1)S(1)}, u32[]{:S(2)}, u32[]{:S(2)}) collective-permute-start(bf16[64,512]{1,0:T(8,128)(2,1)S(1)} %get-tuple-element.66), channel_id=1, source_target_pairs={{0,32},{16,48},{32,0},{48,16},{1,33},{17,49},{33,1},{49,17},{2,34}... | collective-permute-start | bytes 196616 | tf_op jit(solution)/shard_map/ppermute | solution.py:295
  84.6 1.6 %collective-permute-start.18 = (bf16[64,512]{1,0:T(8,128)(2,1)S(1)}, bf16[64,512]{1,0:T(8,128)(2,1)S(1)}, u32[]{:S(2)}, u32[]{:S(2)}) collective-permute-start(bf16[64,512]{1,0:T(8,128)(2,1)S(1)} %get-tuple-element.67), channel_id=1, source_target_pairs={{0,48},{16,0},{32,16},{48,32},{1,49},{17,1},{33,17},{49,33},{2,50}... | collective-permute-start | bytes 196616 | tf_op jit(solution)/shard_map/ppermute | solution.py:295
  86.4 2.5 %collective-permute-done.18.refs_3_ = bf16[64,512]{1,0:T(8,128)(2,1)S(1)} collective-permute-done((bf16[64,512]{1,0:T(8,128)(2,1)S(1)}, bf16[64,512]{1,0:T(8,128)(2,1)S(1)}, u32[]{:S(2)}, u32[]{:S(2)}) %collective-permute-start.18) | collective-permute-done | bytes 65568 | tf_op jit(solution)/shard_map/ppermute | solution.py:295
  89.0 3.0 %collective-permute-start.19 = (bf16[192,512]{1,0:T(8,128)(2,1)S(1)}, bf16[192,512]{1,0:T(8,128)(2,1)S(1)}, u32[]{:S(2)}, u32[]{:S(2)}) collective-permute-start(bf16[192,512]{1,0:T(8,128)(2,1)S(1)} %collective-permute-done.14.refs_5_), channel_id=1, source_target_pairs={{0,6},{2,0},{4,2},{6,4},{1,7},{3,1},{5,3},{7,5},{8,14},{10,8},{12,... | collective-permute-start | bytes 589832 | tf_op jit(solution)/shard_map/ppermute | solution.py:275
  92.0 1.9 %collective-permute-start.22 = (bf16[64,512]{1,0:T(8,128)(2,1)S(1)}, bf16[64,512]{1,0:T(8,128)(2,1)S(1)}, u32[]{:S(2)}, u32[]{:S(2)}) collective-permute-start(bf16[64,512]{1,0:T(8,128)(2,1)S(1)} %sum_z.1.a), channel_id=1, source_target_pairs={{0,72},{8,64},{64,8},{72,0},{1,73},{9,65},{65,9},{73,1},{2,74},{10... | collective-permute-start | bytes 196616 | tf_op jit(solution)/shard_map/ppermute | solution.py:264
  94.5 2.1 %collective-permute-start.20 = (bf16[64,512]{1,0:T(8,128)(2,1)S(1)}, bf16[64,512]{1,0:T(8,128)(2,1)S(1)}, u32[]{:S(2)}, u32[]{:S(2)}) collective-permute-start(bf16[64,512]{1,0:T(8,128)(2,1)S(1)} %sum_z.1.a), channel_id=1, source_target_pairs={{0,8},{8,0},{64,72},{72,64},{1,9},{9,1},{65,73},{73,65},{2,10},{10... | collective-permute-start | bytes 196616 | tf_op jit(solution)/shard_map/ppermute | solution.py:264
  98.1 2.2 %collective-permute-done.20.b = bf16[64,512]{1,0:T(8,128)(2,1)S(1)} collective-permute-done((bf16[64,512]{1,0:T(8,128)(2,1)S(1)}, bf16[64,512]{1,0:T(8,128)(2,1)S(1)}, u32[]{:S(2)}, u32[]{:S(2)}) %collective-permute-start.20) | collective-permute-done | bytes 65568 | tf_op jit(solution)/shard_map/ppermute | solution.py:264
  100.7 4.5 %collective-permute-start.25 = (bf16[64,512]{1,0:T(8,128)(2,1)S(1)}, bf16[64,512]{1,0:T(8,128)(2,1)S(1)}, u32[]{:S(2)}, u32[]{:S(2)}) collective-permute-start(bf16[64,512]{1,0:T(8,128)(2,1)S(1)} %sum_y.1.refs_0_), channel_id=1, source_target_pairs={{0,32},{16,48},{32,0},{48,16},{1,33},{17,49},{33,1},{49,17},{2,34}... | collective-permute-start | bytes 196616 | tf_op jit(solution)/shard_map/ppermute | solution.py:302
  105.2 2.6 %up_near.1.other = f32[1536,512]{1,0:T(8,128)S(1)} custom-call(bf16[3072,1536]{1,0:T(8,128)(2,1)S(1)} %build_2.1.dense, bf16[1536,512]{1,0:T(8,128)(2,1)S(1)} %stack_x.1.rows), custom_call_target="tpu_custom_call" | custom-call | flops 2415919104 | bytes 1048576 | tf_op jit(solution)/shard_map/up_near/pallas_call | solution.py:32
  107.8 3.8 %up_far.1 = bf16[8,192,512]{2,1,0:T(8,128)(2,1)} custom-call(bf16[3072,1536]{1,0:T(8,128)(2,1)S(1)} %build_2.1.dense, bf16[1536,512]{1,0:T(8,128)(2,1)S(1)} %collective-permute-done.23.rows, f32[1536,512]{1,0:T(8,128)S(1)} %up_near.1.other), custom_call_target="tpu_custom_call" | custom-call | flops 2415919104 | bytes 1048576 | tf_op jit(solution)/shard_map/up_far/pallas_call | solution.py:32
  111.6 4.1 %all-to-all-start.1 = ((bf16[8,192,512]{2,1,0:T(8,128)(2,1)}), bf16[8,192,512]{2,1,0:T(8,128)(2,1)S(1)}, u32[]{:S(2)}, u32[]{:S(2)}) async-start(bf16[8,192,512]{2,1,0:T(8,128)(2,1)} %up_far.1), calls=%async_computation.1 | async-start | bytes 3145728 | tf_op jit(solution)/shard_map/all_to_all | solution.py:260
  115.9 1.6 %collective-permute-start.28 = (bf16[256,128]{1,0:T(8,128)(2,1)S(1)}, bf16[256,128]{1,0:T(8,128)(2,1)S(1)}, u32[]{:S(2)}, u32[]{:S(2)}) collective-permute-start(bf16[256,128]{1,0:T(8,128)(2,1)S(1)} %get-tuple-element.80), channel_id=1, source_target_pairs={{0,4},{2,6},{4,0},{6,2},{1,5},{3,7},{5,1},{7,3},{8,12},{10,14},{12... | collective-permute-start | bytes 196616 | tf_op jit(solution)/shard_map/ppermute | solution.py:295
  117.4 1.7 %collective-permute-start.29 = (bf16[256,128]{1,0:T(8,128)(2,1)S(1)}, bf16[256,128]{1,0:T(8,128)(2,1)S(1)}, u32[]{:S(2)}, u32[]{:S(2)}) collective-permute-start(bf16[256,128]{1,0:T(8,128)(2,1)S(1)} %get-tuple-element.81), channel_id=1, source_target_pairs={{0,6},{2,0},{4,2},{6,4},{1,7},{3,1},{5,3},{7,5},{8,14},{10,8},{12,... | collective-permute-start | bytes 196616 | tf_op jit(solution)/shard_map/ppermute | solution.py:295
  119.1 2.9 %collective-permute-done.27.refs_1_ = bf16[256,128]{1,0:T(8,128)(2,1)S(1)} collective-permute-done((bf16[256,128]{1,0:T(8,128)(2,1)S(1)}, bf16[256,128]{1,0:T(8,128)(2,1)S(1)}, u32[]{:S(2)}, u32[]{:S(2)}) %collective-permute-start.27) | collective-permute-done | bytes 65568 | tf_op jit(solution)/shard_map/ppermute | solution.py:295
  124.3 2.5 %collective-permute-start.31 = (bf16[256,128]{1,0:T(8,128)(2,1)S(1)}, bf16[256,128]{1,0:T(8,128)(2,1)S(1)}, u32[]{:S(2)}, u32[]{:S(2)}) collective-permute-start(bf16[256,128]{1,0:T(8,128)(2,1)S(1)} %sum_x.1.refs_0_), channel_id=1, source_target_pairs={{0,4},{2,6},{4,0},{6,2},{1,5},{3,7},{5,1},{7,3},{8,12},{10,14},{12... | collective-permute-start | bytes 196616 | tf_op jit(solution)/shard_map/ppermute | solution.py:302
  128.5 1.6 %collective-permute-done.31.refs_2_ = bf16[256,128]{1,0:T(8,128)(2,1)S(1)} collective-permute-done((bf16[256,128]{1,0:T(8,128)(2,1)S(1)}, bf16[256,128]{1,0:T(8,128)(2,1)S(1)}, u32[]{:S(2)}, u32[]{:S(2)}) %collective-permute-start.31) | collective-permute-done | bytes 65568 | tf_op jit(solution)/shard_map/ppermute | solution.py:302
  133.9 2.0 %all-to-all-done.1 = bf16[8,192,512]{2,1,0:T(8,128)(2,1)S(1)} async-done(((bf16[8,192,512]{2,1,0:T(8,128)(2,1)}), bf16[8,192,512]{2,1,0:T(8,128)(2,1)S(1)}, u32[]{:S(2)}, u32[]{:S(2)}) %all-to-all-start.1) | async-done | bytes 1572896 | tf_op jit(solution)/shard_map/all_to_all | solution.py:260
  (69 shorter events, 27.5 us)
Async XLA Ops:
  0.6 10.6 %collective-permute-start.1 = (bf16[192,512]{1,0:T(8,128)(2,1)}, bf16[192,512]{1,0:T(8,128)(2,1)S(1)}, u32[]{:S(2)}, u32[]{:S(2)}) collective-permute-start(bf16[192,512]{1,0:T(8,128)(2,1)} %refs_0_.1), channel_id=1, source_target_pairs={{0,16},{16,32},{32,48},{48,0},{1,17},{17,33},{33,49},{49,1},{2,18}... | collective-permute-start | bytes 589832 | tf_op jit(solution)/shard_map/ppermute | solution.py:275
  2.7 8.6 %collective-permute-start = (bf16[192,512]{1,0:T(8,128)(2,1)}, bf16[192,512]{1,0:T(8,128)(2,1)S(1)}, u32[]{:S(2)}, u32[]{:S(2)}) collective-permute-start(bf16[192,512]{1,0:T(8,128)(2,1)} %refs_0_.1), channel_id=1, source_target_pairs={{0,64},{64,0},{1,65},{65,1},{2,66},{66,2},{3,67},{67,3},{4,68},{68... | collective-permute-start | bytes 589832 | tf_op jit(solution)/shard_map/ppermute | solution.py:264
  4.3 7.0 %collective-permute-start.2 = (bf16[192,512]{1,0:T(8,128)(2,1)}, bf16[192,512]{1,0:T(8,128)(2,1)S(1)}, u32[]{:S(2)}, u32[]{:S(2)}) collective-permute-start(bf16[192,512]{1,0:T(8,128)(2,1)} %refs_0_.1), channel_id=1, source_target_pairs={{0,48},{16,0},{32,16},{48,32},{1,49},{17,1},{33,17},{49,33},{2,50}... | collective-permute-start | bytes 589832 | tf_op jit(solution)/shard_map/ppermute | solution.py:275
  11.3 6.6 %collective-permute-start.4 = (bf16[192,512]{1,0:T(8,128)(2,1)S(1)}, bf16[192,512]{1,0:T(8,128)(2,1)S(1)}, u32[]{:S(2)}, u32[]{:S(2)}) collective-permute-start(bf16[192,512]{1,0:T(8,128)(2,1)S(1)} %collective-permute-done.refs_4_), channel_id=1, source_target_pairs={{0,48},{16,0},{32,16},{48,32},{1,49},{17,1},{33,17},{49,33},{2,50}... | collective-permute-start | bytes 589832 | tf_op jit(solution)/shard_map/ppermute | solution.py:275
  14.3 6.9 %collective-permute-start.5 = (bf16[192,512]{1,0:T(8,128)(2,1)S(1)}, bf16[192,512]{1,0:T(8,128)(2,1)S(1)}, u32[]{:S(2)}, u32[]{:S(2)}) collective-permute-start(bf16[192,512]{1,0:T(8,128)(2,1)S(1)} %collective-permute-done.1.refs_3_), channel_id=1, source_target_pairs={{0,16},{16,32},{32,48},{48,0},{1,17},{17,33},{33,49},{49,1},{2,18}... | collective-permute-start | bytes 589832 | tf_op jit(solution)/shard_map/ppermute | solution.py:275
  14.3 6.9 %collective-permute-start.3 = (bf16[192,512]{1,0:T(8,128)(2,1)S(1)}, bf16[192,512]{1,0:T(8,128)(2,1)S(1)}, u32[]{:S(2)}, u32[]{:S(2)}) collective-permute-start(bf16[192,512]{1,0:T(8,128)(2,1)S(1)} %collective-permute-done.1.refs_3_), channel_id=1, source_target_pairs={{0,64},{64,0},{1,65},{65,1},{2,66},{66,2},{3,67},{67,3},{4,68},{68... | collective-permute-start | bytes 589832 | tf_op jit(solution)/shard_map/ppermute | solution.py:264
  21.2 5.7 %collective-permute-start.6 = (bf16[192,512]{1,0:T(8,128)(2,1)S(1)}, bf16[192,512]{1,0:T(8,128)(2,1)S(1)}, u32[]{:S(2)}, u32[]{:S(2)}) collective-permute-start(bf16[192,512]{1,0:T(8,128)(2,1)S(1)} %collective-permute-done.4.refs_5_), channel_id=1, source_target_pairs={{0,48},{16,0},{32,16},{48,32},{1,49},{17,1},{33,17},{49,33},{2,50}... | collective-permute-start | bytes 589832 | tf_op jit(solution)/shard_map/ppermute | solution.py:275
  65.2 2.6 %collective-permute-start.12 = (bf16[256,512]{1,0:T(8,128)(2,1)S(1)}, bf16[256,512]{1,0:T(8,128)(2,1)S(1)}, u32[]{:S(2)}, u32[]{:S(2)}) collective-permute-start(bf16[256,512]{1,0:T(8,128)(2,1)S(1)} %get-tuple-element.56), channel_id=1, source_target_pairs={{0,1},{1,0},{2,3},{3,2},{4,5},{5,4},{6,7},{7,6},{8,9},{9,8},{10,11... | collective-permute-start | bytes 786440 | tf_op jit(solution)/shard_map/ppermute | solution.py:264
  65.2 7.3 %collective-permute-start.11 = (bf16[192,512]{1,0:T(8,128)(2,1)S(1)}, bf16[192,512]{1,0:T(8,128)(2,1)S(1)}, u32[]{:S(2)}, u32[]{:S(2)}) collective-permute-start(bf16[192,512]{1,0:T(8,128)(2,1)S(1)} %get-tuple-element.54.refs_0_), channel_id=1, source_target_pairs={{0,6},{2,0},{4,2},{6,4},{1,7},{3,1},{5,3},{7,5},{8,14},{10,8},{12,... | collective-permute-start | bytes 589832 | tf_op jit(solution)/shard_map/ppermute | solution.py:275
  66.3 8.2 %collective-permute-start.10 = (bf16[192,512]{1,0:T(8,128)(2,1)S(1)}, bf16[192,512]{1,0:T(8,128)(2,1)S(1)}, u32[]{:S(2)}, u32[]{:S(2)}) collective-permute-start(bf16[192,512]{1,0:T(8,128)(2,1)S(1)} %get-tuple-element.54.refs_0_), channel_id=1, source_target_pairs={{0,2},{2,4},{4,6},{6,0},{1,3},{3,5},{5,7},{7,1},{8,10},{10,12},{12... | collective-permute-start | bytes 589832 | tf_op jit(solution)/shard_map/ppermute | solution.py:275
  67.2 8.3 %collective-permute-start.9 = (bf16[192,512]{1,0:T(8,128)(2,1)S(1)}, bf16[192,512]{1,0:T(8,128)(2,1)S(1)}, u32[]{:S(2)}, u32[]{:S(2)}) collective-permute-start(bf16[192,512]{1,0:T(8,128)(2,1)S(1)} %get-tuple-element.54.refs_0_), channel_id=1, source_target_pairs={{0,8},{8,0},{1,9},{9,1},{2,10},{10,2},{3,11},{11,3},{4,12},{12,4},... | collective-permute-start | bytes 589832 | tf_op jit(solution)/shard_map/ppermute | solution.py:264
  75.5 13.4 %collective-permute-start.14 = (bf16[192,512]{1,0:T(8,128)(2,1)S(1)}, bf16[192,512]{1,0:T(8,128)(2,1)S(1)}, u32[]{:S(2)}, u32[]{:S(2)}) collective-permute-start(bf16[192,512]{1,0:T(8,128)(2,1)S(1)} %collective-permute-done.9.refs_4_), channel_id=1, source_target_pairs={{0,6},{2,0},{4,2},{6,4},{1,7},{3,1},{5,3},{7,5},{8,14},{10,8},{12,... | collective-permute-start | bytes 589832 | tf_op jit(solution)/shard_map/ppermute | solution.py:275
  77.8 11.1 %collective-permute-start.15 = (bf16[192,512]{1,0:T(8,128)(2,1)S(1)}, bf16[192,512]{1,0:T(8,128)(2,1)S(1)}, u32[]{:S(2)}, u32[]{:S(2)}) collective-permute-start(bf16[192,512]{1,0:T(8,128)(2,1)S(1)} %collective-permute-done.10.refs_3_), channel_id=1, source_target_pairs={{0,2},{2,4},{4,6},{6,0},{1,3},{3,5},{5,7},{7,1},{8,10},{10,12},{12... | collective-permute-start | bytes 589832 | tf_op jit(solution)/shard_map/ppermute | solution.py:275
  77.8 11.1 %collective-permute-start.13 = (bf16[192,512]{1,0:T(8,128)(2,1)S(1)}, bf16[192,512]{1,0:T(8,128)(2,1)S(1)}, u32[]{:S(2)}, u32[]{:S(2)}) collective-permute-start(bf16[192,512]{1,0:T(8,128)(2,1)S(1)} %collective-permute-done.10.refs_3_), channel_id=1, source_target_pairs={{0,8},{8,0},{1,9},{9,1},{2,10},{10,2},{3,11},{11,3},{4,12},{12,4},... | collective-permute-start | bytes 589832 | tf_op jit(solution)/shard_map/ppermute | solution.py:264
  78.7 5.9 %collective-permute-start.16 = (bf16[64,512]{1,0:T(8,128)(2,1)S(1)}, bf16[64,512]{1,0:T(8,128)(2,1)S(1)}, u32[]{:S(2)}, u32[]{:S(2)}) collective-permute-start(bf16[64,512]{1,0:T(8,128)(2,1)S(1)} %get-tuple-element.65), channel_id=1, source_target_pairs={{0,16},{16,32},{32,48},{48,0},{1,17},{17,33},{33,49},{49,1},{2,18}... | collective-permute-start | bytes 196616 | tf_op jit(solution)/shard_map/ppermute | solution.py:295
  78.7 7.6 %collective-permute-start.17 = (bf16[64,512]{1,0:T(8,128)(2,1)S(1)}, bf16[64,512]{1,0:T(8,128)(2,1)S(1)}, u32[]{:S(2)}, u32[]{:S(2)}) collective-permute-start(bf16[64,512]{1,0:T(8,128)(2,1)S(1)} %get-tuple-element.66), channel_id=1, source_target_pairs={{0,32},{16,48},{32,0},{48,16},{1,33},{17,49},{33,1},{49,17},{2,34}... | collective-permute-start | bytes 196616 | tf_op jit(solution)/shard_map/ppermute | solution.py:295
  84.6 4.3 %collective-permute-start.18 = (bf16[64,512]{1,0:T(8,128)(2,1)S(1)}, bf16[64,512]{1,0:T(8,128)(2,1)S(1)}, u32[]{:S(2)}, u32[]{:S(2)}) collective-permute-start(bf16[64,512]{1,0:T(8,128)(2,1)S(1)} %get-tuple-element.67), channel_id=1, source_target_pairs={{0,48},{16,0},{32,16},{48,32},{1,49},{17,1},{33,17},{49,33},{2,50}... | collective-permute-start | bytes 196616 | tf_op jit(solution)/shard_map/ppermute | solution.py:295
  89.0 11.4 %collective-permute-start.19 = (bf16[192,512]{1,0:T(8,128)(2,1)S(1)}, bf16[192,512]{1,0:T(8,128)(2,1)S(1)}, u32[]{:S(2)}, u32[]{:S(2)}) collective-permute-start(bf16[192,512]{1,0:T(8,128)(2,1)S(1)} %collective-permute-done.14.refs_5_), channel_id=1, source_target_pairs={{0,6},{2,0},{4,2},{6,4},{1,7},{3,1},{5,3},{7,5},{8,14},{10,8},{12,... | collective-permute-start | bytes 589832 | tf_op jit(solution)/shard_map/ppermute | solution.py:275
  92.0 5.5 %collective-permute-start.22 = (bf16[64,512]{1,0:T(8,128)(2,1)S(1)}, bf16[64,512]{1,0:T(8,128)(2,1)S(1)}, u32[]{:S(2)}, u32[]{:S(2)}) collective-permute-start(bf16[64,512]{1,0:T(8,128)(2,1)S(1)} %sum_z.1.a), channel_id=1, source_target_pairs={{0,72},{8,64},{64,8},{72,0},{1,73},{9,65},{65,9},{73,1},{2,74},{10... | collective-permute-start | bytes 196616 | tf_op jit(solution)/shard_map/ppermute | solution.py:264
  93.9 4.3 %collective-permute-start.21 = (bf16[64,512]{1,0:T(8,128)(2,1)S(1)}, bf16[64,512]{1,0:T(8,128)(2,1)S(1)}, u32[]{:S(2)}, u32[]{:S(2)}) collective-permute-start(bf16[64,512]{1,0:T(8,128)(2,1)S(1)} %sum_z.1.a), channel_id=1, source_target_pairs={{0,64},{8,72},{64,0},{72,8},{1,65},{9,73},{65,1},{73,9},{2,66},{10... | collective-permute-start | bytes 196616 | tf_op jit(solution)/shard_map/ppermute | solution.py:264
  94.5 5.8 %collective-permute-start.20 = (bf16[64,512]{1,0:T(8,128)(2,1)S(1)}, bf16[64,512]{1,0:T(8,128)(2,1)S(1)}, u32[]{:S(2)}, u32[]{:S(2)}) collective-permute-start(bf16[64,512]{1,0:T(8,128)(2,1)S(1)} %sum_z.1.a), channel_id=1, source_target_pairs={{0,8},{8,0},{64,72},{72,64},{1,9},{9,1},{65,73},{73,65},{2,10},{10... | collective-permute-start | bytes 196616 | tf_op jit(solution)/shard_map/ppermute | solution.py:264
  100.5 7.3 %collective-permute-start.23 = (bf16[1536,512]{1,0:T(8,128)(2,1)S(1)}, bf16[1536,512]{1,0:T(8,128)(2,1)S(1)}, u32[]{:S(2)}, u32[]{:S(2)}) collective-permute-start(bf16[1536,512]{1,0:T(8,128)(2,1)S(1)} %stack_x.1.rows), channel_id=1, source_target_pairs={{0,1},{1,0},{2,3},{3,2},{4,5},{5,4},{6,7},{7,6},{8,9},{9,8},{10,11... | collective-permute-start | bytes 4718600 | tf_op jit(solution)/shard_map/ppermute | solution.py:264
  100.6 11.1 %collective-permute-start.26 = (bf16[64,512]{1,0:T(8,128)(2,1)S(1)}, bf16[64,512]{1,0:T(8,128)(2,1)S(1)}, u32[]{:S(2)}, u32[]{:S(2)}) collective-permute-start(bf16[64,512]{1,0:T(8,128)(2,1)S(1)} %sum_y.1.refs_0_), channel_id=1, source_target_pairs={{0,16},{16,32},{32,48},{48,0},{1,17},{17,33},{33,49},{49,1},{2,18}... | collective-permute-start | bytes 196616 | tf_op jit(solution)/shard_map/ppermute | solution.py:302
  100.7 11.0 %collective-permute-start.25 = (bf16[64,512]{1,0:T(8,128)(2,1)S(1)}, bf16[64,512]{1,0:T(8,128)(2,1)S(1)}, u32[]{:S(2)}, u32[]{:S(2)}) collective-permute-start(bf16[64,512]{1,0:T(8,128)(2,1)S(1)} %sum_y.1.refs_0_), channel_id=1, source_target_pairs={{0,32},{16,48},{32,0},{48,16},{1,33},{17,49},{33,1},{49,17},{2,34}... | collective-permute-start | bytes 196616 | tf_op jit(solution)/shard_map/ppermute | solution.py:302
  105.2 6.4 %collective-permute-start.24 = (bf16[64,512]{1,0:T(8,128)(2,1)S(1)}, bf16[64,512]{1,0:T(8,128)(2,1)S(1)}, u32[]{:S(2)}, u32[]{:S(2)}) collective-permute-start(bf16[64,512]{1,0:T(8,128)(2,1)S(1)} %sum_y.1.refs_0_), channel_id=1, source_target_pairs={{0,48},{16,0},{32,16},{48,32},{1,49},{17,1},{33,17},{49,33},{2,50}... | collective-permute-start | bytes 196616 | tf_op jit(solution)/shard_map/ppermute | solution.py:302
  111.6 24.3 %all-to-all-start.1 = ((bf16[8,192,512]{2,1,0:T(8,128)(2,1)}), bf16[8,192,512]{2,1,0:T(8,128)(2,1)S(1)}, u32[]{:S(2)}, u32[]{:S(2)}) async-start(bf16[8,192,512]{2,1,0:T(8,128)(2,1)} %up_far.1), calls=%async_computation.1 | async-start | bytes 3145728 | tf_op jit(solution)/shard_map/all_to_all | solution.py:260
  115.8 6.2 %collective-permute-start.27 = (bf16[256,128]{1,0:T(8,128)(2,1)S(1)}, bf16[256,128]{1,0:T(8,128)(2,1)S(1)}, u32[]{:S(2)}, u32[]{:S(2)}) collective-permute-start(bf16[256,128]{1,0:T(8,128)(2,1)S(1)} %get-tuple-element.79), channel_id=1, source_target_pairs={{0,2},{2,4},{4,6},{6,0},{1,3},{3,5},{5,7},{7,1},{8,10},{10,12},{12... | collective-permute-start | bytes 196616 | tf_op jit(solution)/shard_map/ppermute | solution.py:295
  115.9 6.2 %collective-permute-start.28 = (bf16[256,128]{1,0:T(8,128)(2,1)S(1)}, bf16[256,128]{1,0:T(8,128)(2,1)S(1)}, u32[]{:S(2)}, u32[]{:S(2)}) collective-permute-start(bf16[256,128]{1,0:T(8,128)(2,1)S(1)} %get-tuple-element.80), channel_id=1, source_target_pairs={{0,4},{2,6},{4,0},{6,2},{1,5},{3,7},{5,1},{7,3},{8,12},{10,14},{12... | collective-permute-start | bytes 196616 | tf_op jit(solution)/shard_map/ppermute | solution.py:295
  117.4 5.5 %collective-permute-start.29 = (bf16[256,128]{1,0:T(8,128)(2,1)S(1)}, bf16[256,128]{1,0:T(8,128)(2,1)S(1)}, u32[]{:S(2)}, u32[]{:S(2)}) collective-permute-start(bf16[256,128]{1,0:T(8,128)(2,1)S(1)} %get-tuple-element.81), channel_id=1, source_target_pairs={{0,6},{2,0},{4,2},{6,4},{1,7},{3,1},{5,3},{7,5},{8,14},{10,8},{12,... | collective-permute-start | bytes 196616 | tf_op jit(solution)/shard_map/ppermute | solution.py:295
  122.9 5.5 %collective-permute-start.32 = (bf16[256,128]{1,0:T(8,128)(2,1)S(1)}, bf16[256,128]{1,0:T(8,128)(2,1)S(1)}, u32[]{:S(2)}, u32[]{:S(2)}) collective-permute-start(bf16[256,128]{1,0:T(8,128)(2,1)S(1)} %sum_x.1.refs_0_), channel_id=1, source_target_pairs={{0,2},{2,4},{4,6},{6,0},{1,3},{3,5},{5,7},{7,1},{8,10},{10,12},{12... | collective-permute-start | bytes 196616 | tf_op jit(solution)/shard_map/ppermute | solution.py:302
  124.3 5.8 %collective-permute-start.31 = (bf16[256,128]{1,0:T(8,128)(2,1)S(1)}, bf16[256,128]{1,0:T(8,128)(2,1)S(1)}, u32[]{:S(2)}, u32[]{:S(2)}) collective-permute-start(bf16[256,128]{1,0:T(8,128)(2,1)S(1)} %sum_x.1.refs_0_), channel_id=1, source_target_pairs={{0,4},{2,6},{4,0},{6,2},{1,5},{3,7},{5,1},{7,3},{8,12},{10,14},{12... | collective-permute-start | bytes 196616 | tf_op jit(solution)/shard_map/ppermute | solution.py:302
  126.8 4.3 %collective-permute-start.30 = (bf16[256,128]{1,0:T(8,128)(2,1)S(1)}, bf16[256,128]{1,0:T(8,128)(2,1)S(1)}, u32[]{:S(2)}, u32[]{:S(2)}) collective-permute-start(bf16[256,128]{1,0:T(8,128)(2,1)S(1)} %sum_x.1.refs_0_), channel_id=1, source_target_pairs={{0,6},{2,0},{4,2},{6,4},{1,7},{3,1},{5,3},{7,5},{8,14},{10,8},{12,... | collective-permute-start | bytes 196616 | tf_op jit(solution)/shard_map/ppermute | solution.py:302
  (8 other events, 79.8 us)

commit v7 on v6

--- a/solution.py
+++ b/solution.py
@@ -87,7 +87,7 @@
             block_col = jnp.where(live, coords[0, 0, 1, slot], 0)
             owner = block_row // per_owner
             half = (owner + me_core) & 1
-            at_row = (half * PEERS + relative(owner >> 1, *CHIP)) * per_owner + block_row % per_owner
+            at_row = (half * PEERS + (owner >> 1)) * per_owner + block_row % per_owner
             at_col = relative(block_col // per_owner, *ROW) * per_owner + block_col % per_owner
             odd = (at_col & 1) == 1
             plain = pairs[k]
@@ -128,26 +128,34 @@
         out[r : r + STEP] = jnp.dot(dense[rows], panel[...], preferred_element_type=jnp.float32).astype(out.dtype)
 
 
-def store(out, place, axes, value):
-    for k in range(2):
-        out[absolute(place + k, *axes)] = value[k * OWN : (k + 1) * OWN].astype(out.dtype)
-
-
 def down_add_kernel(first, count, dense, panel, other, *rest):
-    for r in range(0, count, 2 * OWN):
-        own = jnp.dot(dense[first + r : first + r + 2 * OWN], panel[...], preferred_element_type=jnp.float32)
-        store(rest[-1], (first + r) // OWN, CHIP, own + other[r : r + 2 * OWN].astype(jnp.float32))
-
-
-def up_kernel(dense, rows, out):
-    for r in range(0, ROWS, STEP):
-        out[r : r + STEP] = over_rows(dense[:ROWS, r : r + STEP], rows[...])
-
-
-def up_add_kernel(dense, rows, other, out):
+    out = rest[-1]
+    for r in range(0, count, STEP):
+        rows = slice(first + r, first + r + STEP)
+        own = jnp.dot(dense[rows], panel[...], preferred_element_type=jnp.float32)
+        out[rows] = (own + other[r : r + STEP].astype(jnp.float32)).astype(out.dtype)
+
+
+def up_kernel(dense, rows, out, far, near, sems):
+    strips = [pl.ds(r, STEP) for r in range(0, ROWS, STEP)]
+    copies = [
+        pltpu.make_async_copy(dense.at[pl.ds(0, ROWS), strip], near.at[:, strip], sems.at[n])
+        for n, strip in enumerate(strips)
+    ]
+    copies.append(pltpu.make_async_copy(dense.at[pl.ds(ROWS, ROWS)], far, sems.at[len(strips)]))
+    for copy in copies:
+        copy.start()
+    for copy, r in zip(copies, range(0, ROWS, STEP)):
+        copy.wait()
+        out[r : r + STEP] = over_rows(near[:, r : r + STEP], rows[...])
+    copies[-1].wait()
+
+
+def up_add_kernel(tile, rows, other, out):
     for r in range(0, ROWS, 2 * OWN):
-        total = over_rows(dense[ROWS:, r : r + 2 * OWN], rows[...]) + other[r : r + 2 * OWN]
-        store(out, r // OWN, ROW, total)
+        total = over_rows(tile[:, r : r + 2 * OWN], rows[...]) + other[r : r + 2 * OWN]
+        for k in range(2):
+            out[absolute(r // OWN + k, *ROW)] = total[k * OWN : (k + 1) * OWN].astype(out.dtype)
 
 
 def down_both(dense, panel):
@@ -161,15 +169,9 @@
     for n in range(2):
         kernel = functools.partial(down_add_kernel, n * count, count)
         out = vmem_call(
-            kernel, bf16(PEERS, OWN, WIDTH), f"down_near_{n}", flops=work, aliases={3: 0} if n else {}
+            kernel, bf16(ROWS, WIDTH), f"down_near_{n}", flops=work, aliases={3: 0} if n else {}
         )(dense, panel, others[n], *([out] if n else []))
     return out
-
-
-def up_both(dense, mine, theirs):
-    work = 2 * ROWS * ROWS * WIDTH
-    own = vmem_call(up_kernel, jax.ShapeDtypeStruct((ROWS, WIDTH), jnp.float32), "up_near", flops=work)(dense, mine)
-    return vmem_call(up_add_kernel, bf16(PEERS, OWN, WIDTH), "up_far", flops=work)(dense, theirs, own)
 
 
 def middle_kernel(parts, out_grad, weight, activations, send, wgrad_near, wgrad_far, local):
@@ -193,7 +195,8 @@
     grad_agg = lax.dot_general(
         grad_pre, w, (((1,), (1,)), ((), ())), preferred_element_type=jnp.float32
     ).astype(jnp.bfloat16)
-    send[...] = grad_agg
+    for k in range(PEERS):
+        send[k] = grad_agg
     local[...] = over_rows(aggregated, grad_pre).astype(jnp.bfloat16)
     core = lax.axis_index("core")
     for k in range(RING):
@@ -308,12 +311,12 @@
     tasks = [lambda dense, part=part: build(part, *raw, *dense) for part in range(PARTS)]
     tasks = [lambda dense, task=task: (task(dense),) for task in tasks]
     panel, (dense,) = gather(features, *ROW, tasks, ())
-    parts = exchange(down_both(dense, panel), CHIP)
+    parts = exchange(down_both(dense, panel).reshape(PEERS, OWN, WIDTH), CHIP)
 
     half = bf16(WIDTH // 2, WIDTH)
     activations, send, wgrad_near, wgrad_far = vmem_call(
         middle_kernel,
-        (bf16(OWN, WIDTH), bf16(OWN, WIDTH), half, half),
+        (bf16(OWN, WIDTH), bf16(PEERS, OWN, WIDTH), half, half),
         "middle",
         scratch=[pltpu.VMEM((WIDTH, WIDTH), jnp.bfloat16)],
         flops=2 * 3 * OWN * WIDTH * WIDTH,
@@ -333,10 +336,26 @@
             summed, trade(summed, ys, 1), trade(summed, ys, 2), trade(summed, ys, 3)
         )
 
-    mine, summed = gather(send, *CHIP, (over_core, over_z, over_y), (wgrad_near, wgrad_far))
+    mine = exchange(send, CHIP).reshape(ROWS, WIDTH)
+    summed = over_y(over_z(over_core((wgrad_near, wgrad_far))))
+    summed, mine = lax.optimization_barrier((summed, mine))
+
+    theirs = trade(mine, "core")
+    work = 2 * ROWS * ROWS * WIDTH
+    vmem = pl.BlockSpec(memory_space=pltpu.VMEM)
+    own, far = pl.pallas_call(
+        up_kernel,
+        out_shape=(jax.ShapeDtypeStruct((ROWS, WIDTH), jnp.float32), bf16(ROWS, ROWS)),
+        in_specs=[pl.BlockSpec(memory_space=pltpu.HBM), vmem],
+        out_specs=(vmem, vmem),
+        scratch_shapes=[pltpu.VMEM((ROWS, ROWS), jnp.bfloat16), pltpu.SemaphoreType.DMA((ROWS // STEP + 1,))],
+        compiler_params=pltpu.CompilerParams(vmem_limit_bytes=44 << 20),
+        cost_estimate=pl.CostEstimate(flops=work, bytes_accessed=12 << 20, transcendentals=0),
+        name="up_near",
+    )(dense, mine)
+    summed, own = lax.optimization_barrier((summed, own))
     pieces = gather_ring(summed, "z")
-    theirs = trade(mine, "core")
-    partial_grad = up_both(dense, mine, theirs)
+    partial_grad = vmem_call(up_add_kernel, bf16(PEERS, OWN, WIDTH), "up_far", flops=work)(far, theirs, own)
     partial_grad, *pieces = lax.optimization_barrier((partial_grad, *pieces))
     received = exchange(partial_grad, ROW)
 

time: 138 us -> 133 us (0.964)
  starting transfers between devices: 48.1 us -> 43.6 us
  waiting for transfers between devices: 34.6 us -> 32.5 us
  Pallas kernels: 19.3 us -> 21.4 us
    ppermute x10 -> x5, starting transfers between devices: 16.6 us -> 9.32 us  [ahead(): lax.ppermute(array, fast, [(i, (i - step) % RING) for i in range(RING)])]
    ppermute x10 -> x5, waiting for transfers between devices: 14.3 us -> 8.08 us  [ahead(): lax.ppermute(array, fast, [(i, (i - step) % RING) for i in range(RING)])]
    ppermute x12 -> x10, waiting for transfers between devices: 6.64 us -> 12.1 us  [trade(): lax.ppermute(array, axes, [(i, i ^ bits) for i in range(lax.axis_size(axe...]
    pallas_call x0 -> x1, Pallas kernels: none -> 4.81 us  [per_device(): pl.pallas_call(up_kernel, out_shape=(jax.ShapeDtypeStruct((ROWS, WIDTH),...]
    all_to_all x1 -> x2, starting transfers between devices: 4.09 us -> 7.16 us  [exchange(): return lax.all_to_all(parts, axes, 0, 0)]
    pallas_call x16 -> x14, Pallas kernels: 15.1 us -> 12.9 us  [call(): pl.pallas_call(kernel, out_shape=outs, in_specs=[vmem] * len(args), out_s...]
    ppermute x12 -> x10, starting transfers between devices: 9.03 us -> 7.9 us  [trade(): lax.ppermute(array, axes, [(i, i ^ bits) for i in range(lax.axis_size(axe...]
  transfers between devices with their start and end apart: 35 -> 29, of which waited for: 21 -> 21; matrix products, arithmetic and copies ran while one was open for 0% -> 0% of each run, Pallas kernels for 11% -> 12%
where the time goes in v7:
time: 133 us; the launch traced here: 132 us
  starting transfers between devices  43.6 us (33%)
  waiting for transfers between devices  32.5 us (24%)
  blocking collectives  29.9 us (22%)
  Pallas kernels  21.4 us (16%)
  local copies, waits for them, and re-layouts  2.37 us (2%)
  between operations  1.53 us (1%)
    all_to_all x1, blocking collectives, exchange(): return lax.all_to_all(parts, axes, 0, 0)  29.9 us
    pallas_call x14, Pallas kernels, call(): pl.pallas_call(kernel, out_shape=outs, in_specs=[vmem] * len(args), out_s...  12.9 us
    ppermute x10, waiting for transfers between devices, trade(): lax.ppermute(array, axes, [(i, i ^ bits) for i in range(lax.axis_size(axe...  12.1 us
    ppermute x6, starting transfers between devices, scatter_ring(): lax.ppermute(pieces[k], axis, [(i, (i + k) % RING) for i in range(RING)])  10 us
    ppermute x5, starting transfers between devices, ahead(): lax.ppermute(array, fast, [(i, (i - step) % RING) for i in range(RING)])  9.32 us
    ppermute x6, starting transfers between devices, gather_ring(): lax.ppermute(piece, axis, [(i, (i - k) % RING) for i in range(RING)])  9.17 us
    ppermute x5, waiting for transfers between devices, ahead(): lax.ppermute(array, fast, [(i, (i - step) % RING) for i in range(RING)])  8.08 us
    ppermute x10, starting transfers between devices, trade(): lax.ppermute(array, axes, [(i, i ^ bits) for i in range(lax.axis_size(axe...  7.9 us
  transfers between devices with their start and end apart: 29, of which 21 were waited for; matrix products, arithmetic and copies ran while one was open for 0% of the time, Pallas kernels for 12%

profile of v7, /device:TPU:0, one launch (start us, length us, event | category | flops | bytes accessed | tf_op | source)
XLA Modules:
  0.0 132.2 jit_solution(13496972454163484918)
XLA Ops:
  0.6 2.1 %collective-permute-start.1 = (bf16[192,512]{1,0:T(8,128)(2,1)}, bf16[192,512]{1,0:T(8,128)(2,1)S(1)}, u32[]{:S(2)}, u32[]{:S(2)}) collective-permute-start(bf16[192,512]{1,0:T(8,128)(2,1)} %refs_0_.1), channel_id=1, source_target_pairs={{0,16},{16,32},{32,48},{48,0},{1,17},{17,33},{33,49},{49,1},{2,18}... | collective-permute-start | bytes 589832 | tf_op jit(solution)/shard_map/ppermute | solution.py:278
  2.7 1.6 %collective-permute-start = (bf16[192,512]{1,0:T(8,128)(2,1)}, bf16[192,512]{1,0:T(8,128)(2,1)S(1)}, u32[]{:S(2)}, u32[]{:S(2)}) collective-permute-start(bf16[192,512]{1,0:T(8,128)(2,1)} %refs_0_.1), channel_id=1, source_target_pairs={{0,64},{64,0},{1,65},{65,1},{2,66},{66,2},{3,67},{67,3},{4,68},{68... | collective-permute-start | bytes 589832 | tf_op jit(solution)/shard_map/ppermute | solution.py:267
  4.3 2.2 %collective-permute-start.2 = (bf16[192,512]{1,0:T(8,128)(2,1)}, bf16[192,512]{1,0:T(8,128)(2,1)S(1)}, u32[]{:S(2)}, u32[]{:S(2)}) collective-permute-start(bf16[192,512]{1,0:T(8,128)(2,1)} %refs_0_.1), channel_id=1, source_target_pairs={{0,48},{16,0},{32,16},{48,32},{1,49},{17,1},{33,17},{49,33},{2,50}... | collective-permute-start | bytes 589832 | tf_op jit(solution)/shard_map/ppermute | solution.py:278
  7.2 1.7 %copy-done.1 = bf16[1,1,288,4096]{3,2,1,0:T(8,128)(2,1)S(1)} copy-done((bf16[1,1,288,4096]{3,2,1,0:T(8,128)(2,1)S(1)}, bf16[1,1,288,4096]{3,2,1,0:T(8,128)(2,1)}, u32[]{:S(2)}) %copy-start.1) | copy-done | bytes 2359320
  9.5 1.7 %build_0.1.rest_0_ = bf16[3072,1536]{1,0:T(8,128)(2,1)S(1)} custom-call(s32[1,1,2,288]{3,2,1,0:T(2,128)S(1)} %copy-done.5, s32[1,1]{1,0:T(1,128)S(6)} %copy.15.counts, bf16[1,1,288,4096]{3,2,1,0:T(8,128)(2,1)S(1)} %copy-done.1), custom_call_target="tpu_custom_call" | custom-call | bytes 8388608 | tf_op jit(solution)/shard_map/build_0/pallas_call | solution.py:109
  11.3 3.0 %collective-permute-start.4 = (bf16[192,512]{1,0:T(8,128)(2,1)S(1)}, bf16[192,512]{1,0:T(8,128)(2,1)S(1)}, u32[]{:S(2)}, u32[]{:S(2)}) collective-permute-start(bf16[192,512]{1,0:T(8,128)(2,1)S(1)} %collective-permute-done.refs_4_), channel_id=1, source_target_pairs={{0,48},{16,0},{32,16},{48,32},{1,49},{17,1},{33,17},{49,33},{2,50}... | collective-permute-start | bytes 589832 | tf_op jit(solution)/shard_map/ppermute | solution.py:278
  15.7 1.7 %collective-permute-done.4.refs_5_ = bf16[192,512]{1,0:T(8,128)(2,1)S(1)} collective-permute-done((bf16[192,512]{1,0:T(8,128)(2,1)S(1)}, bf16[192,512]{1,0:T(8,128)(2,1)S(1)}, u32[]{:S(2)}, u32[]{:S(2)}) %collective-permute-start.4) | collective-permute-done | bytes 196640 | tf_op jit(solution)/shard_map/ppermute | solution.py:278
  17.5 3.7 %collective-permute-done.5.refs_2_ = bf16[192,512]{1,0:T(8,128)(2,1)S(1)} collective-permute-done((bf16[192,512]{1,0:T(8,128)(2,1)S(1)}, bf16[192,512]{1,0:T(8,128)(2,1)S(1)}, u32[]{:S(2)}, u32[]{:S(2)}) %collective-permute-start.5) | collective-permute-done | bytes 196640 | tf_op jit(solution)/shard_map/ppermute | solution.py:278
  21.2 2.0 %collective-permute-start.6 = (bf16[192,512]{1,0:T(8,128)(2,1)S(1)}, bf16[192,512]{1,0:T(8,128)(2,1)S(1)}, u32[]{:S(2)}, u32[]{:S(2)}) collective-permute-start(bf16[192,512]{1,0:T(8,128)(2,1)S(1)} %collective-permute-done.4.refs_5_), channel_id=1, source_target_pairs={{0,48},{16,0},{32,16},{48,32},{1,49},{17,1},{33,17},{49,33},{2,50}... | collective-permute-start | bytes 589832 | tf_op jit(solution)/shard_map/ppermute | solution.py:278
  24.2 2.6 %collective-permute-done.6.refs_6_ = bf16[192,512]{1,0:T(8,128)(2,1)S(1)} collective-permute-done((bf16[192,512]{1,0:T(8,128)(2,1)S(1)}, bf16[192,512]{1,0:T(8,128)(2,1)S(1)}, u32[]{:S(2)}, u32[]{:S(2)}) %collective-permute-start.6) | collective-permute-done | bytes 196640 | tf_op jit(solution)/shard_map/ppermute | solution.py:278
  30.7 1.4 %down_near_0.1.rest_0_ = bf16[1536,512]{1,0:T(8,128)(2,1)S(1)} custom-call(bf16[3072,1536]{1,0:T(8,128)(2,1)S(1)} %build_2.1.dense, bf16[1536,512]{1,0:T(8,128)(2,1)S(1)} %stack_z.1.panel, bf16[768,512]{1,0:T(8,128)(2,1)S(1)} %collective-permute-done.8.other), custom_call_target="tpu_custom_call" | custom-call | flops 1207959552 | bytes 1048576 | tf_op jit(solution)/shard_map/down_near_0/pallas_call | solution.py:32
  32.3 1.4 %down_near_1.1 = bf16[1536,512]{1,0:T(8,128)(2,1)S(1)} custom-call(bf16[3072,1536]{1,0:T(8,128)(2,1)S(1)} %build_2.1.dense, bf16[1536,512]{1,0:T(8,128)(2,1)S(1)} %stack_z.1.panel, bf16[768,512]{1,0:T(8,128)(2,1)S(1)} %collective-permute-done.7.other, bf16[1536,512]{1,0:T(8,128)(2,1)S(1)} %down_near_0.1.rest_0_), custom_call_target="tpu_custom_call", output_to_operand_aliasing={{}: (3, {})} | custom-call | flops 1207959552 | bytes 1048576 | tf_op jit(solution)/shard_map/down_near_1/pallas_call | solution.py:32
  33.7 29.9 %all_to_all.15.parts = bf16[8,192,512]{2,1,0:T(8,128)(2,1)S(1)} all-to-all(bf16[8,192,512]{2,1,0:T(8,128)(2,1)S(1)} %bitcast.4), channel_id=1, replica_groups=mesh['y_lo'=2,'z'=4,'y_hi'=2,'x'=4,'core'=2] {'y_hi','x'}, dimensions={0} | all-to-all | bytes 3145728 | tf_op jit(solution)/shard_map/all_to_all | solution.py:263
  63.6 2.1 %middle.1 = (bf16[192,512]{1,0:T(8,128)(2,1)}, bf16[8,192,512]{2,1,0:T(8,128)(2,1)}, bf16[256,512]{1,0:T(8,128)(2,1)S(1)}, bf16[256,512]{1,0:T(8,128)(2,1)S(1)}) custom-call(bf16[8,192,512]{2,1,0:T(8,128)(2,1)S(1)} %all_to_all.15.parts, bf16[192,512]{1,0:T(8,128)(2,1)S(1)} %copy-done.4, bf16[512,512]{1,0:T(8,128)(2,1)S(1)} %copy-done.2), custom_call_target="tpu_custom_call" | custom-call | flops 301989888 | bytes 1048576 | tf_op jit(solution)/shard_map/middle/pallas_call | solution.py:32
  65.7 3.6 %all-to-all-start.1 = ((bf16[8,192,512]{2,1,0:T(8,128)(2,1)}), bf16[8,192,512]{2,1,0:T(8,128)(2,1)S(1)}, u32[]{:S(2)}, u32[]{:S(2)}) async-start(bf16[8,192,512]{2,1,0:T(8,128)(2,1)} %get-tuple-element.53), calls=%async_computation.1 | async-start | bytes 3145728 | tf_op jit(solution)/shard_map/all_to_all | solution.py:263
  69.4 1.5 %collective-permute-done.9.other = bf16[256,512]{1,0:T(8,128)(2,1)S(1)} collective-permute-done((bf16[256,512]{1,0:T(8,128)(2,1)S(1)}, bf16[256,512]{1,0:T(8,128)(2,1)S(1)}, u32[]{:S(2)}, u32[]{:S(2)}) %collective-permute-start.9) | collective-permute-done | bytes 262176 | tf_op jit(solution)/shard_map/ppermute | solution.py:267
  71.0 4.7 %collective-permute-start.11 = (bf16[64,512]{1,0:T(8,128)(2,1)S(1)}, bf16[64,512]{1,0:T(8,128)(2,1)S(1)}, u32[]{:S(2)}, u32[]{:S(2)}) collective-permute-start(bf16[64,512]{1,0:T(8,128)(2,1)S(1)} %get-tuple-element.51), channel_id=1, source_target_pairs={{0,32},{16,48},{32,0},{48,16},{1,33},{17,49},{33,1},{49,17},{2,34}... | collective-permute-start | bytes 196616 | tf_op jit(solution)/shard_map/ppermute | solution.py:298
  76.7 2.6 %collective-permute-done.11.refs_2_ = bf16[64,512]{1,0:T(8,128)(2,1)S(1)} collective-permute-done((bf16[64,512]{1,0:T(8,128)(2,1)S(1)}, bf16[64,512]{1,0:T(8,128)(2,1)S(1)}, u32[]{:S(2)}, u32[]{:S(2)}) %collective-permute-start.11) | collective-permute-done | bytes 65568 | tf_op jit(solution)/shard_map/ppermute | solution.py:298
  80.0 2.9 %collective-permute-start.15 = (bf16[64,512]{1,0:T(8,128)(2,1)S(1)}, bf16[64,512]{1,0:T(8,128)(2,1)S(1)}, u32[]{:S(2)}, u32[]{:S(2)}) collective-permute-start(bf16[64,512]{1,0:T(8,128)(2,1)S(1)} %sum_z.1.a), channel_id=1, source_target_pairs={{0,72},{8,64},{64,8},{72,0},{1,73},{9,65},{65,9},{73,1},{2,74},{10... | collective-permute-start | bytes 196616 | tf_op jit(solution)/shard_map/ppermute | solution.py:267
  84.8 4.5 %collective-permute-done.15.d = bf16[64,512]{1,0:T(8,128)(2,1)S(1)} collective-permute-done((bf16[64,512]{1,0:T(8,128)(2,1)S(1)}, bf16[64,512]{1,0:T(8,128)(2,1)S(1)}, u32[]{:S(2)}, u32[]{:S(2)}) %collective-permute-start.15) | collective-permute-done | bytes 65568 | tf_op jit(solution)/shard_map/ppermute | solution.py:267
  90.5 2.8 %collective-permute-done.13.b = bf16[64,512]{1,0:T(8,128)(2,1)S(1)} collective-permute-done((bf16[64,512]{1,0:T(8,128)(2,1)S(1)}, bf16[64,512]{1,0:T(8,128)(2,1)S(1)}, u32[]{:S(2)}, u32[]{:S(2)}) %collective-permute-start.13) | collective-permute-done | bytes 65568 | tf_op jit(solution)/shard_map/ppermute | solution.py:267
  93.6 4.8 %up_near.1 = (f32[1536,512]{1,0:T(8,128)S(1)}, bf16[1536,1536]{1,0:T(8,128)(2,1)S(1)}) custom-call(bf16[3072,1536]{1,0:T(8,128)(2,1)} %copy-done, bf16[1536,512]{1,0:T(8,128)(2,1)S(1)} %bitcast.6), custom_call_target="tpu_custom_call" | custom-call | flops 2415919104 | bytes 12582912 | tf_op jit(solution)/shard_map/up_near/pallas_call | solution.py:346
  98.5 4.7 %collective-permute-start.18 = (bf16[64,512]{1,0:T(8,128)(2,1)S(1)}, bf16[64,512]{1,0:T(8,128)(2,1)S(1)}, u32[]{:S(2)}, u32[]{:S(2)}) collective-permute-start(bf16[64,512]{1,0:T(8,128)(2,1)S(1)} %sum_y.1.refs_0_), channel_id=1, source_target_pairs={{0,32},{16,48},{32,0},{48,16},{1,33},{17,49},{33,1},{49,17},{2,34}... | collective-permute-start | bytes 196616 | tf_op jit(solution)/shard_map/ppermute | solution.py:305
  103.2 3.8 %up_far.1 = bf16[8,192,512]{2,1,0:T(8,128)(2,1)} custom-call(bf16[1536,1536]{1,0:T(8,128)(2,1)S(1)} %get-tuple-element.55.tile, bf16[1536,512]{1,0:T(8,128)(2,1)S(1)} %collective-permute-done.16.rows, f32[1536,512]{1,0:T(8,128)S(1)} %get-tuple-element.58.other), custom_call_target="tpu_custom_call" | custom-call | flops 2415919104 | bytes 1048576 | tf_op jit(solution)/shard_map/up_far/pallas_call | solution.py:32
  107.5 3.6 %all-to-all-start.2 = ((bf16[8,192,512]{2,1,0:T(8,128)(2,1)}), bf16[8,192,512]{2,1,0:T(8,128)(2,1)S(1)}, u32[]{:S(2)}, u32[]{:S(2)}) async-start(bf16[8,192,512]{2,1,0:T(8,128)(2,1)} %up_far.1), calls=%async_computation.2 | async-start | bytes 3145728 | tf_op jit(solution)/shard_map/all_to_all | solution.py:263
  111.1 2.0 %collective-permute-start.20 = (bf16[256,128]{1,0:T(8,128)(2,1)S(1)}, bf16[256,128]{1,0:T(8,128)(2,1)S(1)}, u32[]{:S(2)}, u32[]{:S(2)}) collective-permute-start(bf16[256,128]{1,0:T(8,128)(2,1)S(1)} %get-tuple-element.65), channel_id=1, source_target_pairs={{0,2},{2,4},{4,6},{6,0},{1,3},{3,5},{5,7},{7,1},{8,10},{10,12},{12... | collective-permute-start | bytes 196616 | tf_op jit(solution)/shard_map/ppermute | solution.py:298
  113.1 1.8 %collective-permute-start.21 = (bf16[256,128]{1,0:T(8,128)(2,1)S(1)}, bf16[256,128]{1,0:T(8,128)(2,1)S(1)}, u32[]{:S(2)}, u32[]{:S(2)}) collective-permute-start(bf16[256,128]{1,0:T(8,128)(2,1)S(1)} %get-tuple-element.66), channel_id=1, source_target_pairs={{0,4},{2,6},{4,0},{6,2},{1,5},{3,7},{5,1},{7,3},{8,12},{10,14},{12... | collective-permute-start | bytes 196616 | tf_op jit(solution)/shard_map/ppermute | solution.py:298
  114.9 1.5 %collective-permute-start.22 = (bf16[256,128]{1,0:T(8,128)(2,1)S(1)}, bf16[256,128]{1,0:T(8,128)(2,1)S(1)}, u32[]{:S(2)}, u32[]{:S(2)}) collective-permute-start(bf16[256,128]{1,0:T(8,128)(2,1)S(1)} %get-tuple-element.67), channel_id=1, source_target_pairs={{0,6},{2,0},{4,2},{6,4},{1,7},{3,1},{5,3},{7,5},{8,14},{10,8},{12,... | collective-permute-start | bytes 196616 | tf_op jit(solution)/shard_map/ppermute | solution.py:298
  116.9 1.9 %collective-permute-done.21.refs_2_ = bf16[256,128]{1,0:T(8,128)(2,1)S(1)} collective-permute-done((bf16[256,128]{1,0:T(8,128)(2,1)S(1)}, bf16[256,128]{1,0:T(8,128)(2,1)S(1)}, u32[]{:S(2)}, u32[]{:S(2)}) %collective-permute-start.21) | collective-permute-done | bytes 65568 | tf_op jit(solution)/shard_map/ppermute | solution.py:298
  120.3 3.1 %collective-permute-start.24 = (bf16[256,128]{1,0:T(8,128)(2,1)S(1)}, bf16[256,128]{1,0:T(8,128)(2,1)S(1)}, u32[]{:S(2)}, u32[]{:S(2)}) collective-permute-start(bf16[256,128]{1,0:T(8,128)(2,1)S(1)} %sum_x.1.refs_0_), channel_id=1, source_target_pairs={{0,4},{2,6},{4,0},{6,2},{1,5},{3,7},{5,1},{7,3},{8,12},{10,14},{12... | collective-permute-start | bytes 196616 | tf_op jit(solution)/shard_map/ppermute | solution.py:305
  124.8 1.6 %collective-permute-done.24.refs_2_ = bf16[256,128]{1,0:T(8,128)(2,1)S(1)} collective-permute-done((bf16[256,128]{1,0:T(8,128)(2,1)S(1)}, bf16[256,128]{1,0:T(8,128)(2,1)S(1)}, u32[]{:S(2)}, u32[]{:S(2)}) %collective-permute-start.24) | collective-permute-done | bytes 65568 | tf_op jit(solution)/shard_map/ppermute | solution.py:305
  127.9 1.5 %collective-permute-done.26.theirs = bf16[256,512]{1,0:T(8,128)(2,1)S(1)} collective-permute-done((bf16[256,512]{1,0:T(8,128)(2,1)S(1)}, bf16[256,512]{1,0:T(8,128)(2,1)S(1)}, u32[]{:S(2)}, u32[]{:S(2)}) %collective-permute-start.26) | collective-permute-done | bytes 262176 | tf_op jit(solution)/shard_map/ppermute | solution.py:267
  (58 shorter events, 20.7 us)
Async XLA Ops:
  0.6 10.6 %collective-permute-start.1 = (bf16[192,512]{1,0:T(8,128)(2,1)}, bf16[192,512]{1,0:T(8,128)(2,1)S(1)}, u32[]{:S(2)}, u32[]{:S(2)}) collective-permute-start(bf16[192,512]{1,0:T(8,128)(2,1)} %refs_0_.1), channel_id=1, source_target_pairs={{0,16},{16,32},{32,48},{48,0},{1,17},{17,33},{33,49},{49,1},{2,18}... | collective-permute-start | bytes 589832 | tf_op jit(solution)/shard_map/ppermute | solution.py:278
  2.7 8.5 %collective-permute-start = (bf16[192,512]{1,0:T(8,128)(2,1)}, bf16[192,512]{1,0:T(8,128)(2,1)S(1)}, u32[]{:S(2)}, u32[]{:S(2)}) collective-permute-start(bf16[192,512]{1,0:T(8,128)(2,1)} %refs_0_.1), channel_id=1, source_target_pairs={{0,64},{64,0},{1,65},{65,1},{2,66},{66,2},{3,67},{67,3},{4,68},{68... | collective-permute-start | bytes 589832 | tf_op jit(solution)/shard_map/ppermute | solution.py:267
  4.3 7.0 %collective-permute-start.2 = (bf16[192,512]{1,0:T(8,128)(2,1)}, bf16[192,512]{1,0:T(8,128)(2,1)S(1)}, u32[]{:S(2)}, u32[]{:S(2)}) collective-permute-start(bf16[192,512]{1,0:T(8,128)(2,1)} %refs_0_.1), channel_id=1, source_target_pairs={{0,48},{16,0},{32,16},{48,32},{1,49},{17,1},{33,17},{49,33},{2,50}... | collective-permute-start | bytes 589832 | tf_op jit(solution)/shard_map/ppermute | solution.py:278
  11.3 6.2 %collective-permute-start.4 = (bf16[192,512]{1,0:T(8,128)(2,1)S(1)}, bf16[192,512]{1,0:T(8,128)(2,1)S(1)}, u32[]{:S(2)}, u32[]{:S(2)}) collective-permute-start(bf16[192,512]{1,0:T(8,128)(2,1)S(1)} %collective-permute-done.refs_4_), channel_id=1, source_target_pairs={{0,48},{16,0},{32,16},{48,32},{1,49},{17,1},{33,17},{49,33},{2,50}... | collective-permute-start | bytes 589832 | tf_op jit(solution)/shard_map/ppermute | solution.py:278
  14.3 6.9 %collective-permute-start.5 = (bf16[192,512]{1,0:T(8,128)(2,1)S(1)}, bf16[192,512]{1,0:T(8,128)(2,1)S(1)}, u32[]{:S(2)}, u32[]{:S(2)}) collective-permute-start(bf16[192,512]{1,0:T(8,128)(2,1)S(1)} %collective-permute-done.1.refs_3_), channel_id=1, source_target_pairs={{0,16},{16,32},{32,48},{48,0},{1,17},{17,33},{33,49},{49,1},{2,18}... | collective-permute-start | bytes 589832 | tf_op jit(solution)/shard_map/ppermute | solution.py:278
  14.3 6.9 %collective-permute-start.3 = (bf16[192,512]{1,0:T(8,128)(2,1)S(1)}, bf16[192,512]{1,0:T(8,128)(2,1)S(1)}, u32[]{:S(2)}, u32[]{:S(2)}) collective-permute-start(bf16[192,512]{1,0:T(8,128)(2,1)S(1)} %collective-permute-done.1.refs_3_), channel_id=1, source_target_pairs={{0,64},{64,0},{1,65},{65,1},{2,66},{66,2},{3,67},{67,3},{4,68},{68... | collective-permute-start | bytes 589832 | tf_op jit(solution)/shard_map/ppermute | solution.py:267
  15.7 11.1 %copy-start.3 = (bf16[192,512]{1,0:T(8,128)(2,1)S(1)}, bf16[192,512]{1,0:T(8,128)(2,1)}, u32[]{:S(2)}) copy-start(bf16[192,512]{1,0:T(8,128)(2,1)} %refs_0_.1) | copy-start | bytes 589828
  21.2 5.7 %collective-permute-start.6 = (bf16[192,512]{1,0:T(8,128)(2,1)S(1)}, bf16[192,512]{1,0:T(8,128)(2,1)S(1)}, u32[]{:S(2)}, u32[]{:S(2)}) collective-permute-start(bf16[192,512]{1,0:T(8,128)(2,1)S(1)} %collective-permute-done.4.refs_5_), channel_id=1, source_target_pairs={{0,48},{16,0},{32,16},{48,32},{1,49},{17,1},{33,17},{49,33},{2,50}... | collective-permute-start | bytes 589832 | tf_op jit(solution)/shard_map/ppermute | solution.py:278
  28.3 2.4 %collective-permute-start.8 = (bf16[768,512]{1,0:T(8,128)(2,1)S(1)}, bf16[768,512]{1,0:T(8,128)(2,1)S(1)}, u32[]{:S(2)}, u32[]{:S(2)}) collective-permute-start(bf16[768,512]{1,0:T(8,128)(2,1)S(1)} %down_far_0.1), channel_id=1, source_target_pairs={{0,1},{1,0},{2,3},{3,2},{4,5},{5,4},{6,7},{7,6},{8,9},{9,8},{10,11... | collective-permute-start | bytes 2359304 | tf_op jit(solution)/shard_map/ppermute | solution.py:267
  29.8 2.5 %collective-permute-start.7 = (bf16[768,512]{1,0:T(8,128)(2,1)S(1)}, bf16[768,512]{1,0:T(8,128)(2,1)S(1)}, u32[]{:S(2)}, u32[]{:S(2)}) collective-permute-start(bf16[768,512]{1,0:T(8,128)(2,1)S(1)} %down_far_1.1), channel_id=1, source_target_pairs={{0,1},{1,0},{2,3},{3,2},{4,5},{5,4},{6,7},{7,6},{8,9},{9,8},{10,11... | collective-permute-start | bytes 2359304 | tf_op jit(solution)/shard_map/ppermute | solution.py:267
  33.7 30.0 %copy-start.2 = (bf16[512,512]{1,0:T(8,128)(2,1)S(1)}, bf16[512,512]{1,0:T(8,128)(2,1)}, u32[]{:S(2)}) copy-start(bf16[512,512]{1,0:T(8,128)(2,1)} %weight.1) | copy-start | bytes 1572868
  33.7 29.9 %copy-start.4 = (bf16[192,512]{1,0:T(8,128)(2,1)S(1)}, bf16[192,512]{1,0:T(8,128)(2,1)}, u32[]{:S(2)}) copy-start(bf16[192,512]{1,0:T(8,128)(2,1)} %out_grad.1) | copy-start | bytes 589828
  65.7 27.6 %all-to-all-start.1 = ((bf16[8,192,512]{2,1,0:T(8,128)(2,1)}), bf16[8,192,512]{2,1,0:T(8,128)(2,1)S(1)}, u32[]{:S(2)}, u32[]{:S(2)}) async-start(bf16[8,192,512]{2,1,0:T(8,128)(2,1)} %get-tuple-element.53), calls=%async_computation.1 | async-start | bytes 3145728 | tf_op jit(solution)/shard_map/all_to_all | solution.py:263
  69.3 1.6 %collective-permute-start.9 = (bf16[256,512]{1,0:T(8,128)(2,1)S(1)}, bf16[256,512]{1,0:T(8,128)(2,1)S(1)}, u32[]{:S(2)}, u32[]{:S(2)}) collective-permute-start(bf16[256,512]{1,0:T(8,128)(2,1)S(1)} %get-tuple-element.48), channel_id=1, source_target_pairs={{0,1},{1,0},{2,3},{3,2},{4,5},{5,4},{6,7},{7,6},{8,9},{9,8},{10,11... | collective-permute-start | bytes 786440 | tf_op jit(solution)/shard_map/ppermute | solution.py:267
  71.0 5.7 %collective-permute-start.10 = (bf16[64,512]{1,0:T(8,128)(2,1)S(1)}, bf16[64,512]{1,0:T(8,128)(2,1)S(1)}, u32[]{:S(2)}, u32[]{:S(2)}) collective-permute-start(bf16[64,512]{1,0:T(8,128)(2,1)S(1)} %get-tuple-element.50), channel_id=1, source_target_pairs={{0,16},{16,32},{32,48},{48,0},{1,17},{17,33},{33,49},{49,1},{2,18}... | collective-permute-start | bytes 196616 | tf_op jit(solution)/shard_map/ppermute | solution.py:298
  71.0 8.2 %collective-permute-start.11 = (bf16[64,512]{1,0:T(8,128)(2,1)S(1)}, bf16[64,512]{1,0:T(8,128)(2,1)S(1)}, u32[]{:S(2)}, u32[]{:S(2)}) collective-permute-start(bf16[64,512]{1,0:T(8,128)(2,1)S(1)} %get-tuple-element.51), channel_id=1, source_target_pairs={{0,32},{16,48},{32,0},{48,16},{1,33},{17,49},{33,1},{49,17},{2,34}... | collective-permute-start | bytes 196616 | tf_op jit(solution)/shard_map/ppermute | solution.py:298
  75.7 4.3 %collective-permute-start.12 = (bf16[64,512]{1,0:T(8,128)(2,1)S(1)}, bf16[64,512]{1,0:T(8,128)(2,1)S(1)}, u32[]{:S(2)}, u32[]{:S(2)}) collective-permute-start(bf16[64,512]{1,0:T(8,128)(2,1)S(1)} %get-tuple-element.52), channel_id=1, source_target_pairs={{0,48},{16,0},{32,16},{48,32},{1,49},{17,1},{33,17},{49,33},{2,50}... | collective-permute-start | bytes 196616 | tf_op jit(solution)/shard_map/ppermute | solution.py:298
  80.0 9.3 %collective-permute-start.15 = (bf16[64,512]{1,0:T(8,128)(2,1)S(1)}, bf16[64,512]{1,0:T(8,128)(2,1)S(1)}, u32[]{:S(2)}, u32[]{:S(2)}) collective-permute-start(bf16[64,512]{1,0:T(8,128)(2,1)S(1)} %sum_z.1.a), channel_id=1, source_target_pairs={{0,72},{8,64},{64,8},{72,0},{1,73},{9,65},{65,9},{73,1},{2,74},{10... | collective-permute-start | bytes 196616 | tf_op jit(solution)/shard_map/ppermute | solution.py:267
  82.9 7.6 %collective-permute-start.14 = (bf16[64,512]{1,0:T(8,128)(2,1)S(1)}, bf16[64,512]{1,0:T(8,128)(2,1)S(1)}, u32[]{:S(2)}, u32[]{:S(2)}) collective-permute-start(bf16[64,512]{1,0:T(8,128)(2,1)S(1)} %sum_z.1.a), channel_id=1, source_target_pairs={{0,64},{8,72},{64,0},{72,8},{1,65},{9,73},{65,1},{73,9},{2,66},{10... | collective-permute-start | bytes 196616 | tf_op jit(solution)/shard_map/ppermute | solution.py:267
  83.4 9.9 %collective-permute-start.13 = (bf16[64,512]{1,0:T(8,128)(2,1)S(1)}, bf16[64,512]{1,0:T(8,128)(2,1)S(1)}, u32[]{:S(2)}, u32[]{:S(2)}) collective-permute-start(bf16[64,512]{1,0:T(8,128)(2,1)S(1)} %sum_z.1.a), channel_id=1, source_target_pairs={{0,8},{8,0},{64,72},{72,64},{1,9},{9,1},{65,73},{73,65},{2,10},{10... | collective-permute-start | bytes 196616 | tf_op jit(solution)/shard_map/ppermute | solution.py:267
  93.3 9.9 %collective-permute-start.16 = (bf16[1536,512]{1,0:T(8,128)(2,1)S(1)}, bf16[1536,512]{1,0:T(8,128)(2,1)S(1)}, u32[]{:S(2)}, u32[]{:S(2)}) collective-permute-start(bf16[1536,512]{1,0:T(8,128)(2,1)S(1)} %bitcast.5), channel_id=1, source_target_pairs={{0,1},{1,0},{2,3},{3,2},{4,5},{5,4},{6,7},{7,6},{8,9},{9,8},{10,11... | collective-permute-start | bytes 4718600 | tf_op jit(solution)/shard_map/ppermute | solution.py:267
  98.4 8.6 %collective-permute-start.19 = (bf16[64,512]{1,0:T(8,128)(2,1)S(1)}, bf16[64,512]{1,0:T(8,128)(2,1)S(1)}, u32[]{:S(2)}, u32[]{:S(2)}) collective-permute-start(bf16[64,512]{1,0:T(8,128)(2,1)S(1)} %sum_y.1.refs_0_), channel_id=1, source_target_pairs={{0,16},{16,32},{32,48},{48,0},{1,17},{17,33},{33,49},{49,1},{2,18}... | collective-permute-start | bytes 196616 | tf_op jit(solution)/shard_map/ppermute | solution.py:305
  98.5 8.6 %collective-permute-start.18 = (bf16[64,512]{1,0:T(8,128)(2,1)S(1)}, bf16[64,512]{1,0:T(8,128)(2,1)S(1)}, u32[]{:S(2)}, u32[]{:S(2)}) collective-permute-start(bf16[64,512]{1,0:T(8,128)(2,1)S(1)} %sum_y.1.refs_0_), channel_id=1, source_target_pairs={{0,32},{16,48},{32,0},{48,16},{1,33},{17,49},{33,1},{49,17},{2,34}... | collective-permute-start | bytes 196616 | tf_op jit(solution)/shard_map/ppermute | solution.py:305
  103.2 4.3 %collective-permute-start.17 = (bf16[64,512]{1,0:T(8,128)(2,1)S(1)}, bf16[64,512]{1,0:T(8,128)(2,1)S(1)}, u32[]{:S(2)}, u32[]{:S(2)}) collective-permute-start(bf16[64,512]{1,0:T(8,128)(2,1)S(1)} %sum_y.1.refs_0_), channel_id=1, source_target_pairs={{0,48},{16,0},{32,16},{48,32},{1,49},{17,1},{33,17},{49,33},{2,50}... | collective-permute-start | bytes 196616 | tf_op jit(solution)/shard_map/ppermute | solution.py:305
  107.5 23.9 %all-to-all-start.2 = ((bf16[8,192,512]{2,1,0:T(8,128)(2,1)}), bf16[8,192,512]{2,1,0:T(8,128)(2,1)S(1)}, u32[]{:S(2)}, u32[]{:S(2)}) async-start(bf16[8,192,512]{2,1,0:T(8,128)(2,1)} %up_far.1), calls=%async_computation.2 | async-start | bytes 3145728 | tf_op jit(solution)/shard_map/all_to_all | solution.py:263
  111.1 5.8 %collective-permute-start.20 = (bf16[256,128]{1,0:T(8,128)(2,1)S(1)}, bf16[256,128]{1,0:T(8,128)(2,1)S(1)}, u32[]{:S(2)}, u32[]{:S(2)}) collective-permute-start(bf16[256,128]{1,0:T(8,128)(2,1)S(1)} %get-tuple-element.65), channel_id=1, source_target_pairs={{0,2},{2,4},{4,6},{6,0},{1,3},{3,5},{5,7},{7,1},{8,10},{10,12},{12... | collective-permute-start | bytes 196616 | tf_op jit(solution)/shard_map/ppermute | solution.py:298
  113.1 5.8 %collective-permute-start.21 = (bf16[256,128]{1,0:T(8,128)(2,1)S(1)}, bf16[256,128]{1,0:T(8,128)(2,1)S(1)}, u32[]{:S(2)}, u32[]{:S(2)}) collective-permute-start(bf16[256,128]{1,0:T(8,128)(2,1)S(1)} %get-tuple-element.66), channel_id=1, source_target_pairs={{0,4},{2,6},{4,0},{6,2},{1,5},{3,7},{5,1},{7,3},{8,12},{10,14},{12... | collective-permute-start | bytes 196616 | tf_op jit(solution)/shard_map/ppermute | solution.py:298
  114.9 4.3 %collective-permute-start.22 = (bf16[256,128]{1,0:T(8,128)(2,1)S(1)}, bf16[256,128]{1,0:T(8,128)(2,1)S(1)}, u32[]{:S(2)}, u32[]{:S(2)}) collective-permute-start(bf16[256,128]{1,0:T(8,128)(2,1)S(1)} %get-tuple-element.67), channel_id=1, source_target_pairs={{0,6},{2,0},{4,2},{6,4},{1,7},{3,1},{5,3},{7,5},{8,14},{10,8},{12,... | collective-permute-start | bytes 196616 | tf_op jit(solution)/shard_map/ppermute | solution.py:298
  119.2 5.5 %collective-permute-start.25 = (bf16[256,128]{1,0:T(8,128)(2,1)S(1)}, bf16[256,128]{1,0:T(8,128)(2,1)S(1)}, u32[]{:S(2)}, u32[]{:S(2)}) collective-permute-start(bf16[256,128]{1,0:T(8,128)(2,1)S(1)} %sum_x.1.refs_0_), channel_id=1, source_target_pairs={{0,2},{2,4},{4,6},{6,0},{1,3},{3,5},{5,7},{7,1},{8,10},{10,12},{12... | collective-permute-start | bytes 196616 | tf_op jit(solution)/shard_map/ppermute | solution.py:305
  120.3 6.1 %collective-permute-start.24 = (bf16[256,128]{1,0:T(8,128)(2,1)S(1)}, bf16[256,128]{1,0:T(8,128)(2,1)S(1)}, u32[]{:S(2)}, u32[]{:S(2)}) collective-permute-start(bf16[256,128]{1,0:T(8,128)(2,1)S(1)} %sum_x.1.refs_0_), channel_id=1, source_target_pairs={{0,4},{2,6},{4,0},{6,2},{1,5},{3,7},{5,1},{7,3},{8,12},{10,14},{12... | collective-permute-start | bytes 196616 | tf_op jit(solution)/shard_map/ppermute | solution.py:305
  123.4 4.3 %collective-permute-start.23 = (bf16[256,128]{1,0:T(8,128)(2,1)S(1)}, bf16[256,128]{1,0:T(8,128)(2,1)S(1)}, u32[]{:S(2)}, u32[]{:S(2)}) collective-permute-start(bf16[256,128]{1,0:T(8,128)(2,1)S(1)} %sum_x.1.refs_0_), channel_id=1, source_target_pairs={{0,6},{2,0},{4,2},{6,4},{1,7},{3,1},{5,3},{7,5},{8,14},{10,8},{12,... | collective-permute-start | bytes 196616 | tf_op jit(solution)/shard_map/ppermute | solution.py:305
  127.8 1.6 %collective-permute-start.26 = (bf16[256,512]{1,0:T(8,128)(2,1)S(1)}, bf16[256,512]{1,0:T(8,128)(2,1)S(1)}, u32[]{:S(2)}, u32[]{:S(2)}) collective-permute-start(bf16[256,512]{1,0:T(8,128)(2,1)S(1)} %join.1.mine), channel_id=1, source_target_pairs={{0,1},{1,0},{2,3},{3,2},{4,5},{5,4},{6,7},{7,6},{8,9},{9,8},{10,11... | collective-permute-start | bytes 786440 | tf_op jit(solution)/shard_map/ppermute | solution.py:267
  (3 other events, 10.5 us)

commit v8 on v7

--- a/solution.py
+++ b/solution.py
@@ -20,7 +20,8 @@
 ROWS = PEERS * OWN
 STEP = 256
 RING = 4
-PARTS = 3
+PARTS = 2
+LAST = 2 * SIDE * 2
 PIECE = WIDTH // 2 // RING
 LANES = WIDTH // RING
 
@@ -51,11 +52,12 @@
 def relative(owner, slow, fast):
     apart = (owner >> 2) ^ lax.axis_index(slow)
     ahead = ((owner & (RING - 1)) - lax.axis_index(fast)) & (RING - 1)
-    return apart * RING + ahead
+    return apart * RING + (ahead ^ (ahead >> 1))
 
 
 def absolute(place, slow, fast):
     apart, ahead = divmod(place, RING)
+    ahead ^= ahead >> 1
     return (lax.axis_index(slow) ^ apart) * RING + ((lax.axis_index(fast) + ahead) & (RING - 1))
 
 
@@ -122,18 +124,32 @@
     return lax.dot_general(a, b, (((0,), (0,)), ((), ())), preferred_element_type=jnp.float32)
 
 
-def down_kernel(first, count, dense, panel, out):
+def down_kernel(*refs):
+    dense, *blocks, out, panel = refs
+    for k, block in enumerate(blocks):
+        panel[k * OWN : (k + 1) * OWN] = block[...]
+    panel[ROWS - OWN :] = jnp.zeros((OWN, WIDTH), panel.dtype)
+    for r in range(0, 2 * ROWS, STEP):
+        out[r : r + STEP] = jnp.dot(dense[r : r + STEP], panel[...], preferred_element_type=jnp.float32)
+
+
+def with_last(dense, block, rows):
+    padded = jnp.concatenate([jnp.zeros((LAST - OWN, WIDTH), block.dtype), block[...]], axis=0)
+    return jnp.dot(dense[rows, ROWS - LAST :], padded, preferred_element_type=jnp.float32)
+
+
+def down_far_kernel(first, count, dense, block, most, out):
     for r in range(0, count, STEP):
         rows = slice(ROWS + first + r, ROWS + first + r + STEP)
-        out[r : r + STEP] = jnp.dot(dense[rows], panel[...], preferred_element_type=jnp.float32).astype(out.dtype)
-
-
-def down_add_kernel(first, count, dense, panel, other, *rest):
+        out[r : r + STEP] = (most[rows] + with_last(dense, block, rows)).astype(out.dtype)
+
+
+def down_near_kernel(first, count, dense, block, most, other, *rest):
     out = rest[-1]
     for r in range(0, count, STEP):
         rows = slice(first + r, first + r + STEP)
-        own = jnp.dot(dense[rows], panel[...], preferred_element_type=jnp.float32)
-        out[rows] = (own + other[r : r + STEP].astype(jnp.float32)).astype(out.dtype)
+        total = most[rows] + with_last(dense, block, rows) + other[r : r + STEP].astype(jnp.float32)
+        out[rows] = total.astype(out.dtype)
 
 
 def up_kernel(dense, rows, out, far, near, sems):
@@ -158,23 +174,34 @@
             out[absolute(r // OWN + k, *ROW)] = total[k * OWN : (k + 1) * OWN].astype(out.dtype)
 
 
-def down_both(dense, panel):
+def down_most(dense, blocks):
+    return vmem_call(
+        down_kernel,
+        jax.ShapeDtypeStruct((2 * ROWS, WIDTH), jnp.float32),
+        "down_most",
+        scratch=[pltpu.VMEM((ROWS, WIDTH), jnp.bfloat16)],
+        flops=4 * ROWS * ROWS * WIDTH,
+    )(dense, *blocks)
+
+
+def down_both(dense, most, block):
     count = ROWS // 2
-    work = 2 * count * ROWS * WIDTH
+    work = 2 * count * LAST * WIDTH
     others = []
     for n in range(2):
-        kernel = functools.partial(down_kernel, n * count, count)
-        others.append(trade(vmem_call(kernel, bf16(count, WIDTH), f"down_far_{n}", flops=work)(dense, panel), "core"))
+        kernel = functools.partial(down_far_kernel, n * count, count)
+        far = vmem_call(kernel, bf16(count, WIDTH), f"down_far_{n}", flops=work)(dense, block, most)
+        others.append(trade(far, "core"))
     out = []
     for n in range(2):
-        kernel = functools.partial(down_add_kernel, n * count, count)
+        kernel = functools.partial(down_near_kernel, n * count, count)
         out = vmem_call(
-            kernel, bf16(ROWS, WIDTH), f"down_near_{n}", flops=work, aliases={3: 0} if n else {}
-        )(dense, panel, others[n], *([out] if n else []))
+            kernel, bf16(ROWS, WIDTH), f"down_near_{n}", flops=work, aliases={4: 0} if n else {}
+        )(dense, block, most, others[n], *([out] if n else []))
     return out
 
 
-def middle_kernel(parts, out_grad, weight, activations, send, wgrad_near, wgrad_far, local):
+def middle_kernel(parts, out_grad, weight, activations, send, aggregated_out, grad_pre_out):
     total = parts[0].astype(jnp.float32)
     for k in range(1, PEERS):
         total = total + parts[k].astype(jnp.float32)
@@ -197,7 +224,12 @@
     ).astype(jnp.bfloat16)
     for k in range(PEERS):
         send[k] = grad_agg
-    local[...] = over_rows(aggregated, grad_pre).astype(jnp.bfloat16)
+    aggregated_out[...] = aggregated
+    grad_pre_out[...] = grad_pre
+
+
+def wgrad_kernel(aggregated, grad_pre, wgrad_near, wgrad_far, local):
+    local[...] = over_rows(aggregated[...], grad_pre[...]).astype(jnp.bfloat16)
     core = lax.axis_index("core")
     for k in range(RING):
         for g in range(RING):
@@ -207,7 +239,7 @@
 
 
 def wgrad_place(half_of, k, g):
-    row = half_of * (WIDTH // 2) + ((lax.axis_index("z") + k) & (RING - 1)) * PIECE
+    row = half_of * (WIDTH // 2) + (lax.axis_index("z") ^ k) * PIECE
     col = ((lax.axis_index("x") + g) & (RING - 1)) * LANES
     return pl.ds(pl.multiple_of(row, PIECE), PIECE), pl.ds(pl.multiple_of(col, LANES), LANES)
 
@@ -235,11 +267,11 @@
     out[...] = (first + (c[...].astype(jnp.float32) + d[...].astype(jnp.float32))).astype(out.dtype)
 
 
-def turn_kernel(*refs):
-    pieces, outs = refs[:RING], refs[RING:]
+def turn_kernel(low, high, *outs):
+    rows = low.shape[0]
     for g, out in enumerate(outs):
-        for k, piece in enumerate(pieces):
-            out[k * PIECE : (k + 1) * PIECE] = piece[:, g * LANES : (g + 1) * LANES]
+        for n, part in enumerate((low, high)):
+            out[n * rows : (n + 1) * rows] = part[:, g * LANES : (g + 1) * LANES]
 
 
 def join_kernel(*refs):
@@ -267,29 +299,28 @@
     return lax.ppermute(array, axes, [(i, i ^ bits) for i in range(lax.axis_size(axes))])
 
 
-def stack_kernel(*refs):
-    *parts, out = refs
-    for k, part in enumerate(parts):
-        out[k * OWN : (k + 1) * OWN] = part[...]
-
-
-def gather(block, slow, fast, tasks, state):
+def double_kernel(first, second, out):
+    rows = first.shape[0]
+    out[:rows] = first[...]
+    out[rows:] = second[...]
+
+
+def gather(block, slow, fast, tasks):
     def ahead(array, step):
         return lax.ppermute(array, fast, [(i, (i - step) % RING) for i in range(RING)])
 
     across = trade(block, slow)
     before, after = ahead(block, -1), ahead(block, 1)
-    across, before, after, state = lax.optimization_barrier((across, before, after, tasks[0](state)))
+    across, before, after, state = lax.optimization_barrier((across, before, after, tasks[0](None, None)))
     across_before = trade(before, slow)
     across_after = ahead(across, 1)
     beyond = ahead(before, -1)
     across_before, across_after, beyond, state = lax.optimization_barrier(
-        (across_before, across_after, beyond, tasks[1](state))
+        (across_before, across_after, beyond, tasks[1](None, state))
     )
     across_beyond = ahead(across_after, 1)
-    across_beyond, state = lax.optimization_barrier((across_beyond, tasks[2](state)))
-    blocks = (block, after, beyond, before, across, across_after, across_beyond, across_before)
-    return vmem_call(stack_kernel, bf16(ROWS, WIDTH), "stack_" + fast)(*blocks), state
+    blocks = (block, after, before, beyond, across, across_after, across_before)
+    return lax.optimization_barrier((across_beyond, tasks[2](blocks, state)))
 
 
 def scatter_ring(pieces, axis, name):
@@ -308,19 +339,26 @@
 
 def per_device(features, out_grad, weight, block_values, block_coords, block_counts):
     raw = (block_coords, block_counts, block_values)
-    tasks = [lambda dense, part=part: build(part, *raw, *dense) for part in range(PARTS)]
-    tasks = [lambda dense, task=task: (task(dense),) for task in tasks]
-    panel, (dense,) = gather(features, *ROW, tasks, ())
-    parts = exchange(down_both(dense, panel).reshape(PEERS, OWN, WIDTH), CHIP)
+    tasks = (
+        lambda blocks, dense: build(0, *raw),
+        lambda blocks, dense: build(1, *raw, dense),
+        lambda blocks, dense: (dense, down_most(dense, blocks)),
+    )
+    block, (dense, most) = gather(features, *ROW, tasks)
+    parts = exchange(down_both(dense, most, block).reshape(PEERS, OWN, WIDTH), CHIP)
 
     half = bf16(WIDTH // 2, WIDTH)
-    activations, send, wgrad_near, wgrad_far = vmem_call(
-        middle_kernel,
-        (bf16(OWN, WIDTH), bf16(PEERS, OWN, WIDTH), half, half),
-        "middle",
+    own = bf16(OWN, WIDTH)
+    activations, send, aggregated, grad_pre = vmem_call(
+        middle_kernel, (own, bf16(PEERS, OWN, WIDTH), own, own), "middle", flops=2 * 2 * OWN * WIDTH * WIDTH
+    )(parts, out_grad, weight)
+    wgrads = vmem_call(
+        wgrad_kernel,
+        (half, half),
+        "wgrad",
         scratch=[pltpu.VMEM((WIDTH, WIDTH), jnp.bfloat16)],
-        flops=2 * 3 * OWN * WIDTH * WIDTH,
-    )(parts, out_grad, weight)
+        flops=2 * OWN * WIDTH * WIDTH,
+    )(aggregated, grad_pre)
 
     piece = bf16(PIECE, WIDTH)
     ys = ("y_lo", "y_hi")
@@ -329,7 +367,8 @@
         return vmem_call(pair_kernel, (piece,) * RING, "pair")(terms[0], trade(terms[1], "core"))
 
     def over_z(pieces):
-        return scatter_ring(pieces, "z", "sum_z")
+        arrived = [pieces[0]] + [trade(pieces[k], "z", k) for k in range(1, RING)]
+        return vmem_call(sum_kernel, piece, "sum_z")(*arrived)
 
     def over_y(summed):
         return vmem_call(square_kernel, piece, "sum_y")(
@@ -337,7 +376,7 @@
         )
 
     mine = exchange(send, CHIP).reshape(ROWS, WIDTH)
-    summed = over_y(over_z(over_core((wgrad_near, wgrad_far))))
+    summed = over_y(over_z(over_core(wgrads)))
     summed, mine = lax.optimization_barrier((summed, mine))
 
     theirs = trade(mine, "core")
@@ -353,14 +392,15 @@
         cost_estimate=pl.CostEstimate(flops=work, bytes_accessed=12 << 20, transcendentals=0),
         name="up_near",
     )(dense, mine)
-    summed, own = lax.optimization_barrier((summed, own))
-    pieces = gather_ring(summed, "z")
+    next_piece, own = lax.optimization_barrier((trade(summed, "z", 1), own))
+    pair = vmem_call(double_kernel, bf16(2 * PIECE, WIDTH), "double")(summed, next_piece)
     partial_grad = vmem_call(up_add_kernel, bf16(PEERS, OWN, WIDTH), "up_far", flops=work)(far, theirs, own)
-    partial_grad, *pieces = lax.optimization_barrier((partial_grad, *pieces))
+    pairs = (pair, trade(pair, "z", 2))
+    partial_grad, *pairs = lax.optimization_barrier((partial_grad, *pairs))
     received = exchange(partial_grad, ROW)
 
     column = bf16(WIDTH // 2, LANES)
-    columns = vmem_call(turn_kernel, (column,) * RING, "turn")(*pieces)
+    columns = vmem_call(turn_kernel, (column,) * RING, "turn")(*pairs)
     summed = scatter_ring(columns, "x", "sum_x")
     columns = gather_ring(summed, "x")
     own_half = vmem_call(join_kernel, half, "join")(*columns)

time: 133 us -> 130 us (0.977)
  waiting for transfers between devices: 32.5 us -> 29.8 us
    ppermute x10 -> x15, starting transfers between devices: 7.9 us -> 15.4 us  [trade(): lax.ppermute(array, axes, [(i, i ^ bits) for i in range(lax.axis_size(axe...]
    ppermute x10 -> x15, waiting for transfers between devices: 12.1 us -> 16.9 us  [trade(): lax.ppermute(array, axes, [(i, i ^ bits) for i in range(lax.axis_size(axe...]
    ppermute x6 -> x3, starting transfers between devices: 9.17 us -> 4.29 us  [gather_ring(): lax.ppermute(piece, axis, [(i, (i - k) % RING) for i in range(RING)])]
    ppermute x6 -> x3, starting transfers between devices: 10 us -> 5.65 us  [scatter_ring(): lax.ppermute(pieces[k], axis, [(i, (i + k) % RING) for i in range(RING)])]
    ppermute x6 -> x3, waiting for transfers between devices: 7.05 us -> 2.81 us  [scatter_ring(): lax.ppermute(pieces[k], axis, [(i, (i + k) % RING) for i in range(RING)])]
    ppermute x5, waiting for transfers between devices: 8.08 us -> 5.88 us  [ahead(): lax.ppermute(array, fast, [(i, (i - step) % RING) for i in range(RING)])]
    pallas_call x14 -> x16, Pallas kernels: 12.9 us -> 14.2 us  [call(): pl.pallas_call(kernel, out_shape=outs, in_specs=[vmem] * len(args), out_s...]
    pallas_call x3 -> x2, Pallas kernels: 3.69 us -> 2.72 us  [build(): pl.pallas_call(functools.partial(build_kernel, part), out_shape=bf16(2 *...]
  transfers between devices with their start and end apart: 29 -> 28, of which waited for: 21 -> 19; matrix products, arithmetic and copies ran while one was open for 0% -> 0% of each run, Pallas kernels for 12% -> 15%
where the time goes in v8:
time: 130 us; the launch traced here: 129 us
  starting transfers between devices  43.1 us (33%)
  waiting for transfers between devices  29.8 us (23%)
  blocking collectives  29.7 us (23%)
  Pallas kernels  21.7 us (17%)
  local copies, waits for them, and re-layouts  2.37 us (2%)
  between operations  1.54 us (1%)
    all_to_all x1, blocking collectives, exchange(): return lax.all_to_all(parts, axes, 0, 0)  29.7 us
    ppermute x15, waiting for transfers between devices, trade(): lax.ppermute(array, axes, [(i, i ^ bits) for i in range(lax.axis_size(axe...  16.9 us
    ppermute x15, starting transfers between devices, trade(): lax.ppermute(array, axes, [(i, i ^ bits) for i in range(lax.axis_size(axe...  15.4 us
    pallas_call x16, Pallas kernels, call(): pl.pallas_call(kernel, out_shape=outs, in_specs=[vmem] * len(args), out_s...  14.2 us
    ppermute x5, starting transfers between devices, ahead(): lax.ppermute(array, fast, [(i, (i - step) % RING) for i in range(RING)])  10.2 us
    all_to_all x2, starting transfers between devices, exchange(): return lax.all_to_all(parts, axes, 0, 0)  7.57 us
    ppermute x5, waiting for transfers between devices, ahead(): lax.ppermute(array, fast, [(i, (i - step) % RING) for i in range(RING)])  5.88 us
    ppermute x3, starting transfers between devices, scatter_ring(): lax.ppermute(pieces[k], axis, [(i, (i + k) % RING) for i in range(RING)])  5.65 us
  transfers between devices with their start and end apart: 28, of which 19 were waited for; matrix products, arithmetic and copies ran while one was open for 0% of the time, Pallas kernels for 15%

profile of v8, /device:TPU:0, one launch (start us, length us, event | category | flops | bytes accessed | tf_op | source)
XLA Modules:
  0.0 129.1 jit_solution(5486608877020477312)
XLA Ops:
  0.6 2.1 %collective-permute-start.1 = (bf16[192,512]{1,0:T(8,128)(2,1)}, bf16[192,512]{1,0:T(8,128)(2,1)S(1)}, u32[]{:S(2)}, u32[]{:S(2)}) collective-permute-start(bf16[192,512]{1,0:T(8,128)(2,1)} %refs_1_.1), channel_id=1, source_target_pairs={{0,16},{16,32},{32,48},{48,0},{1,17},{17,33},{33,49},{49,1},{2,18}... | collective-permute-start | bytes 589832 | tf_op jit(solution)/shard_map/ppermute | solution.py:310
  2.7 1.6 %collective-permute-start = (bf16[192,512]{1,0:T(8,128)(2,1)}, bf16[192,512]{1,0:T(8,128)(2,1)S(1)}, u32[]{:S(2)}, u32[]{:S(2)}) collective-permute-start(bf16[192,512]{1,0:T(8,128)(2,1)} %refs_1_.1), channel_id=1, source_target_pairs={{0,64},{64,0},{1,65},{65,1},{2,66},{66,2},{3,67},{67,3},{4,68},{68... | collective-permute-start | bytes 589832 | tf_op jit(solution)/shard_map/ppermute | solution.py:299
  4.3 2.2 %collective-permute-start.2 = (bf16[192,512]{1,0:T(8,128)(2,1)}, bf16[192,512]{1,0:T(8,128)(2,1)S(1)}, u32[]{:S(2)}, u32[]{:S(2)}) collective-permute-start(bf16[192,512]{1,0:T(8,128)(2,1)} %refs_1_.1), channel_id=1, source_target_pairs={{0,48},{16,0},{32,16},{48,32},{1,49},{17,1},{33,17},{49,33},{2,50}... | collective-permute-start | bytes 589832 | tf_op jit(solution)/shard_map/ppermute | solution.py:310
  7.2 1.7 %copy-done.1 = bf16[1,1,288,4096]{3,2,1,0:T(8,128)(2,1)S(1)} copy-done((bf16[1,1,288,4096]{3,2,1,0:T(8,128)(2,1)S(1)}, bf16[1,1,288,4096]{3,2,1,0:T(8,128)(2,1)}, u32[]{:S(2)}) %copy-start.1) | copy-done | bytes 2359320
  9.5 1.7 %build_0.1.rest_0_ = bf16[3072,1536]{1,0:T(8,128)(2,1)S(1)} custom-call(s32[1,1,2,288]{3,2,1,0:T(2,128)S(1)} %copy-done.4, s32[1,1]{1,0:T(1,128)S(6)} %copy.13.counts, bf16[1,1,288,4096]{3,2,1,0:T(8,128)(2,1)S(1)} %copy-done.1), custom_call_target="tpu_custom_call" | custom-call | bytes 8388608 | tf_op jit(solution)/shard_map/build_0/pallas_call | solution.py:111
  11.3 3.9 %collective-permute-start.4 = (bf16[192,512]{1,0:T(8,128)(2,1)S(1)}, bf16[192,512]{1,0:T(8,128)(2,1)S(1)}, u32[]{:S(2)}, u32[]{:S(2)}) collective-permute-start(bf16[192,512]{1,0:T(8,128)(2,1)S(1)} %collective-permute-done.refs_5_), channel_id=1, source_target_pairs={{0,48},{16,0},{32,16},{48,32},{1,49},{17,1},{33,17},{49,33},{2,50}... | collective-permute-start | bytes 589832 | tf_op jit(solution)/shard_map/ppermute | solution.py:310
  16.2 2.7 %collective-permute-done.4.refs_6_ = bf16[192,512]{1,0:T(8,128)(2,1)S(1)} collective-permute-done((bf16[192,512]{1,0:T(8,128)(2,1)S(1)}, bf16[192,512]{1,0:T(8,128)(2,1)S(1)}, u32[]{:S(2)}, u32[]{:S(2)}) %collective-permute-start.4) | collective-permute-done | bytes 196640 | tf_op jit(solution)/shard_map/ppermute | solution.py:310
  18.9 3.2 %collective-permute-done.5.refs_4_ = bf16[192,512]{1,0:T(8,128)(2,1)S(1)} collective-permute-done((bf16[192,512]{1,0:T(8,128)(2,1)S(1)}, bf16[192,512]{1,0:T(8,128)(2,1)S(1)}, u32[]{:S(2)}, u32[]{:S(2)}) %collective-permute-start.5) | collective-permute-done | bytes 196640 | tf_op jit(solution)/shard_map/ppermute | solution.py:310
  22.1 2.0 %collective-permute-start.6 = (bf16[192,512]{1,0:T(8,128)(2,1)S(1)}, bf16[192,512]{1,0:T(8,128)(2,1)S(1)}, u32[]{:S(2)}, u32[]{:S(2)}) collective-permute-start(bf16[192,512]{1,0:T(8,128)(2,1)S(1)} %collective-permute-done.4.refs_6_), channel_id=1, source_target_pairs={{0,48},{16,0},{32,16},{48,32},{1,49},{17,1},{33,17},{49,33},{2,50}... | collective-permute-start | bytes 589832 | tf_op jit(solution)/shard_map/ppermute | solution.py:310
  24.1 5.0 %down_most.1.most = f32[3072,512]{1,0:T(8,128)S(1)} custom-call(bf16[3072,1536]{1,0:T(8,128)(2,1)S(1)} %build_1.1.refs_0_.dense, bf16[192,512]{1,0:T(8,128)(2,1)S(1)} %copy-done.5, bf16[192,512]{1,0:T(8,128)(2,1)S(1)} %collective-permute-done.2.refs_2_, bf16[192,512]{1,0:T(8,128)(2,1)S(1)} %collective-permute-done.1.refs_3_, ...), custom_call_target="tpu_custom_call" | custom-call | flops 4831838208 | bytes 1048576 | tf_op jit(solution)/shard_map/down_most/pallas_call | solution.py:33
  33.4 29.7 %all_to_all.15.parts = bf16[8,192,512]{2,1,0:T(8,128)(2,1)S(1)} all-to-all(bf16[8,192,512]{2,1,0:T(8,128)(2,1)S(1)} %bitcast.4), channel_id=1, replica_groups=mesh['y_lo'=2,'z'=4,'y_hi'=2,'x'=4,'core'=2] {'y_hi','x'}, dimensions={0} | all-to-all | bytes 3145728 | tf_op jit(solution)/shard_map/all_to_all | solution.py:295
  63.1 2.0 %middle.1 = (bf16[192,512]{1,0:T(8,128)(2,1)}, bf16[8,192,512]{2,1,0:T(8,128)(2,1)}, bf16[192,512]{1,0:T(8,128)(2,1)S(1)}, bf16[192,512]{1,0:T(8,128)(2,1)S(1)}) custom-call(bf16[8,192,512]{2,1,0:T(8,128)(2,1)S(1)} %all_to_all.15.parts, bf16[192,512]{1,0:T(8,128)(2,1)S(1)} %copy-done.3, bf16[512,512]{1,0:T(8,128)(2,1)S(1)} %copy-done.2), custom_call_target="tpu_custom_call" | custom-call | flops 201326592 | bytes 1048576 | tf_op jit(solution)/shard_map/middle/pallas_call | solution.py:33
  65.2 3.6 %all-to-all-start.1 = ((bf16[8,192,512]{2,1,0:T(8,128)(2,1)}), bf16[8,192,512]{2,1,0:T(8,128)(2,1)S(1)}, u32[]{:S(2)}, u32[]{:S(2)}) async-start(bf16[8,192,512]{2,1,0:T(8,128)(2,1)} %get-tuple-element.57), calls=%async_computation.1 | async-start | bytes 3145728 | tf_op jit(solution)/shard_map/all_to_all | solution.py:295
  69.3 1.5 %collective-permute-done.9.other = bf16[256,512]{1,0:T(8,128)(2,1)S(1)} collective-permute-done((bf16[256,512]{1,0:T(8,128)(2,1)S(1)}, bf16[256,512]{1,0:T(8,128)(2,1)S(1)}, u32[]{:S(2)}, u32[]{:S(2)}) %collective-permute-start.9) | collective-permute-done | bytes 262176 | tf_op jit(solution)/shard_map/ppermute | solution.py:299
  70.9 3.3 %collective-permute-start.11 = (bf16[64,512]{1,0:T(8,128)(2,1)S(1)}, bf16[64,512]{1,0:T(8,128)(2,1)S(1)}, u32[]{:S(2)}, u32[]{:S(2)}) collective-permute-start(bf16[64,512]{1,0:T(8,128)(2,1)S(1)} %get-tuple-element.55), channel_id=1, source_target_pairs={{0,32},{16,48},{32,0},{48,16},{1,33},{17,49},{33,1},{49,17},{2,34}... | collective-permute-start | bytes 196616 | tf_op jit(solution)/shard_map/ppermute | solution.py:299
  75.8 1.9 %collective-permute-done.11.refs_2_ = bf16[64,512]{1,0:T(8,128)(2,1)S(1)} collective-permute-done((bf16[64,512]{1,0:T(8,128)(2,1)S(1)}, bf16[64,512]{1,0:T(8,128)(2,1)S(1)}, u32[]{:S(2)}, u32[]{:S(2)}) %collective-permute-start.11) | collective-permute-done | bytes 65568 | tf_op jit(solution)/shard_map/ppermute | solution.py:299
  77.8 2.0 %collective-permute-done.12.refs_3_ = bf16[64,512]{1,0:T(8,128)(2,1)S(1)} collective-permute-done((bf16[64,512]{1,0:T(8,128)(2,1)S(1)}, bf16[64,512]{1,0:T(8,128)(2,1)S(1)}, u32[]{:S(2)}, u32[]{:S(2)}) %collective-permute-start.12) | collective-permute-done | bytes 65568 | tf_op jit(solution)/shard_map/ppermute | solution.py:299
  79.8 2.5 %collective-permute-start.15 = (bf16[64,512]{1,0:T(8,128)(2,1)S(1)}, bf16[64,512]{1,0:T(8,128)(2,1)S(1)}, u32[]{:S(2)}, u32[]{:S(2)}) collective-permute-start(bf16[64,512]{1,0:T(8,128)(2,1)S(1)} %sum_z.1.a), channel_id=1, source_target_pairs={{0,72},{8,64},{64,8},{72,0},{1,73},{9,65},{65,9},{73,1},{2,74},{10... | collective-permute-start | bytes 196616 | tf_op jit(solution)/shard_map/ppermute | solution.py:299
  84.5 3.1 %collective-permute-done.15.d = bf16[64,512]{1,0:T(8,128)(2,1)S(1)} collective-permute-done((bf16[64,512]{1,0:T(8,128)(2,1)S(1)}, bf16[64,512]{1,0:T(8,128)(2,1)S(1)}, u32[]{:S(2)}, u32[]{:S(2)}) %collective-permute-start.15) | collective-permute-done | bytes 65568 | tf_op jit(solution)/shard_map/ppermute | solution.py:299
  87.6 1.7 %collective-permute-done.14.c = bf16[64,512]{1,0:T(8,128)(2,1)S(1)} collective-permute-done((bf16[64,512]{1,0:T(8,128)(2,1)S(1)}, bf16[64,512]{1,0:T(8,128)(2,1)S(1)}, u32[]{:S(2)}, u32[]{:S(2)}) %collective-permute-start.14) | collective-permute-done | bytes 65568 | tf_op jit(solution)/shard_map/ppermute | solution.py:299
  89.4 2.6 %collective-permute-done.13.b = bf16[64,512]{1,0:T(8,128)(2,1)S(1)} collective-permute-done((bf16[64,512]{1,0:T(8,128)(2,1)S(1)}, bf16[64,512]{1,0:T(8,128)(2,1)S(1)}, u32[]{:S(2)}, u32[]{:S(2)}) %collective-permute-start.13) | collective-permute-done | bytes 65568 | tf_op jit(solution)/shard_map/ppermute | solution.py:299
  92.4 4.8 %up_near.1 = (f32[1536,512]{1,0:T(8,128)S(1)}, bf16[1536,1536]{1,0:T(8,128)(2,1)S(1)}) custom-call(bf16[3072,1536]{1,0:T(8,128)(2,1)} %copy-done, bf16[1536,512]{1,0:T(8,128)(2,1)S(1)} %bitcast.6), custom_call_target="tpu_custom_call" | custom-call | flops 2415919104 | bytes 12582912 | tf_op jit(solution)/shard_map/up_near/pallas_call | solution.py:385
  97.2 3.1 %collective-permute-start.18 = (bf16[128,512]{1,0:T(8,128)(2,1)S(1)}, bf16[128,512]{1,0:T(8,128)(2,1)S(1)}, u32[]{:S(2)}, u32[]{:S(2)}) collective-permute-start(bf16[128,512]{1,0:T(8,128)(2,1)S(1)} %double.1.low), channel_id=1, source_target_pairs={{0,32},{16,48},{32,0},{48,16},{1,33},{17,49},{33,1},{49,17},{2,34}... | collective-permute-start | bytes 393224 | tf_op jit(solution)/shard_map/ppermute | solution.py:299
  100.3 3.8 %up_far.1 = bf16[8,192,512]{2,1,0:T(8,128)(2,1)} custom-call(bf16[1536,1536]{1,0:T(8,128)(2,1)S(1)} %get-tuple-element.59.tile, bf16[1536,512]{1,0:T(8,128)(2,1)S(1)} %collective-permute-done.16.rows, f32[1536,512]{1,0:T(8,128)S(1)} %get-tuple-element.62.other), custom_call_target="tpu_custom_call" | custom-call | flops 2415919104 | bytes 1048576 | tf_op jit(solution)/shard_map/up_far/pallas_call | solution.py:33
  104.4 4.0 %all-to-all-start.2 = ((bf16[8,192,512]{2,1,0:T(8,128)(2,1)}), bf16[8,192,512]{2,1,0:T(8,128)(2,1)S(1)}, u32[]{:S(2)}, u32[]{:S(2)}) async-start(bf16[8,192,512]{2,1,0:T(8,128)(2,1)} %up_far.1), calls=%async_computation.2 | async-start | bytes 3145728 | tf_op jit(solution)/shard_map/all_to_all | solution.py:295
  108.5 2.0 %collective-permute-start.19 = (bf16[256,128]{1,0:T(8,128)(2,1)S(1)}, bf16[256,128]{1,0:T(8,128)(2,1)S(1)}, u32[]{:S(2)}, u32[]{:S(2)}) collective-permute-start(bf16[256,128]{1,0:T(8,128)(2,1)S(1)} %get-tuple-element.67), channel_id=1, source_target_pairs={{0,2},{2,4},{4,6},{6,0},{1,3},{3,5},{5,7},{7,1},{8,10},{10,12},{12... | collective-permute-start | bytes 196616 | tf_op jit(solution)/shard_map/ppermute | solution.py:329
  110.5 2.2 %collective-permute-start.20 = (bf16[256,128]{1,0:T(8,128)(2,1)S(1)}, bf16[256,128]{1,0:T(8,128)(2,1)S(1)}, u32[]{:S(2)}, u32[]{:S(2)}) collective-permute-start(bf16[256,128]{1,0:T(8,128)(2,1)S(1)} %get-tuple-element.68), channel_id=1, source_target_pairs={{0,4},{2,6},{4,0},{6,2},{1,5},{3,7},{5,1},{7,3},{8,12},{10,14},{12... | collective-permute-start | bytes 196616 | tf_op jit(solution)/shard_map/ppermute | solution.py:329
  112.7 1.5 %collective-permute-start.21 = (bf16[256,128]{1,0:T(8,128)(2,1)S(1)}, bf16[256,128]{1,0:T(8,128)(2,1)S(1)}, u32[]{:S(2)}, u32[]{:S(2)}) collective-permute-start(bf16[256,128]{1,0:T(8,128)(2,1)S(1)} %get-tuple-element.69), channel_id=1, source_target_pairs={{0,6},{2,0},{4,2},{6,4},{1,7},{3,1},{5,3},{7,5},{8,14},{10,8},{12,... | collective-permute-start | bytes 196616 | tf_op jit(solution)/shard_map/ppermute | solution.py:329
  114.7 1.6 %collective-permute-done.20.refs_2_ = bf16[256,128]{1,0:T(8,128)(2,1)S(1)} collective-permute-done((bf16[256,128]{1,0:T(8,128)(2,1)S(1)}, bf16[256,128]{1,0:T(8,128)(2,1)S(1)}, u32[]{:S(2)}, u32[]{:S(2)}) %collective-permute-start.20) | collective-permute-done | bytes 65568 | tf_op jit(solution)/shard_map/ppermute | solution.py:329
  117.7 3.5 %collective-permute-start.23 = (bf16[256,128]{1,0:T(8,128)(2,1)S(1)}, bf16[256,128]{1,0:T(8,128)(2,1)S(1)}, u32[]{:S(2)}, u32[]{:S(2)}) collective-permute-start(bf16[256,128]{1,0:T(8,128)(2,1)S(1)} %sum_x.1.refs_0_), channel_id=1, source_target_pairs={{0,4},{2,6},{4,0},{6,2},{1,5},{3,7},{5,1},{7,3},{8,12},{10,14},{12... | collective-permute-start | bytes 196616 | tf_op jit(solution)/shard_map/ppermute | solution.py:336
  122.5 1.6 %collective-permute-done.23.refs_2_ = bf16[256,128]{1,0:T(8,128)(2,1)S(1)} collective-permute-done((bf16[256,128]{1,0:T(8,128)(2,1)S(1)}, bf16[256,128]{1,0:T(8,128)(2,1)S(1)}, u32[]{:S(2)}, u32[]{:S(2)}) %collective-permute-start.23) | collective-permute-done | bytes 65568 | tf_op jit(solution)/shard_map/ppermute | solution.py:336
  125.6 1.5 %collective-permute-done.25.theirs = bf16[256,512]{1,0:T(8,128)(2,1)S(1)} collective-permute-done((bf16[256,512]{1,0:T(8,128)(2,1)S(1)}, bf16[256,512]{1,0:T(8,128)(2,1)S(1)}, u32[]{:S(2)}, u32[]{:S(2)}) %collective-permute-start.25) | collective-permute-done | bytes 262176 | tf_op jit(solution)/shard_map/ppermute | solution.py:299
  (57 shorter events, 18.1 us)
Async XLA Ops:
  0.6 10.6 %collective-permute-start.1 = (bf16[192,512]{1,0:T(8,128)(2,1)}, bf16[192,512]{1,0:T(8,128)(2,1)S(1)}, u32[]{:S(2)}, u32[]{:S(2)}) collective-permute-start(bf16[192,512]{1,0:T(8,128)(2,1)} %refs_1_.1), channel_id=1, source_target_pairs={{0,16},{16,32},{32,48},{48,0},{1,17},{17,33},{33,49},{49,1},{2,18}... | collective-permute-start | bytes 589832 | tf_op jit(solution)/shard_map/ppermute | solution.py:310
  2.7 8.6 %collective-permute-start = (bf16[192,512]{1,0:T(8,128)(2,1)}, bf16[192,512]{1,0:T(8,128)(2,1)S(1)}, u32[]{:S(2)}, u32[]{:S(2)}) collective-permute-start(bf16[192,512]{1,0:T(8,128)(2,1)} %refs_1_.1), channel_id=1, source_target_pairs={{0,64},{64,0},{1,65},{65,1},{2,66},{66,2},{3,67},{67,3},{4,68},{68... | collective-permute-start | bytes 589832 | tf_op jit(solution)/shard_map/ppermute | solution.py:299
  4.3 7.0 %collective-permute-start.2 = (bf16[192,512]{1,0:T(8,128)(2,1)}, bf16[192,512]{1,0:T(8,128)(2,1)S(1)}, u32[]{:S(2)}, u32[]{:S(2)}) collective-permute-start(bf16[192,512]{1,0:T(8,128)(2,1)} %refs_1_.1), channel_id=1, source_target_pairs={{0,48},{16,0},{32,16},{48,32},{1,49},{17,1},{33,17},{49,33},{2,50}... | collective-permute-start | bytes 589832 | tf_op jit(solution)/shard_map/ppermute | solution.py:310
  11.2 12.9 %copy-start.5 = (bf16[192,512]{1,0:T(8,128)(2,1)S(1)}, bf16[192,512]{1,0:T(8,128)(2,1)}, u32[]{:S(2)}) copy-start(bf16[192,512]{1,0:T(8,128)(2,1)} %refs_1_.1) | copy-start | bytes 589828
  11.3 7.6 %collective-permute-start.4 = (bf16[192,512]{1,0:T(8,128)(2,1)S(1)}, bf16[192,512]{1,0:T(8,128)(2,1)S(1)}, u32[]{:S(2)}, u32[]{:S(2)}) collective-permute-start(bf16[192,512]{1,0:T(8,128)(2,1)S(1)} %collective-permute-done.refs_5_), channel_id=1, source_target_pairs={{0,48},{16,0},{32,16},{48,32},{1,49},{17,1},{33,17},{49,33},{2,50}... | collective-permute-start | bytes 589832 | tf_op jit(solution)/shard_map/ppermute | solution.py:310
  15.2 6.9 %collective-permute-start.5 = (bf16[192,512]{1,0:T(8,128)(2,1)S(1)}, bf16[192,512]{1,0:T(8,128)(2,1)S(1)}, u32[]{:S(2)}, u32[]{:S(2)}) collective-permute-start(bf16[192,512]{1,0:T(8,128)(2,1)S(1)} %collective-permute-done.1.refs_3_), channel_id=1, source_target_pairs={{0,16},{16,32},{32,48},{48,0},{1,17},{17,33},{33,49},{49,1},{2,18}... | collective-permute-start | bytes 589832 | tf_op jit(solution)/shard_map/ppermute | solution.py:310
  15.2 6.9 %collective-permute-start.3 = (bf16[192,512]{1,0:T(8,128)(2,1)S(1)}, bf16[192,512]{1,0:T(8,128)(2,1)S(1)}, u32[]{:S(2)}, u32[]{:S(2)}) collective-permute-start(bf16[192,512]{1,0:T(8,128)(2,1)S(1)} %collective-permute-done.1.refs_3_), channel_id=1, source_target_pairs={{0,64},{64,0},{1,65},{65,1},{2,66},{66,2},{3,67},{67,3},{4,68},{68... | collective-permute-start | bytes 589832 | tf_op jit(solution)/shard_map/ppermute | solution.py:299
  16.2 16.8 %copy-start = (bf16[3072,1536]{1,0:T(8,128)(2,1)}, bf16[3072,1536]{1,0:T(8,128)(2,1)S(1)}, u32[]{:S(2)}) copy-start(bf16[3072,1536]{1,0:T(8,128)(2,1)S(1)} %build_1.1.refs_0_.dense) | copy-start | bytes 28311556
  22.1 7.1 %collective-permute-start.6 = (bf16[192,512]{1,0:T(8,128)(2,1)S(1)}, bf16[192,512]{1,0:T(8,128)(2,1)S(1)}, u32[]{:S(2)}, u32[]{:S(2)}) collective-permute-start(bf16[192,512]{1,0:T(8,128)(2,1)S(1)} %collective-permute-done.4.refs_6_), channel_id=1, source_target_pairs={{0,48},{16,0},{32,16},{48,32},{1,49},{17,1},{33,17},{49,33},{2,50}... | collective-permute-start | bytes 589832 | tf_op jit(solution)/shard_map/ppermute | solution.py:310
  29.5 2.4 %collective-permute-start.8 = (bf16[768,512]{1,0:T(8,128)(2,1)S(1)}, bf16[768,512]{1,0:T(8,128)(2,1)S(1)}, u32[]{:S(2)}, u32[]{:S(2)}) collective-permute-start(bf16[768,512]{1,0:T(8,128)(2,1)S(1)} %down_far_0.1), channel_id=1, source_target_pairs={{0,1},{1,0},{2,3},{3,2},{4,5},{5,4},{6,7},{7,6},{8,9},{9,8},{10,11... | collective-permute-start | bytes 2359304 | tf_op jit(solution)/shard_map/ppermute | solution.py:299
  30.0 3.0 %collective-permute-start.7 = (bf16[768,512]{1,0:T(8,128)(2,1)S(1)}, bf16[768,512]{1,0:T(8,128)(2,1)S(1)}, u32[]{:S(2)}, u32[]{:S(2)}) collective-permute-start(bf16[768,512]{1,0:T(8,128)(2,1)S(1)} %down_far_1.1), channel_id=1, source_target_pairs={{0,1},{1,0},{2,3},{3,2},{4,5},{5,4},{6,7},{7,6},{8,9},{9,8},{10,11... | collective-permute-start | bytes 2359304 | tf_op jit(solution)/shard_map/ppermute | solution.py:299
  33.4 29.7 %copy-start.2 = (bf16[512,512]{1,0:T(8,128)(2,1)S(1)}, bf16[512,512]{1,0:T(8,128)(2,1)}, u32[]{:S(2)}) copy-start(bf16[512,512]{1,0:T(8,128)(2,1)} %weight.1) | copy-start | bytes 1572868
  33.4 29.7 %copy-start.3 = (bf16[192,512]{1,0:T(8,128)(2,1)S(1)}, bf16[192,512]{1,0:T(8,128)(2,1)}, u32[]{:S(2)}) copy-start(bf16[192,512]{1,0:T(8,128)(2,1)} %out_grad.1) | copy-start | bytes 589828
  65.2 26.8 %all-to-all-start.1 = ((bf16[8,192,512]{2,1,0:T(8,128)(2,1)}), bf16[8,192,512]{2,1,0:T(8,128)(2,1)S(1)}, u32[]{:S(2)}, u32[]{:S(2)}) async-start(bf16[8,192,512]{2,1,0:T(8,128)(2,1)} %get-tuple-element.57), calls=%async_computation.1 | async-start | bytes 3145728 | tf_op jit(solution)/shard_map/all_to_all | solution.py:295
  69.2 1.6 %collective-permute-start.9 = (bf16[256,512]{1,0:T(8,128)(2,1)S(1)}, bf16[256,512]{1,0:T(8,128)(2,1)S(1)}, u32[]{:S(2)}, u32[]{:S(2)}) collective-permute-start(bf16[256,512]{1,0:T(8,128)(2,1)S(1)} %get-tuple-element.52), channel_id=1, source_target_pairs={{0,1},{1,0},{2,3},{3,2},{4,5},{5,4},{6,7},{7,6},{8,9},{9,8},{10,11... | collective-permute-start | bytes 786440 | tf_op jit(solution)/shard_map/ppermute | solution.py:299
  70.9 5.0 %collective-permute-start.10 = (bf16[64,512]{1,0:T(8,128)(2,1)S(1)}, bf16[64,512]{1,0:T(8,128)(2,1)S(1)}, u32[]{:S(2)}, u32[]{:S(2)}) collective-permute-start(bf16[64,512]{1,0:T(8,128)(2,1)S(1)} %get-tuple-element.54), channel_id=1, source_target_pairs={{0,16},{16,0},{32,48},{48,32},{1,17},{17,1},{33,49},{49,33},{2,18}... | collective-permute-start | bytes 196616 | tf_op jit(solution)/shard_map/ppermute | solution.py:299
  70.9 6.8 %collective-permute-start.11 = (bf16[64,512]{1,0:T(8,128)(2,1)S(1)}, bf16[64,512]{1,0:T(8,128)(2,1)S(1)}, u32[]{:S(2)}, u32[]{:S(2)}) collective-permute-start(bf16[64,512]{1,0:T(8,128)(2,1)S(1)} %get-tuple-element.55), channel_id=1, source_target_pairs={{0,32},{16,48},{32,0},{48,16},{1,33},{17,49},{33,1},{49,17},{2,34}... | collective-permute-start | bytes 196616 | tf_op jit(solution)/shard_map/ppermute | solution.py:299
  74.2 5.5 %collective-permute-start.12 = (bf16[64,512]{1,0:T(8,128)(2,1)S(1)}, bf16[64,512]{1,0:T(8,128)(2,1)S(1)}, u32[]{:S(2)}, u32[]{:S(2)}) collective-permute-start(bf16[64,512]{1,0:T(8,128)(2,1)S(1)} %get-tuple-element.56), channel_id=1, source_target_pairs={{0,48},{16,32},{32,16},{48,0},{1,49},{17,33},{33,17},{49,1},{2,50}... | collective-permute-start | bytes 196616 | tf_op jit(solution)/shard_map/ppermute | solution.py:299
  79.8 7.8 %collective-permute-start.15 = (bf16[64,512]{1,0:T(8,128)(2,1)S(1)}, bf16[64,512]{1,0:T(8,128)(2,1)S(1)}, u32[]{:S(2)}, u32[]{:S(2)}) collective-permute-start(bf16[64,512]{1,0:T(8,128)(2,1)S(1)} %sum_z.1.a), channel_id=1, source_target_pairs={{0,72},{8,64},{64,8},{72,0},{1,73},{9,65},{65,9},{73,1},{2,74},{10... | collective-permute-start | bytes 196616 | tf_op jit(solution)/shard_map/ppermute | solution.py:299
  82.3 7.1 %collective-permute-start.14 = (bf16[64,512]{1,0:T(8,128)(2,1)S(1)}, bf16[64,512]{1,0:T(8,128)(2,1)S(1)}, u32[]{:S(2)}, u32[]{:S(2)}) collective-permute-start(bf16[64,512]{1,0:T(8,128)(2,1)S(1)} %sum_z.1.a), channel_id=1, source_target_pairs={{0,64},{8,72},{64,0},{72,8},{1,65},{9,73},{65,1},{73,9},{2,66},{10... | collective-permute-start | bytes 196616 | tf_op jit(solution)/shard_map/ppermute | solution.py:299
  83.2 8.7 %collective-permute-start.13 = (bf16[64,512]{1,0:T(8,128)(2,1)S(1)}, bf16[64,512]{1,0:T(8,128)(2,1)S(1)}, u32[]{:S(2)}, u32[]{:S(2)}) collective-permute-start(bf16[64,512]{1,0:T(8,128)(2,1)S(1)} %sum_z.1.a), channel_id=1, source_target_pairs={{0,8},{8,0},{64,72},{72,64},{1,9},{9,1},{65,73},{73,65},{2,10},{10... | collective-permute-start | bytes 196616 | tf_op jit(solution)/shard_map/ppermute | solution.py:299
  92.0 8.3 %collective-permute-start.16 = (bf16[1536,512]{1,0:T(8,128)(2,1)S(1)}, bf16[1536,512]{1,0:T(8,128)(2,1)S(1)}, u32[]{:S(2)}, u32[]{:S(2)}) collective-permute-start(bf16[1536,512]{1,0:T(8,128)(2,1)S(1)} %bitcast.5), channel_id=1, source_target_pairs={{0,1},{1,0},{2,3},{3,2},{4,5},{5,4},{6,7},{7,6},{8,9},{9,8},{10,11... | collective-permute-start | bytes 4718600 | tf_op jit(solution)/shard_map/ppermute | solution.py:299
  92.1 5.1 %collective-permute-start.17 = (bf16[64,512]{1,0:T(8,128)(2,1)S(1)}, bf16[64,512]{1,0:T(8,128)(2,1)S(1)}, u32[]{:S(2)}, u32[]{:S(2)}) collective-permute-start(bf16[64,512]{1,0:T(8,128)(2,1)S(1)} %sum_y.1.first), channel_id=1, source_target_pairs={{0,16},{16,0},{32,48},{48,32},{1,17},{17,1},{33,49},{49,33},{2,18}... | collective-permute-start | bytes 196616 | tf_op jit(solution)/shard_map/ppermute | solution.py:299
  97.2 7.2 %collective-permute-start.18 = (bf16[128,512]{1,0:T(8,128)(2,1)S(1)}, bf16[128,512]{1,0:T(8,128)(2,1)S(1)}, u32[]{:S(2)}, u32[]{:S(2)}) collective-permute-start(bf16[128,512]{1,0:T(8,128)(2,1)S(1)} %double.1.low), channel_id=1, source_target_pairs={{0,32},{16,48},{32,0},{48,16},{1,33},{17,49},{33,1},{49,17},{2,34}... | collective-permute-start | bytes 393224 | tf_op jit(solution)/shard_map/ppermute | solution.py:299
  104.4 23.8 %all-to-all-start.2 = ((bf16[8,192,512]{2,1,0:T(8,128)(2,1)}), bf16[8,192,512]{2,1,0:T(8,128)(2,1)S(1)}, u32[]{:S(2)}, u32[]{:S(2)}) async-start(bf16[8,192,512]{2,1,0:T(8,128)(2,1)} %up_far.1), calls=%async_computation.2 | async-start | bytes 3145728 | tf_op jit(solution)/shard_map/all_to_all | solution.py:295
  108.5 6.2 %collective-permute-start.19 = (bf16[256,128]{1,0:T(8,128)(2,1)S(1)}, bf16[256,128]{1,0:T(8,128)(2,1)S(1)}, u32[]{:S(2)}, u32[]{:S(2)}) collective-permute-start(bf16[256,128]{1,0:T(8,128)(2,1)S(1)} %get-tuple-element.67), channel_id=1, source_target_pairs={{0,2},{2,4},{4,6},{6,0},{1,3},{3,5},{5,7},{7,1},{8,10},{10,12},{12... | collective-permute-start | bytes 196616 | tf_op jit(solution)/shard_map/ppermute | solution.py:329
  110.5 5.8 %collective-permute-start.20 = (bf16[256,128]{1,0:T(8,128)(2,1)S(1)}, bf16[256,128]{1,0:T(8,128)(2,1)S(1)}, u32[]{:S(2)}, u32[]{:S(2)}) collective-permute-start(bf16[256,128]{1,0:T(8,128)(2,1)S(1)} %get-tuple-element.68), channel_id=1, source_target_pairs={{0,4},{2,6},{4,0},{6,2},{1,5},{3,7},{5,1},{7,3},{8,12},{10,14},{12... | collective-permute-start | bytes 196616 | tf_op jit(solution)/shard_map/ppermute | solution.py:329
  112.7 4.3 %collective-permute-start.21 = (bf16[256,128]{1,0:T(8,128)(2,1)S(1)}, bf16[256,128]{1,0:T(8,128)(2,1)S(1)}, u32[]{:S(2)}, u32[]{:S(2)}) collective-permute-start(bf16[256,128]{1,0:T(8,128)(2,1)S(1)} %get-tuple-element.69), channel_id=1, source_target_pairs={{0,6},{2,0},{4,2},{6,4},{1,7},{3,1},{5,3},{7,5},{8,14},{10,8},{12,... | collective-permute-start | bytes 196616 | tf_op jit(solution)/shard_map/ppermute | solution.py:329
  117.0 5.5 %collective-permute-start.24 = (bf16[256,128]{1,0:T(8,128)(2,1)S(1)}, bf16[256,128]{1,0:T(8,128)(2,1)S(1)}, u32[]{:S(2)}, u32[]{:S(2)}) collective-permute-start(bf16[256,128]{1,0:T(8,128)(2,1)S(1)} %sum_x.1.refs_0_), channel_id=1, source_target_pairs={{0,2},{2,4},{4,6},{6,0},{1,3},{3,5},{5,7},{7,1},{8,10},{10,12},{12... | collective-permute-start | bytes 196616 | tf_op jit(solution)/shard_map/ppermute | solution.py:336
  117.7 6.4 %collective-permute-start.23 = (bf16[256,128]{1,0:T(8,128)(2,1)S(1)}, bf16[256,128]{1,0:T(8,128)(2,1)S(1)}, u32[]{:S(2)}, u32[]{:S(2)}) collective-permute-start(bf16[256,128]{1,0:T(8,128)(2,1)S(1)} %sum_x.1.refs_0_), channel_id=1, source_target_pairs={{0,4},{2,6},{4,0},{6,2},{1,5},{3,7},{5,1},{7,3},{8,12},{10,14},{12... | collective-permute-start | bytes 196616 | tf_op jit(solution)/shard_map/ppermute | solution.py:336
  121.2 4.3 %collective-permute-start.22 = (bf16[256,128]{1,0:T(8,128)(2,1)S(1)}, bf16[256,128]{1,0:T(8,128)(2,1)S(1)}, u32[]{:S(2)}, u32[]{:S(2)}) collective-permute-start(bf16[256,128]{1,0:T(8,128)(2,1)S(1)} %sum_x.1.refs_0_), channel_id=1, source_target_pairs={{0,6},{2,0},{4,2},{6,4},{1,7},{3,1},{5,3},{7,5},{8,14},{10,8},{12,... | collective-permute-start | bytes 196616 | tf_op jit(solution)/shard_map/ppermute | solution.py:336
  125.5 1.6 %collective-permute-start.25 = (bf16[256,512]{1,0:T(8,128)(2,1)S(1)}, bf16[256,512]{1,0:T(8,128)(2,1)S(1)}, u32[]{:S(2)}, u32[]{:S(2)}) collective-permute-start(bf16[256,512]{1,0:T(8,128)(2,1)S(1)} %join.1.mine), channel_id=1, source_target_pairs={{0,1},{1,0},{2,3},{3,2},{4,5},{5,4},{6,7},{7,6},{8,9},{9,8},{10,11... | collective-permute-start | bytes 786440 | tf_op jit(solution)/shard_map/ppermute | solution.py:299
  (2 other events, 2.4 us)

commit v9 on v8

--- a/solution.py
+++ b/solution.py
@@ -61,6 +61,22 @@
     return (lax.axis_index(slow) ^ apart) * RING + ((lax.axis_index(fast) + ahead) & (RING - 1))
 
 
+LEAVING = ((0, 2), (1, 2), (1, 3), (1, 1), (0, 3), (1, 0), (0, 1), (0, 0))
+FIRST = 3
+
+
+def leaving_place(chip):
+    table = sum(place << 4 * (RING * apart + ahead) for place, (apart, ahead) in enumerate(LEAVING))
+    apart = (chip >> 2) ^ lax.axis_index("y_hi")
+    ahead = ((chip & (RING - 1)) - lax.axis_index("x")) & (RING - 1)
+    return (table >> (4 * (RING * apart + ahead))) & 15
+
+
+def leaving_chip(place):
+    apart, ahead = LEAVING[place]
+    return (lax.axis_index("y_hi") ^ apart) * RING + ((lax.axis_index("x") + ahead) & (RING - 1))
+
+
 def build_kernel(part, coords, counts, values, *rest):
     dense = rest[-1]
     rows, cols = dense.shape
@@ -89,7 +105,7 @@
             block_col = jnp.where(live, coords[0, 0, 1, slot], 0)
             owner = block_row // per_owner
             half = (owner + me_core) & 1
-            at_row = (half * PEERS + (owner >> 1)) * per_owner + block_row % per_owner
+            at_row = (half * PEERS + leaving_place(owner >> 1)) * per_owner + block_row % per_owner
             at_col = relative(block_col // per_owner, *ROW) * per_owner + block_col % per_owner
             odd = (at_col & 1) == 1
             plain = pairs[k]
@@ -138,21 +154,25 @@
     return jnp.dot(dense[rows, ROWS - LAST :], padded, preferred_element_type=jnp.float32)
 
 
-def down_far_kernel(first, count, dense, block, most, out):
-    for r in range(0, count, STEP):
-        rows = slice(ROWS + first + r, ROWS + first + r + STEP)
-        out[r : r + STEP] = (most[rows] + with_last(dense, block, rows)).astype(out.dtype)
-
-
-def down_near_kernel(first, count, dense, block, most, other, *rest):
-    out = rest[-1]
-    for r in range(0, count, STEP):
-        rows = slice(first + r, first + r + STEP)
-        total = most[rows] + with_last(dense, block, rows) + other[r : r + STEP].astype(jnp.float32)
-        out[rows] = total.astype(out.dtype)
-
-
-def up_kernel(dense, rows, out, far, near, sems):
+def down_far_kernel(first, dense, block, most, out):
+    for r in range(0, out.shape[0], OWN):
+        rows = slice(ROWS + first + r, ROWS + first + r + OWN)
+        out[r : r + OWN] = (most[rows] + with_last(dense, block, rows)).astype(out.dtype)
+
+
+def down_near_kernel(first, dense, block, most, other, *outs):
+    for k, out in enumerate(outs):
+        rows = slice(first + k * OWN, first + (k + 1) * OWN)
+        total = most[rows] + with_last(dense, block, rows)
+        out[...] = (total + other[k * OWN : (k + 1) * OWN].astype(jnp.float32)).astype(out.dtype)
+
+
+def in_order(rows, ordered):
+    for place in range(PEERS):
+        ordered[place * OWN : (place + 1) * OWN] = rows[leaving_chip(place)]
+
+
+def up_kernel(dense, rows, out, far, near, ordered, sems):
     strips = [pl.ds(r, STEP) for r in range(0, ROWS, STEP)]
     copies = [
         pltpu.make_async_copy(dense.at[pl.ds(0, ROWS), strip], near.at[:, strip], sems.at[n])
@@ -161,15 +181,17 @@
     copies.append(pltpu.make_async_copy(dense.at[pl.ds(ROWS, ROWS)], far, sems.at[len(strips)]))
     for copy in copies:
         copy.start()
+    in_order(rows, ordered)
     for copy, r in zip(copies, range(0, ROWS, STEP)):
         copy.wait()
-        out[r : r + STEP] = over_rows(near[:, r : r + STEP], rows[...])
+        out[r : r + STEP] = over_rows(near[:, r : r + STEP], ordered[...])
     copies[-1].wait()
 
 
-def up_add_kernel(tile, rows, other, out):
+def up_add_kernel(tile, rows, other, out, ordered):
+    in_order(rows, ordered)
     for r in range(0, ROWS, 2 * OWN):
-        total = over_rows(tile[:, r : r + 2 * OWN], rows[...]) + other[r : r + 2 * OWN]
+        total = over_rows(tile[:, r : r + 2 * OWN], ordered[...]) + other[r : r + 2 * OWN]
         for k in range(2):
             out[absolute(r // OWN + k, *ROW)] = total[k * OWN : (k + 1) * OWN].astype(out.dtype)
 
@@ -184,27 +206,52 @@
     )(dense, *blocks)
 
 
-def down_both(dense, most, block):
-    count = ROWS // 2
-    work = 2 * count * LAST * WIDTH
+def down_blocks(dense, most, block):
+    runs = ((0, FIRST), (FIRST, PEERS - FIRST))
     others = []
-    for n in range(2):
-        kernel = functools.partial(down_far_kernel, n * count, count)
-        far = vmem_call(kernel, bf16(count, WIDTH), f"down_far_{n}", flops=work)(dense, block, most)
+    for n, (first, count) in enumerate(runs):
+        kernel = functools.partial(down_far_kernel, first * OWN)
+        far = vmem_call(kernel, bf16(count * OWN, WIDTH), f"down_far_{n}", flops=2 * count * OWN * LAST * WIDTH)(
+            dense, block, most
+        )
+        far, most = lax.optimization_barrier((far, most))
         others.append(trade(far, "core"))
-    out = []
-    for n in range(2):
-        kernel = functools.partial(down_near_kernel, n * count, count)
-        out = vmem_call(
-            kernel, bf16(ROWS, WIDTH), f"down_near_{n}", flops=work, aliases={4: 0} if n else {}
-        )(dense, block, most, others[n], *([out] if n else []))
-    return out
-
-
-def middle_kernel(parts, out_grad, weight, activations, send, aggregated_out, grad_pre_out):
-    total = parts[0].astype(jnp.float32)
-    for k in range(1, PEERS):
-        total = total + parts[k].astype(jnp.float32)
+
+    def near(n):
+        first, count = runs[n]
+        kernel = functools.partial(down_near_kernel, first * OWN)
+        return vmem_call(
+            kernel, (bf16(OWN, WIDTH),) * count, f"down_near_{n}", flops=2 * count * OWN * LAST * WIDTH
+        )(dense, block, most, others[n])
+
+    return near(0), lambda: near(1)
+
+
+def meet_kernel(a, b, c, d, e, out_ab, out_cde):
+    out_ab[...] = add(a[...], b[...])
+    total = c[...].astype(jnp.float32) + d[...].astype(jnp.float32) + e[...].astype(jnp.float32)
+    out_cde[...] = total.astype(out_cde.dtype)
+
+
+def scatter(first, rest, slow, fast):
+    def pass_on(array, step):
+        return lax.ppermute(array, fast, [(i, (i + step) % RING) for i in range(RING)])
+
+    s02, s12, s13 = first
+    r1, r2, r3 = pass_on(s12, 1), trade(s13, slow), pass_on(s02, -1)
+    r1, r2, r3, rest = lax.optimization_barrier((r1, r2, r3, rest()))
+    s11, s03, s10, s01, s00 = rest
+    block = bf16(OWN, WIDTH)
+    t11, t03 = vmem_call(meet_kernel, (block, block), "meet")(s11, r1, s03, r2, r3)
+    r4, r5 = lax.optimization_barrier((pass_on(t11, 1), pass_on(t03, -1)))
+    t10 = vmem_call(sum_kernel, block, "sum_across")(s10, r4)
+    return s00, r5, trade(t10, slow), pass_on(s01, 1)
+
+
+def middle_kernel(a, b, c, d, out_grad, weight, activations, send, aggregated_out, grad_pre_out):
+    total = a[...].astype(jnp.float32)
+    for part in (b, c, d):
+        total = total + part[...].astype(jnp.float32)
     aggregated = total.astype(jnp.bfloat16)
     at = lax.broadcasted_iota(jnp.int32, (OWN, OWN), 0)
     to = lax.broadcasted_iota(jnp.int32, (OWN, OWN), 1)
@@ -345,13 +392,13 @@
         lambda blocks, dense: (dense, down_most(dense, blocks)),
     )
     block, (dense, most) = gather(features, *ROW, tasks)
-    parts = exchange(down_both(dense, most, block).reshape(PEERS, OWN, WIDTH), CHIP)
+    parts = scatter(*down_blocks(dense, most, block), *CHIP)
 
     half = bf16(WIDTH // 2, WIDTH)
     own = bf16(OWN, WIDTH)
     activations, send, aggregated, grad_pre = vmem_call(
         middle_kernel, (own, bf16(PEERS, OWN, WIDTH), own, own), "middle", flops=2 * 2 * OWN * WIDTH * WIDTH
-    )(parts, out_grad, weight)
+    )(*parts, out_grad, weight)
     wgrads = vmem_call(
         wgrad_kernel,
         (half, half),
@@ -375,7 +422,7 @@
             summed, trade(summed, ys, 1), trade(summed, ys, 2), trade(summed, ys, 3)
         )
 
-    mine = exchange(send, CHIP).reshape(ROWS, WIDTH)
+    mine = exchange(send, CHIP)
     summed = over_y(over_z(over_core(wgrads)))
     summed, mine = lax.optimization_barrier((summed, mine))
 
@@ -387,14 +434,21 @@
         out_shape=(jax.ShapeDtypeStruct((ROWS, WIDTH), jnp.float32), bf16(ROWS, ROWS)),
         in_specs=[pl.BlockSpec(memory_space=pltpu.HBM), vmem],
         out_specs=(vmem, vmem),
-        scratch_shapes=[pltpu.VMEM((ROWS, ROWS), jnp.bfloat16), pltpu.SemaphoreType.DMA((ROWS // STEP + 1,))],
+        scratch_shapes=[
+            pltpu.VMEM((ROWS, ROWS), jnp.bfloat16),
+            pltpu.VMEM((ROWS, WIDTH), jnp.bfloat16),
+            pltpu.SemaphoreType.DMA((ROWS // STEP + 1,)),
+        ],
         compiler_params=pltpu.CompilerParams(vmem_limit_bytes=44 << 20),
         cost_estimate=pl.CostEstimate(flops=work, bytes_accessed=12 << 20, transcendentals=0),
         name="up_near",
     )(dense, mine)
     next_piece, own = lax.optimization_barrier((trade(summed, "z", 1), own))
     pair = vmem_call(double_kernel, bf16(2 * PIECE, WIDTH), "double")(summed, next_piece)
-    partial_grad = vmem_call(up_add_kernel, bf16(PEERS, OWN, WIDTH), "up_far", flops=work)(far, theirs, own)
+    ordered = pltpu.VMEM((ROWS, WIDTH), jnp.bfloat16)
+    partial_grad = vmem_call(
+        up_add_kernel, bf16(PEERS, OWN, WIDTH), "up_far", scratch=[ordered], flops=work
+    )(far, theirs, own)
     pairs = (pair, trade(pair, "z", 2))
     partial_grad, *pairs = lax.optimization_barrier((partial_grad, *pairs))
     received = exchange(partial_grad, ROW)

time: 130 us -> 129 us (level)
  blocking collectives: 29.7 us -> 0 us
  waiting for transfers between devices: 29.8 us -> 44.8 us
  starting transfers between devices: 43.1 us -> 55.5 us
    all_to_all x1 -> x0, blocking collectives: 29.7 us -> none  [exchange(): return lax.all_to_all(parts, axes, 0, 0)]
    ppermute x0 -> x5, waiting for transfers between devices: none -> 9.35 us  [pass_on(): lax.ppermute(array, fast, [(i, (i + step) % RING) for i in range(RING)])]
    ppermute x15 -> x17, starting transfers between devices: 15.4 us -> 22.8 us  [trade(): lax.ppermute(array, axes, [(i, i ^ bits) for i in range(lax.axis_size(axe...]
    ppermute x0 -> x5, starting transfers between devices: none -> 6.19 us  [pass_on(): lax.ppermute(array, fast, [(i, (i + step) % RING) for i in range(RING)])]
    ppermute x15 -> x17, waiting for transfers between devices: 16.9 us -> 22.7 us  [trade(): lax.ppermute(array, axes, [(i, i ^ bits) for i in range(lax.axis_size(axe...]
    pallas_call x16 -> x18, Pallas kernels: 14.2 us -> 14.3 us  [call(): pl.pallas_call(kernel, out_shape=outs, in_specs=[vmem] * len(args), out_s...]
  transfers between devices with their start and end apart: 28 -> 35, of which waited for: 19 -> 24; matrix products, arithmetic and copies ran while one was open for 0% -> 0% of each run, Pallas kernels for 15% -> 15%
where the time goes in v9:
time: 129 us; the launch traced here: 128 us
  starting transfers between devices  55.5 us (43%)
  waiting for transfers between devices  44.8 us (35%)
  Pallas kernels  22.5 us (17%)
  local copies, waits for them, and re-layouts  2.36 us (2%)
  between operations  1.53 us (1%)
    ppermute x17, starting transfers between devices, trade(): lax.ppermute(array, axes, [(i, i ^ bits) for i in range(lax.axis_size(axe...  22.8 us
    ppermute x17, waiting for transfers between devices, trade(): lax.ppermute(array, axes, [(i, i ^ bits) for i in range(lax.axis_size(axe...  22.7 us
    pallas_call x18, Pallas kernels, call(): pl.pallas_call(kernel, out_shape=outs, in_specs=[vmem] * len(args), out_s...  14.3 us
    ppermute x5, waiting for transfers between devices, pass_on(): lax.ppermute(array, fast, [(i, (i + step) % RING) for i in range(RING)])  9.35 us
    ppermute x5, starting transfers between devices, ahead(): lax.ppermute(array, fast, [(i, (i - step) % RING) for i in range(RING)])  9.25 us
    all_to_all x2, starting transfers between devices, exchange(): return lax.all_to_all(parts, axes, 0, 0)  8.17 us
    ppermute x5, starting transfers between devices, pass_on(): lax.ppermute(array, fast, [(i, (i + step) % RING) for i in range(RING)])  6.19 us
    ppermute x5, waiting for transfers between devices, ahead(): lax.ppermute(array, fast, [(i, (i - step) % RING) for i in range(RING)])  4.89 us
  transfers between devices with their start and end apart: 35, of which 24 were waited for; matrix products, arithmetic and copies ran while one was open for 0% of the time, Pallas kernels for 15%

profile of v9, /device:TPU:0, one launch (start us, length us, event | category | flops | bytes accessed | tf_op | source)
XLA Modules:
  0.0 127.5 jit_solution(18219666431881241405)
XLA Ops:
  0.6 2.1 %collective-permute-start.1 = (bf16[192,512]{1,0:T(8,128)(2,1)}, bf16[192,512]{1,0:T(8,128)(2,1)S(1)}, u32[]{:S(2)}, u32[]{:S(2)}) collective-permute-start(bf16[192,512]{1,0:T(8,128)(2,1)} %refs_1_.1), channel_id=1, source_target_pairs={{0,16},{16,32},{32,48},{48,0},{1,17},{17,33},{33,49},{49,1},{2,18}... | collective-permute-start | bytes 589832 | tf_op jit(solution)/shard_map/ppermute | solution.py:357
  2.7 1.6 %collective-permute-start = (bf16[192,512]{1,0:T(8,128)(2,1)}, bf16[192,512]{1,0:T(8,128)(2,1)S(1)}, u32[]{:S(2)}, u32[]{:S(2)}) collective-permute-start(bf16[192,512]{1,0:T(8,128)(2,1)} %refs_1_.1), channel_id=1, source_target_pairs={{0,64},{64,0},{1,65},{65,1},{2,66},{66,2},{3,67},{67,3},{4,68},{68... | collective-permute-start | bytes 589832 | tf_op jit(solution)/shard_map/ppermute | solution.py:346
  4.3 2.2 %collective-permute-start.2 = (bf16[192,512]{1,0:T(8,128)(2,1)}, bf16[192,512]{1,0:T(8,128)(2,1)S(1)}, u32[]{:S(2)}, u32[]{:S(2)}) collective-permute-start(bf16[192,512]{1,0:T(8,128)(2,1)} %refs_1_.1), channel_id=1, source_target_pairs={{0,48},{16,0},{32,16},{48,32},{1,49},{17,1},{33,17},{49,33},{2,50}... | collective-permute-start | bytes 589832 | tf_op jit(solution)/shard_map/ppermute | solution.py:357
  7.2 1.7 %copy-done.1 = bf16[1,1,288,4096]{3,2,1,0:T(8,128)(2,1)S(1)} copy-done((bf16[1,1,288,4096]{3,2,1,0:T(8,128)(2,1)S(1)}, bf16[1,1,288,4096]{3,2,1,0:T(8,128)(2,1)}, u32[]{:S(2)}) %copy-start.1) | copy-done | bytes 2359320
  9.5 1.8 %build_0.1.rest_0_ = bf16[3072,1536]{1,0:T(8,128)(2,1)S(1)} custom-call(s32[1,1,2,288]{3,2,1,0:T(2,128)S(1)} %copy-done.4, s32[1,1]{1,0:T(1,128)S(6)} %copy.11.counts, bf16[1,1,288,4096]{3,2,1,0:T(8,128)(2,1)S(1)} %copy-done.1), custom_call_target="tpu_custom_call" | custom-call | bytes 8388608 | tf_op jit(solution)/shard_map/build_0/pallas_call | solution.py:127
  11.3 2.9 %collective-permute-start.4 = (bf16[192,512]{1,0:T(8,128)(2,1)S(1)}, bf16[192,512]{1,0:T(8,128)(2,1)S(1)}, u32[]{:S(2)}, u32[]{:S(2)}) collective-permute-start(bf16[192,512]{1,0:T(8,128)(2,1)S(1)} %collective-permute-done.refs_5_), channel_id=1, source_target_pairs={{0,48},{16,0},{32,16},{48,32},{1,49},{17,1},{33,17},{49,33},{2,50}... | collective-permute-start | bytes 589832 | tf_op jit(solution)/shard_map/ppermute | solution.py:357
  16.3 2.5 %collective-permute-done.4.refs_6_ = bf16[192,512]{1,0:T(8,128)(2,1)S(1)} collective-permute-done((bf16[192,512]{1,0:T(8,128)(2,1)S(1)}, bf16[192,512]{1,0:T(8,128)(2,1)S(1)}, u32[]{:S(2)}, u32[]{:S(2)}) %collective-permute-start.4) | collective-permute-done | bytes 196640 | tf_op jit(solution)/shard_map/ppermute | solution.py:357
  18.8 2.4 %collective-permute-done.5.refs_4_ = bf16[192,512]{1,0:T(8,128)(2,1)S(1)} collective-permute-done((bf16[192,512]{1,0:T(8,128)(2,1)S(1)}, bf16[192,512]{1,0:T(8,128)(2,1)S(1)}, u32[]{:S(2)}, u32[]{:S(2)}) %collective-permute-start.5) | collective-permute-done | bytes 196640 | tf_op jit(solution)/shard_map/ppermute | solution.py:357
  21.2 2.0 %collective-permute-start.6 = (bf16[192,512]{1,0:T(8,128)(2,1)S(1)}, bf16[192,512]{1,0:T(8,128)(2,1)S(1)}, u32[]{:S(2)}, u32[]{:S(2)}) collective-permute-start(bf16[192,512]{1,0:T(8,128)(2,1)S(1)} %collective-permute-done.4.refs_6_), channel_id=1, source_target_pairs={{0,48},{16,0},{32,16},{48,32},{1,49},{17,1},{33,17},{49,33},{2,50}... | collective-permute-start | bytes 589832 | tf_op jit(solution)/shard_map/ppermute | solution.py:357
  23.2 5.0 %down_most.1.most = f32[3072,512]{1,0:T(8,128)S(1)} custom-call(bf16[3072,1536]{1,0:T(8,128)(2,1)S(1)} %build_1.1.refs_0_.dense, bf16[192,512]{1,0:T(8,128)(2,1)S(1)} %copy-done.5, bf16[192,512]{1,0:T(8,128)(2,1)S(1)} %collective-permute-done.2.refs_2_, bf16[192,512]{1,0:T(8,128)(2,1)S(1)} %collective-permute-done.1.refs_3_, ...), custom_call_target="tpu_custom_call" | custom-call | flops 4831838208 | bytes 1048576 | tf_op jit(solution)/shard_map/down_most/pallas_call | solution.py:33
  29.6 2.9 %collective-permute-done.7.other = bf16[576,512]{1,0:T(8,128)(2,1)S(1)} collective-permute-done((bf16[576,512]{1,0:T(8,128)(2,1)S(1)}, bf16[576,512]{1,0:T(8,128)(2,1)S(1)}, u32[]{:S(2)}, u32[]{:S(2)}) %collective-permute-start.7) | collective-permute-done | bytes 589856 | tf_op jit(solution)/shard_map/ppermute | solution.py:346
  32.8 1.6 %collective-permute-start.8 = (bf16[192,512]{1,0:T(8,128)(2,1)S(1)}, bf16[192,512]{1,0:T(8,128)(2,1)S(1)}, u32[]{:S(2)}, u32[]{:S(2)}) collective-permute-start(bf16[192,512]{1,0:T(8,128)(2,1)S(1)} %get-tuple-element.75), channel_id=1, source_target_pairs={{0,2},{2,4},{4,6},{6,0},{1,3},{3,5},{5,7},{7,1},{8,10},{10,12},{12... | collective-permute-start | bytes 589832 | tf_op jit(solution)/shard_map/ppermute | solution.py:238
  34.4 4.6 %collective-permute-start.9 = (bf16[192,512]{1,0:T(8,128)(2,1)S(1)}, bf16[192,512]{1,0:T(8,128)(2,1)S(1)}, u32[]{:S(2)}, u32[]{:S(2)}) collective-permute-start(bf16[192,512]{1,0:T(8,128)(2,1)S(1)} %get-tuple-element.76), channel_id=1, source_target_pairs={{0,8},{8,0},{1,9},{9,1},{2,10},{10,2},{3,11},{11,3},{4,12},{12,4},... | collective-permute-start | bytes 589832 | tf_op jit(solution)/shard_map/ppermute | solution.py:346
  40.7 1.8 %collective-permute-done.8.b = bf16[192,512]{1,0:T(8,128)(2,1)S(1)} collective-permute-done((bf16[192,512]{1,0:T(8,128)(2,1)S(1)}, bf16[192,512]{1,0:T(8,128)(2,1)S(1)}, u32[]{:S(2)}, u32[]{:S(2)}) %collective-permute-start.8) | collective-permute-done | bytes 196640 | tf_op jit(solution)/shard_map/ppermute | solution.py:238
  45.9 2.9 %collective-permute-start.13 = (bf16[192,512]{1,0:T(8,128)(2,1)S(1)}, bf16[192,512]{1,0:T(8,128)(2,1)S(1)}, u32[]{:S(2)}, u32[]{:S(2)}) collective-permute-start(bf16[192,512]{1,0:T(8,128)(2,1)S(1)} %get-tuple-element.91), channel_id=1, source_target_pairs={{0,6},{2,0},{4,2},{6,4},{1,7},{3,1},{5,3},{7,5},{8,14},{10,8},{12,... | collective-permute-start | bytes 589832 | tf_op jit(solution)/shard_map/ppermute | solution.py:238
  48.8 5.5 %collective-permute-done.12.refs_1_ = bf16[192,512]{1,0:T(8,128)(2,1)S(1)} collective-permute-done((bf16[192,512]{1,0:T(8,128)(2,1)S(1)}, bf16[192,512]{1,0:T(8,128)(2,1)S(1)}, u32[]{:S(2)}, u32[]{:S(2)}) %collective-permute-start.12) | collective-permute-done | bytes 196640 | tf_op jit(solution)/shard_map/ppermute | solution.py:238
  54.3 1.7 %collective-permute-start.14 = (bf16[192,512]{1,0:T(8,128)(2,1)S(1)}, bf16[192,512]{1,0:T(8,128)(2,1)S(1)}, u32[]{:S(2)}, u32[]{:S(2)}) collective-permute-start(bf16[192,512]{1,0:T(8,128)(2,1)S(1)} %sum_across.1), channel_id=1, source_target_pairs={{0,8},{8,0},{1,9},{9,1},{2,10},{10,2},{3,11},{11,3},{4,12},{12,4},... | collective-permute-start | bytes 589832 | tf_op jit(solution)/shard_map/ppermute | solution.py:346
  56.6 4.9 %collective-permute-done.14.c = bf16[192,512]{1,0:T(8,128)(2,1)S(1)} collective-permute-done((bf16[192,512]{1,0:T(8,128)(2,1)S(1)}, bf16[192,512]{1,0:T(8,128)(2,1)S(1)}, u32[]{:S(2)}, u32[]{:S(2)}) %collective-permute-start.14) | collective-permute-done | bytes 196640 | tf_op jit(solution)/shard_map/ppermute | solution.py:346
  61.6 2.0 %middle.1 = (bf16[192,512]{1,0:T(8,128)(2,1)}, bf16[8,192,512]{2,1,0:T(8,128)(2,1)}, bf16[192,512]{1,0:T(8,128)(2,1)S(1)}, bf16[192,512]{1,0:T(8,128)(2,1)S(1)}) custom-call(bf16[192,512]{1,0:T(8,128)(2,1)S(1)} %get-tuple-element.84.a, bf16[192,512]{1,0:T(8,128)(2,1)S(1)} %collective-permute-done.13.b, bf16[192,512]{1,0:T(8,128)(2,1)S(1)} %collective-permute-done.14.c, ...), custom_call_target="tpu_custom_call" | custom-call | flops 201326592 | bytes 1048576 | tf_op jit(solution)/shard_map/middle/pallas_call | solution.py:33
  63.6 3.9 %all-to-all-start = ((bf16[8,192,512]{2,1,0:T(8,128)(2,1)}), bf16[8,192,512]{2,1,0:T(8,128)(2,1)S(1)}, u32[]{:S(2)}, u32[]{:S(2)}) async-start(bf16[8,192,512]{2,1,0:T(8,128)(2,1)} %get-tuple-element.105), calls=%async_computation | async-start | bytes 3145728 | tf_op jit(solution)/shard_map/all_to_all | solution.py:342
  69.7 3.3 %collective-permute-start.18 = (bf16[64,512]{1,0:T(8,128)(2,1)S(1)}, bf16[64,512]{1,0:T(8,128)(2,1)S(1)}, u32[]{:S(2)}, u32[]{:S(2)}) collective-permute-start(bf16[64,512]{1,0:T(8,128)(2,1)S(1)} %get-tuple-element.103), channel_id=1, source_target_pairs={{0,32},{16,48},{32,0},{48,16},{1,33},{17,49},{33,1},{49,17},{2,34}... | collective-permute-start | bytes 196616 | tf_op jit(solution)/shard_map/ppermute | solution.py:346
  74.6 1.9 %collective-permute-done.18.refs_2_ = bf16[64,512]{1,0:T(8,128)(2,1)S(1)} collective-permute-done((bf16[64,512]{1,0:T(8,128)(2,1)S(1)}, bf16[64,512]{1,0:T(8,128)(2,1)S(1)}, u32[]{:S(2)}, u32[]{:S(2)}) %collective-permute-start.18) | collective-permute-done | bytes 65568 | tf_op jit(solution)/shard_map/ppermute | solution.py:346
  76.5 2.0 %collective-permute-done.19.refs_3_ = bf16[64,512]{1,0:T(8,128)(2,1)S(1)} collective-permute-done((bf16[64,512]{1,0:T(8,128)(2,1)S(1)}, bf16[64,512]{1,0:T(8,128)(2,1)S(1)}, u32[]{:S(2)}, u32[]{:S(2)}) %collective-permute-start.19) | collective-permute-done | bytes 65568 | tf_op jit(solution)/shard_map/ppermute | solution.py:346
  78.5 3.8 %collective-permute-start.22 = (bf16[64,512]{1,0:T(8,128)(2,1)S(1)}, bf16[64,512]{1,0:T(8,128)(2,1)S(1)}, u32[]{:S(2)}, u32[]{:S(2)}) collective-permute-start(bf16[64,512]{1,0:T(8,128)(2,1)S(1)} %sum_z.1.a), channel_id=1, source_target_pairs={{0,72},{8,64},{64,8},{72,0},{1,73},{9,65},{65,9},{73,1},{2,74},{10... | collective-permute-start | bytes 196616 | tf_op jit(solution)/shard_map/ppermute | solution.py:346
  83.8 4.8 %collective-permute-done.22.d = bf16[64,512]{1,0:T(8,128)(2,1)S(1)} collective-permute-done((bf16[64,512]{1,0:T(8,128)(2,1)S(1)}, bf16[64,512]{1,0:T(8,128)(2,1)S(1)}, u32[]{:S(2)}, u32[]{:S(2)}) %collective-permute-start.22) | collective-permute-done | bytes 65568 | tf_op jit(solution)/shard_map/ppermute | solution.py:346
  90.2 4.8 %up_near.1 = (f32[1536,512]{1,0:T(8,128)S(1)}, bf16[1536,1536]{1,0:T(8,128)(2,1)S(1)}) custom-call(bf16[3072,1536]{1,0:T(8,128)(2,1)} %copy-done, bf16[8,192,512]{2,1,0:T(8,128)(2,1)S(1)} %all-to-all-done.rows), custom_call_target="tpu_custom_call" | custom-call | flops 2415919104 | bytes 12582912 | tf_op jit(solution)/shard_map/up_near/pallas_call | solution.py:432
  95.0 3.3 %collective-permute-start.25 = (bf16[128,512]{1,0:T(8,128)(2,1)S(1)}, bf16[128,512]{1,0:T(8,128)(2,1)S(1)}, u32[]{:S(2)}, u32[]{:S(2)}) collective-permute-start(bf16[128,512]{1,0:T(8,128)(2,1)S(1)} %double.1.low), channel_id=1, source_target_pairs={{0,32},{16,48},{32,0},{48,16},{1,33},{17,49},{33,1},{49,17},{2,34}... | collective-permute-start | bytes 393224 | tf_op jit(solution)/shard_map/ppermute | solution.py:346
  98.4 3.8 %up_far.1 = bf16[8,192,512]{2,1,0:T(8,128)(2,1)} custom-call(bf16[1536,1536]{1,0:T(8,128)(2,1)S(1)} %get-tuple-element.107.tile, bf16[8,192,512]{2,1,0:T(8,128)(2,1)S(1)} %collective-permute-done.23.rows, f32[1536,512]{1,0:T(8,128)S(1)} %get-tuple-element.110.other), custom_call_target="tpu_custom_call" | custom-call | flops 2415919104 | bytes 1048576 | tf_op jit(solution)/shard_map/up_far/pallas_call | solution.py:33
  102.5 4.3 %all-to-all-start.1 = ((bf16[8,192,512]{2,1,0:T(8,128)(2,1)}), bf16[8,192,512]{2,1,0:T(8,128)(2,1)S(1)}, u32[]{:S(2)}, u32[]{:S(2)}) async-start(bf16[8,192,512]{2,1,0:T(8,128)(2,1)} %up_far.1), calls=%async_computation.1 | async-start | bytes 3145728 | tf_op jit(solution)/shard_map/all_to_all | solution.py:342
  107.5 2.7 %collective-permute-start.27 = (bf16[256,128]{1,0:T(8,128)(2,1)S(1)}, bf16[256,128]{1,0:T(8,128)(2,1)S(1)}, u32[]{:S(2)}, u32[]{:S(2)}) collective-permute-start(bf16[256,128]{1,0:T(8,128)(2,1)S(1)} %get-tuple-element.116), channel_id=1, source_target_pairs={{0,4},{2,6},{4,0},{6,2},{1,5},{3,7},{5,1},{7,3},{8,12},{10,14},{12... | collective-permute-start | bytes 196616 | tf_op jit(solution)/shard_map/ppermute | solution.py:376
  115.5 3.1 %collective-permute-start.30 = (bf16[256,128]{1,0:T(8,128)(2,1)S(1)}, bf16[256,128]{1,0:T(8,128)(2,1)S(1)}, u32[]{:S(2)}, u32[]{:S(2)}) collective-permute-start(bf16[256,128]{1,0:T(8,128)(2,1)S(1)} %sum_x.1.refs_0_), channel_id=1, source_target_pairs={{0,4},{2,6},{4,0},{6,2},{1,5},{3,7},{5,1},{7,3},{8,12},{10,14},{12... | collective-permute-start | bytes 196616 | tf_op jit(solution)/shard_map/ppermute | solution.py:383
  120.0 1.6 %collective-permute-done.30.refs_2_ = bf16[256,128]{1,0:T(8,128)(2,1)S(1)} collective-permute-done((bf16[256,128]{1,0:T(8,128)(2,1)S(1)}, bf16[256,128]{1,0:T(8,128)(2,1)S(1)}, u32[]{:S(2)}, u32[]{:S(2)}) %collective-permute-start.30) | collective-permute-done | bytes 65568 | tf_op jit(solution)/shard_map/ppermute | solution.py:383
  (72 shorter events, 30.6 us)
Async XLA Ops:
  0.6 10.7 %collective-permute-start.1 = (bf16[192,512]{1,0:T(8,128)(2,1)}, bf16[192,512]{1,0:T(8,128)(2,1)S(1)}, u32[]{:S(2)}, u32[]{:S(2)}) collective-permute-start(bf16[192,512]{1,0:T(8,128)(2,1)} %refs_1_.1), channel_id=1, source_target_pairs={{0,16},{16,32},{32,48},{48,0},{1,17},{17,33},{33,49},{49,1},{2,18}... | collective-permute-start | bytes 589832 | tf_op jit(solution)/shard_map/ppermute | solution.py:357
  2.7 8.6 %collective-permute-start = (bf16[192,512]{1,0:T(8,128)(2,1)}, bf16[192,512]{1,0:T(8,128)(2,1)S(1)}, u32[]{:S(2)}, u32[]{:S(2)}) collective-permute-start(bf16[192,512]{1,0:T(8,128)(2,1)} %refs_1_.1), channel_id=1, source_target_pairs={{0,64},{64,0},{1,65},{65,1},{2,66},{66,2},{3,67},{67,3},{4,68},{68... | collective-permute-start | bytes 589832 | tf_op jit(solution)/shard_map/ppermute | solution.py:346
  4.3 7.1 %collective-permute-start.2 = (bf16[192,512]{1,0:T(8,128)(2,1)}, bf16[192,512]{1,0:T(8,128)(2,1)S(1)}, u32[]{:S(2)}, u32[]{:S(2)}) collective-permute-start(bf16[192,512]{1,0:T(8,128)(2,1)} %refs_1_.1), channel_id=1, source_target_pairs={{0,48},{16,0},{32,16},{48,32},{1,49},{17,1},{33,17},{49,33},{2,50}... | collective-permute-start | bytes 589832 | tf_op jit(solution)/shard_map/ppermute | solution.py:357
  11.3 7.4 %collective-permute-start.4 = (bf16[192,512]{1,0:T(8,128)(2,1)S(1)}, bf16[192,512]{1,0:T(8,128)(2,1)S(1)}, u32[]{:S(2)}, u32[]{:S(2)}) collective-permute-start(bf16[192,512]{1,0:T(8,128)(2,1)S(1)} %collective-permute-done.refs_5_), channel_id=1, source_target_pairs={{0,48},{16,0},{32,16},{48,32},{1,49},{17,1},{33,17},{49,33},{2,50}... | collective-permute-start | bytes 589832 | tf_op jit(solution)/shard_map/ppermute | solution.py:357
  14.3 6.9 %collective-permute-start.5 = (bf16[192,512]{1,0:T(8,128)(2,1)S(1)}, bf16[192,512]{1,0:T(8,128)(2,1)S(1)}, u32[]{:S(2)}, u32[]{:S(2)}) collective-permute-start(bf16[192,512]{1,0:T(8,128)(2,1)S(1)} %collective-permute-done.1.refs_3_), channel_id=1, source_target_pairs={{0,16},{16,32},{32,48},{48,0},{1,17},{17,33},{33,49},{49,1},{2,18}... | collective-permute-start | bytes 589832 | tf_op jit(solution)/shard_map/ppermute | solution.py:357
  14.3 6.9 %collective-permute-start.3 = (bf16[192,512]{1,0:T(8,128)(2,1)S(1)}, bf16[192,512]{1,0:T(8,128)(2,1)S(1)}, u32[]{:S(2)}, u32[]{:S(2)}) collective-permute-start(bf16[192,512]{1,0:T(8,128)(2,1)S(1)} %collective-permute-done.1.refs_3_), channel_id=1, source_target_pairs={{0,64},{64,0},{1,65},{65,1},{2,66},{66,2},{3,67},{67,3},{4,68},{68... | collective-permute-start | bytes 589832 | tf_op jit(solution)/shard_map/ppermute | solution.py:346
  21.2 7.1 %collective-permute-start.6 = (bf16[192,512]{1,0:T(8,128)(2,1)S(1)}, bf16[192,512]{1,0:T(8,128)(2,1)S(1)}, u32[]{:S(2)}, u32[]{:S(2)}) collective-permute-start(bf16[192,512]{1,0:T(8,128)(2,1)S(1)} %collective-permute-done.4.refs_6_), channel_id=1, source_target_pairs={{0,48},{16,0},{32,16},{48,32},{1,49},{17,1},{33,17},{49,33},{2,50}... | collective-permute-start | bytes 589832 | tf_op jit(solution)/shard_map/ppermute | solution.py:357
  29.0 11.3 %collective-permute-start.11 = (bf16[960,512]{1,0:T(8,128)(2,1)S(1)}, bf16[960,512]{1,0:T(8,128)(2,1)S(1)}, u32[]{:S(2)}, u32[]{:S(2)}) collective-permute-start(bf16[960,512]{1,0:T(8,128)(2,1)S(1)} %down_far_1.1), channel_id=1, source_target_pairs={{0,1},{1,0},{2,3},{3,2},{4,5},{5,4},{6,7},{7,6},{8,9},{9,8},{10,11... | collective-permute-start | bytes 2949128 | tf_op jit(solution)/shard_map/ppermute | solution.py:346
  32.8 9.7 %collective-permute-start.8 = (bf16[192,512]{1,0:T(8,128)(2,1)S(1)}, bf16[192,512]{1,0:T(8,128)(2,1)S(1)}, u32[]{:S(2)}, u32[]{:S(2)}) collective-permute-start(bf16[192,512]{1,0:T(8,128)(2,1)S(1)} %get-tuple-element.75), channel_id=1, source_target_pairs={{0,2},{2,4},{4,6},{6,0},{1,3},{3,5},{5,7},{7,1},{8,10},{10,12},{12... | collective-permute-start | bytes 589832 | tf_op jit(solution)/shard_map/ppermute | solution.py:238
  34.4 9.5 %collective-permute-start.9 = (bf16[192,512]{1,0:T(8,128)(2,1)S(1)}, bf16[192,512]{1,0:T(8,128)(2,1)S(1)}, u32[]{:S(2)}, u32[]{:S(2)}) collective-permute-start(bf16[192,512]{1,0:T(8,128)(2,1)S(1)} %get-tuple-element.76), channel_id=1, source_target_pairs={{0,8},{8,0},{1,9},{9,1},{2,10},{10,2},{3,11},{11,3},{4,12},{12,4},... | collective-permute-start | bytes 589832 | tf_op jit(solution)/shard_map/ppermute | solution.py:346
  39.0 6.4 %collective-permute-start.10 = (bf16[192,512]{1,0:T(8,128)(2,1)S(1)}, bf16[192,512]{1,0:T(8,128)(2,1)S(1)}, u32[]{:S(2)}, u32[]{:S(2)}) collective-permute-start(bf16[192,512]{1,0:T(8,128)(2,1)S(1)} %get-tuple-element.77), channel_id=1, source_target_pairs={{0,6},{2,0},{4,2},{6,4},{1,7},{3,1},{5,3},{7,5},{8,14},{10,8},{12,... | collective-permute-start | bytes 589832 | tf_op jit(solution)/shard_map/ppermute | solution.py:238
  45.5 8.8 %collective-permute-start.12 = (bf16[192,512]{1,0:T(8,128)(2,1)S(1)}, bf16[192,512]{1,0:T(8,128)(2,1)S(1)}, u32[]{:S(2)}, u32[]{:S(2)}) collective-permute-start(bf16[192,512]{1,0:T(8,128)(2,1)S(1)} %get-tuple-element.90), channel_id=1, source_target_pairs={{0,2},{2,4},{4,6},{6,0},{1,3},{3,5},{5,7},{7,1},{8,10},{10,12},{12... | collective-permute-start | bytes 589832 | tf_op jit(solution)/shard_map/ppermute | solution.py:238
  45.9 8.3 %collective-permute-start.13 = (bf16[192,512]{1,0:T(8,128)(2,1)S(1)}, bf16[192,512]{1,0:T(8,128)(2,1)S(1)}, u32[]{:S(2)}, u32[]{:S(2)}) collective-permute-start(bf16[192,512]{1,0:T(8,128)(2,1)S(1)} %get-tuple-element.91), channel_id=1, source_target_pairs={{0,6},{2,0},{4,2},{6,4},{1,7},{3,1},{5,3},{7,5},{8,14},{10,8},{12,... | collective-permute-start | bytes 589832 | tf_op jit(solution)/shard_map/ppermute | solution.py:238
  48.8 7.9 %collective-permute-start.15 = (bf16[192,512]{1,0:T(8,128)(2,1)S(1)}, bf16[192,512]{1,0:T(8,128)(2,1)S(1)}, u32[]{:S(2)}, u32[]{:S(2)}) collective-permute-start(bf16[192,512]{1,0:T(8,128)(2,1)S(1)} %get-tuple-element.95), channel_id=1, source_target_pairs={{0,2},{2,4},{4,6},{6,0},{1,3},{3,5},{5,7},{7,1},{8,10},{10,12},{12... | collective-permute-start | bytes 589832 | tf_op jit(solution)/shard_map/ppermute | solution.py:238
  54.3 7.3 %collective-permute-start.14 = (bf16[192,512]{1,0:T(8,128)(2,1)S(1)}, bf16[192,512]{1,0:T(8,128)(2,1)S(1)}, u32[]{:S(2)}, u32[]{:S(2)}) collective-permute-start(bf16[192,512]{1,0:T(8,128)(2,1)S(1)} %sum_across.1), channel_id=1, source_target_pairs={{0,8},{8,0},{1,9},{9,1},{2,10},{10,2},{3,11},{11,3},{4,12},{12,4},... | collective-permute-start | bytes 589832 | tf_op jit(solution)/shard_map/ppermute | solution.py:346
  63.6 26.4 %all-to-all-start = ((bf16[8,192,512]{2,1,0:T(8,128)(2,1)}), bf16[8,192,512]{2,1,0:T(8,128)(2,1)S(1)}, u32[]{:S(2)}, u32[]{:S(2)}) async-start(bf16[8,192,512]{2,1,0:T(8,128)(2,1)} %get-tuple-element.105), calls=%async_computation | async-start | bytes 3145728 | tf_op jit(solution)/shard_map/all_to_all | solution.py:342
  69.6 5.0 %collective-permute-start.17 = (bf16[64,512]{1,0:T(8,128)(2,1)S(1)}, bf16[64,512]{1,0:T(8,128)(2,1)S(1)}, u32[]{:S(2)}, u32[]{:S(2)}) collective-permute-start(bf16[64,512]{1,0:T(8,128)(2,1)S(1)} %get-tuple-element.102), channel_id=1, source_target_pairs={{0,16},{16,0},{32,48},{48,32},{1,17},{17,1},{33,49},{49,33},{2,18}... | collective-permute-start | bytes 196616 | tf_op jit(solution)/shard_map/ppermute | solution.py:346
  69.7 6.8 %collective-permute-start.18 = (bf16[64,512]{1,0:T(8,128)(2,1)S(1)}, bf16[64,512]{1,0:T(8,128)(2,1)S(1)}, u32[]{:S(2)}, u32[]{:S(2)}) collective-permute-start(bf16[64,512]{1,0:T(8,128)(2,1)S(1)} %get-tuple-element.103), channel_id=1, source_target_pairs={{0,32},{16,48},{32,0},{48,16},{1,33},{17,49},{33,1},{49,17},{2,34}... | collective-permute-start | bytes 196616 | tf_op jit(solution)/shard_map/ppermute | solution.py:346
  73.0 5.5 %collective-permute-start.19 = (bf16[64,512]{1,0:T(8,128)(2,1)S(1)}, bf16[64,512]{1,0:T(8,128)(2,1)S(1)}, u32[]{:S(2)}, u32[]{:S(2)}) collective-permute-start(bf16[64,512]{1,0:T(8,128)(2,1)S(1)} %get-tuple-element.104), channel_id=1, source_target_pairs={{0,48},{16,32},{32,16},{48,0},{1,49},{17,33},{33,17},{49,1},{2,50}... | collective-permute-start | bytes 196616 | tf_op jit(solution)/shard_map/ppermute | solution.py:346
  78.5 10.1 %collective-permute-start.22 = (bf16[64,512]{1,0:T(8,128)(2,1)S(1)}, bf16[64,512]{1,0:T(8,128)(2,1)S(1)}, u32[]{:S(2)}, u32[]{:S(2)}) collective-permute-start(bf16[64,512]{1,0:T(8,128)(2,1)S(1)} %sum_z.1.a), channel_id=1, source_target_pairs={{0,72},{8,64},{64,8},{72,0},{1,73},{9,65},{65,9},{73,1},{2,74},{10... | collective-permute-start | bytes 196616 | tf_op jit(solution)/shard_map/ppermute | solution.py:346
  82.3 6.4 %collective-permute-start.21 = (bf16[64,512]{1,0:T(8,128)(2,1)S(1)}, bf16[64,512]{1,0:T(8,128)(2,1)S(1)}, u32[]{:S(2)}, u32[]{:S(2)}) collective-permute-start(bf16[64,512]{1,0:T(8,128)(2,1)S(1)} %sum_z.1.a), channel_id=1, source_target_pairs={{0,64},{8,72},{64,0},{72,8},{1,65},{9,73},{65,1},{73,9},{2,66},{10... | collective-permute-start | bytes 196616 | tf_op jit(solution)/shard_map/ppermute | solution.py:346
  82.3 7.7 %collective-permute-start.20 = (bf16[64,512]{1,0:T(8,128)(2,1)S(1)}, bf16[64,512]{1,0:T(8,128)(2,1)S(1)}, u32[]{:S(2)}, u32[]{:S(2)}) collective-permute-start(bf16[64,512]{1,0:T(8,128)(2,1)S(1)} %sum_z.1.a), channel_id=1, source_target_pairs={{0,8},{8,0},{64,72},{72,64},{1,9},{9,1},{65,73},{73,65},{2,10},{10... | collective-permute-start | bytes 196616 | tf_op jit(solution)/shard_map/ppermute | solution.py:346
  90.0 8.4 %collective-permute-start.23 = (bf16[8,192,512]{2,1,0:T(8,128)(2,1)S(1)}, bf16[8,192,512]{2,1,0:T(8,128)(2,1)S(1)}, u32[]{:S(2)}, u32[]{:S(2)}) collective-permute-start(bf16[8,192,512]{2,1,0:T(8,128)(2,1)S(1)} %all-to-all-done.rows), channel_id=1, source_target_pairs={{0,1},{1,0},{2,3},{3,2},{4,5},{5,4},{6,7},{7,6},{8,9},{9,8},{10,11... | collective-permute-start | bytes 4718600 | tf_op jit(solution)/shard_map/ppermute | solution.py:346
  90.1 4.9 %collective-permute-start.24 = (bf16[64,512]{1,0:T(8,128)(2,1)S(1)}, bf16[64,512]{1,0:T(8,128)(2,1)S(1)}, u32[]{:S(2)}, u32[]{:S(2)}) collective-permute-start(bf16[64,512]{1,0:T(8,128)(2,1)S(1)} %sum_y.1.first), channel_id=1, source_target_pairs={{0,16},{16,0},{32,48},{48,32},{1,17},{17,1},{33,49},{49,33},{2,18}... | collective-permute-start | bytes 196616 | tf_op jit(solution)/shard_map/ppermute | solution.py:346
  95.0 7.4 %collective-permute-start.25 = (bf16[128,512]{1,0:T(8,128)(2,1)S(1)}, bf16[128,512]{1,0:T(8,128)(2,1)S(1)}, u32[]{:S(2)}, u32[]{:S(2)}) collective-permute-start(bf16[128,512]{1,0:T(8,128)(2,1)S(1)} %double.1.low), channel_id=1, source_target_pairs={{0,32},{16,48},{32,0},{48,16},{1,33},{17,49},{33,1},{49,17},{2,34}... | collective-permute-start | bytes 393224 | tf_op jit(solution)/shard_map/ppermute | solution.py:346
  102.5 24.2 %all-to-all-start.1 = ((bf16[8,192,512]{2,1,0:T(8,128)(2,1)}), bf16[8,192,512]{2,1,0:T(8,128)(2,1)S(1)}, u32[]{:S(2)}, u32[]{:S(2)}) async-start(bf16[8,192,512]{2,1,0:T(8,128)(2,1)} %up_far.1), calls=%async_computation.1 | async-start | bytes 3145728 | tf_op jit(solution)/shard_map/all_to_all | solution.py:342
  106.8 5.5 %collective-permute-start.26 = (bf16[256,128]{1,0:T(8,128)(2,1)S(1)}, bf16[256,128]{1,0:T(8,128)(2,1)S(1)}, u32[]{:S(2)}, u32[]{:S(2)}) collective-permute-start(bf16[256,128]{1,0:T(8,128)(2,1)S(1)} %get-tuple-element.115), channel_id=1, source_target_pairs={{0,2},{2,4},{4,6},{6,0},{1,3},{3,5},{5,7},{7,1},{8,10},{10,12},{12... | collective-permute-start | bytes 196616 | tf_op jit(solution)/shard_map/ppermute | solution.py:376
  107.5 5.8 %collective-permute-start.27 = (bf16[256,128]{1,0:T(8,128)(2,1)S(1)}, bf16[256,128]{1,0:T(8,128)(2,1)S(1)}, u32[]{:S(2)}, u32[]{:S(2)}) collective-permute-start(bf16[256,128]{1,0:T(8,128)(2,1)S(1)} %get-tuple-element.116), channel_id=1, source_target_pairs={{0,4},{2,6},{4,0},{6,2},{1,5},{3,7},{5,1},{7,3},{8,12},{10,14},{12... | collective-permute-start | bytes 196616 | tf_op jit(solution)/shard_map/ppermute | solution.py:376
  110.1 4.3 %collective-permute-start.28 = (bf16[256,128]{1,0:T(8,128)(2,1)S(1)}, bf16[256,128]{1,0:T(8,128)(2,1)S(1)}, u32[]{:S(2)}, u32[]{:S(2)}) collective-permute-start(bf16[256,128]{1,0:T(8,128)(2,1)S(1)} %get-tuple-element.117), channel_id=1, source_target_pairs={{0,6},{2,0},{4,2},{6,4},{1,7},{3,1},{5,3},{7,5},{8,14},{10,8},{12,... | collective-permute-start | bytes 196616 | tf_op jit(solution)/shard_map/ppermute | solution.py:376
  114.4 5.5 %collective-permute-start.31 = (bf16[256,128]{1,0:T(8,128)(2,1)S(1)}, bf16[256,128]{1,0:T(8,128)(2,1)S(1)}, u32[]{:S(2)}, u32[]{:S(2)}) collective-permute-start(bf16[256,128]{1,0:T(8,128)(2,1)S(1)} %sum_x.1.refs_0_), channel_id=1, source_target_pairs={{0,2},{2,4},{4,6},{6,0},{1,3},{3,5},{5,7},{7,1},{8,10},{10,12},{12... | collective-permute-start | bytes 196616 | tf_op jit(solution)/shard_map/ppermute | solution.py:383
  115.5 6.1 %collective-permute-start.30 = (bf16[256,128]{1,0:T(8,128)(2,1)S(1)}, bf16[256,128]{1,0:T(8,128)(2,1)S(1)}, u32[]{:S(2)}, u32[]{:S(2)}) collective-permute-start(bf16[256,128]{1,0:T(8,128)(2,1)S(1)} %sum_x.1.refs_0_), channel_id=1, source_target_pairs={{0,4},{2,6},{4,0},{6,2},{1,5},{3,7},{5,1},{7,3},{8,12},{10,14},{12... | collective-permute-start | bytes 196616 | tf_op jit(solution)/shard_map/ppermute | solution.py:383
  118.6 4.3 %collective-permute-start.29 = (bf16[256,128]{1,0:T(8,128)(2,1)S(1)}, bf16[256,128]{1,0:T(8,128)(2,1)S(1)}, u32[]{:S(2)}, u32[]{:S(2)}) collective-permute-start(bf16[256,128]{1,0:T(8,128)(2,1)S(1)} %sum_x.1.refs_0_), channel_id=1, source_target_pairs={{0,6},{2,0},{4,2},{6,4},{1,7},{3,1},{5,3},{7,5},{8,14},{10,8},{12,... | collective-permute-start | bytes 196616 | tf_op jit(solution)/shard_map/ppermute | solution.py:383
  (9 other events, 90.1 us)

commit v10 on v9

--- a/solution.py
+++ b/solution.py
@@ -214,8 +214,10 @@
         far = vmem_call(kernel, bf16(count * OWN, WIDTH), f"down_far_{n}", flops=2 * count * OWN * LAST * WIDTH)(
             dense, block, most
         )
-        far, most = lax.optimization_barrier((far, most))
-        others.append(trade(far, "core"))
+        other = trade(far, "core")
+        if n == 0:
+            other, most = lax.optimization_barrier((other, most))
+        others.append(other)
 
     def near(n):
         first, count = runs[n]
@@ -248,7 +250,7 @@
     return s00, r5, trade(t10, slow), pass_on(s01, 1)
 
 
-def middle_kernel(a, b, c, d, out_grad, weight, activations, send, aggregated_out, grad_pre_out):
+def middle_kernel(a, b, c, d, out_grad, weight, activations, aggregated_out, grad_pre_out, send, grad_agg, sems):
     total = a[...].astype(jnp.float32)
     for part in (b, c, d):
         total = total + part[...].astype(jnp.float32)
@@ -262,17 +264,20 @@
     w = weight[...]
     pre_act = jnp.dot(aggregated, w, preferred_element_type=jnp.float32)
     sig = jax.nn.sigmoid(pre_act)
+    cotangent = jnp.dot(turn, out_grad[...], preferred_element_type=jnp.float32)
+    grad_pre = (cotangent * sig * (1.0 + pre_act * (1.0 - sig))).astype(jnp.bfloat16)
+    grad_agg[...] = lax.dot_general(
+        grad_pre, w, (((1,), (1,)), ((), ())), preferred_element_type=jnp.float32
+    ).astype(jnp.bfloat16)
+    copies = [pltpu.make_async_copy(grad_agg, send.at[k], sems.at[k]) for k in range(PEERS)]
+    for copy in copies:
+        copy.start()
     act = (pre_act * sig).astype(jnp.bfloat16)
     activations[...] = over_rows(turn, act).astype(jnp.bfloat16)
-    cotangent = jnp.dot(turn, out_grad[...], preferred_element_type=jnp.float32)
-    grad_pre = (cotangent * sig * (1.0 + pre_act * (1.0 - sig))).astype(jnp.bfloat16)
-    grad_agg = lax.dot_general(
-        grad_pre, w, (((1,), (1,)), ((), ())), preferred_element_type=jnp.float32
-    ).astype(jnp.bfloat16)
-    for k in range(PEERS):
-        send[k] = grad_agg
     aggregated_out[...] = aggregated
     grad_pre_out[...] = grad_pre
+    for copy in copies:
+        copy.wait()
 
 
 def wgrad_kernel(aggregated, grad_pre, wgrad_near, wgrad_far, local):
@@ -396,8 +401,18 @@
 
     half = bf16(WIDTH // 2, WIDTH)
     own = bf16(OWN, WIDTH)
-    activations, send, aggregated, grad_pre = vmem_call(
-        middle_kernel, (own, bf16(PEERS, OWN, WIDTH), own, own), "middle", flops=2 * 2 * OWN * WIDTH * WIDTH
+    vmem = pl.BlockSpec(memory_space=pltpu.VMEM)
+    activations, aggregated, grad_pre, send = pl.pallas_call(
+        middle_kernel,
+        out_shape=(own, own, own, bf16(PEERS, OWN, WIDTH)),
+        in_specs=[vmem] * 6,
+        out_specs=(vmem, vmem, vmem, pl.BlockSpec(memory_space=pltpu.HBM)),
+        scratch_shapes=[pltpu.VMEM((OWN, WIDTH), jnp.bfloat16), pltpu.SemaphoreType.DMA((PEERS,))],
+        compiler_params=pltpu.CompilerParams(vmem_limit_bytes=16 << 20),
+        cost_estimate=pl.CostEstimate(
+            flops=2 * 2 * OWN * WIDTH * WIDTH, bytes_accessed=4 << 20, transcendentals=OWN * WIDTH
+        ),
+        name="middle",
     )(*parts, out_grad, weight)
     wgrads = vmem_call(
         wgrad_kernel,
@@ -428,7 +443,6 @@
 
     theirs = trade(mine, "core")
     work = 2 * ROWS * ROWS * WIDTH
-    vmem = pl.BlockSpec(memory_space=pltpu.VMEM)
     own, far = pl.pallas_call(
         up_kernel,
         out_shape=(jax.ShapeDtypeStruct((ROWS, WIDTH), jnp.float32), bf16(ROWS, ROWS)),

time: 129 us -> 129 us (level)
  starting transfers between devices: 55.5 us -> 52.2 us
  waiting for transfers between devices: 44.8 us -> 47.4 us
  Pallas kernels: 22.5 us -> 23.9 us
    ppermute x5, starting transfers between devices: 6.19 us -> 3.39 us  [pass_on(): lax.ppermute(array, fast, [(i, (i + step) % RING) for i in range(RING)])]
    pallas_call x0 -> x1, Pallas kernels: none -> 2.5 us  [per_device(): pl.pallas_call(middle_kernel, out_shape=(own, own, own, bf16(PEERS, OWN,...]
    pallas_call x18 -> x17, Pallas kernels: 14.3 us -> 12.3 us  [call(): pl.pallas_call(kernel, out_shape=outs, in_specs=[vmem] * len(args), out_s...]
    ppermute x3, starting transfers between devices: 4.81 us -> 3.34 us  [scatter_ring(): lax.ppermute(pieces[k], axis, [(i, (i + k) % RING) for i in range(RING)])]
    ppermute x5, waiting for transfers between devices: 9.35 us -> 10.6 us  [pass_on(): lax.ppermute(array, fast, [(i, (i + step) % RING) for i in range(RING)])]
  transfers between devices with their start and end apart: 35 -> 35, of which waited for: 24 -> 22; matrix products, arithmetic and copies ran while one was open for 0% -> 0% of each run, Pallas kernels for 15% -> 16%
where the time goes in v10:
time: 129 us; the launch traced here: 128 us
  starting transfers between devices  52.2 us (40%)
  waiting for transfers between devices  47.4 us (37%)
  Pallas kernels  23.9 us (19%)
  local copies, waits for them, and re-layouts  2.36 us (2%)
  between operations  1.55 us (1%)
    ppermute x17, starting transfers between devices, trade(): lax.ppermute(array, axes, [(i, i ^ bits) for i in range(lax.axis_size(axe...  23.5 us
    ppermute x17, waiting for transfers between devices, trade(): lax.ppermute(array, axes, [(i, i ^ bits) for i in range(lax.axis_size(axe...  21.9 us
    pallas_call x17, Pallas kernels, call(): pl.pallas_call(kernel, out_shape=outs, in_specs=[vmem] * len(args), out_s...  12.3 us
    ppermute x5, waiting for transfers between devices, pass_on(): lax.ppermute(array, fast, [(i, (i + step) % RING) for i in range(RING)])  10.6 us
    ppermute x5, starting transfers between devices, ahead(): lax.ppermute(array, fast, [(i, (i - step) % RING) for i in range(RING)])  9.09 us
    all_to_all x2, starting transfers between devices, exchange(): return lax.all_to_all(parts, axes, 0, 0)  8.71 us
    ppermute x5, waiting for transfers between devices, ahead(): lax.ppermute(array, fast, [(i, (i - step) % RING) for i in range(RING)])  5.35 us
    pallas_call x1, Pallas kernels, per_device(): pl.pallas_call(up_kernel, out_shape=(jax.ShapeDtypeStruct((ROWS, WIDTH),...  4.85 us
  transfers between devices with their start and end apart: 35, of which 22 were waited for; matrix products, arithmetic and copies ran while one was open for 0% of the time, Pallas kernels for 16%

profile of v10, /device:TPU:0, one launch (start us, length us, event | category | flops | bytes accessed | tf_op | source)
XLA Modules:
  0.0 128.2 jit_solution(11702670513905238842)
XLA Ops:
  0.6 2.1 %collective-permute-start.1 = (bf16[192,512]{1,0:T(8,128)(2,1)}, bf16[192,512]{1,0:T(8,128)(2,1)S(1)}, u32[]{:S(2)}, u32[]{:S(2)}) collective-permute-start(bf16[192,512]{1,0:T(8,128)(2,1)} %refs_1_.1), channel_id=1, source_target_pairs={{0,16},{16,32},{32,48},{48,0},{1,17},{17,33},{33,49},{49,1},{2,18}... | collective-permute-start | bytes 589832 | tf_op jit(solution)/shard_map/ppermute | solution.py:362
  2.7 1.6 %collective-permute-start = (bf16[192,512]{1,0:T(8,128)(2,1)}, bf16[192,512]{1,0:T(8,128)(2,1)S(1)}, u32[]{:S(2)}, u32[]{:S(2)}) collective-permute-start(bf16[192,512]{1,0:T(8,128)(2,1)} %refs_1_.1), channel_id=1, source_target_pairs={{0,64},{64,0},{1,65},{65,1},{2,66},{66,2},{3,67},{67,3},{4,68},{68... | collective-permute-start | bytes 589832 | tf_op jit(solution)/shard_map/ppermute | solution.py:351
  4.3 2.2 %collective-permute-start.2 = (bf16[192,512]{1,0:T(8,128)(2,1)}, bf16[192,512]{1,0:T(8,128)(2,1)S(1)}, u32[]{:S(2)}, u32[]{:S(2)}) collective-permute-start(bf16[192,512]{1,0:T(8,128)(2,1)} %refs_1_.1), channel_id=1, source_target_pairs={{0,48},{16,0},{32,16},{48,32},{1,49},{17,1},{33,17},{49,33},{2,50}... | collective-permute-start | bytes 589832 | tf_op jit(solution)/shard_map/ppermute | solution.py:362
  7.2 1.7 %copy-done.1 = bf16[1,1,288,4096]{3,2,1,0:T(8,128)(2,1)S(1)} copy-done((bf16[1,1,288,4096]{3,2,1,0:T(8,128)(2,1)S(1)}, bf16[1,1,288,4096]{3,2,1,0:T(8,128)(2,1)}, u32[]{:S(2)}) %copy-start.1) | copy-done | bytes 2359320
  9.5 2.2 %build_0.1.rest_0_ = bf16[3072,1536]{1,0:T(8,128)(2,1)S(1)} custom-call(s32[1,1,2,288]{3,2,1,0:T(2,128)S(1)} %copy-done.4, s32[1,1]{1,0:T(1,128)S(6)} %copy.11.counts, bf16[1,1,288,4096]{3,2,1,0:T(8,128)(2,1)S(1)} %copy-done.1), custom_call_target="tpu_custom_call" | custom-call | bytes 8388608 | tf_op jit(solution)/shard_map/build_0/pallas_call | solution.py:127
  11.8 2.5 %collective-permute-start.4 = (bf16[192,512]{1,0:T(8,128)(2,1)S(1)}, bf16[192,512]{1,0:T(8,128)(2,1)S(1)}, u32[]{:S(2)}, u32[]{:S(2)}) collective-permute-start(bf16[192,512]{1,0:T(8,128)(2,1)S(1)} %collective-permute-done.refs_5_), channel_id=1, source_target_pairs={{0,48},{16,0},{32,16},{48,32},{1,49},{17,1},{33,17},{49,33},{2,50}... | collective-permute-start | bytes 589832 | tf_op jit(solution)/shard_map/ppermute | solution.py:362
  15.6 1.9 %build_1.1.refs_0_.dense = bf16[3072,1536]{1,0:T(8,128)(2,1)S(1)} custom-call(s32[1,1,2,288]{3,2,1,0:T(2,128)S(1)} %copy-done.4, s32[1,1]{1,0:T(1,128)S(6)} %copy.11.counts, bf16[1,1,288,4096]{3,2,1,0:T(8,128)(2,1)S(1)} %copy-done.1, bf16[3072,1536]{1,0:T(8,128)(2,1)S(1)} %build_0.1.rest_0_), custom_call_target="tpu_custom_call", output_to_operand_aliasing={{}: (3, {})} | custom-call | bytes 8388608 | tf_op jit(solution)/shard_map/build_1/pallas_call | solution.py:127
  19.0 3.9 %collective-permute-done.5.refs_4_ = bf16[192,512]{1,0:T(8,128)(2,1)S(1)} collective-permute-done((bf16[192,512]{1,0:T(8,128)(2,1)S(1)}, bf16[192,512]{1,0:T(8,128)(2,1)S(1)}, u32[]{:S(2)}, u32[]{:S(2)}) %collective-permute-start.5) | collective-permute-done | bytes 196640 | tf_op jit(solution)/shard_map/ppermute | solution.py:362
  22.9 2.3 %collective-permute-start.6 = (bf16[192,512]{1,0:T(8,128)(2,1)S(1)}, bf16[192,512]{1,0:T(8,128)(2,1)S(1)}, u32[]{:S(2)}, u32[]{:S(2)}) collective-permute-start(bf16[192,512]{1,0:T(8,128)(2,1)S(1)} %collective-permute-done.4.refs_6_), channel_id=1, source_target_pairs={{0,48},{16,0},{32,16},{48,32},{1,49},{17,1},{33,17},{49,33},{2,50}... | collective-permute-start | bytes 589832 | tf_op jit(solution)/shard_map/ppermute | solution.py:362
  25.3 5.0 %down_most.1.most = f32[3072,512]{1,0:T(8,128)S(1)} custom-call(bf16[3072,1536]{1,0:T(8,128)(2,1)S(1)} %build_1.1.refs_0_.dense, bf16[192,512]{1,0:T(8,128)(2,1)S(1)} %copy-done.5, bf16[192,512]{1,0:T(8,128)(2,1)S(1)} %collective-permute-done.2.refs_2_, bf16[192,512]{1,0:T(8,128)(2,1)S(1)} %collective-permute-done.1.refs_3_, ...), custom_call_target="tpu_custom_call" | custom-call | flops 4831838208 | bytes 1048576 | tf_op jit(solution)/shard_map/down_most/pallas_call | solution.py:33
  30.7 2.0 %collective-permute-done.7.other = bf16[576,512]{1,0:T(8,128)(2,1)S(1)} collective-permute-done((bf16[576,512]{1,0:T(8,128)(2,1)S(1)}, bf16[576,512]{1,0:T(8,128)(2,1)S(1)}, u32[]{:S(2)}, u32[]{:S(2)}) %collective-permute-start.7) | collective-permute-done | bytes 589856 | tf_op jit(solution)/shard_map/ppermute | solution.py:351
  33.8 4.5 %collective-permute-start.9 = (bf16[192,512]{1,0:T(8,128)(2,1)S(1)}, bf16[192,512]{1,0:T(8,128)(2,1)S(1)}, u32[]{:S(2)}, u32[]{:S(2)}) collective-permute-start(bf16[192,512]{1,0:T(8,128)(2,1)S(1)} %get-tuple-element.73), channel_id=1, source_target_pairs={{0,8},{8,0},{1,9},{9,1},{2,10},{10,2},{3,11},{11,3},{4,12},{12,4},... | collective-permute-start | bytes 589832 | tf_op jit(solution)/shard_map/ppermute | solution.py:351
  38.7 3.5 %collective-permute-done.8.b = bf16[192,512]{1,0:T(8,128)(2,1)S(1)} collective-permute-done((bf16[192,512]{1,0:T(8,128)(2,1)S(1)}, bf16[192,512]{1,0:T(8,128)(2,1)S(1)}, u32[]{:S(2)}, u32[]{:S(2)}) %collective-permute-start.8) | collective-permute-done | bytes 196640 | tf_op jit(solution)/shard_map/ppermute | solution.py:240
  45.5 2.7 %collective-permute-start.13 = (bf16[192,512]{1,0:T(8,128)(2,1)S(1)}, bf16[192,512]{1,0:T(8,128)(2,1)S(1)}, u32[]{:S(2)}, u32[]{:S(2)}) collective-permute-start(bf16[192,512]{1,0:T(8,128)(2,1)S(1)} %get-tuple-element.87), channel_id=1, source_target_pairs={{0,6},{2,0},{4,2},{6,4},{1,7},{3,1},{5,3},{7,5},{8,14},{10,8},{12,... | collective-permute-start | bytes 589832 | tf_op jit(solution)/shard_map/ppermute | solution.py:240
  48.3 5.3 %collective-permute-done.12.refs_1_ = bf16[192,512]{1,0:T(8,128)(2,1)S(1)} collective-permute-done((bf16[192,512]{1,0:T(8,128)(2,1)S(1)}, bf16[192,512]{1,0:T(8,128)(2,1)S(1)}, u32[]{:S(2)}, u32[]{:S(2)}) %collective-permute-start.12) | collective-permute-done | bytes 196640 | tf_op jit(solution)/shard_map/ppermute | solution.py:240
  53.6 2.1 %collective-permute-start.14 = (bf16[192,512]{1,0:T(8,128)(2,1)S(1)}, bf16[192,512]{1,0:T(8,128)(2,1)S(1)}, u32[]{:S(2)}, u32[]{:S(2)}) collective-permute-start(bf16[192,512]{1,0:T(8,128)(2,1)S(1)} %sum_across.1), channel_id=1, source_target_pairs={{0,8},{8,0},{1,9},{9,1},{2,10},{10,2},{3,11},{11,3},{4,12},{12,4},... | collective-permute-start | bytes 589832 | tf_op jit(solution)/shard_map/ppermute | solution.py:351
  56.2 4.7 %collective-permute-done.14.c = bf16[192,512]{1,0:T(8,128)(2,1)S(1)} collective-permute-done((bf16[192,512]{1,0:T(8,128)(2,1)S(1)}, bf16[192,512]{1,0:T(8,128)(2,1)S(1)}, u32[]{:S(2)}, u32[]{:S(2)}) %collective-permute-start.14) | collective-permute-done | bytes 196640 | tf_op jit(solution)/shard_map/ppermute | solution.py:351
  60.9 2.5 %middle.1 = (bf16[192,512]{1,0:T(8,128)(2,1)}, bf16[192,512]{1,0:T(8,128)(2,1)S(1)}, bf16[192,512]{1,0:T(8,128)(2,1)S(1)}, bf16[8,192,512]{2,1,0:T(8,128)(2,1)}) custom-call(bf16[192,512]{1,0:T(8,128)(2,1)S(1)} %get-tuple-element.80.a, bf16[192,512]{1,0:T(8,128)(2,1)S(1)} %collective-permute-done.13.b, bf16[192,512]{1,0:T(8,128)(2,1)S(1)} %collective-permute-done.14.c, ...), custom_call_target="tpu_custom_call" | custom-call | flops 201326592 | bytes 4194304 | tf_op jit(solution)/shard_map/middle/pallas_call | solution.py:405
  63.4 4.2 %all-to-all-start = ((bf16[8,192,512]{2,1,0:T(8,128)(2,1)}), bf16[8,192,512]{2,1,0:T(8,128)(2,1)S(1)}, u32[]{:S(2)}, u32[]{:S(2)}) async-start(bf16[8,192,512]{2,1,0:T(8,128)(2,1)} %get-tuple-element.101), calls=%async_computation | async-start | bytes 3145728 | tf_op jit(solution)/shard_map/all_to_all | solution.py:347
  69.8 3.9 %collective-permute-start.18 = (bf16[64,512]{1,0:T(8,128)(2,1)S(1)}, bf16[64,512]{1,0:T(8,128)(2,1)S(1)}, u32[]{:S(2)}, u32[]{:S(2)}) collective-permute-start(bf16[64,512]{1,0:T(8,128)(2,1)S(1)} %get-tuple-element.99), channel_id=1, source_target_pairs={{0,32},{16,48},{32,0},{48,16},{1,33},{17,49},{33,1},{49,17},{2,34}... | collective-permute-start | bytes 196616 | tf_op jit(solution)/shard_map/ppermute | solution.py:351
  74.4 2.7 %collective-permute-done.18.refs_2_ = bf16[64,512]{1,0:T(8,128)(2,1)S(1)} collective-permute-done((bf16[64,512]{1,0:T(8,128)(2,1)S(1)}, bf16[64,512]{1,0:T(8,128)(2,1)S(1)}, u32[]{:S(2)}, u32[]{:S(2)}) %collective-permute-start.18) | collective-permute-done | bytes 65568 | tf_op jit(solution)/shard_map/ppermute | solution.py:351
  77.2 2.0 %collective-permute-done.19.refs_3_ = bf16[64,512]{1,0:T(8,128)(2,1)S(1)} collective-permute-done((bf16[64,512]{1,0:T(8,128)(2,1)S(1)}, bf16[64,512]{1,0:T(8,128)(2,1)S(1)}, u32[]{:S(2)}, u32[]{:S(2)}) %collective-permute-start.19) | collective-permute-done | bytes 65568 | tf_op jit(solution)/shard_map/ppermute | solution.py:351
  79.2 3.0 %collective-permute-start.22 = (bf16[64,512]{1,0:T(8,128)(2,1)S(1)}, bf16[64,512]{1,0:T(8,128)(2,1)S(1)}, u32[]{:S(2)}, u32[]{:S(2)}) collective-permute-start(bf16[64,512]{1,0:T(8,128)(2,1)S(1)} %sum_z.1.a), channel_id=1, source_target_pairs={{0,72},{8,64},{64,8},{72,0},{1,73},{9,65},{65,9},{73,1},{2,74},{10... | collective-permute-start | bytes 196616 | tf_op jit(solution)/shard_map/ppermute | solution.py:351
  83.9 4.8 %collective-permute-done.22.d = bf16[64,512]{1,0:T(8,128)(2,1)S(1)} collective-permute-done((bf16[64,512]{1,0:T(8,128)(2,1)S(1)}, bf16[64,512]{1,0:T(8,128)(2,1)S(1)}, u32[]{:S(2)}, u32[]{:S(2)}) %collective-permute-start.22) | collective-permute-done | bytes 65568 | tf_op jit(solution)/shard_map/ppermute | solution.py:351
  90.4 4.8 %up_near.1 = (f32[1536,512]{1,0:T(8,128)S(1)}, bf16[1536,1536]{1,0:T(8,128)(2,1)S(1)}) custom-call(bf16[3072,1536]{1,0:T(8,128)(2,1)} %copy-done, bf16[8,192,512]{2,1,0:T(8,128)(2,1)S(1)} %all-to-all-done.rows), custom_call_target="tpu_custom_call" | custom-call | flops 2415919104 | bytes 12582912 | tf_op jit(solution)/shard_map/up_near/pallas_call | solution.py:446
  95.3 3.8 %collective-permute-start.25 = (bf16[128,512]{1,0:T(8,128)(2,1)S(1)}, bf16[128,512]{1,0:T(8,128)(2,1)S(1)}, u32[]{:S(2)}, u32[]{:S(2)}) collective-permute-start(bf16[128,512]{1,0:T(8,128)(2,1)S(1)} %double.1.low), channel_id=1, source_target_pairs={{0,32},{16,48},{32,0},{48,16},{1,33},{17,49},{33,1},{49,17},{2,34}... | collective-permute-start | bytes 393224 | tf_op jit(solution)/shard_map/ppermute | solution.py:351
  99.1 3.8 %up_far.1 = bf16[8,192,512]{2,1,0:T(8,128)(2,1)} custom-call(bf16[1536,1536]{1,0:T(8,128)(2,1)S(1)} %get-tuple-element.103.tile, bf16[8,192,512]{2,1,0:T(8,128)(2,1)S(1)} %collective-permute-done.23.rows, f32[1536,512]{1,0:T(8,128)S(1)} %get-tuple-element.106.other), custom_call_target="tpu_custom_call" | custom-call | flops 2415919104 | bytes 1048576 | tf_op jit(solution)/shard_map/up_far/pallas_call | solution.py:33
  102.9 4.5 %all-to-all-start.1 = ((bf16[8,192,512]{2,1,0:T(8,128)(2,1)}), bf16[8,192,512]{2,1,0:T(8,128)(2,1)S(1)}, u32[]{:S(2)}, u32[]{:S(2)}) async-start(bf16[8,192,512]{2,1,0:T(8,128)(2,1)} %up_far.1), calls=%async_computation.1 | async-start | bytes 3145728 | tf_op jit(solution)/shard_map/all_to_all | solution.py:347
  110.8 2.2 %collective-permute-done.26.refs_1_ = bf16[256,128]{1,0:T(8,128)(2,1)S(1)} collective-permute-done((bf16[256,128]{1,0:T(8,128)(2,1)S(1)}, bf16[256,128]{1,0:T(8,128)(2,1)S(1)}, u32[]{:S(2)}, u32[]{:S(2)}) %collective-permute-start.26) | collective-permute-done | bytes 65568 | tf_op jit(solution)/shard_map/ppermute | solution.py:381
  116.0 2.6 %collective-permute-start.30 = (bf16[256,128]{1,0:T(8,128)(2,1)S(1)}, bf16[256,128]{1,0:T(8,128)(2,1)S(1)}, u32[]{:S(2)}, u32[]{:S(2)}) collective-permute-start(bf16[256,128]{1,0:T(8,128)(2,1)S(1)} %sum_x.1.refs_0_), channel_id=1, source_target_pairs={{0,4},{2,6},{4,0},{6,2},{1,5},{3,7},{5,1},{7,3},{8,12},{10,14},{12... | collective-permute-start | bytes 196616 | tf_op jit(solution)/shard_map/ppermute | solution.py:388
  120.2 1.6 %collective-permute-done.30.refs_2_ = bf16[256,128]{1,0:T(8,128)(2,1)S(1)} collective-permute-done((bf16[256,128]{1,0:T(8,128)(2,1)S(1)}, bf16[256,128]{1,0:T(8,128)(2,1)S(1)}, u32[]{:S(2)}, u32[]{:S(2)}) %collective-permute-start.30) | collective-permute-done | bytes 65568 | tf_op jit(solution)/shard_map/ppermute | solution.py:388
  125.6 1.7 %all-to-all-done.1 = bf16[8,192,512]{2,1,0:T(8,128)(2,1)S(1)} async-done(((bf16[8,192,512]{2,1,0:T(8,128)(2,1)}), bf16[8,192,512]{2,1,0:T(8,128)(2,1)S(1)}, u32[]{:S(2)}, u32[]{:S(2)}) %all-to-all-start.1) | async-done | bytes 1572896 | tf_op jit(solution)/shard_map/all_to_all | solution.py:347
  (72 shorter events, 28.4 us)
Async XLA Ops:
  0.6 11.1 %collective-permute-start.1 = (bf16[192,512]{1,0:T(8,128)(2,1)}, bf16[192,512]{1,0:T(8,128)(2,1)S(1)}, u32[]{:S(2)}, u32[]{:S(2)}) collective-permute-start(bf16[192,512]{1,0:T(8,128)(2,1)} %refs_1_.1), channel_id=1, source_target_pairs={{0,16},{16,32},{32,48},{48,0},{1,17},{17,33},{33,49},{49,1},{2,18}... | collective-permute-start | bytes 589832 | tf_op jit(solution)/shard_map/ppermute | solution.py:362
  2.7 9.1 %collective-permute-start = (bf16[192,512]{1,0:T(8,128)(2,1)}, bf16[192,512]{1,0:T(8,128)(2,1)S(1)}, u32[]{:S(2)}, u32[]{:S(2)}) collective-permute-start(bf16[192,512]{1,0:T(8,128)(2,1)} %refs_1_.1), channel_id=1, source_target_pairs={{0,64},{64,0},{1,65},{65,1},{2,66},{66,2},{3,67},{67,3},{4,68},{68... | collective-permute-start | bytes 589832 | tf_op jit(solution)/shard_map/ppermute | solution.py:351
  4.3 7.5 %collective-permute-start.2 = (bf16[192,512]{1,0:T(8,128)(2,1)}, bf16[192,512]{1,0:T(8,128)(2,1)S(1)}, u32[]{:S(2)}, u32[]{:S(2)}) collective-permute-start(bf16[192,512]{1,0:T(8,128)(2,1)} %refs_1_.1), channel_id=1, source_target_pairs={{0,48},{16,0},{32,16},{48,32},{1,49},{17,1},{33,17},{49,33},{2,50}... | collective-permute-start | bytes 589832 | tf_op jit(solution)/shard_map/ppermute | solution.py:362
  11.8 7.3 %collective-permute-start.4 = (bf16[192,512]{1,0:T(8,128)(2,1)S(1)}, bf16[192,512]{1,0:T(8,128)(2,1)S(1)}, u32[]{:S(2)}, u32[]{:S(2)}) collective-permute-start(bf16[192,512]{1,0:T(8,128)(2,1)S(1)} %collective-permute-done.refs_5_), channel_id=1, source_target_pairs={{0,48},{16,0},{32,16},{48,32},{1,49},{17,1},{33,17},{49,33},{2,50}... | collective-permute-start | bytes 589832 | tf_op jit(solution)/shard_map/ppermute | solution.py:362
  14.3 8.7 %collective-permute-start.5 = (bf16[192,512]{1,0:T(8,128)(2,1)S(1)}, bf16[192,512]{1,0:T(8,128)(2,1)S(1)}, u32[]{:S(2)}, u32[]{:S(2)}) collective-permute-start(bf16[192,512]{1,0:T(8,128)(2,1)S(1)} %collective-permute-done.1.refs_3_), channel_id=1, source_target_pairs={{0,16},{16,32},{32,48},{48,0},{1,17},{17,33},{33,49},{49,1},{2,18}... | collective-permute-start | bytes 589832 | tf_op jit(solution)/shard_map/ppermute | solution.py:362
  14.3 8.7 %collective-permute-start.3 = (bf16[192,512]{1,0:T(8,128)(2,1)S(1)}, bf16[192,512]{1,0:T(8,128)(2,1)S(1)}, u32[]{:S(2)}, u32[]{:S(2)}) collective-permute-start(bf16[192,512]{1,0:T(8,128)(2,1)S(1)} %collective-permute-done.1.refs_3_), channel_id=1, source_target_pairs={{0,64},{64,0},{1,65},{65,1},{2,66},{66,2},{3,67},{67,3},{4,68},{68... | collective-permute-start | bytes 589832 | tf_op jit(solution)/shard_map/ppermute | solution.py:351
  22.9 7.3 %collective-permute-start.6 = (bf16[192,512]{1,0:T(8,128)(2,1)S(1)}, bf16[192,512]{1,0:T(8,128)(2,1)S(1)}, u32[]{:S(2)}, u32[]{:S(2)}) collective-permute-start(bf16[192,512]{1,0:T(8,128)(2,1)S(1)} %collective-permute-done.4.refs_6_), channel_id=1, source_target_pairs={{0,48},{16,0},{32,16},{48,32},{1,49},{17,1},{33,17},{49,33},{2,50}... | collective-permute-start | bytes 589832 | tf_op jit(solution)/shard_map/ppermute | solution.py:362
  33.1 5.1 %collective-permute-start.11 = (bf16[960,512]{1,0:T(8,128)(2,1)S(1)}, bf16[960,512]{1,0:T(8,128)(2,1)S(1)}, u32[]{:S(2)}, u32[]{:S(2)}) collective-permute-start(bf16[960,512]{1,0:T(8,128)(2,1)S(1)} %down_far_1.1), channel_id=1, source_target_pairs={{0,1},{1,0},{2,3},{3,2},{4,5},{5,4},{6,7},{7,6},{8,9},{9,8},{10,11... | collective-permute-start | bytes 2949128 | tf_op jit(solution)/shard_map/ppermute | solution.py:351
  33.7 8.5 %collective-permute-start.8 = (bf16[192,512]{1,0:T(8,128)(2,1)S(1)}, bf16[192,512]{1,0:T(8,128)(2,1)S(1)}, u32[]{:S(2)}, u32[]{:S(2)}) collective-permute-start(bf16[192,512]{1,0:T(8,128)(2,1)S(1)} %get-tuple-element.72), channel_id=1, source_target_pairs={{0,2},{2,4},{4,6},{6,0},{1,3},{3,5},{5,7},{7,1},{8,10},{10,12},{12... | collective-permute-start | bytes 589832 | tf_op jit(solution)/shard_map/ppermute | solution.py:240
  33.8 9.6 %collective-permute-start.9 = (bf16[192,512]{1,0:T(8,128)(2,1)S(1)}, bf16[192,512]{1,0:T(8,128)(2,1)S(1)}, u32[]{:S(2)}, u32[]{:S(2)}) collective-permute-start(bf16[192,512]{1,0:T(8,128)(2,1)S(1)} %get-tuple-element.73), channel_id=1, source_target_pairs={{0,8},{8,0},{1,9},{9,1},{2,10},{10,2},{3,11},{11,3},{4,12},{12,4},... | collective-permute-start | bytes 589832 | tf_op jit(solution)/shard_map/ppermute | solution.py:351
  38.2 6.6 %collective-permute-start.10 = (bf16[192,512]{1,0:T(8,128)(2,1)S(1)}, bf16[192,512]{1,0:T(8,128)(2,1)S(1)}, u32[]{:S(2)}, u32[]{:S(2)}) collective-permute-start(bf16[192,512]{1,0:T(8,128)(2,1)S(1)} %get-tuple-element.74), channel_id=1, source_target_pairs={{0,6},{2,0},{4,2},{6,4},{1,7},{3,1},{5,3},{7,5},{8,14},{10,8},{12,... | collective-permute-start | bytes 589832 | tf_op jit(solution)/shard_map/ppermute | solution.py:240
  45.0 8.6 %collective-permute-start.12 = (bf16[192,512]{1,0:T(8,128)(2,1)S(1)}, bf16[192,512]{1,0:T(8,128)(2,1)S(1)}, u32[]{:S(2)}, u32[]{:S(2)}) collective-permute-start(bf16[192,512]{1,0:T(8,128)(2,1)S(1)} %get-tuple-element.86), channel_id=1, source_target_pairs={{0,2},{2,4},{4,6},{6,0},{1,3},{3,5},{5,7},{7,1},{8,10},{10,12},{12... | collective-permute-start | bytes 589832 | tf_op jit(solution)/shard_map/ppermute | solution.py:240
  45.5 8.0 %collective-permute-start.13 = (bf16[192,512]{1,0:T(8,128)(2,1)S(1)}, bf16[192,512]{1,0:T(8,128)(2,1)S(1)}, u32[]{:S(2)}, u32[]{:S(2)}) collective-permute-start(bf16[192,512]{1,0:T(8,128)(2,1)S(1)} %get-tuple-element.87), channel_id=1, source_target_pairs={{0,6},{2,0},{4,2},{6,4},{1,7},{3,1},{5,3},{7,5},{8,14},{10,8},{12,... | collective-permute-start | bytes 589832 | tf_op jit(solution)/shard_map/ppermute | solution.py:240
  48.3 7.9 %collective-permute-start.15 = (bf16[192,512]{1,0:T(8,128)(2,1)S(1)}, bf16[192,512]{1,0:T(8,128)(2,1)S(1)}, u32[]{:S(2)}, u32[]{:S(2)}) collective-permute-start(bf16[192,512]{1,0:T(8,128)(2,1)S(1)} %get-tuple-element.91), channel_id=1, source_target_pairs={{0,2},{2,4},{4,6},{6,0},{1,3},{3,5},{5,7},{7,1},{8,10},{10,12},{12... | collective-permute-start | bytes 589832 | tf_op jit(solution)/shard_map/ppermute | solution.py:240
  53.6 7.3 %collective-permute-start.14 = (bf16[192,512]{1,0:T(8,128)(2,1)S(1)}, bf16[192,512]{1,0:T(8,128)(2,1)S(1)}, u32[]{:S(2)}, u32[]{:S(2)}) collective-permute-start(bf16[192,512]{1,0:T(8,128)(2,1)S(1)} %sum_across.1), channel_id=1, source_target_pairs={{0,8},{8,0},{1,9},{9,1},{2,10},{10,2},{3,11},{11,3},{4,12},{12,4},... | collective-permute-start | bytes 589832 | tf_op jit(solution)/shard_map/ppermute | solution.py:351
  63.4 26.9 %all-to-all-start = ((bf16[8,192,512]{2,1,0:T(8,128)(2,1)}), bf16[8,192,512]{2,1,0:T(8,128)(2,1)S(1)}, u32[]{:S(2)}, u32[]{:S(2)}) async-start(bf16[8,192,512]{2,1,0:T(8,128)(2,1)} %get-tuple-element.101), calls=%async_computation | async-start | bytes 3145728 | tf_op jit(solution)/shard_map/all_to_all | solution.py:347
  69.7 4.8 %collective-permute-start.17 = (bf16[64,512]{1,0:T(8,128)(2,1)S(1)}, bf16[64,512]{1,0:T(8,128)(2,1)S(1)}, u32[]{:S(2)}, u32[]{:S(2)}) collective-permute-start(bf16[64,512]{1,0:T(8,128)(2,1)S(1)} %get-tuple-element.98), channel_id=1, source_target_pairs={{0,16},{16,0},{32,48},{48,32},{1,17},{17,1},{33,49},{49,33},{2,18}... | collective-permute-start | bytes 196616 | tf_op jit(solution)/shard_map/ppermute | solution.py:351
  69.8 7.4 %collective-permute-start.18 = (bf16[64,512]{1,0:T(8,128)(2,1)S(1)}, bf16[64,512]{1,0:T(8,128)(2,1)S(1)}, u32[]{:S(2)}, u32[]{:S(2)}) collective-permute-start(bf16[64,512]{1,0:T(8,128)(2,1)S(1)} %get-tuple-element.99), channel_id=1, source_target_pairs={{0,32},{16,48},{32,0},{48,16},{1,33},{17,49},{33,1},{49,17},{2,34}... | collective-permute-start | bytes 196616 | tf_op jit(solution)/shard_map/ppermute | solution.py:351
  73.7 5.5 %collective-permute-start.19 = (bf16[64,512]{1,0:T(8,128)(2,1)S(1)}, bf16[64,512]{1,0:T(8,128)(2,1)S(1)}, u32[]{:S(2)}, u32[]{:S(2)}) collective-permute-start(bf16[64,512]{1,0:T(8,128)(2,1)S(1)} %get-tuple-element.100), channel_id=1, source_target_pairs={{0,48},{16,32},{32,16},{48,0},{1,49},{17,33},{33,17},{49,1},{2,50}... | collective-permute-start | bytes 196616 | tf_op jit(solution)/shard_map/ppermute | solution.py:351
  79.2 9.6 %collective-permute-start.22 = (bf16[64,512]{1,0:T(8,128)(2,1)S(1)}, bf16[64,512]{1,0:T(8,128)(2,1)S(1)}, u32[]{:S(2)}, u32[]{:S(2)}) collective-permute-start(bf16[64,512]{1,0:T(8,128)(2,1)S(1)} %sum_z.1.a), channel_id=1, source_target_pairs={{0,72},{8,64},{64,8},{72,0},{1,73},{9,65},{65,9},{73,1},{2,74},{10... | collective-permute-start | bytes 196616 | tf_op jit(solution)/shard_map/ppermute | solution.py:351
  82.2 6.6 %collective-permute-start.21 = (bf16[64,512]{1,0:T(8,128)(2,1)S(1)}, bf16[64,512]{1,0:T(8,128)(2,1)S(1)}, u32[]{:S(2)}, u32[]{:S(2)}) collective-permute-start(bf16[64,512]{1,0:T(8,128)(2,1)S(1)} %sum_z.1.a), channel_id=1, source_target_pairs={{0,64},{8,72},{64,0},{72,8},{1,65},{9,73},{65,1},{73,9},{2,66},{10... | collective-permute-start | bytes 196616 | tf_op jit(solution)/shard_map/ppermute | solution.py:351
  82.7 7.4 %collective-permute-start.20 = (bf16[64,512]{1,0:T(8,128)(2,1)S(1)}, bf16[64,512]{1,0:T(8,128)(2,1)S(1)}, u32[]{:S(2)}, u32[]{:S(2)}) collective-permute-start(bf16[64,512]{1,0:T(8,128)(2,1)S(1)} %sum_z.1.a), channel_id=1, source_target_pairs={{0,8},{8,0},{64,72},{72,64},{1,9},{9,1},{65,73},{73,65},{2,10},{10... | collective-permute-start | bytes 196616 | tf_op jit(solution)/shard_map/ppermute | solution.py:351
  90.2 8.9 %collective-permute-start.23 = (bf16[8,192,512]{2,1,0:T(8,128)(2,1)S(1)}, bf16[8,192,512]{2,1,0:T(8,128)(2,1)S(1)}, u32[]{:S(2)}, u32[]{:S(2)}) collective-permute-start(bf16[8,192,512]{2,1,0:T(8,128)(2,1)S(1)} %all-to-all-done.rows), channel_id=1, source_target_pairs={{0,1},{1,0},{2,3},{3,2},{4,5},{5,4},{6,7},{7,6},{8,9},{9,8},{10,11... | collective-permute-start | bytes 4718600 | tf_op jit(solution)/shard_map/ppermute | solution.py:351
  90.3 5.0 %collective-permute-start.24 = (bf16[64,512]{1,0:T(8,128)(2,1)S(1)}, bf16[64,512]{1,0:T(8,128)(2,1)S(1)}, u32[]{:S(2)}, u32[]{:S(2)}) collective-permute-start(bf16[64,512]{1,0:T(8,128)(2,1)S(1)} %sum_y.1.first), channel_id=1, source_target_pairs={{0,16},{16,0},{32,48},{48,32},{1,17},{17,1},{33,49},{49,33},{2,18}... | collective-permute-start | bytes 196616 | tf_op jit(solution)/shard_map/ppermute | solution.py:351
  95.3 7.6 %collective-permute-start.25 = (bf16[128,512]{1,0:T(8,128)(2,1)S(1)}, bf16[128,512]{1,0:T(8,128)(2,1)S(1)}, u32[]{:S(2)}, u32[]{:S(2)}) collective-permute-start(bf16[128,512]{1,0:T(8,128)(2,1)S(1)} %double.1.low), channel_id=1, source_target_pairs={{0,32},{16,48},{32,0},{48,16},{1,33},{17,49},{33,1},{49,17},{2,34}... | collective-permute-start | bytes 393224 | tf_op jit(solution)/shard_map/ppermute | solution.py:351
  102.9 24.4 %all-to-all-start.1 = ((bf16[8,192,512]{2,1,0:T(8,128)(2,1)}), bf16[8,192,512]{2,1,0:T(8,128)(2,1)S(1)}, u32[]{:S(2)}, u32[]{:S(2)}) async-start(bf16[8,192,512]{2,1,0:T(8,128)(2,1)} %up_far.1), calls=%async_computation.1 | async-start | bytes 3145728 | tf_op jit(solution)/shard_map/all_to_all | solution.py:347
  107.5 5.5 %collective-permute-start.26 = (bf16[256,128]{1,0:T(8,128)(2,1)S(1)}, bf16[256,128]{1,0:T(8,128)(2,1)S(1)}, u32[]{:S(2)}, u32[]{:S(2)}) collective-permute-start(bf16[256,128]{1,0:T(8,128)(2,1)S(1)} %get-tuple-element.111), channel_id=1, source_target_pairs={{0,2},{2,4},{4,6},{6,0},{1,3},{3,5},{5,7},{7,1},{8,10},{10,12},{12... | collective-permute-start | bytes 196616 | tf_op jit(solution)/shard_map/ppermute | solution.py:381
  108.0 5.8 %collective-permute-start.27 = (bf16[256,128]{1,0:T(8,128)(2,1)S(1)}, bf16[256,128]{1,0:T(8,128)(2,1)S(1)}, u32[]{:S(2)}, u32[]{:S(2)}) collective-permute-start(bf16[256,128]{1,0:T(8,128)(2,1)S(1)} %get-tuple-element.112), channel_id=1, source_target_pairs={{0,4},{2,6},{4,0},{6,2},{1,5},{3,7},{5,1},{7,3},{8,12},{10,14},{12... | collective-permute-start | bytes 196616 | tf_op jit(solution)/shard_map/ppermute | solution.py:381
  109.6 5.0 %collective-permute-start.28 = (bf16[256,128]{1,0:T(8,128)(2,1)S(1)}, bf16[256,128]{1,0:T(8,128)(2,1)S(1)}, u32[]{:S(2)}, u32[]{:S(2)}) collective-permute-start(bf16[256,128]{1,0:T(8,128)(2,1)S(1)} %get-tuple-element.113), channel_id=1, source_target_pairs={{0,6},{2,0},{4,2},{6,4},{1,7},{3,1},{5,3},{7,5},{8,14},{10,8},{12,... | collective-permute-start | bytes 196616 | tf_op jit(solution)/shard_map/ppermute | solution.py:381
  114.6 5.5 %collective-permute-start.31 = (bf16[256,128]{1,0:T(8,128)(2,1)S(1)}, bf16[256,128]{1,0:T(8,128)(2,1)S(1)}, u32[]{:S(2)}, u32[]{:S(2)}) collective-permute-start(bf16[256,128]{1,0:T(8,128)(2,1)S(1)} %sum_x.1.refs_0_), channel_id=1, source_target_pairs={{0,2},{2,4},{4,6},{6,0},{1,3},{3,5},{5,7},{7,1},{8,10},{10,12},{12... | collective-permute-start | bytes 196616 | tf_op jit(solution)/shard_map/ppermute | solution.py:388
  116.0 5.8 %collective-permute-start.30 = (bf16[256,128]{1,0:T(8,128)(2,1)S(1)}, bf16[256,128]{1,0:T(8,128)(2,1)S(1)}, u32[]{:S(2)}, u32[]{:S(2)}) collective-permute-start(bf16[256,128]{1,0:T(8,128)(2,1)S(1)} %sum_x.1.refs_0_), channel_id=1, source_target_pairs={{0,4},{2,6},{4,0},{6,2},{1,5},{3,7},{5,1},{7,3},{8,12},{10,14},{12... | collective-permute-start | bytes 196616 | tf_op jit(solution)/shard_map/ppermute | solution.py:388
  118.6 4.3 %collective-permute-start.29 = (bf16[256,128]{1,0:T(8,128)(2,1)S(1)}, bf16[256,128]{1,0:T(8,128)(2,1)S(1)}, u32[]{:S(2)}, u32[]{:S(2)}) collective-permute-start(bf16[256,128]{1,0:T(8,128)(2,1)S(1)} %sum_x.1.refs_0_), channel_id=1, source_target_pairs={{0,6},{2,0},{4,2},{6,4},{1,7},{3,1},{5,3},{7,5},{8,14},{10,8},{12,... | collective-permute-start | bytes 196616 | tf_op jit(solution)/shard_map/ppermute | solution.py:388
  (9 other events, 87.1 us)

commit v11 on v9

--- a/solution.py
+++ b/solution.py
@@ -77,11 +77,20 @@
     return (lax.axis_index("y_hi") ^ apart) * RING + ((lax.axis_index("x") + ahead) & (RING - 1))
 
 
-def build_kernel(part, coords, counts, values, *rest):
+def build_places(coords, counts):
+    per_owner = OWN // SIDE
+    block_row, block_col = coords[0, 0, 0], coords[0, 0, 1]
+    live = lax.iota(jnp.int32, block_row.shape[0]) < counts[0, 0]
+    owner = block_row // per_owner
+    half = (owner + lax.axis_index("core")) & 1
+    at_row = (half * PEERS + leaving_place(owner >> 1)) * per_owner + block_row % per_owner
+    at_col = relative(block_col // per_owner, *ROW) * per_owner + block_col % per_owner
+    return jnp.where(live, at_row + (at_col << 8), 1 << 16)
+
+
+def build_kernel(part, places, counts, values, *rest):
     dense = rest[-1]
     rows, cols = dense.shape
-    per_owner = OWN // SIDE
-    me_core = lax.axis_index("core")
 
     if part == 0:
 
@@ -89,10 +98,8 @@
         def _(r):
             dense[pl.ds(pl.multiple_of(r * SIDE, SIDE), SIDE), :] = jnp.zeros((SIDE, cols), dense.dtype)
 
-    count = counts[0, 0]
     lane = lax.broadcasted_iota(jnp.int32, (SIDE, 2 * SIDE), 1)
-
-    groups = (count + 15) >> 4
+    groups = (counts[0, 0] + 15) >> 4
 
     @pl.loop((groups * part) // PARTS, (groups * (part + 1)) // PARTS)
     def _(g):
@@ -100,29 +107,24 @@
         pairs = group.astype(jnp.float32).reshape(16, SIDE // 2, 2 * SIDE)
         for k in range(16):
             slot = g * 16 + k
-            live = slot < count
-            block_row = jnp.where(live, coords[0, 0, 0, slot], 0)
-            block_col = jnp.where(live, coords[0, 0, 1, slot], 0)
-            owner = block_row // per_owner
-            half = (owner + me_core) & 1
-            at_row = (half * PEERS + leaving_place(owner >> 1)) * per_owner + block_row % per_owner
-            at_col = relative(block_col // per_owner, *ROW) * per_owner + block_col % per_owner
+            code = places[slot]
+            at_row, at_col = code & 255, (code >> 8) & 255
+            row, col = at_row * SIDE, (at_col >> 1) * 2 * SIDE
             odd = (at_col & 1) == 1
+            first = (at_col & 1) * SIDE + (code >> 16) * 4 * SIDE
             plain = pairs[k]
             turned = pltpu.roll(plain, SIDE, 1)
             block = jnp.concatenate(
                 [jnp.where(odd, turned, plain), jnp.where(odd, plain, turned)], axis=0
             ).astype(dense.dtype)
-            first = jnp.where(live, (at_col & 1) * SIDE, 4 * SIDE)
             mask = (lane >= first) & (lane < first + SIDE)
             place = dense.at[
-                pl.ds(pl.multiple_of(at_row * SIDE, SIDE), SIDE),
-                pl.ds(pl.multiple_of((at_col >> 1) * 2 * SIDE, 2 * SIDE), 2 * SIDE),
+                pl.ds(pl.multiple_of(row, SIDE), SIDE), pl.ds(pl.multiple_of(col, 2 * SIDE), 2 * SIDE)
             ]
             place[...] = jnp.where(mask, block, place[...])
 
 
-def build(part, coords, counts, values, *dense):
+def build(part, places, counts, values, *dense):
     vmem = pl.BlockSpec(memory_space=pltpu.VMEM)
     return pl.pallas_call(
         functools.partial(build_kernel, part),
@@ -133,7 +135,7 @@
         compiler_params=pltpu.CompilerParams(vmem_limit_bytes=16 << 20),
         cost_estimate=pl.CostEstimate(flops=0, bytes_accessed=8 << 20, transcendentals=0),
         name=f"build_{part}",
-    )(coords, counts, values, *dense)
+    )(places, counts, values, *dense)
 
 
 def over_rows(a, b):
@@ -214,8 +216,10 @@
         far = vmem_call(kernel, bf16(count * OWN, WIDTH), f"down_far_{n}", flops=2 * count * OWN * LAST * WIDTH)(
             dense, block, most
         )
-        far, most = lax.optimization_barrier((far, most))
-        others.append(trade(far, "core"))
+        other = trade(far, "core")
+        if n == 0:
+            other, most = lax.optimization_barrier((other, most))
+        others.append(other)
 
     def near(n):
         first, count = runs[n]
@@ -385,7 +389,7 @@
 
 
 def per_device(features, out_grad, weight, block_values, block_coords, block_counts):
-    raw = (block_coords, block_counts, block_values)
+    raw = (build_places(block_coords, block_counts), block_counts, block_values)
     tasks = (
         lambda blocks, dense: build(0, *raw),
         lambda blocks, dense: build(1, *raw, dense),

time: 129 us -> 127 us (0.984)
  starting transfers between devices: 55.5 us -> 52.7 us
  other arithmetic: 0.88 us -> 2.48 us
    ppermute x17, starting transfers between devices: 22.8 us -> 19.8 us  [trade(): lax.ppermute(array, axes, [(i, i ^ bits) for i in range(lax.axis_size(axe...]
    ppermute x5, starting transfers between devices: 6.19 us -> 7.6 us  [pass_on(): lax.ppermute(array, fast, [(i, (i + step) % RING) for i in range(RING)])]
  transfers between devices with their start and end apart: 35 -> 35, of which waited for: 24 -> 24; matrix products, arithmetic and copies ran while one was open for 0% -> 1% of each run, Pallas kernels for 15% -> 16%
where the time goes in v11:
time: 127 us; the launch traced here: 126 us
  starting transfers between devices  52.7 us (41%)
  waiting for transfers between devices  44.8 us (35%)
  Pallas kernels  22.6 us (18%)
  other arithmetic  2.48 us (2%)
  local copies, waits for them, and re-layouts  1.68 us (1%)
  between operations  1.53 us (1%)
    ppermute x17, waiting for transfers between devices, trade(): lax.ppermute(array, axes, [(i, i ^ bits) for i in range(lax.axis_size(axe...  22.8 us
    ppermute x17, starting transfers between devices, trade(): lax.ppermute(array, axes, [(i, i ^ bits) for i in range(lax.axis_size(axe...  19.8 us
    pallas_call x18, Pallas kernels, call(): pl.pallas_call(kernel, out_shape=outs, in_specs=[vmem] * len(args), out_s...  14.3 us
    all_to_all x2, starting transfers between devices, exchange(): return lax.all_to_all(parts, axes, 0, 0)  8.84 us
    ppermute x5, starting transfers between devices, ahead(): lax.ppermute(array, fast, [(i, (i - step) % RING) for i in range(RING)])  8.4 us
    ppermute x5, waiting for transfers between devices, pass_on(): lax.ppermute(array, fast, [(i, (i + step) % RING) for i in range(RING)])  8.07 us
    ppermute x5, starting transfers between devices, pass_on(): lax.ppermute(array, fast, [(i, (i + step) % RING) for i in range(RING)])  7.6 us
    ppermute x5, waiting for transfers between devices, ahead(): lax.ppermute(array, fast, [(i, (i - step) % RING) for i in range(RING)])  5.08 us
  transfers between devices with their start and end apart: 35, of which 24 were waited for; matrix products, arithmetic and copies ran while one was open for 1% of the time, Pallas kernels for 16%

profile of v11, /device:TPU:0, one launch (start us, length us, event | category | flops | bytes accessed | tf_op | source)
XLA Modules:
  0.0 125.8 jit_solution(17650441143836848411)
XLA Ops:
  0.6 2.1 %collective-permute-start.1 = (bf16[192,512]{1,0:T(8,128)(2,1)}, bf16[192,512]{1,0:T(8,128)(2,1)S(1)}, u32[]{:S(2)}, u32[]{:S(2)}) collective-permute-start(bf16[192,512]{1,0:T(8,128)(2,1)} %refs_1_.1), channel_id=1, source_target_pairs={{0,16},{16,32},{32,48},{48,0},{1,17},{17,33},{33,49},{49,1},{2,18}... | collective-permute-start | bytes 589832 | tf_op jit(solution)/shard_map/ppermute | solution.py:361
  4.3 2.2 %collective-permute-start.2 = (bf16[192,512]{1,0:T(8,128)(2,1)}, bf16[192,512]{1,0:T(8,128)(2,1)S(1)}, u32[]{:S(2)}, u32[]{:S(2)}) collective-permute-start(bf16[192,512]{1,0:T(8,128)(2,1)} %refs_1_.1), channel_id=1, source_target_pairs={{0,48},{16,0},{32,16},{48,32},{1,49},{17,1},{33,17},{49,33},{2,50}... | collective-permute-start | bytes 589832 | tf_op jit(solution)/shard_map/ppermute | solution.py:361
  8.8 1.7 %copy-done.1 = bf16[1,1,288,4096]{3,2,1,0:T(8,128)(2,1)S(1)} copy-done((bf16[1,1,288,4096]{3,2,1,0:T(8,128)(2,1)S(1)}, bf16[1,1,288,4096]{3,2,1,0:T(8,128)(2,1)}, u32[]{:S(2)}) %copy-start.1) | copy-done | bytes 2359320
  10.4 2.1 %build_0.1.rest_0_ = bf16[3072,1536]{1,0:T(8,128)(2,1)S(1)} custom-call(s32[288]{0:T(512)S(1)} %fusion.3.places, s32[1,1]{1,0:T(1,128)} %copy.11.counts, bf16[1,1,288,4096]{3,2,1,0:T(8,128)(2,1)S(1)} %copy-done.1), custom_call_target="tpu_custom_call" | custom-call | bytes 8388608 | tf_op jit(solution)/shard_map/build_0/pallas_call | solution.py:129
  12.6 1.8 %collective-permute-start.4 = (bf16[192,512]{1,0:T(8,128)(2,1)S(1)}, bf16[192,512]{1,0:T(8,128)(2,1)S(1)}, u32[]{:S(2)}, u32[]{:S(2)}) collective-permute-start(bf16[192,512]{1,0:T(8,128)(2,1)S(1)} %collective-permute-done.refs_5_), channel_id=1, source_target_pairs={{0,48},{16,0},{32,16},{48,32},{1,49},{17,1},{33,17},{49,33},{2,50}... | collective-permute-start | bytes 589832 | tf_op jit(solution)/shard_map/ppermute | solution.py:361
  16.2 2.9 %collective-permute-done.4.refs_6_ = bf16[192,512]{1,0:T(8,128)(2,1)S(1)} collective-permute-done((bf16[192,512]{1,0:T(8,128)(2,1)S(1)}, bf16[192,512]{1,0:T(8,128)(2,1)S(1)}, u32[]{:S(2)}, u32[]{:S(2)}) %collective-permute-start.4) | collective-permute-done | bytes 196640 | tf_op jit(solution)/shard_map/ppermute | solution.py:361
  19.1 2.2 %collective-permute-done.5.refs_4_ = bf16[192,512]{1,0:T(8,128)(2,1)S(1)} collective-permute-done((bf16[192,512]{1,0:T(8,128)(2,1)S(1)}, bf16[192,512]{1,0:T(8,128)(2,1)S(1)}, u32[]{:S(2)}, u32[]{:S(2)}) %collective-permute-start.5) | collective-permute-done | bytes 196640 | tf_op jit(solution)/shard_map/ppermute | solution.py:361
  21.3 2.0 %collective-permute-start.6 = (bf16[192,512]{1,0:T(8,128)(2,1)S(1)}, bf16[192,512]{1,0:T(8,128)(2,1)S(1)}, u32[]{:S(2)}, u32[]{:S(2)}) collective-permute-start(bf16[192,512]{1,0:T(8,128)(2,1)S(1)} %collective-permute-done.4.refs_6_), channel_id=1, source_target_pairs={{0,48},{16,0},{32,16},{48,32},{1,49},{17,1},{33,17},{49,33},{2,50}... | collective-permute-start | bytes 589832 | tf_op jit(solution)/shard_map/ppermute | solution.py:361
  23.3 5.0 %down_most.1.most = f32[3072,512]{1,0:T(8,128)S(1)} custom-call(bf16[3072,1536]{1,0:T(8,128)(2,1)S(1)} %build_1.1.refs_0_.dense, bf16[192,512]{1,0:T(8,128)(2,1)S(1)} %copy-done.4, bf16[192,512]{1,0:T(8,128)(2,1)S(1)} %collective-permute-done.2.refs_2_, bf16[192,512]{1,0:T(8,128)(2,1)S(1)} %collective-permute-done.1.refs_3_, ...), custom_call_target="tpu_custom_call" | custom-call | flops 4831838208 | bytes 1048576 | tf_op jit(solution)/shard_map/down_most/pallas_call | solution.py:33
  28.7 2.0 %collective-permute-done.7.other = bf16[576,512]{1,0:T(8,128)(2,1)S(1)} collective-permute-done((bf16[576,512]{1,0:T(8,128)(2,1)S(1)}, bf16[576,512]{1,0:T(8,128)(2,1)S(1)}, u32[]{:S(2)}, u32[]{:S(2)}) %collective-permute-start.7) | collective-permute-done | bytes 589856 | tf_op jit(solution)/shard_map/ppermute | solution.py:350
  31.7 2.7 %collective-permute-start.8 = (bf16[192,512]{1,0:T(8,128)(2,1)S(1)}, bf16[192,512]{1,0:T(8,128)(2,1)S(1)}, u32[]{:S(2)}, u32[]{:S(2)}) collective-permute-start(bf16[192,512]{1,0:T(8,128)(2,1)S(1)} %get-tuple-element.72), channel_id=1, source_target_pairs={{0,2},{2,4},{4,6},{6,0},{1,3},{3,5},{5,7},{7,1},{8,10},{10,12},{12... | collective-permute-start | bytes 589832 | tf_op jit(solution)/shard_map/ppermute | solution.py:242
  34.4 2.1 %collective-permute-start.9 = (bf16[192,512]{1,0:T(8,128)(2,1)S(1)}, bf16[192,512]{1,0:T(8,128)(2,1)S(1)}, u32[]{:S(2)}, u32[]{:S(2)}) collective-permute-start(bf16[192,512]{1,0:T(8,128)(2,1)S(1)} %get-tuple-element.73), channel_id=1, source_target_pairs={{0,8},{8,0},{1,9},{9,1},{2,10},{10,2},{3,11},{11,3},{4,12},{12,4},... | collective-permute-start | bytes 589832 | tf_op jit(solution)/shard_map/ppermute | solution.py:350
  38.5 2.0 %collective-permute-done.8.b = bf16[192,512]{1,0:T(8,128)(2,1)S(1)} collective-permute-done((bf16[192,512]{1,0:T(8,128)(2,1)S(1)}, bf16[192,512]{1,0:T(8,128)(2,1)S(1)}, u32[]{:S(2)}, u32[]{:S(2)}) %collective-permute-start.8) | collective-permute-done | bytes 196640 | tf_op jit(solution)/shard_map/ppermute | solution.py:242
  40.6 2.3 %collective-permute-done.9.d = bf16[192,512]{1,0:T(8,128)(2,1)S(1)} collective-permute-done((bf16[192,512]{1,0:T(8,128)(2,1)S(1)}, bf16[192,512]{1,0:T(8,128)(2,1)S(1)}, u32[]{:S(2)}, u32[]{:S(2)}) %collective-permute-start.9) | collective-permute-done | bytes 196640 | tf_op jit(solution)/shard_map/ppermute | solution.py:350
  44.6 2.0 %collective-permute-start.13 = (bf16[192,512]{1,0:T(8,128)(2,1)S(1)}, bf16[192,512]{1,0:T(8,128)(2,1)S(1)}, u32[]{:S(2)}, u32[]{:S(2)}) collective-permute-start(bf16[192,512]{1,0:T(8,128)(2,1)S(1)} %get-tuple-element.87), channel_id=1, source_target_pairs={{0,6},{2,0},{4,2},{6,4},{1,7},{3,1},{5,3},{7,5},{8,14},{10,8},{12,... | collective-permute-start | bytes 589832 | tf_op jit(solution)/shard_map/ppermute | solution.py:242
  46.7 5.2 %collective-permute-done.12.refs_1_ = bf16[192,512]{1,0:T(8,128)(2,1)S(1)} collective-permute-done((bf16[192,512]{1,0:T(8,128)(2,1)S(1)}, bf16[192,512]{1,0:T(8,128)(2,1)S(1)}, u32[]{:S(2)}, u32[]{:S(2)}) %collective-permute-start.12) | collective-permute-done | bytes 196640 | tf_op jit(solution)/shard_map/ppermute | solution.py:242
  51.9 2.2 %collective-permute-start.14 = (bf16[192,512]{1,0:T(8,128)(2,1)S(1)}, bf16[192,512]{1,0:T(8,128)(2,1)S(1)}, u32[]{:S(2)}, u32[]{:S(2)}) collective-permute-start(bf16[192,512]{1,0:T(8,128)(2,1)S(1)} %sum_across.1), channel_id=1, source_target_pairs={{0,8},{8,0},{1,9},{9,1},{2,10},{10,2},{3,11},{11,3},{4,12},{12,4},... | collective-permute-start | bytes 589832 | tf_op jit(solution)/shard_map/ppermute | solution.py:350
  54.6 4.6 %collective-permute-done.14.c = bf16[192,512]{1,0:T(8,128)(2,1)S(1)} collective-permute-done((bf16[192,512]{1,0:T(8,128)(2,1)S(1)}, bf16[192,512]{1,0:T(8,128)(2,1)S(1)}, u32[]{:S(2)}, u32[]{:S(2)}) %collective-permute-start.14) | collective-permute-done | bytes 196640 | tf_op jit(solution)/shard_map/ppermute | solution.py:350
  59.2 2.0 %middle.1 = (bf16[192,512]{1,0:T(8,128)(2,1)}, bf16[8,192,512]{2,1,0:T(8,128)(2,1)}, bf16[192,512]{1,0:T(8,128)(2,1)S(1)}, bf16[192,512]{1,0:T(8,128)(2,1)S(1)}) custom-call(bf16[192,512]{1,0:T(8,128)(2,1)S(1)} %get-tuple-element.80.a, bf16[192,512]{1,0:T(8,128)(2,1)S(1)} %collective-permute-done.13.b, bf16[192,512]{1,0:T(8,128)(2,1)S(1)} %collective-permute-done.14.c, ...), custom_call_target="tpu_custom_call" | custom-call | flops 201326592 | bytes 1048576 | tf_op jit(solution)/shard_map/middle/pallas_call | solution.py:33
  61.2 4.6 %all-to-all-start = ((bf16[8,192,512]{2,1,0:T(8,128)(2,1)}), bf16[8,192,512]{2,1,0:T(8,128)(2,1)S(1)}, u32[]{:S(2)}, u32[]{:S(2)}) async-start(bf16[8,192,512]{2,1,0:T(8,128)(2,1)} %get-tuple-element.101), calls=%async_computation | async-start | bytes 3145728 | tf_op jit(solution)/shard_map/all_to_all | solution.py:346
  68.1 3.3 %collective-permute-start.18 = (bf16[64,512]{1,0:T(8,128)(2,1)S(1)}, bf16[64,512]{1,0:T(8,128)(2,1)S(1)}, u32[]{:S(2)}, u32[]{:S(2)}) collective-permute-start(bf16[64,512]{1,0:T(8,128)(2,1)S(1)} %get-tuple-element.99), channel_id=1, source_target_pairs={{0,32},{16,48},{32,0},{48,16},{1,33},{17,49},{33,1},{49,17},{2,34}... | collective-permute-start | bytes 196616 | tf_op jit(solution)/shard_map/ppermute | solution.py:350
  73.0 1.9 %collective-permute-done.18.refs_2_ = bf16[64,512]{1,0:T(8,128)(2,1)S(1)} collective-permute-done((bf16[64,512]{1,0:T(8,128)(2,1)S(1)}, bf16[64,512]{1,0:T(8,128)(2,1)S(1)}, u32[]{:S(2)}, u32[]{:S(2)}) %collective-permute-start.18) | collective-permute-done | bytes 65568 | tf_op jit(solution)/shard_map/ppermute | solution.py:350
  74.9 2.0 %collective-permute-done.19.refs_3_ = bf16[64,512]{1,0:T(8,128)(2,1)S(1)} collective-permute-done((bf16[64,512]{1,0:T(8,128)(2,1)S(1)}, bf16[64,512]{1,0:T(8,128)(2,1)S(1)}, u32[]{:S(2)}, u32[]{:S(2)}) %collective-permute-start.19) | collective-permute-done | bytes 65568 | tf_op jit(solution)/shard_map/ppermute | solution.py:350
  76.9 2.7 %collective-permute-start.22 = (bf16[64,512]{1,0:T(8,128)(2,1)S(1)}, bf16[64,512]{1,0:T(8,128)(2,1)S(1)}, u32[]{:S(2)}, u32[]{:S(2)}) collective-permute-start(bf16[64,512]{1,0:T(8,128)(2,1)S(1)} %sum_z.1.a), channel_id=1, source_target_pairs={{0,72},{8,64},{64,8},{72,0},{1,73},{9,65},{65,9},{73,1},{2,74},{10... | collective-permute-start | bytes 196616 | tf_op jit(solution)/shard_map/ppermute | solution.py:350
  81.7 5.2 %collective-permute-done.22.d = bf16[64,512]{1,0:T(8,128)(2,1)S(1)} collective-permute-done((bf16[64,512]{1,0:T(8,128)(2,1)S(1)}, bf16[64,512]{1,0:T(8,128)(2,1)S(1)}, u32[]{:S(2)}, u32[]{:S(2)}) %collective-permute-start.22) | collective-permute-done | bytes 65568 | tf_op jit(solution)/shard_map/ppermute | solution.py:350
  88.5 4.8 %up_near.1 = (f32[1536,512]{1,0:T(8,128)S(1)}, bf16[1536,1536]{1,0:T(8,128)(2,1)S(1)}) custom-call(bf16[3072,1536]{1,0:T(8,128)(2,1)} %copy-done, bf16[8,192,512]{2,1,0:T(8,128)(2,1)S(1)} %all-to-all-done.rows), custom_call_target="tpu_custom_call" | custom-call | flops 2415919104 | bytes 12582912 | tf_op jit(solution)/shard_map/up_near/pallas_call | solution.py:436
  93.4 3.3 %collective-permute-start.25 = (bf16[128,512]{1,0:T(8,128)(2,1)S(1)}, bf16[128,512]{1,0:T(8,128)(2,1)S(1)}, u32[]{:S(2)}, u32[]{:S(2)}) collective-permute-start(bf16[128,512]{1,0:T(8,128)(2,1)S(1)} %double.1.low), channel_id=1, source_target_pairs={{0,32},{16,48},{32,0},{48,16},{1,33},{17,49},{33,1},{49,17},{2,34}... | collective-permute-start | bytes 393224 | tf_op jit(solution)/shard_map/ppermute | solution.py:350
  96.7 3.8 %up_far.1 = bf16[8,192,512]{2,1,0:T(8,128)(2,1)} custom-call(bf16[1536,1536]{1,0:T(8,128)(2,1)S(1)} %get-tuple-element.103.tile, bf16[8,192,512]{2,1,0:T(8,128)(2,1)S(1)} %collective-permute-done.23.rows, f32[1536,512]{1,0:T(8,128)S(1)} %get-tuple-element.106.other), custom_call_target="tpu_custom_call" | custom-call | flops 2415919104 | bytes 1048576 | tf_op jit(solution)/shard_map/up_far/pallas_call | solution.py:33
  100.8 4.3 %all-to-all-start.1 = ((bf16[8,192,512]{2,1,0:T(8,128)(2,1)}), bf16[8,192,512]{2,1,0:T(8,128)(2,1)S(1)}, u32[]{:S(2)}, u32[]{:S(2)}) async-start(bf16[8,192,512]{2,1,0:T(8,128)(2,1)} %up_far.1), calls=%async_computation.1 | async-start | bytes 3145728 | tf_op jit(solution)/shard_map/all_to_all | solution.py:346
  105.8 1.8 %collective-permute-start.27 = (bf16[256,128]{1,0:T(8,128)(2,1)S(1)}, bf16[256,128]{1,0:T(8,128)(2,1)S(1)}, u32[]{:S(2)}, u32[]{:S(2)}) collective-permute-start(bf16[256,128]{1,0:T(8,128)(2,1)S(1)} %get-tuple-element.112), channel_id=1, source_target_pairs={{0,4},{2,6},{4,0},{6,2},{1,5},{3,7},{5,1},{7,3},{8,12},{10,14},{12... | collective-permute-start | bytes 196616 | tf_op jit(solution)/shard_map/ppermute | solution.py:380
  109.0 1.6 %collective-permute-done.26.refs_1_ = bf16[256,128]{1,0:T(8,128)(2,1)S(1)} collective-permute-done((bf16[256,128]{1,0:T(8,128)(2,1)S(1)}, bf16[256,128]{1,0:T(8,128)(2,1)S(1)}, u32[]{:S(2)}, u32[]{:S(2)}) %collective-permute-start.26) | collective-permute-done | bytes 65568 | tf_op jit(solution)/shard_map/ppermute | solution.py:380
  113.6 2.8 %collective-permute-start.30 = (bf16[256,128]{1,0:T(8,128)(2,1)S(1)}, bf16[256,128]{1,0:T(8,128)(2,1)S(1)}, u32[]{:S(2)}, u32[]{:S(2)}) collective-permute-start(bf16[256,128]{1,0:T(8,128)(2,1)S(1)} %sum_x.1.refs_0_), channel_id=1, source_target_pairs={{0,4},{2,6},{4,0},{6,2},{1,5},{3,7},{5,1},{7,3},{8,12},{10,14},{12... | collective-permute-start | bytes 196616 | tf_op jit(solution)/shard_map/ppermute | solution.py:387
  (73 shorter events, 33.1 us)
Async XLA Ops:
  0.6 11.9 %collective-permute-start.1 = (bf16[192,512]{1,0:T(8,128)(2,1)}, bf16[192,512]{1,0:T(8,128)(2,1)S(1)}, u32[]{:S(2)}, u32[]{:S(2)}) collective-permute-start(bf16[192,512]{1,0:T(8,128)(2,1)} %refs_1_.1), channel_id=1, source_target_pairs={{0,16},{16,32},{32,48},{48,0},{1,17},{17,33},{33,49},{49,1},{2,18}... | collective-permute-start | bytes 589832 | tf_op jit(solution)/shard_map/ppermute | solution.py:361
  2.7 9.8 %collective-permute-start = (bf16[192,512]{1,0:T(8,128)(2,1)}, bf16[192,512]{1,0:T(8,128)(2,1)S(1)}, u32[]{:S(2)}, u32[]{:S(2)}) collective-permute-start(bf16[192,512]{1,0:T(8,128)(2,1)} %refs_1_.1), channel_id=1, source_target_pairs={{0,64},{64,0},{1,65},{65,1},{2,66},{66,2},{3,67},{67,3},{4,68},{68... | collective-permute-start | bytes 589832 | tf_op jit(solution)/shard_map/ppermute | solution.py:350
  4.3 8.3 %collective-permute-start.2 = (bf16[192,512]{1,0:T(8,128)(2,1)}, bf16[192,512]{1,0:T(8,128)(2,1)S(1)}, u32[]{:S(2)}, u32[]{:S(2)}) collective-permute-start(bf16[192,512]{1,0:T(8,128)(2,1)} %refs_1_.1), channel_id=1, source_target_pairs={{0,48},{16,0},{32,16},{48,32},{1,49},{17,1},{33,17},{49,33},{2,50}... | collective-permute-start | bytes 589832 | tf_op jit(solution)/shard_map/ppermute | solution.py:361
  12.6 6.5 %collective-permute-start.4 = (bf16[192,512]{1,0:T(8,128)(2,1)S(1)}, bf16[192,512]{1,0:T(8,128)(2,1)S(1)}, u32[]{:S(2)}, u32[]{:S(2)}) collective-permute-start(bf16[192,512]{1,0:T(8,128)(2,1)S(1)} %collective-permute-done.refs_5_), channel_id=1, source_target_pairs={{0,48},{16,0},{32,16},{48,32},{1,49},{17,1},{33,17},{49,33},{2,50}... | collective-permute-start | bytes 589832 | tf_op jit(solution)/shard_map/ppermute | solution.py:361
  14.4 6.9 %collective-permute-start.5 = (bf16[192,512]{1,0:T(8,128)(2,1)S(1)}, bf16[192,512]{1,0:T(8,128)(2,1)S(1)}, u32[]{:S(2)}, u32[]{:S(2)}) collective-permute-start(bf16[192,512]{1,0:T(8,128)(2,1)S(1)} %collective-permute-done.1.refs_3_), channel_id=1, source_target_pairs={{0,16},{16,32},{32,48},{48,0},{1,17},{17,33},{33,49},{49,1},{2,18}... | collective-permute-start | bytes 589832 | tf_op jit(solution)/shard_map/ppermute | solution.py:361
  14.7 6.6 %collective-permute-start.3 = (bf16[192,512]{1,0:T(8,128)(2,1)S(1)}, bf16[192,512]{1,0:T(8,128)(2,1)S(1)}, u32[]{:S(2)}, u32[]{:S(2)}) collective-permute-start(bf16[192,512]{1,0:T(8,128)(2,1)S(1)} %collective-permute-done.1.refs_3_), channel_id=1, source_target_pairs={{0,64},{64,0},{1,65},{65,1},{2,66},{66,2},{3,67},{67,3},{4,68},{68... | collective-permute-start | bytes 589832 | tf_op jit(solution)/shard_map/ppermute | solution.py:350
  21.3 7.1 %collective-permute-start.6 = (bf16[192,512]{1,0:T(8,128)(2,1)S(1)}, bf16[192,512]{1,0:T(8,128)(2,1)S(1)}, u32[]{:S(2)}, u32[]{:S(2)}) collective-permute-start(bf16[192,512]{1,0:T(8,128)(2,1)S(1)} %collective-permute-done.4.refs_6_), channel_id=1, source_target_pairs={{0,48},{16,0},{32,16},{48,32},{1,49},{17,1},{33,17},{49,33},{2,50}... | collective-permute-start | bytes 589832 | tf_op jit(solution)/shard_map/ppermute | solution.py:361
  31.2 6.9 %collective-permute-start.11 = (bf16[960,512]{1,0:T(8,128)(2,1)S(1)}, bf16[960,512]{1,0:T(8,128)(2,1)S(1)}, u32[]{:S(2)}, u32[]{:S(2)}) collective-permute-start(bf16[960,512]{1,0:T(8,128)(2,1)S(1)} %down_far_1.1), channel_id=1, source_target_pairs={{0,1},{1,0},{2,3},{3,2},{4,5},{5,4},{6,7},{7,6},{8,9},{9,8},{10,11... | collective-permute-start | bytes 2949128 | tf_op jit(solution)/shard_map/ppermute | solution.py:350
  31.7 8.8 %collective-permute-start.8 = (bf16[192,512]{1,0:T(8,128)(2,1)S(1)}, bf16[192,512]{1,0:T(8,128)(2,1)S(1)}, u32[]{:S(2)}, u32[]{:S(2)}) collective-permute-start(bf16[192,512]{1,0:T(8,128)(2,1)S(1)} %get-tuple-element.72), channel_id=1, source_target_pairs={{0,2},{2,4},{4,6},{6,0},{1,3},{3,5},{5,7},{7,1},{8,10},{10,12},{12... | collective-permute-start | bytes 589832 | tf_op jit(solution)/shard_map/ppermute | solution.py:242
  34.4 8.4 %collective-permute-start.9 = (bf16[192,512]{1,0:T(8,128)(2,1)S(1)}, bf16[192,512]{1,0:T(8,128)(2,1)S(1)}, u32[]{:S(2)}, u32[]{:S(2)}) collective-permute-start(bf16[192,512]{1,0:T(8,128)(2,1)S(1)} %get-tuple-element.73), channel_id=1, source_target_pairs={{0,8},{8,0},{1,9},{9,1},{2,10},{10,2},{3,11},{11,3},{4,12},{12,4},... | collective-permute-start | bytes 589832 | tf_op jit(solution)/shard_map/ppermute | solution.py:350
  36.6 6.6 %collective-permute-start.10 = (bf16[192,512]{1,0:T(8,128)(2,1)S(1)}, bf16[192,512]{1,0:T(8,128)(2,1)S(1)}, u32[]{:S(2)}, u32[]{:S(2)}) collective-permute-start(bf16[192,512]{1,0:T(8,128)(2,1)S(1)} %get-tuple-element.74), channel_id=1, source_target_pairs={{0,6},{2,0},{4,2},{6,4},{1,7},{3,1},{5,3},{7,5},{8,14},{10,8},{12,... | collective-permute-start | bytes 589832 | tf_op jit(solution)/shard_map/ppermute | solution.py:242
  43.3 8.6 %collective-permute-start.12 = (bf16[192,512]{1,0:T(8,128)(2,1)S(1)}, bf16[192,512]{1,0:T(8,128)(2,1)S(1)}, u32[]{:S(2)}, u32[]{:S(2)}) collective-permute-start(bf16[192,512]{1,0:T(8,128)(2,1)S(1)} %get-tuple-element.86), channel_id=1, source_target_pairs={{0,2},{2,4},{4,6},{6,0},{1,3},{3,5},{5,7},{7,1},{8,10},{10,12},{12... | collective-permute-start | bytes 589832 | tf_op jit(solution)/shard_map/ppermute | solution.py:242
  44.6 7.2 %collective-permute-start.13 = (bf16[192,512]{1,0:T(8,128)(2,1)S(1)}, bf16[192,512]{1,0:T(8,128)(2,1)S(1)}, u32[]{:S(2)}, u32[]{:S(2)}) collective-permute-start(bf16[192,512]{1,0:T(8,128)(2,1)S(1)} %get-tuple-element.87), channel_id=1, source_target_pairs={{0,6},{2,0},{4,2},{6,4},{1,7},{3,1},{5,3},{7,5},{8,14},{10,8},{12,... | collective-permute-start | bytes 589832 | tf_op jit(solution)/shard_map/ppermute | solution.py:242
  46.6 8.0 %collective-permute-start.15 = (bf16[192,512]{1,0:T(8,128)(2,1)S(1)}, bf16[192,512]{1,0:T(8,128)(2,1)S(1)}, u32[]{:S(2)}, u32[]{:S(2)}) collective-permute-start(bf16[192,512]{1,0:T(8,128)(2,1)S(1)} %get-tuple-element.91), channel_id=1, source_target_pairs={{0,2},{2,4},{4,6},{6,0},{1,3},{3,5},{5,7},{7,1},{8,10},{10,12},{12... | collective-permute-start | bytes 589832 | tf_op jit(solution)/shard_map/ppermute | solution.py:242
  51.9 7.3 %collective-permute-start.14 = (bf16[192,512]{1,0:T(8,128)(2,1)S(1)}, bf16[192,512]{1,0:T(8,128)(2,1)S(1)}, u32[]{:S(2)}, u32[]{:S(2)}) collective-permute-start(bf16[192,512]{1,0:T(8,128)(2,1)S(1)} %sum_across.1), channel_id=1, source_target_pairs={{0,8},{8,0},{1,9},{9,1},{2,10},{10,2},{3,11},{11,3},{4,12},{12,4},... | collective-permute-start | bytes 589832 | tf_op jit(solution)/shard_map/ppermute | solution.py:350
  61.2 27.1 %all-to-all-start = ((bf16[8,192,512]{2,1,0:T(8,128)(2,1)}), bf16[8,192,512]{2,1,0:T(8,128)(2,1)S(1)}, u32[]{:S(2)}, u32[]{:S(2)}) async-start(bf16[8,192,512]{2,1,0:T(8,128)(2,1)} %get-tuple-element.101), calls=%async_computation | async-start | bytes 3145728 | tf_op jit(solution)/shard_map/all_to_all | solution.py:346
  68.1 5.0 %collective-permute-start.17 = (bf16[64,512]{1,0:T(8,128)(2,1)S(1)}, bf16[64,512]{1,0:T(8,128)(2,1)S(1)}, u32[]{:S(2)}, u32[]{:S(2)}) collective-permute-start(bf16[64,512]{1,0:T(8,128)(2,1)S(1)} %get-tuple-element.98), channel_id=1, source_target_pairs={{0,16},{16,0},{32,48},{48,32},{1,17},{17,1},{33,49},{49,33},{2,18}... | collective-permute-start | bytes 196616 | tf_op jit(solution)/shard_map/ppermute | solution.py:350
  68.1 6.8 %collective-permute-start.18 = (bf16[64,512]{1,0:T(8,128)(2,1)S(1)}, bf16[64,512]{1,0:T(8,128)(2,1)S(1)}, u32[]{:S(2)}, u32[]{:S(2)}) collective-permute-start(bf16[64,512]{1,0:T(8,128)(2,1)S(1)} %get-tuple-element.99), channel_id=1, source_target_pairs={{0,32},{16,48},{32,0},{48,16},{1,33},{17,49},{33,1},{49,17},{2,34}... | collective-permute-start | bytes 196616 | tf_op jit(solution)/shard_map/ppermute | solution.py:350
  71.4 5.5 %collective-permute-start.19 = (bf16[64,512]{1,0:T(8,128)(2,1)S(1)}, bf16[64,512]{1,0:T(8,128)(2,1)S(1)}, u32[]{:S(2)}, u32[]{:S(2)}) collective-permute-start(bf16[64,512]{1,0:T(8,128)(2,1)S(1)} %get-tuple-element.100), channel_id=1, source_target_pairs={{0,48},{16,32},{32,16},{48,0},{1,49},{17,33},{33,17},{49,1},{2,50}... | collective-permute-start | bytes 196616 | tf_op jit(solution)/shard_map/ppermute | solution.py:350
  76.9 10.0 %collective-permute-start.22 = (bf16[64,512]{1,0:T(8,128)(2,1)S(1)}, bf16[64,512]{1,0:T(8,128)(2,1)S(1)}, u32[]{:S(2)}, u32[]{:S(2)}) collective-permute-start(bf16[64,512]{1,0:T(8,128)(2,1)S(1)} %sum_z.1.a), channel_id=1, source_target_pairs={{0,72},{8,64},{64,8},{72,0},{1,73},{9,65},{65,9},{73,1},{2,74},{10... | collective-permute-start | bytes 196616 | tf_op jit(solution)/shard_map/ppermute | solution.py:350
  79.6 7.3 %collective-permute-start.21 = (bf16[64,512]{1,0:T(8,128)(2,1)S(1)}, bf16[64,512]{1,0:T(8,128)(2,1)S(1)}, u32[]{:S(2)}, u32[]{:S(2)}) collective-permute-start(bf16[64,512]{1,0:T(8,128)(2,1)S(1)} %sum_z.1.a), channel_id=1, source_target_pairs={{0,64},{8,72},{64,0},{72,8},{1,65},{9,73},{65,1},{73,9},{2,66},{10... | collective-permute-start | bytes 196616 | tf_op jit(solution)/shard_map/ppermute | solution.py:350
  80.5 7.7 %collective-permute-start.20 = (bf16[64,512]{1,0:T(8,128)(2,1)S(1)}, bf16[64,512]{1,0:T(8,128)(2,1)S(1)}, u32[]{:S(2)}, u32[]{:S(2)}) collective-permute-start(bf16[64,512]{1,0:T(8,128)(2,1)S(1)} %sum_z.1.a), channel_id=1, source_target_pairs={{0,8},{8,0},{64,72},{72,64},{1,9},{9,1},{65,73},{73,65},{2,10},{10... | collective-permute-start | bytes 196616 | tf_op jit(solution)/shard_map/ppermute | solution.py:350
  88.3 8.4 %collective-permute-start.23 = (bf16[8,192,512]{2,1,0:T(8,128)(2,1)S(1)}, bf16[8,192,512]{2,1,0:T(8,128)(2,1)S(1)}, u32[]{:S(2)}, u32[]{:S(2)}) collective-permute-start(bf16[8,192,512]{2,1,0:T(8,128)(2,1)S(1)} %all-to-all-done.rows), channel_id=1, source_target_pairs={{0,1},{1,0},{2,3},{3,2},{4,5},{5,4},{6,7},{7,6},{8,9},{9,8},{10,11... | collective-permute-start | bytes 4718600 | tf_op jit(solution)/shard_map/ppermute | solution.py:350
  88.4 4.9 %collective-permute-start.24 = (bf16[64,512]{1,0:T(8,128)(2,1)S(1)}, bf16[64,512]{1,0:T(8,128)(2,1)S(1)}, u32[]{:S(2)}, u32[]{:S(2)}) collective-permute-start(bf16[64,512]{1,0:T(8,128)(2,1)S(1)} %sum_y.1.first), channel_id=1, source_target_pairs={{0,16},{16,0},{32,48},{48,32},{1,17},{17,1},{33,49},{49,33},{2,18}... | collective-permute-start | bytes 196616 | tf_op jit(solution)/shard_map/ppermute | solution.py:350
  93.4 7.4 %collective-permute-start.25 = (bf16[128,512]{1,0:T(8,128)(2,1)S(1)}, bf16[128,512]{1,0:T(8,128)(2,1)S(1)}, u32[]{:S(2)}, u32[]{:S(2)}) collective-permute-start(bf16[128,512]{1,0:T(8,128)(2,1)S(1)} %double.1.low), channel_id=1, source_target_pairs={{0,32},{16,48},{32,0},{48,16},{1,33},{17,49},{33,1},{49,17},{2,34}... | collective-permute-start | bytes 393224 | tf_op jit(solution)/shard_map/ppermute | solution.py:350
  100.8 24.2 %all-to-all-start.1 = ((bf16[8,192,512]{2,1,0:T(8,128)(2,1)}), bf16[8,192,512]{2,1,0:T(8,128)(2,1)S(1)}, u32[]{:S(2)}, u32[]{:S(2)}) async-start(bf16[8,192,512]{2,1,0:T(8,128)(2,1)} %up_far.1), calls=%async_computation.1 | async-start | bytes 3145728 | tf_op jit(solution)/shard_map/all_to_all | solution.py:346
  105.1 5.5 %collective-permute-start.26 = (bf16[256,128]{1,0:T(8,128)(2,1)S(1)}, bf16[256,128]{1,0:T(8,128)(2,1)S(1)}, u32[]{:S(2)}, u32[]{:S(2)}) collective-permute-start(bf16[256,128]{1,0:T(8,128)(2,1)S(1)} %get-tuple-element.111), channel_id=1, source_target_pairs={{0,2},{2,4},{4,6},{6,0},{1,3},{3,5},{5,7},{7,1},{8,10},{10,12},{12... | collective-permute-start | bytes 196616 | tf_op jit(solution)/shard_map/ppermute | solution.py:380
  105.8 5.8 %collective-permute-start.27 = (bf16[256,128]{1,0:T(8,128)(2,1)S(1)}, bf16[256,128]{1,0:T(8,128)(2,1)S(1)}, u32[]{:S(2)}, u32[]{:S(2)}) collective-permute-start(bf16[256,128]{1,0:T(8,128)(2,1)S(1)} %get-tuple-element.112), channel_id=1, source_target_pairs={{0,4},{2,6},{4,0},{6,2},{1,5},{3,7},{5,1},{7,3},{8,12},{10,14},{12... | collective-permute-start | bytes 196616 | tf_op jit(solution)/shard_map/ppermute | solution.py:380
  107.5 4.7 %collective-permute-start.28 = (bf16[256,128]{1,0:T(8,128)(2,1)S(1)}, bf16[256,128]{1,0:T(8,128)(2,1)S(1)}, u32[]{:S(2)}, u32[]{:S(2)}) collective-permute-start(bf16[256,128]{1,0:T(8,128)(2,1)S(1)} %get-tuple-element.113), channel_id=1, source_target_pairs={{0,6},{2,0},{4,2},{6,4},{1,7},{3,1},{5,3},{7,5},{8,14},{10,8},{12,... | collective-permute-start | bytes 196616 | tf_op jit(solution)/shard_map/ppermute | solution.py:380
  112.2 5.5 %collective-permute-start.31 = (bf16[256,128]{1,0:T(8,128)(2,1)S(1)}, bf16[256,128]{1,0:T(8,128)(2,1)S(1)}, u32[]{:S(2)}, u32[]{:S(2)}) collective-permute-start(bf16[256,128]{1,0:T(8,128)(2,1)S(1)} %sum_x.1.refs_0_), channel_id=1, source_target_pairs={{0,2},{2,4},{4,6},{6,0},{1,3},{3,5},{5,7},{7,1},{8,10},{10,12},{12... | collective-permute-start | bytes 196616 | tf_op jit(solution)/shard_map/ppermute | solution.py:387
  113.6 5.8 %collective-permute-start.30 = (bf16[256,128]{1,0:T(8,128)(2,1)S(1)}, bf16[256,128]{1,0:T(8,128)(2,1)S(1)}, u32[]{:S(2)}, u32[]{:S(2)}) collective-permute-start(bf16[256,128]{1,0:T(8,128)(2,1)S(1)} %sum_x.1.refs_0_), channel_id=1, source_target_pairs={{0,4},{2,6},{4,0},{6,2},{1,5},{3,7},{5,1},{7,3},{8,12},{10,14},{12... | collective-permute-start | bytes 196616 | tf_op jit(solution)/shard_map/ppermute | solution.py:387
  116.4 4.3 %collective-permute-start.29 = (bf16[256,128]{1,0:T(8,128)(2,1)S(1)}, bf16[256,128]{1,0:T(8,128)(2,1)S(1)}, u32[]{:S(2)}, u32[]{:S(2)}) collective-permute-start(bf16[256,128]{1,0:T(8,128)(2,1)S(1)} %sum_x.1.refs_0_), channel_id=1, source_target_pairs={{0,6},{2,0},{4,2},{6,4},{1,7},{3,1},{5,3},{7,5},{8,14},{10,8},{12,... | collective-permute-start | bytes 196616 | tf_op jit(solution)/shard_map/ppermute | solution.py:387
  (8 other events, 85.0 us)

commit v12 on v11

--- a/solution.py
+++ b/solution.py
@@ -190,12 +190,18 @@
     copies[-1].wait()
 
 
-def up_add_kernel(tile, rows, other, out, ordered):
+def up_add_kernel(tile, rows, other, out, ordered, done, sems):
     in_order(rows, ordered)
+    copies = []
     for r in range(0, ROWS, 2 * OWN):
         total = over_rows(tile[:, r : r + 2 * OWN], ordered[...]) + other[r : r + 2 * OWN]
         for k in range(2):
-            out[absolute(r // OWN + k, *ROW)] = total[k * OWN : (k + 1) * OWN].astype(out.dtype)
+            place = r // OWN + k
+            done[place] = total[k * OWN : (k + 1) * OWN].astype(done.dtype)
+            copies.append(pltpu.make_async_copy(done.at[place], out.at[absolute(place, *ROW)], sems.at[place]))
+            copies[-1].start()
+    for copy in copies:
+        copy.wait()
 
 
 def down_most(dense, blocks):
@@ -313,6 +319,13 @@
     out[...] = total.astype(out.dtype)
 
 
+def total_kernel(parts, out):
+    total = parts[0].astype(jnp.float32)
+    for k in range(1, PEERS):
+        total = total + parts[k].astype(jnp.float32)
+    out[...] = total.astype(out.dtype)
+
+
 def square_kernel(a, b, c, d, out):
     first = a[...].astype(jnp.float32) + b[...].astype(jnp.float32)
     out[...] = (first + (c[...].astype(jnp.float32) + d[...].astype(jnp.float32))).astype(out.dtype)
@@ -449,9 +462,19 @@
     )(dense, mine)
     next_piece, own = lax.optimization_barrier((trade(summed, "z", 1), own))
     pair = vmem_call(double_kernel, bf16(2 * PIECE, WIDTH), "double")(summed, next_piece)
-    ordered = pltpu.VMEM((ROWS, WIDTH), jnp.bfloat16)
-    partial_grad = vmem_call(
-        up_add_kernel, bf16(PEERS, OWN, WIDTH), "up_far", scratch=[ordered], flops=work
+    partial_grad = pl.pallas_call(
+        up_add_kernel,
+        out_shape=bf16(PEERS, OWN, WIDTH),
+        in_specs=[vmem] * 3,
+        out_specs=pl.BlockSpec(memory_space=pltpu.HBM),
+        scratch_shapes=[
+            pltpu.VMEM((ROWS, WIDTH), jnp.bfloat16),
+            pltpu.VMEM((PEERS, OWN, WIDTH), jnp.bfloat16),
+            pltpu.SemaphoreType.DMA((PEERS,)),
+        ],
+        compiler_params=pltpu.CompilerParams(vmem_limit_bytes=16 << 20),
+        cost_estimate=pl.CostEstimate(flops=work, bytes_accessed=12 << 20, transcendentals=0),
+        name="up_far",
     )(far, theirs, own)
     pairs = (pair, trade(pair, "z", 2))
     partial_grad, *pairs = lax.optimization_barrier((partial_grad, *pairs))
@@ -466,10 +489,7 @@
         own_half, trade(own_half, "core")
     )
 
-    total = received[0].astype(jnp.float32)
-    for k in range(1, PEERS):
-        total = total + received[k].astype(jnp.float32)
-    feature_grad = total.astype(jnp.bfloat16)
+    feature_grad = vmem_call(total_kernel, bf16(OWN, WIDTH), "total")(received)
     return (activations, weight_grad, feature_grad)
 
 

time: 127 us -> 126 us (level)
  starting transfers between devices: 52.7 us -> 54.4 us
  waiting for transfers between devices: 44.8 us -> 43.1 us
    pallas_call x0 -> x1, Pallas kernels: none -> 3.38 us  [per_device(): pl.pallas_call(up_add_kernel, out_shape=bf16(PEERS, OWN, WIDTH), in_specs...]
    pallas_call x18, Pallas kernels: 14.3 us -> 11.4 us  [call(): pl.pallas_call(kernel, out_shape=outs, in_specs=[vmem] * len(args), out_s...]
  transfers between devices with their start and end apart: 35 -> 35, of which waited for: 24 -> 24; matrix products, arithmetic and copies ran while one was open for 1% -> 1% of each run, Pallas kernels for 16% -> 15%
where the time goes in v12:
time: 126 us; the launch traced here: 125 us
  starting transfers between devices  54.4 us (43%)
  waiting for transfers between devices  43.1 us (34%)
  Pallas kernels  23.1 us (18%)
  local copies, waits for them, and re-layouts  1.68 us (1%)
  other arithmetic  1.6 us (1%)
  between operations  1.53 us (1%)
    ppermute x17, waiting for transfers between devices, trade(): lax.ppermute(array, axes, [(i, i ^ bits) for i in range(lax.axis_size(axe...  22 us
    ppermute x17, starting transfers between devices, trade(): lax.ppermute(array, axes, [(i, i ^ bits) for i in range(lax.axis_size(axe...  20.9 us
    pallas_call x18, Pallas kernels, call(): pl.pallas_call(kernel, out_shape=outs, in_specs=[vmem] * len(args), out_s...  11.4 us
    all_to_all x2, starting transfers between devices, exchange(): return lax.all_to_all(parts, axes, 0, 0)  8.86 us
    ppermute x5, starting transfers between devices, ahead(): lax.ppermute(array, fast, [(i, (i - step) % RING) for i in range(RING)])  8.4 us
    ppermute x5, waiting for transfers between devices, pass_on(): lax.ppermute(array, fast, [(i, (i + step) % RING) for i in range(RING)])  8.22 us
    ppermute x5, starting transfers between devices, pass_on(): lax.ppermute(array, fast, [(i, (i + step) % RING) for i in range(RING)])  7.07 us
    ppermute x5, waiting for transfers between devices, ahead(): lax.ppermute(array, fast, [(i, (i - step) % RING) for i in range(RING)])  5.08 us
  transfers between devices with their start and end apart: 35, of which 24 were waited for; matrix products, arithmetic and copies ran while one was open for 1% of the time, Pallas kernels for 15%

profile of v12, /device:TPU:0, one launch (start us, length us, event | category | flops | bytes accessed | tf_op | source)
XLA Modules:
  0.0 125.4 jit_solution(13816748147196151382)
XLA Ops:
  0.6 2.1 %collective-permute-start.1 = (bf16[192,512]{1,0:T(8,128)(2,1)}, bf16[192,512]{1,0:T(8,128)(2,1)S(1)}, u32[]{:S(2)}, u32[]{:S(2)}) collective-permute-start(bf16[192,512]{1,0:T(8,128)(2,1)} %refs_1_.1), channel_id=1, source_target_pairs={{0,16},{16,32},{32,48},{48,0},{1,17},{17,33},{33,49},{49,1},{2,18}... | collective-permute-start | bytes 589832 | tf_op jit(solution)/shard_map/ppermute | solution.py:374
  4.3 2.2 %collective-permute-start.2 = (bf16[192,512]{1,0:T(8,128)(2,1)}, bf16[192,512]{1,0:T(8,128)(2,1)S(1)}, u32[]{:S(2)}, u32[]{:S(2)}) collective-permute-start(bf16[192,512]{1,0:T(8,128)(2,1)} %refs_1_.1), channel_id=1, source_target_pairs={{0,48},{16,0},{32,16},{48,32},{1,49},{17,1},{33,17},{49,33},{2,50}... | collective-permute-start | bytes 589832 | tf_op jit(solution)/shard_map/ppermute | solution.py:374
  8.8 1.7 %copy-done.1 = bf16[1,1,288,4096]{3,2,1,0:T(8,128)(2,1)S(1)} copy-done((bf16[1,1,288,4096]{3,2,1,0:T(8,128)(2,1)S(1)}, bf16[1,1,288,4096]{3,2,1,0:T(8,128)(2,1)}, u32[]{:S(2)}) %copy-start.1) | copy-done | bytes 2359320
  10.4 2.1 %build_0.1.rest_0_ = bf16[3072,1536]{1,0:T(8,128)(2,1)S(1)} custom-call(s32[288]{0:T(512)S(1)} %fusion.2.places, s32[1,1]{1,0:T(1,128)} %copy.11.counts, bf16[1,1,288,4096]{3,2,1,0:T(8,128)(2,1)S(1)} %copy-done.1), custom_call_target="tpu_custom_call" | custom-call | bytes 8388608 | tf_op jit(solution)/shard_map/build_0/pallas_call | solution.py:129
  12.6 1.7 %collective-permute-start.4 = (bf16[192,512]{1,0:T(8,128)(2,1)S(1)}, bf16[192,512]{1,0:T(8,128)(2,1)S(1)}, u32[]{:S(2)}, u32[]{:S(2)}) collective-permute-start(bf16[192,512]{1,0:T(8,128)(2,1)S(1)} %collective-permute-done.refs_5_), channel_id=1, source_target_pairs={{0,48},{16,0},{32,16},{48,32},{1,49},{17,1},{33,17},{49,33},{2,50}... | collective-permute-start | bytes 589832 | tf_op jit(solution)/shard_map/ppermute | solution.py:374
  16.1 2.6 %collective-permute-done.4.refs_6_ = bf16[192,512]{1,0:T(8,128)(2,1)S(1)} collective-permute-done((bf16[192,512]{1,0:T(8,128)(2,1)S(1)}, bf16[192,512]{1,0:T(8,128)(2,1)S(1)}, u32[]{:S(2)}, u32[]{:S(2)}) %collective-permute-start.4) | collective-permute-done | bytes 196640 | tf_op jit(solution)/shard_map/ppermute | solution.py:374
  18.7 2.4 %collective-permute-done.5.refs_4_ = bf16[192,512]{1,0:T(8,128)(2,1)S(1)} collective-permute-done((bf16[192,512]{1,0:T(8,128)(2,1)S(1)}, bf16[192,512]{1,0:T(8,128)(2,1)S(1)}, u32[]{:S(2)}, u32[]{:S(2)}) %collective-permute-start.5) | collective-permute-done | bytes 196640 | tf_op jit(solution)/shard_map/ppermute | solution.py:374
  21.2 2.0 %collective-permute-start.6 = (bf16[192,512]{1,0:T(8,128)(2,1)S(1)}, bf16[192,512]{1,0:T(8,128)(2,1)S(1)}, u32[]{:S(2)}, u32[]{:S(2)}) collective-permute-start(bf16[192,512]{1,0:T(8,128)(2,1)S(1)} %collective-permute-done.4.refs_6_), channel_id=1, source_target_pairs={{0,48},{16,0},{32,16},{48,32},{1,49},{17,1},{33,17},{49,33},{2,50}... | collective-permute-start | bytes 589832 | tf_op jit(solution)/shard_map/ppermute | solution.py:374
  23.2 5.0 %down_most.1.most = f32[3072,512]{1,0:T(8,128)S(1)} custom-call(bf16[3072,1536]{1,0:T(8,128)(2,1)S(1)} %build_1.1.refs_0_.dense, bf16[192,512]{1,0:T(8,128)(2,1)S(1)} %copy-done.4, bf16[192,512]{1,0:T(8,128)(2,1)S(1)} %collective-permute-done.2.refs_2_, bf16[192,512]{1,0:T(8,128)(2,1)S(1)} %collective-permute-done.1.refs_3_, ...), custom_call_target="tpu_custom_call" | custom-call | flops 4831838208 | bytes 1048576 | tf_op jit(solution)/shard_map/down_most/pallas_call | solution.py:33
  28.7 2.0 %collective-permute-done.7.other = bf16[576,512]{1,0:T(8,128)(2,1)S(1)} collective-permute-done((bf16[576,512]{1,0:T(8,128)(2,1)S(1)}, bf16[576,512]{1,0:T(8,128)(2,1)S(1)}, u32[]{:S(2)}, u32[]{:S(2)}) %collective-permute-start.7) | collective-permute-done | bytes 589856 | tf_op jit(solution)/shard_map/ppermute | solution.py:363
  31.6 1.7 %collective-permute-start.8 = (bf16[192,512]{1,0:T(8,128)(2,1)S(1)}, bf16[192,512]{1,0:T(8,128)(2,1)S(1)}, u32[]{:S(2)}, u32[]{:S(2)}) collective-permute-start(bf16[192,512]{1,0:T(8,128)(2,1)S(1)} %get-tuple-element.72), channel_id=1, source_target_pairs={{0,2},{2,4},{4,6},{6,0},{1,3},{3,5},{5,7},{7,1},{8,10},{10,12},{12... | collective-permute-start | bytes 589832 | tf_op jit(solution)/shard_map/ppermute | solution.py:248
  33.3 2.8 %collective-permute-start.9 = (bf16[192,512]{1,0:T(8,128)(2,1)S(1)}, bf16[192,512]{1,0:T(8,128)(2,1)S(1)}, u32[]{:S(2)}, u32[]{:S(2)}) collective-permute-start(bf16[192,512]{1,0:T(8,128)(2,1)S(1)} %get-tuple-element.73), channel_id=1, source_target_pairs={{0,8},{8,0},{1,9},{9,1},{2,10},{10,2},{3,11},{11,3},{4,12},{12,4},... | collective-permute-start | bytes 589832 | tf_op jit(solution)/shard_map/ppermute | solution.py:363
  36.1 1.8 %collective-permute-start.10 = (bf16[192,512]{1,0:T(8,128)(2,1)S(1)}, bf16[192,512]{1,0:T(8,128)(2,1)S(1)}, u32[]{:S(2)}, u32[]{:S(2)}) collective-permute-start(bf16[192,512]{1,0:T(8,128)(2,1)S(1)} %get-tuple-element.74), channel_id=1, source_target_pairs={{0,6},{2,0},{4,2},{6,4},{1,7},{3,1},{5,3},{7,5},{8,14},{10,8},{12,... | collective-permute-start | bytes 589832 | tf_op jit(solution)/shard_map/ppermute | solution.py:248
  38.3 1.7 %collective-permute-done.8.b = bf16[192,512]{1,0:T(8,128)(2,1)S(1)} collective-permute-done((bf16[192,512]{1,0:T(8,128)(2,1)S(1)}, bf16[192,512]{1,0:T(8,128)(2,1)S(1)}, u32[]{:S(2)}, u32[]{:S(2)}) %collective-permute-start.8) | collective-permute-done | bytes 196640 | tf_op jit(solution)/shard_map/ppermute | solution.py:248
  40.1 1.6 %collective-permute-done.9.d = bf16[192,512]{1,0:T(8,128)(2,1)S(1)} collective-permute-done((bf16[192,512]{1,0:T(8,128)(2,1)S(1)}, bf16[192,512]{1,0:T(8,128)(2,1)S(1)}, u32[]{:S(2)}, u32[]{:S(2)}) %collective-permute-start.9) | collective-permute-done | bytes 196640 | tf_op jit(solution)/shard_map/ppermute | solution.py:363
  44.4 1.7 %collective-permute-start.13 = (bf16[192,512]{1,0:T(8,128)(2,1)S(1)}, bf16[192,512]{1,0:T(8,128)(2,1)S(1)}, u32[]{:S(2)}, u32[]{:S(2)}) collective-permute-start(bf16[192,512]{1,0:T(8,128)(2,1)S(1)} %get-tuple-element.87), channel_id=1, source_target_pairs={{0,6},{2,0},{4,2},{6,4},{1,7},{3,1},{5,3},{7,5},{8,14},{10,8},{12,... | collective-permute-start | bytes 589832 | tf_op jit(solution)/shard_map/ppermute | solution.py:248
  46.4 5.0 %collective-permute-done.12.refs_1_ = bf16[192,512]{1,0:T(8,128)(2,1)S(1)} collective-permute-done((bf16[192,512]{1,0:T(8,128)(2,1)S(1)}, bf16[192,512]{1,0:T(8,128)(2,1)S(1)}, u32[]{:S(2)}, u32[]{:S(2)}) %collective-permute-start.12) | collective-permute-done | bytes 196640 | tf_op jit(solution)/shard_map/ppermute | solution.py:248
  51.4 2.2 %collective-permute-start.14 = (bf16[192,512]{1,0:T(8,128)(2,1)S(1)}, bf16[192,512]{1,0:T(8,128)(2,1)S(1)}, u32[]{:S(2)}, u32[]{:S(2)}) collective-permute-start(bf16[192,512]{1,0:T(8,128)(2,1)S(1)} %sum_across.1), channel_id=1, source_target_pairs={{0,8},{8,0},{1,9},{9,1},{2,10},{10,2},{3,11},{11,3},{4,12},{12,4},... | collective-permute-start | bytes 589832 | tf_op jit(solution)/shard_map/ppermute | solution.py:363
  54.1 4.6 %collective-permute-done.14.c = bf16[192,512]{1,0:T(8,128)(2,1)S(1)} collective-permute-done((bf16[192,512]{1,0:T(8,128)(2,1)S(1)}, bf16[192,512]{1,0:T(8,128)(2,1)S(1)}, u32[]{:S(2)}, u32[]{:S(2)}) %collective-permute-start.14) | collective-permute-done | bytes 196640 | tf_op jit(solution)/shard_map/ppermute | solution.py:363
  58.7 2.0 %middle.1 = (bf16[192,512]{1,0:T(8,128)(2,1)}, bf16[8,192,512]{2,1,0:T(8,128)(2,1)}, bf16[192,512]{1,0:T(8,128)(2,1)S(1)}, bf16[192,512]{1,0:T(8,128)(2,1)S(1)}) custom-call(bf16[192,512]{1,0:T(8,128)(2,1)S(1)} %get-tuple-element.80.a, bf16[192,512]{1,0:T(8,128)(2,1)S(1)} %collective-permute-done.13.b, bf16[192,512]{1,0:T(8,128)(2,1)S(1)} %collective-permute-done.14.c, ...), custom_call_target="tpu_custom_call" | custom-call | flops 201326592 | bytes 1048576 | tf_op jit(solution)/shard_map/middle/pallas_call | solution.py:33
  60.7 4.6 %all-to-all-start = ((bf16[8,192,512]{2,1,0:T(8,128)(2,1)}), bf16[8,192,512]{2,1,0:T(8,128)(2,1)S(1)}, u32[]{:S(2)}, u32[]{:S(2)}) async-start(bf16[8,192,512]{2,1,0:T(8,128)(2,1)} %get-tuple-element.101), calls=%async_computation | async-start | bytes 3145728 | tf_op jit(solution)/shard_map/all_to_all | solution.py:359
  67.7 3.3 %collective-permute-start.18 = (bf16[64,512]{1,0:T(8,128)(2,1)S(1)}, bf16[64,512]{1,0:T(8,128)(2,1)S(1)}, u32[]{:S(2)}, u32[]{:S(2)}) collective-permute-start(bf16[64,512]{1,0:T(8,128)(2,1)S(1)} %get-tuple-element.99), channel_id=1, source_target_pairs={{0,32},{16,48},{32,0},{48,16},{1,33},{17,49},{33,1},{49,17},{2,34}... | collective-permute-start | bytes 196616 | tf_op jit(solution)/shard_map/ppermute | solution.py:363
  72.5 1.9 %collective-permute-done.18.refs_2_ = bf16[64,512]{1,0:T(8,128)(2,1)S(1)} collective-permute-done((bf16[64,512]{1,0:T(8,128)(2,1)S(1)}, bf16[64,512]{1,0:T(8,128)(2,1)S(1)}, u32[]{:S(2)}, u32[]{:S(2)}) %collective-permute-start.18) | collective-permute-done | bytes 65568 | tf_op jit(solution)/shard_map/ppermute | solution.py:363
  74.5 2.0 %collective-permute-done.19.refs_3_ = bf16[64,512]{1,0:T(8,128)(2,1)S(1)} collective-permute-done((bf16[64,512]{1,0:T(8,128)(2,1)S(1)}, bf16[64,512]{1,0:T(8,128)(2,1)S(1)}, u32[]{:S(2)}, u32[]{:S(2)}) %collective-permute-start.19) | collective-permute-done | bytes 65568 | tf_op jit(solution)/shard_map/ppermute | solution.py:363
  76.5 3.8 %collective-permute-start.22 = (bf16[64,512]{1,0:T(8,128)(2,1)S(1)}, bf16[64,512]{1,0:T(8,128)(2,1)S(1)}, u32[]{:S(2)}, u32[]{:S(2)}) collective-permute-start(bf16[64,512]{1,0:T(8,128)(2,1)S(1)} %sum_z.1.a), channel_id=1, source_target_pairs={{0,72},{8,64},{64,8},{72,0},{1,73},{9,65},{65,9},{73,1},{2,74},{10... | collective-permute-start | bytes 196616 | tf_op jit(solution)/shard_map/ppermute | solution.py:363
  81.8 4.7 %collective-permute-done.22.d = bf16[64,512]{1,0:T(8,128)(2,1)S(1)} collective-permute-done((bf16[64,512]{1,0:T(8,128)(2,1)S(1)}, bf16[64,512]{1,0:T(8,128)(2,1)S(1)}, u32[]{:S(2)}, u32[]{:S(2)}) %collective-permute-start.22) | collective-permute-done | bytes 65568 | tf_op jit(solution)/shard_map/ppermute | solution.py:363
  88.0 4.8 %up_near.1 = (f32[1536,512]{1,0:T(8,128)S(1)}, bf16[1536,1536]{1,0:T(8,128)(2,1)S(1)}) custom-call(bf16[3072,1536]{1,0:T(8,128)(2,1)} %copy-done, bf16[8,192,512]{2,1,0:T(8,128)(2,1)S(1)} %all-to-all-done.rows), custom_call_target="tpu_custom_call" | custom-call | flops 2415919104 | bytes 12582912 | tf_op jit(solution)/shard_map/up_near/pallas_call | solution.py:449
  92.9 3.4 %collective-permute-start.25 = (bf16[128,512]{1,0:T(8,128)(2,1)S(1)}, bf16[128,512]{1,0:T(8,128)(2,1)S(1)}, u32[]{:S(2)}, u32[]{:S(2)}) collective-permute-start(bf16[128,512]{1,0:T(8,128)(2,1)S(1)} %double.1.low), channel_id=1, source_target_pairs={{0,32},{16,48},{32,0},{48,16},{1,33},{17,49},{33,1},{49,17},{2,34}... | collective-permute-start | bytes 393224 | tf_op jit(solution)/shard_map/ppermute | solution.py:363
  96.2 3.4 %up_far.1 = bf16[8,192,512]{2,1,0:T(8,128)(2,1)} custom-call(bf16[1536,1536]{1,0:T(8,128)(2,1)S(1)} %get-tuple-element.103.tile, bf16[8,192,512]{2,1,0:T(8,128)(2,1)S(1)} %collective-permute-done.23.rows, f32[1536,512]{1,0:T(8,128)S(1)} %get-tuple-element.106.other), custom_call_target="tpu_custom_call" | custom-call | flops 2415919104 | bytes 12582912 | tf_op jit(solution)/shard_map/up_far/pallas_call | solution.py:465
  100.3 4.3 %all-to-all-start.1 = ((bf16[8,192,512]{2,1,0:T(8,128)(2,1)}), bf16[8,192,512]{2,1,0:T(8,128)(2,1)S(1)}, u32[]{:S(2)}, u32[]{:S(2)}) async-start(bf16[8,192,512]{2,1,0:T(8,128)(2,1)} %up_far.1), calls=%async_computation.1 | async-start | bytes 3145728 | tf_op jit(solution)/shard_map/all_to_all | solution.py:359
  105.4 2.7 %collective-permute-start.27 = (bf16[256,128]{1,0:T(8,128)(2,1)S(1)}, bf16[256,128]{1,0:T(8,128)(2,1)S(1)}, u32[]{:S(2)}, u32[]{:S(2)}) collective-permute-start(bf16[256,128]{1,0:T(8,128)(2,1)S(1)} %get-tuple-element.112), channel_id=1, source_target_pairs={{0,4},{2,6},{4,0},{6,2},{1,5},{3,7},{5,1},{7,3},{8,12},{10,14},{12... | collective-permute-start | bytes 196616 | tf_op jit(solution)/shard_map/ppermute | solution.py:393
  113.4 3.1 %collective-permute-start.30 = (bf16[256,128]{1,0:T(8,128)(2,1)S(1)}, bf16[256,128]{1,0:T(8,128)(2,1)S(1)}, u32[]{:S(2)}, u32[]{:S(2)}) collective-permute-start(bf16[256,128]{1,0:T(8,128)(2,1)S(1)} %sum_x.1.refs_0_), channel_id=1, source_target_pairs={{0,4},{2,6},{4,0},{6,2},{1,5},{3,7},{5,1},{7,3},{8,12},{10,14},{12... | collective-permute-start | bytes 196616 | tf_op jit(solution)/shard_map/ppermute | solution.py:400
  (73 shorter events, 33.1 us)
Async XLA Ops:
  0.6 11.9 %collective-permute-start.1 = (bf16[192,512]{1,0:T(8,128)(2,1)}, bf16[192,512]{1,0:T(8,128)(2,1)S(1)}, u32[]{:S(2)}, u32[]{:S(2)}) collective-permute-start(bf16[192,512]{1,0:T(8,128)(2,1)} %refs_1_.1), channel_id=1, source_target_pairs={{0,16},{16,32},{32,48},{48,0},{1,17},{17,33},{33,49},{49,1},{2,18}... | collective-permute-start | bytes 589832 | tf_op jit(solution)/shard_map/ppermute | solution.py:374
  2.7 9.8 %collective-permute-start = (bf16[192,512]{1,0:T(8,128)(2,1)}, bf16[192,512]{1,0:T(8,128)(2,1)S(1)}, u32[]{:S(2)}, u32[]{:S(2)}) collective-permute-start(bf16[192,512]{1,0:T(8,128)(2,1)} %refs_1_.1), channel_id=1, source_target_pairs={{0,64},{64,0},{1,65},{65,1},{2,66},{66,2},{3,67},{67,3},{4,68},{68... | collective-permute-start | bytes 589832 | tf_op jit(solution)/shard_map/ppermute | solution.py:363
  4.3 8.3 %collective-permute-start.2 = (bf16[192,512]{1,0:T(8,128)(2,1)}, bf16[192,512]{1,0:T(8,128)(2,1)S(1)}, u32[]{:S(2)}, u32[]{:S(2)}) collective-permute-start(bf16[192,512]{1,0:T(8,128)(2,1)} %refs_1_.1), channel_id=1, source_target_pairs={{0,48},{16,0},{32,16},{48,32},{1,49},{17,1},{33,17},{49,33},{2,50}... | collective-permute-start | bytes 589832 | tf_op jit(solution)/shard_map/ppermute | solution.py:374
  12.6 6.2 %collective-permute-start.4 = (bf16[192,512]{1,0:T(8,128)(2,1)S(1)}, bf16[192,512]{1,0:T(8,128)(2,1)S(1)}, u32[]{:S(2)}, u32[]{:S(2)}) collective-permute-start(bf16[192,512]{1,0:T(8,128)(2,1)S(1)} %collective-permute-done.refs_5_), channel_id=1, source_target_pairs={{0,48},{16,0},{32,16},{48,32},{1,49},{17,1},{33,17},{49,33},{2,50}... | collective-permute-start | bytes 589832 | tf_op jit(solution)/shard_map/ppermute | solution.py:374
  14.3 6.9 %collective-permute-start.5 = (bf16[192,512]{1,0:T(8,128)(2,1)S(1)}, bf16[192,512]{1,0:T(8,128)(2,1)S(1)}, u32[]{:S(2)}, u32[]{:S(2)}) collective-permute-start(bf16[192,512]{1,0:T(8,128)(2,1)S(1)} %collective-permute-done.1.refs_3_), channel_id=1, source_target_pairs={{0,16},{16,32},{32,48},{48,0},{1,17},{17,33},{33,49},{49,1},{2,18}... | collective-permute-start | bytes 589832 | tf_op jit(solution)/shard_map/ppermute | solution.py:374
  14.7 6.5 %collective-permute-start.3 = (bf16[192,512]{1,0:T(8,128)(2,1)S(1)}, bf16[192,512]{1,0:T(8,128)(2,1)S(1)}, u32[]{:S(2)}, u32[]{:S(2)}) collective-permute-start(bf16[192,512]{1,0:T(8,128)(2,1)S(1)} %collective-permute-done.1.refs_3_), channel_id=1, source_target_pairs={{0,64},{64,0},{1,65},{65,1},{2,66},{66,2},{3,67},{67,3},{4,68},{68... | collective-permute-start | bytes 589832 | tf_op jit(solution)/shard_map/ppermute | solution.py:363
  21.2 7.1 %collective-permute-start.6 = (bf16[192,512]{1,0:T(8,128)(2,1)S(1)}, bf16[192,512]{1,0:T(8,128)(2,1)S(1)}, u32[]{:S(2)}, u32[]{:S(2)}) collective-permute-start(bf16[192,512]{1,0:T(8,128)(2,1)S(1)} %collective-permute-done.4.refs_6_), channel_id=1, source_target_pairs={{0,48},{16,0},{32,16},{48,32},{1,49},{17,1},{33,17},{49,33},{2,50}... | collective-permute-start | bytes 589832 | tf_op jit(solution)/shard_map/ppermute | solution.py:374
  31.1 6.8 %collective-permute-start.11 = (bf16[960,512]{1,0:T(8,128)(2,1)S(1)}, bf16[960,512]{1,0:T(8,128)(2,1)S(1)}, u32[]{:S(2)}, u32[]{:S(2)}) collective-permute-start(bf16[960,512]{1,0:T(8,128)(2,1)S(1)} %down_far_1.1), channel_id=1, source_target_pairs={{0,1},{1,0},{2,3},{3,2},{4,5},{5,4},{6,7},{7,6},{8,9},{9,8},{10,11... | collective-permute-start | bytes 2949128 | tf_op jit(solution)/shard_map/ppermute | solution.py:363
  31.6 8.5 %collective-permute-start.8 = (bf16[192,512]{1,0:T(8,128)(2,1)S(1)}, bf16[192,512]{1,0:T(8,128)(2,1)S(1)}, u32[]{:S(2)}, u32[]{:S(2)}) collective-permute-start(bf16[192,512]{1,0:T(8,128)(2,1)S(1)} %get-tuple-element.72), channel_id=1, source_target_pairs={{0,2},{2,4},{4,6},{6,0},{1,3},{3,5},{5,7},{7,1},{8,10},{10,12},{12... | collective-permute-start | bytes 589832 | tf_op jit(solution)/shard_map/ppermute | solution.py:248
  33.3 8.4 %collective-permute-start.9 = (bf16[192,512]{1,0:T(8,128)(2,1)S(1)}, bf16[192,512]{1,0:T(8,128)(2,1)S(1)}, u32[]{:S(2)}, u32[]{:S(2)}) collective-permute-start(bf16[192,512]{1,0:T(8,128)(2,1)S(1)} %get-tuple-element.73), channel_id=1, source_target_pairs={{0,8},{8,0},{1,9},{9,1},{2,10},{10,2},{3,11},{11,3},{4,12},{12,4},... | collective-permute-start | bytes 589832 | tf_op jit(solution)/shard_map/ppermute | solution.py:363
  36.1 6.6 %collective-permute-start.10 = (bf16[192,512]{1,0:T(8,128)(2,1)S(1)}, bf16[192,512]{1,0:T(8,128)(2,1)S(1)}, u32[]{:S(2)}, u32[]{:S(2)}) collective-permute-start(bf16[192,512]{1,0:T(8,128)(2,1)S(1)} %get-tuple-element.74), channel_id=1, source_target_pairs={{0,6},{2,0},{4,2},{6,4},{1,7},{3,1},{5,3},{7,5},{8,14},{10,8},{12,... | collective-permute-start | bytes 589832 | tf_op jit(solution)/shard_map/ppermute | solution.py:248
  42.8 8.6 %collective-permute-start.12 = (bf16[192,512]{1,0:T(8,128)(2,1)S(1)}, bf16[192,512]{1,0:T(8,128)(2,1)S(1)}, u32[]{:S(2)}, u32[]{:S(2)}) collective-permute-start(bf16[192,512]{1,0:T(8,128)(2,1)S(1)} %get-tuple-element.86), channel_id=1, source_target_pairs={{0,2},{2,4},{4,6},{6,0},{1,3},{3,5},{5,7},{7,1},{8,10},{10,12},{12... | collective-permute-start | bytes 589832 | tf_op jit(solution)/shard_map/ppermute | solution.py:248
  44.4 7.0 %collective-permute-start.13 = (bf16[192,512]{1,0:T(8,128)(2,1)S(1)}, bf16[192,512]{1,0:T(8,128)(2,1)S(1)}, u32[]{:S(2)}, u32[]{:S(2)}) collective-permute-start(bf16[192,512]{1,0:T(8,128)(2,1)S(1)} %get-tuple-element.87), channel_id=1, source_target_pairs={{0,6},{2,0},{4,2},{6,4},{1,7},{3,1},{5,3},{7,5},{8,14},{10,8},{12,... | collective-permute-start | bytes 589832 | tf_op jit(solution)/shard_map/ppermute | solution.py:248
  46.1 8.0 %collective-permute-start.15 = (bf16[192,512]{1,0:T(8,128)(2,1)S(1)}, bf16[192,512]{1,0:T(8,128)(2,1)S(1)}, u32[]{:S(2)}, u32[]{:S(2)}) collective-permute-start(bf16[192,512]{1,0:T(8,128)(2,1)S(1)} %get-tuple-element.91), channel_id=1, source_target_pairs={{0,2},{2,4},{4,6},{6,0},{1,3},{3,5},{5,7},{7,1},{8,10},{10,12},{12... | collective-permute-start | bytes 589832 | tf_op jit(solution)/shard_map/ppermute | solution.py:248
  51.4 7.3 %collective-permute-start.14 = (bf16[192,512]{1,0:T(8,128)(2,1)S(1)}, bf16[192,512]{1,0:T(8,128)(2,1)S(1)}, u32[]{:S(2)}, u32[]{:S(2)}) collective-permute-start(bf16[192,512]{1,0:T(8,128)(2,1)S(1)} %sum_across.1), channel_id=1, source_target_pairs={{0,8},{8,0},{1,9},{9,1},{2,10},{10,2},{3,11},{11,3},{4,12},{12,4},... | collective-permute-start | bytes 589832 | tf_op jit(solution)/shard_map/ppermute | solution.py:363
  60.7 27.1 %all-to-all-start = ((bf16[8,192,512]{2,1,0:T(8,128)(2,1)}), bf16[8,192,512]{2,1,0:T(8,128)(2,1)S(1)}, u32[]{:S(2)}, u32[]{:S(2)}) async-start(bf16[8,192,512]{2,1,0:T(8,128)(2,1)} %get-tuple-element.101), calls=%async_computation | async-start | bytes 3145728 | tf_op jit(solution)/shard_map/all_to_all | solution.py:359
  67.6 5.0 %collective-permute-start.17 = (bf16[64,512]{1,0:T(8,128)(2,1)S(1)}, bf16[64,512]{1,0:T(8,128)(2,1)S(1)}, u32[]{:S(2)}, u32[]{:S(2)}) collective-permute-start(bf16[64,512]{1,0:T(8,128)(2,1)S(1)} %get-tuple-element.98), channel_id=1, source_target_pairs={{0,16},{16,0},{32,48},{48,32},{1,17},{17,1},{33,49},{49,33},{2,18}... | collective-permute-start | bytes 196616 | tf_op jit(solution)/shard_map/ppermute | solution.py:363
  67.7 6.8 %collective-permute-start.18 = (bf16[64,512]{1,0:T(8,128)(2,1)S(1)}, bf16[64,512]{1,0:T(8,128)(2,1)S(1)}, u32[]{:S(2)}, u32[]{:S(2)}) collective-permute-start(bf16[64,512]{1,0:T(8,128)(2,1)S(1)} %get-tuple-element.99), channel_id=1, source_target_pairs={{0,32},{16,48},{32,0},{48,16},{1,33},{17,49},{33,1},{49,17},{2,34}... | collective-permute-start | bytes 196616 | tf_op jit(solution)/shard_map/ppermute | solution.py:363
  70.9 5.5 %collective-permute-start.19 = (bf16[64,512]{1,0:T(8,128)(2,1)S(1)}, bf16[64,512]{1,0:T(8,128)(2,1)S(1)}, u32[]{:S(2)}, u32[]{:S(2)}) collective-permute-start(bf16[64,512]{1,0:T(8,128)(2,1)S(1)} %get-tuple-element.100), channel_id=1, source_target_pairs={{0,48},{16,32},{32,16},{48,0},{1,49},{17,33},{33,17},{49,1},{2,50}... | collective-permute-start | bytes 196616 | tf_op jit(solution)/shard_map/ppermute | solution.py:363
  76.5 10.0 %collective-permute-start.22 = (bf16[64,512]{1,0:T(8,128)(2,1)S(1)}, bf16[64,512]{1,0:T(8,128)(2,1)S(1)}, u32[]{:S(2)}, u32[]{:S(2)}) collective-permute-start(bf16[64,512]{1,0:T(8,128)(2,1)S(1)} %sum_z.1.a), channel_id=1, source_target_pairs={{0,72},{8,64},{64,8},{72,0},{1,73},{9,65},{65,9},{73,1},{2,74},{10... | collective-permute-start | bytes 196616 | tf_op jit(solution)/shard_map/ppermute | solution.py:363
  80.2 6.2 %collective-permute-start.21 = (bf16[64,512]{1,0:T(8,128)(2,1)S(1)}, bf16[64,512]{1,0:T(8,128)(2,1)S(1)}, u32[]{:S(2)}, u32[]{:S(2)}) collective-permute-start(bf16[64,512]{1,0:T(8,128)(2,1)S(1)} %sum_z.1.a), channel_id=1, source_target_pairs={{0,64},{8,72},{64,0},{72,8},{1,65},{9,73},{65,1},{73,9},{2,66},{10... | collective-permute-start | bytes 196616 | tf_op jit(solution)/shard_map/ppermute | solution.py:363
  80.2 7.5 %collective-permute-start.20 = (bf16[64,512]{1,0:T(8,128)(2,1)S(1)}, bf16[64,512]{1,0:T(8,128)(2,1)S(1)}, u32[]{:S(2)}, u32[]{:S(2)}) collective-permute-start(bf16[64,512]{1,0:T(8,128)(2,1)S(1)} %sum_z.1.a), channel_id=1, source_target_pairs={{0,8},{8,0},{64,72},{72,64},{1,9},{9,1},{65,73},{73,65},{2,10},{10... | collective-permute-start | bytes 196616 | tf_op jit(solution)/shard_map/ppermute | solution.py:363
  87.8 8.4 %collective-permute-start.23 = (bf16[8,192,512]{2,1,0:T(8,128)(2,1)S(1)}, bf16[8,192,512]{2,1,0:T(8,128)(2,1)S(1)}, u32[]{:S(2)}, u32[]{:S(2)}) collective-permute-start(bf16[8,192,512]{2,1,0:T(8,128)(2,1)S(1)} %all-to-all-done.rows), channel_id=1, source_target_pairs={{0,1},{1,0},{2,3},{3,2},{4,5},{5,4},{6,7},{7,6},{8,9},{9,8},{10,11... | collective-permute-start | bytes 4718600 | tf_op jit(solution)/shard_map/ppermute | solution.py:363
  87.9 4.9 %collective-permute-start.24 = (bf16[64,512]{1,0:T(8,128)(2,1)S(1)}, bf16[64,512]{1,0:T(8,128)(2,1)S(1)}, u32[]{:S(2)}, u32[]{:S(2)}) collective-permute-start(bf16[64,512]{1,0:T(8,128)(2,1)S(1)} %sum_y.1.first), channel_id=1, source_target_pairs={{0,16},{16,0},{32,48},{48,32},{1,17},{17,1},{33,49},{49,33},{2,18}... | collective-permute-start | bytes 196616 | tf_op jit(solution)/shard_map/ppermute | solution.py:363
  92.9 7.4 %collective-permute-start.25 = (bf16[128,512]{1,0:T(8,128)(2,1)S(1)}, bf16[128,512]{1,0:T(8,128)(2,1)S(1)}, u32[]{:S(2)}, u32[]{:S(2)}) collective-permute-start(bf16[128,512]{1,0:T(8,128)(2,1)S(1)} %double.1.low), channel_id=1, source_target_pairs={{0,32},{16,48},{32,0},{48,16},{1,33},{17,49},{33,1},{49,17},{2,34}... | collective-permute-start | bytes 393224 | tf_op jit(solution)/shard_map/ppermute | solution.py:363
  100.3 24.2 %all-to-all-start.1 = ((bf16[8,192,512]{2,1,0:T(8,128)(2,1)}), bf16[8,192,512]{2,1,0:T(8,128)(2,1)S(1)}, u32[]{:S(2)}, u32[]{:S(2)}) async-start(bf16[8,192,512]{2,1,0:T(8,128)(2,1)} %up_far.1), calls=%async_computation.1 | async-start | bytes 3145728 | tf_op jit(solution)/shard_map/all_to_all | solution.py:359
  104.6 5.5 %collective-permute-start.26 = (bf16[256,128]{1,0:T(8,128)(2,1)S(1)}, bf16[256,128]{1,0:T(8,128)(2,1)S(1)}, u32[]{:S(2)}, u32[]{:S(2)}) collective-permute-start(bf16[256,128]{1,0:T(8,128)(2,1)S(1)} %get-tuple-element.111), channel_id=1, source_target_pairs={{0,2},{2,4},{4,6},{6,0},{1,3},{3,5},{5,7},{7,1},{8,10},{10,12},{12... | collective-permute-start | bytes 196616 | tf_op jit(solution)/shard_map/ppermute | solution.py:393
  105.4 5.8 %collective-permute-start.27 = (bf16[256,128]{1,0:T(8,128)(2,1)S(1)}, bf16[256,128]{1,0:T(8,128)(2,1)S(1)}, u32[]{:S(2)}, u32[]{:S(2)}) collective-permute-start(bf16[256,128]{1,0:T(8,128)(2,1)S(1)} %get-tuple-element.112), channel_id=1, source_target_pairs={{0,4},{2,6},{4,0},{6,2},{1,5},{3,7},{5,1},{7,3},{8,12},{10,14},{12... | collective-permute-start | bytes 196616 | tf_op jit(solution)/shard_map/ppermute | solution.py:393
  108.1 4.3 %collective-permute-start.28 = (bf16[256,128]{1,0:T(8,128)(2,1)S(1)}, bf16[256,128]{1,0:T(8,128)(2,1)S(1)}, u32[]{:S(2)}, u32[]{:S(2)}) collective-permute-start(bf16[256,128]{1,0:T(8,128)(2,1)S(1)} %get-tuple-element.113), channel_id=1, source_target_pairs={{0,6},{2,0},{4,2},{6,4},{1,7},{3,1},{5,3},{7,5},{8,14},{10,8},{12,... | collective-permute-start | bytes 196616 | tf_op jit(solution)/shard_map/ppermute | solution.py:393
  112.4 5.5 %collective-permute-start.31 = (bf16[256,128]{1,0:T(8,128)(2,1)S(1)}, bf16[256,128]{1,0:T(8,128)(2,1)S(1)}, u32[]{:S(2)}, u32[]{:S(2)}) collective-permute-start(bf16[256,128]{1,0:T(8,128)(2,1)S(1)} %sum_x.1.refs_0_), channel_id=1, source_target_pairs={{0,2},{2,4},{4,6},{6,0},{1,3},{3,5},{5,7},{7,1},{8,10},{10,12},{12... | collective-permute-start | bytes 196616 | tf_op jit(solution)/shard_map/ppermute | solution.py:400
  113.4 6.1 %collective-permute-start.30 = (bf16[256,128]{1,0:T(8,128)(2,1)S(1)}, bf16[256,128]{1,0:T(8,128)(2,1)S(1)}, u32[]{:S(2)}, u32[]{:S(2)}) collective-permute-start(bf16[256,128]{1,0:T(8,128)(2,1)S(1)} %sum_x.1.refs_0_), channel_id=1, source_target_pairs={{0,4},{2,6},{4,0},{6,2},{1,5},{3,7},{5,1},{7,3},{8,12},{10,14},{12... | collective-permute-start | bytes 196616 | tf_op jit(solution)/shard_map/ppermute | solution.py:400
  116.6 4.3 %collective-permute-start.29 = (bf16[256,128]{1,0:T(8,128)(2,1)S(1)}, bf16[256,128]{1,0:T(8,128)(2,1)S(1)}, u32[]{:S(2)}, u32[]{:S(2)}) collective-permute-start(bf16[256,128]{1,0:T(8,128)(2,1)S(1)} %sum_x.1.refs_0_), channel_id=1, source_target_pairs={{0,6},{2,0},{4,2},{6,4},{1,7},{3,1},{5,3},{7,5},{8,14},{10,8},{12,... | collective-permute-start | bytes 196616 | tf_op jit(solution)/shard_map/ppermute | solution.py:400
  (8 other events, 84.9 us)

commit v13 on v12

--- a/solution.py
+++ b/solution.py
@@ -70,11 +70,6 @@
     apart = (chip >> 2) ^ lax.axis_index("y_hi")
     ahead = ((chip & (RING - 1)) - lax.axis_index("x")) & (RING - 1)
     return (table >> (4 * (RING * apart + ahead))) & 15
-
-
-def leaving_chip(place):
-    apart, ahead = LEAVING[place]
-    return (lax.axis_index("y_hi") ^ apart) * RING + ((lax.axis_index("x") + ahead) & (RING - 1))
 
 
 def build_places(coords, counts):
@@ -169,32 +164,21 @@
         out[...] = (total + other[k * OWN : (k + 1) * OWN].astype(jnp.float32)).astype(out.dtype)
 
 
-def in_order(rows, ordered):
-    for place in range(PEERS):
-        ordered[place * OWN : (place + 1) * OWN] = rows[leaving_chip(place)]
-
-
-def up_kernel(dense, rows, out, far, near, ordered, sems):
-    strips = [pl.ds(r, STEP) for r in range(0, ROWS, STEP)]
-    copies = [
-        pltpu.make_async_copy(dense.at[pl.ds(0, ROWS), strip], near.at[:, strip], sems.at[n])
-        for n, strip in enumerate(strips)
-    ]
-    copies.append(pltpu.make_async_copy(dense.at[pl.ds(ROWS, ROWS)], far, sems.at[len(strips)]))
-    for copy in copies:
-        copy.start()
-    in_order(rows, ordered)
-    for copy, r in zip(copies, range(0, ROWS, STEP)):
-        copy.wait()
-        out[r : r + STEP] = over_rows(near[:, r : r + STEP], ordered[...])
-    copies[-1].wait()
-
-
-def up_add_kernel(tile, rows, other, out, ordered, done, sems):
-    in_order(rows, ordered)
+def order_kernel(*refs):
+    *pairs, out = refs
+    for place, (apart, ahead) in enumerate(LEAVING):
+        out[place * OWN : (place + 1) * OWN] = pairs[ahead][apart * OWN : (apart + 1) * OWN]
+
+
+def up_kernel(dense, rows, out):
+    for r in range(0, ROWS, STEP):
+        out[r : r + STEP] = over_rows(dense[:ROWS, r : r + STEP], rows[...])
+
+
+def up_add_kernel(dense, rows, other, out, done, sems):
     copies = []
     for r in range(0, ROWS, 2 * OWN):
-        total = over_rows(tile[:, r : r + 2 * OWN], ordered[...]) + other[r : r + 2 * OWN]
+        total = over_rows(dense[ROWS:, r : r + 2 * OWN], rows[...]) + other[r : r + 2 * OWN]
         for k in range(2):
             place = r // OWN + k
             done[place] = total[k * OWN : (k + 1) * OWN].astype(done.dtype)
@@ -279,8 +263,7 @@
     grad_agg = lax.dot_general(
         grad_pre, w, (((1,), (1,)), ((), ())), preferred_element_type=jnp.float32
     ).astype(jnp.bfloat16)
-    for k in range(PEERS):
-        send[k] = grad_agg
+    send[...] = grad_agg
     aggregated_out[...] = aggregated
     grad_pre_out[...] = grad_pre
 
@@ -414,7 +397,7 @@
     half = bf16(WIDTH // 2, WIDTH)
     own = bf16(OWN, WIDTH)
     activations, send, aggregated, grad_pre = vmem_call(
-        middle_kernel, (own, bf16(PEERS, OWN, WIDTH), own, own), "middle", flops=2 * 2 * OWN * WIDTH * WIDTH
+        middle_kernel, (own, own, own, own), "middle", flops=2 * 2 * OWN * WIDTH * WIDTH
     )(*parts, out_grad, weight)
     wgrads = vmem_call(
         wgrad_kernel,
@@ -439,45 +422,28 @@
             summed, trade(summed, ys, 1), trade(summed, ys, 2), trade(summed, ys, 3)
         )
 
-    mine = exchange(send, CHIP)
+    pair = vmem_call(double_kernel, bf16(2 * OWN, WIDTH), "pair_y")(send, trade(send, "y_hi"))
+    wgrads, pair = lax.optimization_barrier((wgrads, pair))
+    mine = [pair] + [lax.ppermute(pair, "x", [(i, (i - k) % RING) for i in range(RING)]) for k in range(1, RING)]
     summed = over_y(over_z(over_core(wgrads)))
-    summed, mine = lax.optimization_barrier((summed, mine))
+    low = vmem_call(double_kernel, bf16(2 * PIECE, WIDTH), "double")(summed, trade(summed, "z", 1))
+    mine, *pairs = lax.optimization_barrier((mine, low, trade(low, "z", 2)))
+    mine = vmem_call(order_kernel, bf16(ROWS, WIDTH), "order")(*mine)
 
     theirs = trade(mine, "core")
     work = 2 * ROWS * ROWS * WIDTH
     vmem = pl.BlockSpec(memory_space=pltpu.VMEM)
-    own, far = pl.pallas_call(
-        up_kernel,
-        out_shape=(jax.ShapeDtypeStruct((ROWS, WIDTH), jnp.float32), bf16(ROWS, ROWS)),
-        in_specs=[pl.BlockSpec(memory_space=pltpu.HBM), vmem],
-        out_specs=(vmem, vmem),
-        scratch_shapes=[
-            pltpu.VMEM((ROWS, ROWS), jnp.bfloat16),
-            pltpu.VMEM((ROWS, WIDTH), jnp.bfloat16),
-            pltpu.SemaphoreType.DMA((ROWS // STEP + 1,)),
-        ],
-        compiler_params=pltpu.CompilerParams(vmem_limit_bytes=44 << 20),
-        cost_estimate=pl.CostEstimate(flops=work, bytes_accessed=12 << 20, transcendentals=0),
-        name="up_near",
-    )(dense, mine)
-    next_piece, own = lax.optimization_barrier((trade(summed, "z", 1), own))
-    pair = vmem_call(double_kernel, bf16(2 * PIECE, WIDTH), "double")(summed, next_piece)
+    own = vmem_call(up_kernel, jax.ShapeDtypeStruct((ROWS, WIDTH), jnp.float32), "up_near", flops=work)(dense, mine)
     partial_grad = pl.pallas_call(
         up_add_kernel,
         out_shape=bf16(PEERS, OWN, WIDTH),
         in_specs=[vmem] * 3,
         out_specs=pl.BlockSpec(memory_space=pltpu.HBM),
-        scratch_shapes=[
-            pltpu.VMEM((ROWS, WIDTH), jnp.bfloat16),
-            pltpu.VMEM((PEERS, OWN, WIDTH), jnp.bfloat16),
-            pltpu.SemaphoreType.DMA((PEERS,)),
-        ],
+        scratch_shapes=[pltpu.VMEM((PEERS, OWN, WIDTH), jnp.bfloat16), pltpu.SemaphoreType.DMA((PEERS,))],
         compiler_params=pltpu.CompilerParams(vmem_limit_bytes=16 << 20),
         cost_estimate=pl.CostEstimate(flops=work, bytes_accessed=12 << 20, transcendentals=0),
         name="up_far",
-    )(far, theirs, own)
-    pairs = (pair, trade(pair, "z", 2))
-    partial_grad, *pairs = lax.optimization_barrier((partial_grad, *pairs))
+    )(dense, theirs, own)
     received = exchange(partial_grad, ROW)
 
     column = bf16(WIDTH // 2, LANES)

time: 126 us -> 135 us (1.071)
  waiting for transfers between devices: 43.1 us -> 59.7 us
  starting transfers between devices: 54.4 us -> 49 us
  Pallas kernels: 23.1 us -> 20.8 us
    ppermute x17 -> x18, waiting for transfers between devices: 22 us -> 36.6 us  [trade(): lax.ppermute(array, axes, [(i, i ^ bits) for i in range(lax.axis_size(axe...]
    all_to_all x2 -> x1, starting transfers between devices: 8.86 us -> 3.59 us  [exchange(): return lax.all_to_all(parts, axes, 0, 0)]
    pallas_call x1 -> x0, Pallas kernels: 4.85 us -> none  [per_device(): pl.pallas_call(up_kernel, out_shape=(jax.ShapeDtypeStruct((ROWS, WIDTH),...]
    ppermute x17 -> x18, starting transfers between devices: 20.9 us -> 16.1 us  [trade(): lax.ppermute(array, axes, [(i, i ^ bits) for i in range(lax.axis_size(axe...]
    ppermute x0 -> x3, starting transfers between devices: none -> 4.34 us  [per_device(): lax.ppermute(pair, 'x', [(i, (i - k) % RING) for i in range(RING)])]
    pallas_call x18 -> x21, Pallas kernels: 11.4 us -> 13.4 us  [call(): pl.pallas_call(kernel, out_shape=outs, in_specs=[vmem] * len(args), out_s...]
  transfers between devices with their start and end apart: 35 -> 38, of which waited for: 24 -> 24; matrix products, arithmetic and copies ran while one was open for 1% -> 1% of each run, Pallas kernels for 15% -> 11%
where the time goes in v13:
time: 135 us; the launch traced here: 134 us
  waiting for transfers between devices  59.7 us (44%)
  starting transfers between devices  49 us (36%)
  Pallas kernels  20.8 us (15%)
  local copies, waits for them, and re-layouts  1.67 us (1%)
  other arithmetic  1.6 us (1%)
  between operations  1.54 us (1%)
    ppermute x18, waiting for transfers between devices, trade(): lax.ppermute(array, axes, [(i, i ^ bits) for i in range(lax.axis_size(axe...  36.6 us
    ppermute x18, starting transfers between devices, trade(): lax.ppermute(array, axes, [(i, i ^ bits) for i in range(lax.axis_size(axe...  16.1 us
    pallas_call x21, Pallas kernels, call(): pl.pallas_call(kernel, out_shape=outs, in_specs=[vmem] * len(args), out_s...  13.4 us
    ppermute x5, waiting for transfers between devices, pass_on(): lax.ppermute(array, fast, [(i, (i + step) % RING) for i in range(RING)])  8.79 us
    ppermute x5, starting transfers between devices, ahead(): lax.ppermute(array, fast, [(i, (i - step) % RING) for i in range(RING)])  8.4 us
    ppermute x5, starting transfers between devices, pass_on(): lax.ppermute(array, fast, [(i, (i + step) % RING) for i in range(RING)])  7.97 us
    ppermute x5, waiting for transfers between devices, ahead(): lax.ppermute(array, fast, [(i, (i - step) % RING) for i in range(RING)])  4.9 us
    ppermute x3, starting transfers between devices, scatter_ring(): lax.ppermute(pieces[k], axis, [(i, (i + k) % RING) for i in range(RING)])  4.46 us
  transfers between devices with their start and end apart: 38, of which 24 were waited for; matrix products, arithmetic and copies ran while one was open for 1% of the time, Pallas kernels for 11%

profile of v13, /device:TPU:0, one launch (start us, length us, event | category | flops | bytes accessed | tf_op | source)
XLA Modules:
  0.0 134.3 jit_solution(10240334682409932424)
XLA Ops:
  0.6 2.1 %collective-permute-start.1 = (bf16[192,512]{1,0:T(8,128)(2,1)}, bf16[192,512]{1,0:T(8,128)(2,1)S(1)}, u32[]{:S(2)}, u32[]{:S(2)}) collective-permute-start(bf16[192,512]{1,0:T(8,128)(2,1)} %refs_1_.1), channel_id=1, source_target_pairs={{0,16},{16,32},{32,48},{48,0},{1,17},{17,33},{33,49},{49,1},{2,18}... | collective-permute-start | bytes 589832 | tf_op jit(solution)/shard_map/ppermute | solution.py:357
  2.7 1.6 %collective-permute-start = (bf16[192,512]{1,0:T(8,128)(2,1)}, bf16[192,512]{1,0:T(8,128)(2,1)S(1)}, u32[]{:S(2)}, u32[]{:S(2)}) collective-permute-start(bf16[192,512]{1,0:T(8,128)(2,1)} %refs_1_.1), channel_id=1, source_target_pairs={{0,64},{64,0},{1,65},{65,1},{2,66},{66,2},{3,67},{67,3},{4,68},{68... | collective-permute-start | bytes 589832 | tf_op jit(solution)/shard_map/ppermute | solution.py:346
  4.3 2.2 %collective-permute-start.2 = (bf16[192,512]{1,0:T(8,128)(2,1)}, bf16[192,512]{1,0:T(8,128)(2,1)S(1)}, u32[]{:S(2)}, u32[]{:S(2)}) collective-permute-start(bf16[192,512]{1,0:T(8,128)(2,1)} %refs_1_.1), channel_id=1, source_target_pairs={{0,48},{16,0},{32,16},{48,32},{1,49},{17,1},{33,17},{49,33},{2,50}... | collective-permute-start | bytes 589832 | tf_op jit(solution)/shard_map/ppermute | solution.py:357
  8.8 1.7 %copy-done = bf16[1,1,288,4096]{3,2,1,0:T(8,128)(2,1)S(1)} copy-done((bf16[1,1,288,4096]{3,2,1,0:T(8,128)(2,1)S(1)}, bf16[1,1,288,4096]{3,2,1,0:T(8,128)(2,1)}, u32[]{:S(2)}) %copy-start) | copy-done | bytes 2359320
  10.4 2.3 %build_0.1.rest_0_ = bf16[3072,1536]{1,0:T(8,128)(2,1)S(1)} custom-call(s32[288]{0:T(512)S(1)} %fusion.2.places, s32[1,1]{1,0:T(1,128)} %copy.11.counts, bf16[1,1,288,4096]{3,2,1,0:T(8,128)(2,1)S(1)} %copy-done), custom_call_target="tpu_custom_call" | custom-call | bytes 8388608 | tf_op jit(solution)/shard_map/build_0/pallas_call | solution.py:124
  12.8 2.0 %collective-permute-start.4 = (bf16[192,512]{1,0:T(8,128)(2,1)S(1)}, bf16[192,512]{1,0:T(8,128)(2,1)S(1)}, u32[]{:S(2)}, u32[]{:S(2)}) collective-permute-start(bf16[192,512]{1,0:T(8,128)(2,1)S(1)} %collective-permute-done.refs_5_), channel_id=1, source_target_pairs={{0,48},{16,0},{32,16},{48,32},{1,49},{17,1},{33,17},{49,33},{2,50}... | collective-permute-start | bytes 589832 | tf_op jit(solution)/shard_map/ppermute | solution.py:357
  15.0 1.7 %build_1.1.refs_0_.dense = bf16[3072,1536]{1,0:T(8,128)(2,1)S(1)} custom-call(s32[288]{0:T(512)S(1)} %fusion.2.places, s32[1,1]{1,0:T(1,128)} %copy.11.counts, bf16[1,1,288,4096]{3,2,1,0:T(8,128)(2,1)S(1)} %copy-done, bf16[3072,1536]{1,0:T(8,128)(2,1)S(1)} %build_0.1.rest_0_), custom_call_target="tpu_custom_call", output_to_operand_aliasing={{}: (3, {})} | custom-call | bytes 8388608 | tf_op jit(solution)/shard_map/build_1/pallas_call | solution.py:124
  16.7 1.8 %collective-permute-done.4.refs_6_ = bf16[192,512]{1,0:T(8,128)(2,1)S(1)} collective-permute-done((bf16[192,512]{1,0:T(8,128)(2,1)S(1)}, bf16[192,512]{1,0:T(8,128)(2,1)S(1)}, u32[]{:S(2)}, u32[]{:S(2)}) %collective-permute-start.4) | collective-permute-done | bytes 196640 | tf_op jit(solution)/shard_map/ppermute | solution.py:357
  18.5 3.1 %collective-permute-done.5.refs_4_ = bf16[192,512]{1,0:T(8,128)(2,1)S(1)} collective-permute-done((bf16[192,512]{1,0:T(8,128)(2,1)S(1)}, bf16[192,512]{1,0:T(8,128)(2,1)S(1)}, u32[]{:S(2)}, u32[]{:S(2)}) %collective-permute-start.5) | collective-permute-done | bytes 196640 | tf_op jit(solution)/shard_map/ppermute | solution.py:357
  21.6 2.0 %collective-permute-start.6 = (bf16[192,512]{1,0:T(8,128)(2,1)S(1)}, bf16[192,512]{1,0:T(8,128)(2,1)S(1)}, u32[]{:S(2)}, u32[]{:S(2)}) collective-permute-start(bf16[192,512]{1,0:T(8,128)(2,1)S(1)} %collective-permute-done.4.refs_6_), channel_id=1, source_target_pairs={{0,48},{16,0},{32,16},{48,32},{1,49},{17,1},{33,17},{49,33},{2,50}... | collective-permute-start | bytes 589832 | tf_op jit(solution)/shard_map/ppermute | solution.py:357
  23.7 5.0 %down_most.1.most = f32[3072,512]{1,0:T(8,128)S(1)} custom-call(bf16[3072,1536]{1,0:T(8,128)(2,1)S(1)} %build_1.1.refs_0_.dense, bf16[192,512]{1,0:T(8,128)(2,1)S(1)} %copy-done.3, bf16[192,512]{1,0:T(8,128)(2,1)S(1)} %collective-permute-done.2.refs_2_, bf16[192,512]{1,0:T(8,128)(2,1)S(1)} %collective-permute-done.1.refs_3_, ...), custom_call_target="tpu_custom_call" | custom-call | flops 4831838208 | bytes 1048576 | tf_op jit(solution)/shard_map/down_most/pallas_call | solution.py:33
  29.1 2.0 %collective-permute-done.7.other = bf16[576,512]{1,0:T(8,128)(2,1)S(1)} collective-permute-done((bf16[576,512]{1,0:T(8,128)(2,1)S(1)}, bf16[576,512]{1,0:T(8,128)(2,1)S(1)}, u32[]{:S(2)}, u32[]{:S(2)}) %collective-permute-start.7) | collective-permute-done | bytes 589856 | tf_op jit(solution)/shard_map/ppermute | solution.py:346
  32.1 1.6 %collective-permute-start.8 = (bf16[192,512]{1,0:T(8,128)(2,1)S(1)}, bf16[192,512]{1,0:T(8,128)(2,1)S(1)}, u32[]{:S(2)}, u32[]{:S(2)}) collective-permute-start(bf16[192,512]{1,0:T(8,128)(2,1)S(1)} %get-tuple-element.72), channel_id=1, source_target_pairs={{0,2},{2,4},{4,6},{6,0},{1,3},{3,5},{5,7},{7,1},{8,10},{10,12},{12... | collective-permute-start | bytes 589832 | tf_op jit(solution)/shard_map/ppermute | solution.py:232
  33.7 2.5 %collective-permute-start.9 = (bf16[192,512]{1,0:T(8,128)(2,1)S(1)}, bf16[192,512]{1,0:T(8,128)(2,1)S(1)}, u32[]{:S(2)}, u32[]{:S(2)}) collective-permute-start(bf16[192,512]{1,0:T(8,128)(2,1)S(1)} %get-tuple-element.73), channel_id=1, source_target_pairs={{0,8},{8,0},{1,9},{9,1},{2,10},{10,2},{3,11},{11,3},{4,12},{12,4},... | collective-permute-start | bytes 589832 | tf_op jit(solution)/shard_map/ppermute | solution.py:346
  36.1 2.6 %collective-permute-start.10 = (bf16[192,512]{1,0:T(8,128)(2,1)S(1)}, bf16[192,512]{1,0:T(8,128)(2,1)S(1)}, u32[]{:S(2)}, u32[]{:S(2)}) collective-permute-start(bf16[192,512]{1,0:T(8,128)(2,1)S(1)} %get-tuple-element.74), channel_id=1, source_target_pairs={{0,6},{2,0},{4,2},{6,4},{1,7},{3,1},{5,3},{7,5},{8,14},{10,8},{12,... | collective-permute-start | bytes 589832 | tf_op jit(solution)/shard_map/ppermute | solution.py:232
  44.4 2.4 %collective-permute-start.13 = (bf16[192,512]{1,0:T(8,128)(2,1)S(1)}, bf16[192,512]{1,0:T(8,128)(2,1)S(1)}, u32[]{:S(2)}, u32[]{:S(2)}) collective-permute-start(bf16[192,512]{1,0:T(8,128)(2,1)S(1)} %get-tuple-element.87), channel_id=1, source_target_pairs={{0,6},{2,0},{4,2},{6,4},{1,7},{3,1},{5,3},{7,5},{8,14},{10,8},{12,... | collective-permute-start | bytes 589832 | tf_op jit(solution)/shard_map/ppermute | solution.py:232
  46.8 5.4 %collective-permute-done.12.refs_1_ = bf16[192,512]{1,0:T(8,128)(2,1)S(1)} collective-permute-done((bf16[192,512]{1,0:T(8,128)(2,1)S(1)}, bf16[192,512]{1,0:T(8,128)(2,1)S(1)}, u32[]{:S(2)}, u32[]{:S(2)}) %collective-permute-start.12) | collective-permute-done | bytes 196640 | tf_op jit(solution)/shard_map/ppermute | solution.py:232
  54.9 4.6 %collective-permute-done.14.c = bf16[192,512]{1,0:T(8,128)(2,1)S(1)} collective-permute-done((bf16[192,512]{1,0:T(8,128)(2,1)S(1)}, bf16[192,512]{1,0:T(8,128)(2,1)S(1)}, u32[]{:S(2)}, u32[]{:S(2)}) %collective-permute-start.14) | collective-permute-done | bytes 196640 | tf_op jit(solution)/shard_map/ppermute | solution.py:346
  62.5 5.4 %collective-permute-done.16.second = bf16[192,512]{1,0:T(8,128)(2,1)S(1)} collective-permute-done((bf16[192,512]{1,0:T(8,128)(2,1)S(1)}, bf16[192,512]{1,0:T(8,128)(2,1)S(1)}, u32[]{:S(2)}, u32[]{:S(2)}) %collective-permute-start.16) | collective-permute-done | bytes 196640 | tf_op jit(solution)/shard_map/ppermute | solution.py:346
  69.9 3.3 %collective-permute-start.22 = (bf16[64,512]{1,0:T(8,128)(2,1)S(1)}, bf16[64,512]{1,0:T(8,128)(2,1)S(1)}, u32[]{:S(2)}, u32[]{:S(2)}) collective-permute-start(bf16[64,512]{1,0:T(8,128)(2,1)S(1)} %get-tuple-element.103), channel_id=1, source_target_pairs={{0,32},{16,48},{32,0},{48,16},{1,33},{17,49},{33,1},{49,17},{2,34}... | collective-permute-start | bytes 196616 | tf_op jit(solution)/shard_map/ppermute | solution.py:346
  74.6 3.8 %collective-permute-start.18 = (bf16[384,512]{1,0:T(8,128)(2,1)S(1)}, bf16[384,512]{1,0:T(8,128)(2,1)S(1)}, u32[]{:S(2)}, u32[]{:S(2)}) collective-permute-start(bf16[384,512]{1,0:T(8,128)(2,1)S(1)} %pair_y.1.refs_0_), channel_id=1, source_target_pairs={{0,4},{2,6},{4,0},{6,2},{1,5},{3,7},{5,1},{7,3},{8,12},{10,14},{12... | collective-permute-start | bytes 1179656 | tf_op jit(solution)/shard_map/ppermute | solution.py:427
  80.7 3.8 %collective-permute-done.26.d = bf16[64,512]{1,0:T(8,128)(2,1)S(1)} collective-permute-done((bf16[64,512]{1,0:T(8,128)(2,1)S(1)}, bf16[64,512]{1,0:T(8,128)(2,1)S(1)}, u32[]{:S(2)}, u32[]{:S(2)}) %collective-permute-start.26) | collective-permute-done | bytes 65568 | tf_op jit(solution)/shard_map/ppermute | solution.py:346
  85.0 5.3 %collective-permute-done.24.b = bf16[64,512]{1,0:T(8,128)(2,1)S(1)} collective-permute-done((bf16[64,512]{1,0:T(8,128)(2,1)S(1)}, bf16[64,512]{1,0:T(8,128)(2,1)S(1)}, u32[]{:S(2)}, u32[]{:S(2)}) %collective-permute-start.24) | collective-permute-done | bytes 65568 | tf_op jit(solution)/shard_map/ppermute | solution.py:346
  90.4 5.0 %collective-permute-done.27.second = bf16[64,512]{1,0:T(8,128)(2,1)S(1)} collective-permute-done((bf16[64,512]{1,0:T(8,128)(2,1)S(1)}, bf16[64,512]{1,0:T(8,128)(2,1)S(1)}, u32[]{:S(2)}, u32[]{:S(2)}) %collective-permute-start.27) | collective-permute-done | bytes 65568 | tf_op jit(solution)/shard_map/ppermute | solution.py:346
  96.7 5.3 %collective-permute-done.28.high = bf16[128,512]{1,0:T(8,128)(2,1)S(1)} collective-permute-done((bf16[128,512]{1,0:T(8,128)(2,1)S(1)}, bf16[128,512]{1,0:T(8,128)(2,1)S(1)}, u32[]{:S(2)}, u32[]{:S(2)}) %collective-permute-start.28) | collective-permute-done | bytes 131104 | tf_op jit(solution)/shard_map/ppermute | solution.py:346
  102.2 2.6 %up_near.1.other = f32[1536,512]{1,0:T(8,128)S(1)} custom-call(bf16[3072,1536]{1,0:T(8,128)(2,1)S(1)} %build_1.1.refs_0_.dense, bf16[1536,512]{1,0:T(8,128)(2,1)S(1)} %order.1.rows), custom_call_target="tpu_custom_call" | custom-call | flops 2415919104 | bytes 1048576 | tf_op jit(solution)/shard_map/up_near/pallas_call | solution.py:33
  105.6 3.4 %up_far.1 = bf16[8,192,512]{2,1,0:T(8,128)(2,1)} custom-call(bf16[3072,1536]{1,0:T(8,128)(2,1)S(1)} %build_1.1.refs_0_.dense, bf16[1536,512]{1,0:T(8,128)(2,1)S(1)} %collective-permute-done.36.rows, f32[1536,512]{1,0:T(8,128)S(1)} %up_near.1.other), custom_call_target="tpu_custom_call" | custom-call | flops 2415919104 | bytes 12582912 | tf_op jit(solution)/shard_map/up_far/pallas_call | solution.py:437
  108.9 3.6 %all-to-all-start = ((bf16[8,192,512]{2,1,0:T(8,128)(2,1)}), bf16[8,192,512]{2,1,0:T(8,128)(2,1)S(1)}, u32[]{:S(2)}, u32[]{:S(2)}) async-start(bf16[8,192,512]{2,1,0:T(8,128)(2,1)} %up_far.1), calls=%async_computation | async-start | bytes 3145728 | tf_op jit(solution)/shard_map/all_to_all | solution.py:342
  114.1 2.1 %collective-permute-start.30 = (bf16[256,128]{1,0:T(8,128)(2,1)S(1)}, bf16[256,128]{1,0:T(8,128)(2,1)S(1)}, u32[]{:S(2)}, u32[]{:S(2)}) collective-permute-start(bf16[256,128]{1,0:T(8,128)(2,1)S(1)} %get-tuple-element.109), channel_id=1, source_target_pairs={{0,4},{2,6},{4,0},{6,2},{1,5},{3,7},{5,1},{7,3},{8,12},{10,14},{12... | collective-permute-start | bytes 196616 | tf_op jit(solution)/shard_map/ppermute | solution.py:376
  118.2 1.7 %collective-permute-done.30.refs_2_ = bf16[256,128]{1,0:T(8,128)(2,1)S(1)} collective-permute-done((bf16[256,128]{1,0:T(8,128)(2,1)S(1)}, bf16[256,128]{1,0:T(8,128)(2,1)S(1)}, u32[]{:S(2)}, u32[]{:S(2)}) %collective-permute-start.30) | collective-permute-done | bytes 65568 | tf_op jit(solution)/shard_map/ppermute | solution.py:376
  121.4 2.9 %collective-permute-start.33 = (bf16[256,128]{1,0:T(8,128)(2,1)S(1)}, bf16[256,128]{1,0:T(8,128)(2,1)S(1)}, u32[]{:S(2)}, u32[]{:S(2)}) collective-permute-start(bf16[256,128]{1,0:T(8,128)(2,1)S(1)} %sum_x.1.refs_0_), channel_id=1, source_target_pairs={{0,4},{2,6},{4,0},{6,2},{1,5},{3,7},{5,1},{7,3},{8,12},{10,14},{12... | collective-permute-start | bytes 196616 | tf_op jit(solution)/shard_map/ppermute | solution.py:383
  131.4 2.1 %all-to-all-done.parts = bf16[8,192,512]{2,1,0:T(8,128)(2,1)S(1)} async-done(((bf16[8,192,512]{2,1,0:T(8,128)(2,1)}), bf16[8,192,512]{2,1,0:T(8,128)(2,1)S(1)}, u32[]{:S(2)}, u32[]{:S(2)}) %all-to-all-start) | async-done | bytes 1572896 | tf_op jit(solution)/shard_map/all_to_all | solution.py:342
  (79 shorter events, 36.1 us)
Async XLA Ops:
  0.6 12.1 %collective-permute-start.1 = (bf16[192,512]{1,0:T(8,128)(2,1)}, bf16[192,512]{1,0:T(8,128)(2,1)S(1)}, u32[]{:S(2)}, u32[]{:S(2)}) collective-permute-start(bf16[192,512]{1,0:T(8,128)(2,1)} %refs_1_.1), channel_id=1, source_target_pairs={{0,16},{16,32},{32,48},{48,0},{1,17},{17,33},{33,49},{49,1},{2,18}... | collective-permute-start | bytes 589832 | tf_op jit(solution)/shard_map/ppermute | solution.py:357
  2.7 10.0 %collective-permute-start = (bf16[192,512]{1,0:T(8,128)(2,1)}, bf16[192,512]{1,0:T(8,128)(2,1)S(1)}, u32[]{:S(2)}, u32[]{:S(2)}) collective-permute-start(bf16[192,512]{1,0:T(8,128)(2,1)} %refs_1_.1), channel_id=1, source_target_pairs={{0,64},{64,0},{1,65},{65,1},{2,66},{66,2},{3,67},{67,3},{4,68},{68... | collective-permute-start | bytes 589832 | tf_op jit(solution)/shard_map/ppermute | solution.py:346
  4.3 8.5 %collective-permute-start.2 = (bf16[192,512]{1,0:T(8,128)(2,1)}, bf16[192,512]{1,0:T(8,128)(2,1)S(1)}, u32[]{:S(2)}, u32[]{:S(2)}) collective-permute-start(bf16[192,512]{1,0:T(8,128)(2,1)} %refs_1_.1), channel_id=1, source_target_pairs={{0,48},{16,0},{32,16},{48,32},{1,49},{17,1},{33,17},{49,33},{2,50}... | collective-permute-start | bytes 589832 | tf_op jit(solution)/shard_map/ppermute | solution.py:357
  12.8 5.7 %collective-permute-start.4 = (bf16[192,512]{1,0:T(8,128)(2,1)S(1)}, bf16[192,512]{1,0:T(8,128)(2,1)S(1)}, u32[]{:S(2)}, u32[]{:S(2)}) collective-permute-start(bf16[192,512]{1,0:T(8,128)(2,1)S(1)} %collective-permute-done.refs_5_), channel_id=1, source_target_pairs={{0,48},{16,0},{32,16},{48,32},{1,49},{17,1},{33,17},{49,33},{2,50}... | collective-permute-start | bytes 589832 | tf_op jit(solution)/shard_map/ppermute | solution.py:357
  14.8 6.9 %collective-permute-start.5 = (bf16[192,512]{1,0:T(8,128)(2,1)S(1)}, bf16[192,512]{1,0:T(8,128)(2,1)S(1)}, u32[]{:S(2)}, u32[]{:S(2)}) collective-permute-start(bf16[192,512]{1,0:T(8,128)(2,1)S(1)} %collective-permute-done.1.refs_3_), channel_id=1, source_target_pairs={{0,16},{16,32},{32,48},{48,0},{1,17},{17,33},{33,49},{49,1},{2,18}... | collective-permute-start | bytes 589832 | tf_op jit(solution)/shard_map/ppermute | solution.py:357
  14.9 6.8 %collective-permute-start.3 = (bf16[192,512]{1,0:T(8,128)(2,1)S(1)}, bf16[192,512]{1,0:T(8,128)(2,1)S(1)}, u32[]{:S(2)}, u32[]{:S(2)}) collective-permute-start(bf16[192,512]{1,0:T(8,128)(2,1)S(1)} %collective-permute-done.1.refs_3_), channel_id=1, source_target_pairs={{0,64},{64,0},{1,65},{65,1},{2,66},{66,2},{3,67},{67,3},{4,68},{68... | collective-permute-start | bytes 589832 | tf_op jit(solution)/shard_map/ppermute | solution.py:346
  21.6 7.1 %collective-permute-start.6 = (bf16[192,512]{1,0:T(8,128)(2,1)S(1)}, bf16[192,512]{1,0:T(8,128)(2,1)S(1)}, u32[]{:S(2)}, u32[]{:S(2)}) collective-permute-start(bf16[192,512]{1,0:T(8,128)(2,1)S(1)} %collective-permute-done.4.refs_6_), channel_id=1, source_target_pairs={{0,48},{16,0},{32,16},{48,32},{1,49},{17,1},{33,17},{49,33},{2,50}... | collective-permute-start | bytes 589832 | tf_op jit(solution)/shard_map/ppermute | solution.py:357
  31.6 7.2 %collective-permute-start.11 = (bf16[960,512]{1,0:T(8,128)(2,1)S(1)}, bf16[960,512]{1,0:T(8,128)(2,1)S(1)}, u32[]{:S(2)}, u32[]{:S(2)}) collective-permute-start(bf16[960,512]{1,0:T(8,128)(2,1)S(1)} %down_far_1.1), channel_id=1, source_target_pairs={{0,1},{1,0},{2,3},{3,2},{4,5},{5,4},{6,7},{7,6},{8,9},{9,8},{10,11... | collective-permute-start | bytes 2949128 | tf_op jit(solution)/shard_map/ppermute | solution.py:346
  32.1 8.5 %collective-permute-start.8 = (bf16[192,512]{1,0:T(8,128)(2,1)S(1)}, bf16[192,512]{1,0:T(8,128)(2,1)S(1)}, u32[]{:S(2)}, u32[]{:S(2)}) collective-permute-start(bf16[192,512]{1,0:T(8,128)(2,1)S(1)} %get-tuple-element.72), channel_id=1, source_target_pairs={{0,2},{2,4},{4,6},{6,0},{1,3},{3,5},{5,7},{7,1},{8,10},{10,12},{12... | collective-permute-start | bytes 589832 | tf_op jit(solution)/shard_map/ppermute | solution.py:232
  33.7 8.4 %collective-permute-start.9 = (bf16[192,512]{1,0:T(8,128)(2,1)S(1)}, bf16[192,512]{1,0:T(8,128)(2,1)S(1)}, u32[]{:S(2)}, u32[]{:S(2)}) collective-permute-start(bf16[192,512]{1,0:T(8,128)(2,1)S(1)} %get-tuple-element.73), channel_id=1, source_target_pairs={{0,8},{8,0},{1,9},{9,1},{2,10},{10,2},{3,11},{11,3},{4,12},{12,4},... | collective-permute-start | bytes 589832 | tf_op jit(solution)/shard_map/ppermute | solution.py:346
  36.1 6.7 %collective-permute-start.10 = (bf16[192,512]{1,0:T(8,128)(2,1)S(1)}, bf16[192,512]{1,0:T(8,128)(2,1)S(1)}, u32[]{:S(2)}, u32[]{:S(2)}) collective-permute-start(bf16[192,512]{1,0:T(8,128)(2,1)S(1)} %get-tuple-element.74), channel_id=1, source_target_pairs={{0,6},{2,0},{4,2},{6,4},{1,7},{3,1},{5,3},{7,5},{8,14},{10,8},{12,... | collective-permute-start | bytes 589832 | tf_op jit(solution)/shard_map/ppermute | solution.py:232
  42.9 9.2 %collective-permute-start.12 = (bf16[192,512]{1,0:T(8,128)(2,1)S(1)}, bf16[192,512]{1,0:T(8,128)(2,1)S(1)}, u32[]{:S(2)}, u32[]{:S(2)}) collective-permute-start(bf16[192,512]{1,0:T(8,128)(2,1)S(1)} %get-tuple-element.86), channel_id=1, source_target_pairs={{0,2},{2,4},{4,6},{6,0},{1,3},{3,5},{5,7},{7,1},{8,10},{10,12},{12... | collective-permute-start | bytes 589832 | tf_op jit(solution)/shard_map/ppermute | solution.py:232
  44.4 7.8 %collective-permute-start.13 = (bf16[192,512]{1,0:T(8,128)(2,1)S(1)}, bf16[192,512]{1,0:T(8,128)(2,1)S(1)}, u32[]{:S(2)}, u32[]{:S(2)}) collective-permute-start(bf16[192,512]{1,0:T(8,128)(2,1)S(1)} %get-tuple-element.87), channel_id=1, source_target_pairs={{0,6},{2,0},{4,2},{6,4},{1,7},{3,1},{5,3},{7,5},{8,14},{10,8},{12,... | collective-permute-start | bytes 589832 | tf_op jit(solution)/shard_map/ppermute | solution.py:232
  46.8 8.1 %collective-permute-start.15 = (bf16[192,512]{1,0:T(8,128)(2,1)S(1)}, bf16[192,512]{1,0:T(8,128)(2,1)S(1)}, u32[]{:S(2)}, u32[]{:S(2)}) collective-permute-start(bf16[192,512]{1,0:T(8,128)(2,1)S(1)} %get-tuple-element.91), channel_id=1, source_target_pairs={{0,2},{2,4},{4,6},{6,0},{1,3},{3,5},{5,7},{7,1},{8,10},{10,12},{12... | collective-permute-start | bytes 589832 | tf_op jit(solution)/shard_map/ppermute | solution.py:232
  52.2 7.3 %collective-permute-start.14 = (bf16[192,512]{1,0:T(8,128)(2,1)S(1)}, bf16[192,512]{1,0:T(8,128)(2,1)S(1)}, u32[]{:S(2)}, u32[]{:S(2)}) collective-permute-start(bf16[192,512]{1,0:T(8,128)(2,1)S(1)} %sum_across.1), channel_id=1, source_target_pairs={{0,8},{8,0},{1,9},{9,1},{2,10},{10,2},{3,11},{11,3},{4,12},{12,4},... | collective-permute-start | bytes 589832 | tf_op jit(solution)/shard_map/ppermute | solution.py:346
  60.7 7.2 %collective-permute-start.16 = (bf16[192,512]{1,0:T(8,128)(2,1)S(1)}, bf16[192,512]{1,0:T(8,128)(2,1)S(1)}, u32[]{:S(2)}, u32[]{:S(2)}) collective-permute-start(bf16[192,512]{1,0:T(8,128)(2,1)S(1)} %get-tuple-element.97.first), channel_id=1, source_target_pairs={{0,8},{8,0},{1,9},{9,1},{2,10},{10,2},{3,11},{11,3},{4,12},{12,4},... | collective-permute-start | bytes 589832 | tf_op jit(solution)/shard_map/ppermute | solution.py:346
  69.8 8.6 %collective-permute-start.21 = (bf16[64,512]{1,0:T(8,128)(2,1)S(1)}, bf16[64,512]{1,0:T(8,128)(2,1)S(1)}, u32[]{:S(2)}, u32[]{:S(2)}) collective-permute-start(bf16[64,512]{1,0:T(8,128)(2,1)S(1)} %get-tuple-element.102), channel_id=1, source_target_pairs={{0,16},{16,0},{32,48},{48,32},{1,17},{17,1},{33,49},{49,33},{2,18}... | collective-permute-start | bytes 196616 | tf_op jit(solution)/shard_map/ppermute | solution.py:346
  69.9 9.0 %collective-permute-start.22 = (bf16[64,512]{1,0:T(8,128)(2,1)S(1)}, bf16[64,512]{1,0:T(8,128)(2,1)S(1)}, u32[]{:S(2)}, u32[]{:S(2)}) collective-permute-start(bf16[64,512]{1,0:T(8,128)(2,1)S(1)} %get-tuple-element.103), channel_id=1, source_target_pairs={{0,32},{16,48},{32,0},{48,16},{1,33},{17,49},{33,1},{49,17},{2,34}... | collective-permute-start | bytes 196616 | tf_op jit(solution)/shard_map/ppermute | solution.py:346
  73.2 5.7 %collective-permute-start.23 = (bf16[64,512]{1,0:T(8,128)(2,1)S(1)}, bf16[64,512]{1,0:T(8,128)(2,1)S(1)}, u32[]{:S(2)}, u32[]{:S(2)}) collective-permute-start(bf16[64,512]{1,0:T(8,128)(2,1)S(1)} %get-tuple-element.104), channel_id=1, source_target_pairs={{0,48},{16,32},{32,16},{48,0},{1,49},{17,33},{33,17},{49,1},{2,50}... | collective-permute-start | bytes 196616 | tf_op jit(solution)/shard_map/ppermute | solution.py:346
  74.6 22.1 %collective-permute-start.19 = (bf16[384,512]{1,0:T(8,128)(2,1)S(1)}, bf16[384,512]{1,0:T(8,128)(2,1)S(1)}, u32[]{:S(2)}, u32[]{:S(2)}) collective-permute-start(bf16[384,512]{1,0:T(8,128)(2,1)S(1)} %pair_y.1.refs_0_), channel_id=1, source_target_pairs={{0,2},{2,4},{4,6},{6,0},{1,3},{3,5},{5,7},{7,1},{8,10},{10,12},{12... | collective-permute-start | bytes 1179656 | tf_op jit(solution)/shard_map/ppermute | solution.py:427
  74.6 22.1 %collective-permute-start.18 = (bf16[384,512]{1,0:T(8,128)(2,1)S(1)}, bf16[384,512]{1,0:T(8,128)(2,1)S(1)}, u32[]{:S(2)}, u32[]{:S(2)}) collective-permute-start(bf16[384,512]{1,0:T(8,128)(2,1)S(1)} %pair_y.1.refs_0_), channel_id=1, source_target_pairs={{0,4},{2,6},{4,0},{6,2},{1,5},{3,7},{5,1},{7,3},{8,12},{10,14},{12... | collective-permute-start | bytes 1179656 | tf_op jit(solution)/shard_map/ppermute | solution.py:427
  78.4 18.2 %collective-permute-start.17 = (bf16[384,512]{1,0:T(8,128)(2,1)S(1)}, bf16[384,512]{1,0:T(8,128)(2,1)S(1)}, u32[]{:S(2)}, u32[]{:S(2)}) collective-permute-start(bf16[384,512]{1,0:T(8,128)(2,1)S(1)} %pair_y.1.refs_0_), channel_id=1, source_target_pairs={{0,6},{2,0},{4,2},{6,4},{1,7},{3,1},{5,3},{7,5},{8,14},{10,8},{12,... | collective-permute-start | bytes 1179656 | tf_op jit(solution)/shard_map/ppermute | solution.py:427
  79.0 5.6 %collective-permute-start.26 = (bf16[64,512]{1,0:T(8,128)(2,1)S(1)}, bf16[64,512]{1,0:T(8,128)(2,1)S(1)}, u32[]{:S(2)}, u32[]{:S(2)}) collective-permute-start(bf16[64,512]{1,0:T(8,128)(2,1)S(1)} %sum_z.1.a), channel_id=1, source_target_pairs={{0,72},{8,64},{64,8},{72,0},{1,73},{9,65},{65,9},{73,1},{2,74},{10... | collective-permute-start | bytes 196616 | tf_op jit(solution)/shard_map/ppermute | solution.py:346
  79.7 5.3 %collective-permute-start.25 = (bf16[64,512]{1,0:T(8,128)(2,1)S(1)}, bf16[64,512]{1,0:T(8,128)(2,1)S(1)}, u32[]{:S(2)}, u32[]{:S(2)}) collective-permute-start(bf16[64,512]{1,0:T(8,128)(2,1)S(1)} %sum_z.1.a), channel_id=1, source_target_pairs={{0,64},{8,72},{64,0},{72,8},{1,65},{9,73},{65,1},{73,9},{2,66},{10... | collective-permute-start | bytes 196616 | tf_op jit(solution)/shard_map/ppermute | solution.py:346
  84.5 5.8 %collective-permute-start.24 = (bf16[64,512]{1,0:T(8,128)(2,1)S(1)}, bf16[64,512]{1,0:T(8,128)(2,1)S(1)}, u32[]{:S(2)}, u32[]{:S(2)}) collective-permute-start(bf16[64,512]{1,0:T(8,128)(2,1)S(1)} %sum_z.1.a), channel_id=1, source_target_pairs={{0,8},{8,0},{64,72},{72,64},{1,9},{9,1},{65,73},{73,65},{2,10},{10... | collective-permute-start | bytes 196616 | tf_op jit(solution)/shard_map/ppermute | solution.py:346
  90.4 5.0 %collective-permute-start.27 = (bf16[64,512]{1,0:T(8,128)(2,1)S(1)}, bf16[64,512]{1,0:T(8,128)(2,1)S(1)}, u32[]{:S(2)}, u32[]{:S(2)}) collective-permute-start(bf16[64,512]{1,0:T(8,128)(2,1)S(1)} %sum_y.1.first), channel_id=1, source_target_pairs={{0,16},{16,0},{32,48},{48,32},{1,17},{17,1},{33,49},{49,33},{2,18}... | collective-permute-start | bytes 196616 | tf_op jit(solution)/shard_map/ppermute | solution.py:346
  95.4 6.6 %collective-permute-start.28 = (bf16[128,512]{1,0:T(8,128)(2,1)S(1)}, bf16[128,512]{1,0:T(8,128)(2,1)S(1)}, u32[]{:S(2)}, u32[]{:S(2)}) collective-permute-start(bf16[128,512]{1,0:T(8,128)(2,1)S(1)} %double.1.low), channel_id=1, source_target_pairs={{0,32},{16,48},{32,0},{48,16},{1,33},{17,49},{33,1},{49,17},{2,34}... | collective-permute-start | bytes 393224 | tf_op jit(solution)/shard_map/ppermute | solution.py:346
  108.9 24.5 %all-to-all-start = ((bf16[8,192,512]{2,1,0:T(8,128)(2,1)}), bf16[8,192,512]{2,1,0:T(8,128)(2,1)S(1)}, u32[]{:S(2)}, u32[]{:S(2)}) async-start(bf16[8,192,512]{2,1,0:T(8,128)(2,1)} %up_far.1), calls=%async_computation | async-start | bytes 3145728 | tf_op jit(solution)/shard_map/all_to_all | solution.py:342
  112.6 5.6 %collective-permute-start.29 = (bf16[256,128]{1,0:T(8,128)(2,1)S(1)}, bf16[256,128]{1,0:T(8,128)(2,1)S(1)}, u32[]{:S(2)}, u32[]{:S(2)}) collective-permute-start(bf16[256,128]{1,0:T(8,128)(2,1)S(1)} %get-tuple-element.108), channel_id=1, source_target_pairs={{0,2},{2,4},{4,6},{6,0},{1,3},{3,5},{5,7},{7,1},{8,10},{10,12},{12... | collective-permute-start | bytes 196616 | tf_op jit(solution)/shard_map/ppermute | solution.py:376
  114.1 5.8 %collective-permute-start.30 = (bf16[256,128]{1,0:T(8,128)(2,1)S(1)}, bf16[256,128]{1,0:T(8,128)(2,1)S(1)}, u32[]{:S(2)}, u32[]{:S(2)}) collective-permute-start(bf16[256,128]{1,0:T(8,128)(2,1)S(1)} %get-tuple-element.109), channel_id=1, source_target_pairs={{0,4},{2,6},{4,0},{6,2},{1,5},{3,7},{5,1},{7,3},{8,12},{10,14},{12... | collective-permute-start | bytes 196616 | tf_op jit(solution)/shard_map/ppermute | solution.py:376
  120.6 5.5 %collective-permute-start.34 = (bf16[256,128]{1,0:T(8,128)(2,1)S(1)}, bf16[256,128]{1,0:T(8,128)(2,1)S(1)}, u32[]{:S(2)}, u32[]{:S(2)}) collective-permute-start(bf16[256,128]{1,0:T(8,128)(2,1)S(1)} %sum_x.1.refs_0_), channel_id=1, source_target_pairs={{0,2},{2,4},{4,6},{6,0},{1,3},{3,5},{5,7},{7,1},{8,10},{10,12},{12... | collective-permute-start | bytes 196616 | tf_op jit(solution)/shard_map/ppermute | solution.py:383
  121.4 5.9 %collective-permute-start.33 = (bf16[256,128]{1,0:T(8,128)(2,1)S(1)}, bf16[256,128]{1,0:T(8,128)(2,1)S(1)}, u32[]{:S(2)}, u32[]{:S(2)}) collective-permute-start(bf16[256,128]{1,0:T(8,128)(2,1)S(1)} %sum_x.1.refs_0_), channel_id=1, source_target_pairs={{0,4},{2,6},{4,0},{6,2},{1,5},{3,7},{5,1},{7,3},{8,12},{10,14},{12... | collective-permute-start | bytes 196616 | tf_op jit(solution)/shard_map/ppermute | solution.py:383
  (10 other events, 76.8 us)

commit v14 on v13

--- a/solution.py
+++ b/solution.py
@@ -423,17 +423,16 @@
         )
 
     pair = vmem_call(double_kernel, bf16(2 * OWN, WIDTH), "pair_y")(send, trade(send, "y_hi"))
-    wgrads, pair = lax.optimization_barrier((wgrads, pair))
     mine = [pair] + [lax.ppermute(pair, "x", [(i, (i - k) % RING) for i in range(RING)]) for k in range(1, RING)]
     summed = over_y(over_z(over_core(wgrads)))
-    low = vmem_call(double_kernel, bf16(2 * PIECE, WIDTH), "double")(summed, trade(summed, "z", 1))
-    mine, *pairs = lax.optimization_barrier((mine, low, trade(low, "z", 2)))
+    mine, summed, next_piece = lax.optimization_barrier((mine, summed, trade(summed, "z", 1)))
     mine = vmem_call(order_kernel, bf16(ROWS, WIDTH), "order")(*mine)
 
     theirs = trade(mine, "core")
     work = 2 * ROWS * ROWS * WIDTH
     vmem = pl.BlockSpec(memory_space=pltpu.VMEM)
     own = vmem_call(up_kernel, jax.ShapeDtypeStruct((ROWS, WIDTH), jnp.float32), "up_near", flops=work)(dense, mine)
+    low = vmem_call(double_kernel, bf16(2 * PIECE, WIDTH), "double")(summed, next_piece)
     partial_grad = pl.pallas_call(
         up_add_kernel,
         out_shape=bf16(PEERS, OWN, WIDTH),
@@ -444,6 +443,7 @@
         cost_estimate=pl.CostEstimate(flops=work, bytes_accessed=12 << 20, transcendentals=0),
         name="up_far",
     )(dense, theirs, own)
+    partial_grad, *pairs = lax.optimization_barrier((partial_grad, low, trade(low, "z", 2)))
     received = exchange(partial_grad, ROW)
 
     column = bf16(WIDTH // 2, LANES)

time: 135 us -> 134 us (level)
  starting transfers between devices: 49 us -> 52 us
  waiting for transfers between devices: 59.7 us -> 57.1 us
  Pallas kernels: 20.8 us -> 19.3 us
    ppermute x18, waiting for transfers between devices: 36.6 us -> 34.8 us  [trade(): lax.ppermute(array, axes, [(i, i ^ bits) for i in range(lax.axis_size(axe...]
    ppermute x18, starting transfers between devices: 16.1 us -> 17.7 us  [trade(): lax.ppermute(array, axes, [(i, i ^ bits) for i in range(lax.axis_size(axe...]
    pallas_call x2, Pallas kernels: 4.01 us -> 2.47 us  [build(): pl.pallas_call(functools.partial(build_kernel, part), out_shape=bf16(2 *...]
  transfers between devices with their start and end apart: 38 -> 38, of which waited for: 24 -> 24; matrix products, arithmetic and copies ran while one was open for 1% -> 1% of each run, Pallas kernels for 11% -> 12%
where the time goes in v14:
time: 134 us; the launch traced here: 133 us
  waiting for transfers between devices  57.1 us (43%)
  starting transfers between devices  52 us (39%)
  Pallas kernels  19.3 us (14%)
  local copies, waits for them, and re-layouts  1.67 us (1%)
  other arithmetic  1.6 us (1%)
  between operations  1.57 us (1%)
    ppermute x18, waiting for transfers between devices, trade(): lax.ppermute(array, axes, [(i, i ^ bits) for i in range(lax.axis_size(axe...  34.8 us
    ppermute x18, starting transfers between devices, trade(): lax.ppermute(array, axes, [(i, i ^ bits) for i in range(lax.axis_size(axe...  17.7 us
    pallas_call x21, Pallas kernels, call(): pl.pallas_call(kernel, out_shape=outs, in_specs=[vmem] * len(args), out_s...  13.4 us
    ppermute x5, waiting for transfers between devices, pass_on(): lax.ppermute(array, fast, [(i, (i + step) % RING) for i in range(RING)])  8.74 us
    ppermute x5, starting transfers between devices, ahead(): lax.ppermute(array, fast, [(i, (i - step) % RING) for i in range(RING)])  8.46 us
    ppermute x5, starting transfers between devices, pass_on(): lax.ppermute(array, fast, [(i, (i + step) % RING) for i in range(RING)])  7.93 us
    ppermute x5, waiting for transfers between devices, ahead(): lax.ppermute(array, fast, [(i, (i - step) % RING) for i in range(RING)])  5.52 us
    ppermute x3, starting transfers between devices, scatter_ring(): lax.ppermute(pieces[k], axis, [(i, (i + k) % RING) for i in range(RING)])  5.15 us
  transfers between devices with their start and end apart: 38, of which 24 were waited for; matrix products, arithmetic and copies ran while one was open for 1% of the time, Pallas kernels for 12%

profile of v14, /device:TPU:0, one launch (start us, length us, event | category | flops | bytes accessed | tf_op | source)
XLA Modules:
  0.0 133.3 jit_solution(9633302719597142169)
XLA Ops:
  0.6 2.1 %collective-permute-start.1 = (bf16[192,512]{1,0:T(8,128)(2,1)}, bf16[192,512]{1,0:T(8,128)(2,1)S(1)}, u32[]{:S(2)}, u32[]{:S(2)}) collective-permute-start(bf16[192,512]{1,0:T(8,128)(2,1)} %refs_1_.1), channel_id=1, source_target_pairs={{0,16},{16,32},{32,48},{48,0},{1,17},{17,33},{33,49},{49,1},{2,18}... | collective-permute-start | bytes 589832 | tf_op jit(solution)/shard_map/ppermute | solution.py:357
  2.7 1.6 %collective-permute-start = (bf16[192,512]{1,0:T(8,128)(2,1)}, bf16[192,512]{1,0:T(8,128)(2,1)S(1)}, u32[]{:S(2)}, u32[]{:S(2)}) collective-permute-start(bf16[192,512]{1,0:T(8,128)(2,1)} %refs_1_.1), channel_id=1, source_target_pairs={{0,64},{64,0},{1,65},{65,1},{2,66},{66,2},{3,67},{67,3},{4,68},{68... | collective-permute-start | bytes 589832 | tf_op jit(solution)/shard_map/ppermute | solution.py:346
  4.3 2.2 %collective-permute-start.2 = (bf16[192,512]{1,0:T(8,128)(2,1)}, bf16[192,512]{1,0:T(8,128)(2,1)S(1)}, u32[]{:S(2)}, u32[]{:S(2)}) collective-permute-start(bf16[192,512]{1,0:T(8,128)(2,1)} %refs_1_.1), channel_id=1, source_target_pairs={{0,48},{16,0},{32,16},{48,32},{1,49},{17,1},{33,17},{49,33},{2,50}... | collective-permute-start | bytes 589832 | tf_op jit(solution)/shard_map/ppermute | solution.py:357
  8.8 1.7 %copy-done = bf16[1,1,288,4096]{3,2,1,0:T(8,128)(2,1)S(1)} copy-done((bf16[1,1,288,4096]{3,2,1,0:T(8,128)(2,1)S(1)}, bf16[1,1,288,4096]{3,2,1,0:T(8,128)(2,1)}, u32[]{:S(2)}) %copy-start) | copy-done | bytes 2359320
  12.0 2.3 %collective-permute-start.4 = (bf16[192,512]{1,0:T(8,128)(2,1)S(1)}, bf16[192,512]{1,0:T(8,128)(2,1)S(1)}, u32[]{:S(2)}, u32[]{:S(2)}) collective-permute-start(bf16[192,512]{1,0:T(8,128)(2,1)S(1)} %collective-permute-done.refs_5_), channel_id=1, source_target_pairs={{0,48},{16,0},{32,16},{48,32},{1,49},{17,1},{33,17},{49,33},{2,50}... | collective-permute-start | bytes 589832 | tf_op jit(solution)/shard_map/ppermute | solution.py:357
  15.8 2.4 %collective-permute-done.4.refs_6_ = bf16[192,512]{1,0:T(8,128)(2,1)S(1)} collective-permute-done((bf16[192,512]{1,0:T(8,128)(2,1)S(1)}, bf16[192,512]{1,0:T(8,128)(2,1)S(1)}, u32[]{:S(2)}, u32[]{:S(2)}) %collective-permute-start.4) | collective-permute-done | bytes 196640 | tf_op jit(solution)/shard_map/ppermute | solution.py:357
  18.1 3.2 %collective-permute-done.5.refs_4_ = bf16[192,512]{1,0:T(8,128)(2,1)S(1)} collective-permute-done((bf16[192,512]{1,0:T(8,128)(2,1)S(1)}, bf16[192,512]{1,0:T(8,128)(2,1)S(1)}, u32[]{:S(2)}, u32[]{:S(2)}) %collective-permute-start.5) | collective-permute-done | bytes 196640 | tf_op jit(solution)/shard_map/ppermute | solution.py:357
  21.3 1.9 %collective-permute-start.6 = (bf16[192,512]{1,0:T(8,128)(2,1)S(1)}, bf16[192,512]{1,0:T(8,128)(2,1)S(1)}, u32[]{:S(2)}, u32[]{:S(2)}) collective-permute-start(bf16[192,512]{1,0:T(8,128)(2,1)S(1)} %collective-permute-done.4.refs_6_), channel_id=1, source_target_pairs={{0,48},{16,0},{32,16},{48,32},{1,49},{17,1},{33,17},{49,33},{2,50}... | collective-permute-start | bytes 589832 | tf_op jit(solution)/shard_map/ppermute | solution.py:357
  23.2 5.0 %down_most.1.most = f32[3072,512]{1,0:T(8,128)S(1)} custom-call(bf16[3072,1536]{1,0:T(8,128)(2,1)S(1)} %build_1.1.refs_0_.dense, bf16[192,512]{1,0:T(8,128)(2,1)S(1)} %copy-done.3, bf16[192,512]{1,0:T(8,128)(2,1)S(1)} %collective-permute-done.2.refs_2_, bf16[192,512]{1,0:T(8,128)(2,1)S(1)} %collective-permute-done.1.refs_3_, ...), custom_call_target="tpu_custom_call" | custom-call | flops 4831838208 | bytes 1048576 | tf_op jit(solution)/shard_map/down_most/pallas_call | solution.py:33
  28.7 2.0 %collective-permute-done.7.other = bf16[576,512]{1,0:T(8,128)(2,1)S(1)} collective-permute-done((bf16[576,512]{1,0:T(8,128)(2,1)S(1)}, bf16[576,512]{1,0:T(8,128)(2,1)S(1)}, u32[]{:S(2)}, u32[]{:S(2)}) %collective-permute-start.7) | collective-permute-done | bytes 589856 | tf_op jit(solution)/shard_map/ppermute | solution.py:346
  31.6 1.6 %collective-permute-start.8 = (bf16[192,512]{1,0:T(8,128)(2,1)S(1)}, bf16[192,512]{1,0:T(8,128)(2,1)S(1)}, u32[]{:S(2)}, u32[]{:S(2)}) collective-permute-start(bf16[192,512]{1,0:T(8,128)(2,1)S(1)} %get-tuple-element.72), channel_id=1, source_target_pairs={{0,2},{2,4},{4,6},{6,0},{1,3},{3,5},{5,7},{7,1},{8,10},{10,12},{12... | collective-permute-start | bytes 589832 | tf_op jit(solution)/shard_map/ppermute | solution.py:232
  33.2 3.0 %collective-permute-start.9 = (bf16[192,512]{1,0:T(8,128)(2,1)S(1)}, bf16[192,512]{1,0:T(8,128)(2,1)S(1)}, u32[]{:S(2)}, u32[]{:S(2)}) collective-permute-start(bf16[192,512]{1,0:T(8,128)(2,1)S(1)} %get-tuple-element.73), channel_id=1, source_target_pairs={{0,8},{8,0},{1,9},{9,1},{2,10},{10,2},{3,11},{11,3},{4,12},{12,4},... | collective-permute-start | bytes 589832 | tf_op jit(solution)/shard_map/ppermute | solution.py:346
  36.2 2.5 %collective-permute-start.10 = (bf16[192,512]{1,0:T(8,128)(2,1)S(1)}, bf16[192,512]{1,0:T(8,128)(2,1)S(1)}, u32[]{:S(2)}, u32[]{:S(2)}) collective-permute-start(bf16[192,512]{1,0:T(8,128)(2,1)S(1)} %get-tuple-element.74), channel_id=1, source_target_pairs={{0,6},{2,0},{4,2},{6,4},{1,7},{3,1},{5,3},{7,5},{8,14},{10,8},{12,... | collective-permute-start | bytes 589832 | tf_op jit(solution)/shard_map/ppermute | solution.py:232
  44.4 2.3 %collective-permute-start.13 = (bf16[192,512]{1,0:T(8,128)(2,1)S(1)}, bf16[192,512]{1,0:T(8,128)(2,1)S(1)}, u32[]{:S(2)}, u32[]{:S(2)}) collective-permute-start(bf16[192,512]{1,0:T(8,128)(2,1)S(1)} %get-tuple-element.87), channel_id=1, source_target_pairs={{0,6},{2,0},{4,2},{6,4},{1,7},{3,1},{5,3},{7,5},{8,14},{10,8},{12,... | collective-permute-start | bytes 589832 | tf_op jit(solution)/shard_map/ppermute | solution.py:232
  46.8 5.4 %collective-permute-done.12.refs_1_ = bf16[192,512]{1,0:T(8,128)(2,1)S(1)} collective-permute-done((bf16[192,512]{1,0:T(8,128)(2,1)S(1)}, bf16[192,512]{1,0:T(8,128)(2,1)S(1)}, u32[]{:S(2)}, u32[]{:S(2)}) %collective-permute-start.12) | collective-permute-done | bytes 196640 | tf_op jit(solution)/shard_map/ppermute | solution.py:232
  54.9 4.6 %collective-permute-done.14.c = bf16[192,512]{1,0:T(8,128)(2,1)S(1)} collective-permute-done((bf16[192,512]{1,0:T(8,128)(2,1)S(1)}, bf16[192,512]{1,0:T(8,128)(2,1)S(1)}, u32[]{:S(2)}, u32[]{:S(2)}) %collective-permute-start.14) | collective-permute-done | bytes 196640 | tf_op jit(solution)/shard_map/ppermute | solution.py:346
  61.3 1.7 %collective-permute-start.16 = (bf16[192,512]{1,0:T(8,128)(2,1)S(1)}, bf16[192,512]{1,0:T(8,128)(2,1)S(1)}, u32[]{:S(2)}, u32[]{:S(2)}) collective-permute-start(bf16[192,512]{1,0:T(8,128)(2,1)S(1)} %get-tuple-element.93.first), channel_id=1, source_target_pairs={{0,8},{8,0},{1,9},{9,1},{2,10},{10,2},{3,11},{11,3},{4,12},{12,4},... | collective-permute-start | bytes 589832 | tf_op jit(solution)/shard_map/ppermute | solution.py:346
  62.9 7.1 %collective-permute-done.16.second = bf16[192,512]{1,0:T(8,128)(2,1)S(1)} collective-permute-done((bf16[192,512]{1,0:T(8,128)(2,1)S(1)}, bf16[192,512]{1,0:T(8,128)(2,1)S(1)}, u32[]{:S(2)}, u32[]{:S(2)}) %collective-permute-start.16) | collective-permute-done | bytes 196640 | tf_op jit(solution)/shard_map/ppermute | solution.py:346
  70.2 3.8 %collective-permute-start.18 = (bf16[384,512]{1,0:T(8,128)(2,1)S(1)}, bf16[384,512]{1,0:T(8,128)(2,1)S(1)}, u32[]{:S(2)}, u32[]{:S(2)}) collective-permute-start(bf16[384,512]{1,0:T(8,128)(2,1)S(1)} %pair_y.1.refs_0_), channel_id=1, source_target_pairs={{0,4},{2,6},{4,0},{6,2},{1,5},{3,7},{5,1},{7,3},{8,12},{10,14},{12... | collective-permute-start | bytes 1179656 | tf_op jit(solution)/shard_map/ppermute | solution.py:426
  74.7 3.3 %collective-permute-start.22 = (bf16[64,512]{1,0:T(8,128)(2,1)S(1)}, bf16[64,512]{1,0:T(8,128)(2,1)S(1)}, u32[]{:S(2)}, u32[]{:S(2)}) collective-permute-start(bf16[64,512]{1,0:T(8,128)(2,1)S(1)} %get-tuple-element.100), channel_id=1, source_target_pairs={{0,32},{16,48},{32,0},{48,16},{1,33},{17,49},{33,1},{49,17},{2,34}... | collective-permute-start | bytes 196616 | tf_op jit(solution)/shard_map/ppermute | solution.py:346
  78.9 1.8 %collective-permute-start.23 = (bf16[64,512]{1,0:T(8,128)(2,1)S(1)}, bf16[64,512]{1,0:T(8,128)(2,1)S(1)}, u32[]{:S(2)}, u32[]{:S(2)}) collective-permute-start(bf16[64,512]{1,0:T(8,128)(2,1)S(1)} %get-tuple-element.101), channel_id=1, source_target_pairs={{0,48},{16,32},{32,16},{48,0},{1,49},{17,33},{33,17},{49,1},{2,50}... | collective-permute-start | bytes 196616 | tf_op jit(solution)/shard_map/ppermute | solution.py:346
  81.0 3.5 %collective-permute-done.23.refs_3_ = bf16[64,512]{1,0:T(8,128)(2,1)S(1)} collective-permute-done((bf16[64,512]{1,0:T(8,128)(2,1)S(1)}, bf16[64,512]{1,0:T(8,128)(2,1)S(1)}, u32[]{:S(2)}, u32[]{:S(2)}) %collective-permute-start.23) | collective-permute-done | bytes 65568 | tf_op jit(solution)/shard_map/ppermute | solution.py:346
  86.2 3.8 %collective-permute-done.26.d = bf16[64,512]{1,0:T(8,128)(2,1)S(1)} collective-permute-done((bf16[64,512]{1,0:T(8,128)(2,1)S(1)}, bf16[64,512]{1,0:T(8,128)(2,1)S(1)}, u32[]{:S(2)}, u32[]{:S(2)}) %collective-permute-start.26) | collective-permute-done | bytes 65568 | tf_op jit(solution)/shard_map/ppermute | solution.py:346
  90.5 5.3 %collective-permute-done.24.b = bf16[64,512]{1,0:T(8,128)(2,1)S(1)} collective-permute-done((bf16[64,512]{1,0:T(8,128)(2,1)S(1)}, bf16[64,512]{1,0:T(8,128)(2,1)S(1)}, u32[]{:S(2)}, u32[]{:S(2)}) %collective-permute-start.24) | collective-permute-done | bytes 65568 | tf_op jit(solution)/shard_map/ppermute | solution.py:346
  95.9 4.3 %collective-permute-done.27.second = bf16[64,512]{1,0:T(8,128)(2,1)S(1)} collective-permute-done((bf16[64,512]{1,0:T(8,128)(2,1)S(1)}, bf16[64,512]{1,0:T(8,128)(2,1)S(1)}, u32[]{:S(2)}, u32[]{:S(2)}) %collective-permute-start.27) | collective-permute-done | bytes 65568 | tf_op jit(solution)/shard_map/ppermute | solution.py:346
  101.8 2.6 %up_near.1.other = f32[1536,512]{1,0:T(8,128)S(1)} custom-call(bf16[3072,1536]{1,0:T(8,128)(2,1)S(1)} %build_1.1.refs_0_.dense, bf16[1536,512]{1,0:T(8,128)(2,1)S(1)} %order.1.rows), custom_call_target="tpu_custom_call" | custom-call | flops 2415919104 | bytes 1048576 | tf_op jit(solution)/shard_map/up_near/pallas_call | solution.py:33
  104.4 3.4 %up_far.1 = bf16[8,192,512]{2,1,0:T(8,128)(2,1)} custom-call(bf16[3072,1536]{1,0:T(8,128)(2,1)S(1)} %build_1.1.refs_0_.dense, bf16[1536,512]{1,0:T(8,128)(2,1)S(1)} %collective-permute-done.28.rows, f32[1536,512]{1,0:T(8,128)S(1)} %up_near.1.other), custom_call_target="tpu_custom_call" | custom-call | flops 2415919104 | bytes 12582912 | tf_op jit(solution)/shard_map/up_far/pallas_call | solution.py:436
  107.9 3.6 %all-to-all-start = ((bf16[8,192,512]{2,1,0:T(8,128)(2,1)}), bf16[8,192,512]{2,1,0:T(8,128)(2,1)S(1)}, u32[]{:S(2)}, u32[]{:S(2)}) async-start(bf16[8,192,512]{2,1,0:T(8,128)(2,1)} %up_far.1), calls=%async_computation | async-start | bytes 3145728 | tf_op jit(solution)/shard_map/all_to_all | solution.py:342
  111.5 2.2 %collective-permute-start.30 = (bf16[256,128]{1,0:T(8,128)(2,1)S(1)}, bf16[256,128]{1,0:T(8,128)(2,1)S(1)}, u32[]{:S(2)}, u32[]{:S(2)}) collective-permute-start(bf16[256,128]{1,0:T(8,128)(2,1)S(1)} %get-tuple-element.111), channel_id=1, source_target_pairs={{0,2},{2,4},{4,6},{6,0},{1,3},{3,5},{5,7},{7,1},{8,10},{10,12},{12... | collective-permute-start | bytes 196616 | tf_op jit(solution)/shard_map/ppermute | solution.py:376
  114.1 2.5 %collective-permute-start.32 = (bf16[256,128]{1,0:T(8,128)(2,1)S(1)}, bf16[256,128]{1,0:T(8,128)(2,1)S(1)}, u32[]{:S(2)}, u32[]{:S(2)}) collective-permute-start(bf16[256,128]{1,0:T(8,128)(2,1)S(1)} %get-tuple-element.113), channel_id=1, source_target_pairs={{0,6},{2,0},{4,2},{6,4},{1,7},{3,1},{5,3},{7,5},{8,14},{10,8},{12,... | collective-permute-start | bytes 196616 | tf_op jit(solution)/shard_map/ppermute | solution.py:376
  117.1 2.5 %collective-permute-done.31.refs_2_ = bf16[256,128]{1,0:T(8,128)(2,1)S(1)} collective-permute-done((bf16[256,128]{1,0:T(8,128)(2,1)S(1)}, bf16[256,128]{1,0:T(8,128)(2,1)S(1)}, u32[]{:S(2)}, u32[]{:S(2)}) %collective-permute-start.31) | collective-permute-done | bytes 65568 | tf_op jit(solution)/shard_map/ppermute | solution.py:376
  120.8 3.0 %collective-permute-start.34 = (bf16[256,128]{1,0:T(8,128)(2,1)S(1)}, bf16[256,128]{1,0:T(8,128)(2,1)S(1)}, u32[]{:S(2)}, u32[]{:S(2)}) collective-permute-start(bf16[256,128]{1,0:T(8,128)(2,1)S(1)} %sum_x.1.refs_0_), channel_id=1, source_target_pairs={{0,4},{2,6},{4,0},{6,2},{1,5},{3,7},{5,1},{7,3},{8,12},{10,14},{12... | collective-permute-start | bytes 196616 | tf_op jit(solution)/shard_map/ppermute | solution.py:383
  (79 shorter events, 33.7 us)
Async XLA Ops:
  0.6 11.3 %collective-permute-start.1 = (bf16[192,512]{1,0:T(8,128)(2,1)}, bf16[192,512]{1,0:T(8,128)(2,1)S(1)}, u32[]{:S(2)}, u32[]{:S(2)}) collective-permute-start(bf16[192,512]{1,0:T(8,128)(2,1)} %refs_1_.1), channel_id=1, source_target_pairs={{0,16},{16,32},{32,48},{48,0},{1,17},{17,33},{33,49},{49,1},{2,18}... | collective-permute-start | bytes 589832 | tf_op jit(solution)/shard_map/ppermute | solution.py:357
  2.7 9.3 %collective-permute-start = (bf16[192,512]{1,0:T(8,128)(2,1)}, bf16[192,512]{1,0:T(8,128)(2,1)S(1)}, u32[]{:S(2)}, u32[]{:S(2)}) collective-permute-start(bf16[192,512]{1,0:T(8,128)(2,1)} %refs_1_.1), channel_id=1, source_target_pairs={{0,64},{64,0},{1,65},{65,1},{2,66},{66,2},{3,67},{67,3},{4,68},{68... | collective-permute-start | bytes 589832 | tf_op jit(solution)/shard_map/ppermute | solution.py:346
  4.3 7.7 %collective-permute-start.2 = (bf16[192,512]{1,0:T(8,128)(2,1)}, bf16[192,512]{1,0:T(8,128)(2,1)S(1)}, u32[]{:S(2)}, u32[]{:S(2)}) collective-permute-start(bf16[192,512]{1,0:T(8,128)(2,1)} %refs_1_.1), channel_id=1, source_target_pairs={{0,48},{16,0},{32,16},{48,32},{1,49},{17,1},{33,17},{49,33},{2,50}... | collective-permute-start | bytes 589832 | tf_op jit(solution)/shard_map/ppermute | solution.py:357
  12.0 6.2 %collective-permute-start.4 = (bf16[192,512]{1,0:T(8,128)(2,1)S(1)}, bf16[192,512]{1,0:T(8,128)(2,1)S(1)}, u32[]{:S(2)}, u32[]{:S(2)}) collective-permute-start(bf16[192,512]{1,0:T(8,128)(2,1)S(1)} %collective-permute-done.refs_5_), channel_id=1, source_target_pairs={{0,48},{16,0},{32,16},{48,32},{1,49},{17,1},{33,17},{49,33},{2,50}... | collective-permute-start | bytes 589832 | tf_op jit(solution)/shard_map/ppermute | solution.py:357
  14.3 7.0 %collective-permute-start.5 = (bf16[192,512]{1,0:T(8,128)(2,1)S(1)}, bf16[192,512]{1,0:T(8,128)(2,1)S(1)}, u32[]{:S(2)}, u32[]{:S(2)}) collective-permute-start(bf16[192,512]{1,0:T(8,128)(2,1)S(1)} %collective-permute-done.1.refs_3_), channel_id=1, source_target_pairs={{0,16},{16,32},{32,48},{48,0},{1,17},{17,33},{33,49},{49,1},{2,18}... | collective-permute-start | bytes 589832 | tf_op jit(solution)/shard_map/ppermute | solution.py:357
  14.3 7.0 %collective-permute-start.3 = (bf16[192,512]{1,0:T(8,128)(2,1)S(1)}, bf16[192,512]{1,0:T(8,128)(2,1)S(1)}, u32[]{:S(2)}, u32[]{:S(2)}) collective-permute-start(bf16[192,512]{1,0:T(8,128)(2,1)S(1)} %collective-permute-done.1.refs_3_), channel_id=1, source_target_pairs={{0,64},{64,0},{1,65},{65,1},{2,66},{66,2},{3,67},{67,3},{4,68},{68... | collective-permute-start | bytes 589832 | tf_op jit(solution)/shard_map/ppermute | solution.py:346
  21.3 6.9 %collective-permute-start.6 = (bf16[192,512]{1,0:T(8,128)(2,1)S(1)}, bf16[192,512]{1,0:T(8,128)(2,1)S(1)}, u32[]{:S(2)}, u32[]{:S(2)}) collective-permute-start(bf16[192,512]{1,0:T(8,128)(2,1)S(1)} %collective-permute-done.4.refs_6_), channel_id=1, source_target_pairs={{0,48},{16,0},{32,16},{48,32},{1,49},{17,1},{33,17},{49,33},{2,50}... | collective-permute-start | bytes 589832 | tf_op jit(solution)/shard_map/ppermute | solution.py:357
  31.1 7.6 %collective-permute-start.11 = (bf16[960,512]{1,0:T(8,128)(2,1)S(1)}, bf16[960,512]{1,0:T(8,128)(2,1)S(1)}, u32[]{:S(2)}, u32[]{:S(2)}) collective-permute-start(bf16[960,512]{1,0:T(8,128)(2,1)S(1)} %down_far_1.1), channel_id=1, source_target_pairs={{0,1},{1,0},{2,3},{3,2},{4,5},{5,4},{6,7},{7,6},{8,9},{9,8},{10,11... | collective-permute-start | bytes 2949128 | tf_op jit(solution)/shard_map/ppermute | solution.py:346
  31.6 8.5 %collective-permute-start.8 = (bf16[192,512]{1,0:T(8,128)(2,1)S(1)}, bf16[192,512]{1,0:T(8,128)(2,1)S(1)}, u32[]{:S(2)}, u32[]{:S(2)}) collective-permute-start(bf16[192,512]{1,0:T(8,128)(2,1)S(1)} %get-tuple-element.72), channel_id=1, source_target_pairs={{0,2},{2,4},{4,6},{6,0},{1,3},{3,5},{5,7},{7,1},{8,10},{10,12},{12... | collective-permute-start | bytes 589832 | tf_op jit(solution)/shard_map/ppermute | solution.py:232
  33.2 8.4 %collective-permute-start.9 = (bf16[192,512]{1,0:T(8,128)(2,1)S(1)}, bf16[192,512]{1,0:T(8,128)(2,1)S(1)}, u32[]{:S(2)}, u32[]{:S(2)}) collective-permute-start(bf16[192,512]{1,0:T(8,128)(2,1)S(1)} %get-tuple-element.73), channel_id=1, source_target_pairs={{0,8},{8,0},{1,9},{9,1},{2,10},{10,2},{3,11},{11,3},{4,12},{12,4},... | collective-permute-start | bytes 589832 | tf_op jit(solution)/shard_map/ppermute | solution.py:346
  36.2 6.6 %collective-permute-start.10 = (bf16[192,512]{1,0:T(8,128)(2,1)S(1)}, bf16[192,512]{1,0:T(8,128)(2,1)S(1)}, u32[]{:S(2)}, u32[]{:S(2)}) collective-permute-start(bf16[192,512]{1,0:T(8,128)(2,1)S(1)} %get-tuple-element.74), channel_id=1, source_target_pairs={{0,6},{2,0},{4,2},{6,4},{1,7},{3,1},{5,3},{7,5},{8,14},{10,8},{12,... | collective-permute-start | bytes 589832 | tf_op jit(solution)/shard_map/ppermute | solution.py:232
  42.9 9.2 %collective-permute-start.12 = (bf16[192,512]{1,0:T(8,128)(2,1)S(1)}, bf16[192,512]{1,0:T(8,128)(2,1)S(1)}, u32[]{:S(2)}, u32[]{:S(2)}) collective-permute-start(bf16[192,512]{1,0:T(8,128)(2,1)S(1)} %get-tuple-element.86), channel_id=1, source_target_pairs={{0,2},{2,4},{4,6},{6,0},{1,3},{3,5},{5,7},{7,1},{8,10},{10,12},{12... | collective-permute-start | bytes 589832 | tf_op jit(solution)/shard_map/ppermute | solution.py:232
  44.4 7.7 %collective-permute-start.13 = (bf16[192,512]{1,0:T(8,128)(2,1)S(1)}, bf16[192,512]{1,0:T(8,128)(2,1)S(1)}, u32[]{:S(2)}, u32[]{:S(2)}) collective-permute-start(bf16[192,512]{1,0:T(8,128)(2,1)S(1)} %get-tuple-element.87), channel_id=1, source_target_pairs={{0,6},{2,0},{4,2},{6,4},{1,7},{3,1},{5,3},{7,5},{8,14},{10,8},{12,... | collective-permute-start | bytes 589832 | tf_op jit(solution)/shard_map/ppermute | solution.py:232
  46.8 8.1 %collective-permute-start.15 = (bf16[192,512]{1,0:T(8,128)(2,1)S(1)}, bf16[192,512]{1,0:T(8,128)(2,1)S(1)}, u32[]{:S(2)}, u32[]{:S(2)}) collective-permute-start(bf16[192,512]{1,0:T(8,128)(2,1)S(1)} %get-tuple-element.91), channel_id=1, source_target_pairs={{0,2},{2,4},{4,6},{6,0},{1,3},{3,5},{5,7},{7,1},{8,10},{10,12},{12... | collective-permute-start | bytes 589832 | tf_op jit(solution)/shard_map/ppermute | solution.py:232
  52.2 7.3 %collective-permute-start.14 = (bf16[192,512]{1,0:T(8,128)(2,1)S(1)}, bf16[192,512]{1,0:T(8,128)(2,1)S(1)}, u32[]{:S(2)}, u32[]{:S(2)}) collective-permute-start(bf16[192,512]{1,0:T(8,128)(2,1)S(1)} %sum_across.1), channel_id=1, source_target_pairs={{0,8},{8,0},{1,9},{9,1},{2,10},{10,2},{3,11},{11,3},{4,12},{12,4},... | collective-permute-start | bytes 589832 | tf_op jit(solution)/shard_map/ppermute | solution.py:346
  61.2 13.3 %collective-permute-start.20 = (bf16[256,512]{1,0:T(8,128)(2,1)S(1)}, bf16[256,512]{1,0:T(8,128)(2,1)S(1)}, u32[]{:S(2)}, u32[]{:S(2)}) collective-permute-start(bf16[256,512]{1,0:T(8,128)(2,1)S(1)} %get-tuple-element.97), channel_id=1, source_target_pairs={{0,1},{1,0},{2,3},{3,2},{4,5},{5,4},{6,7},{7,6},{8,9},{9,8},{10,11... | collective-permute-start | bytes 786440 | tf_op jit(solution)/shard_map/ppermute | solution.py:346
  61.3 8.8 %collective-permute-start.16 = (bf16[192,512]{1,0:T(8,128)(2,1)S(1)}, bf16[192,512]{1,0:T(8,128)(2,1)S(1)}, u32[]{:S(2)}, u32[]{:S(2)}) collective-permute-start(bf16[192,512]{1,0:T(8,128)(2,1)S(1)} %get-tuple-element.93.first), channel_id=1, source_target_pairs={{0,8},{8,0},{1,9},{9,1},{2,10},{10,2},{3,11},{11,3},{4,12},{12,4},... | collective-permute-start | bytes 589832 | tf_op jit(solution)/shard_map/ppermute | solution.py:346
  70.1 30.1 %collective-permute-start.19 = (bf16[384,512]{1,0:T(8,128)(2,1)S(1)}, bf16[384,512]{1,0:T(8,128)(2,1)S(1)}, u32[]{:S(2)}, u32[]{:S(2)}) collective-permute-start(bf16[384,512]{1,0:T(8,128)(2,1)S(1)} %pair_y.1.refs_0_), channel_id=1, source_target_pairs={{0,2},{2,4},{4,6},{6,0},{1,3},{3,5},{5,7},{7,1},{8,10},{10,12},{12... | collective-permute-start | bytes 1179656 | tf_op jit(solution)/shard_map/ppermute | solution.py:426
  70.2 30.0 %collective-permute-start.18 = (bf16[384,512]{1,0:T(8,128)(2,1)S(1)}, bf16[384,512]{1,0:T(8,128)(2,1)S(1)}, u32[]{:S(2)}, u32[]{:S(2)}) collective-permute-start(bf16[384,512]{1,0:T(8,128)(2,1)S(1)} %pair_y.1.refs_0_), channel_id=1, source_target_pairs={{0,4},{2,6},{4,0},{6,2},{1,5},{3,7},{5,1},{7,3},{8,12},{10,14},{12... | collective-permute-start | bytes 1179656 | tf_op jit(solution)/shard_map/ppermute | solution.py:426
  74.0 26.1 %collective-permute-start.17 = (bf16[384,512]{1,0:T(8,128)(2,1)S(1)}, bf16[384,512]{1,0:T(8,128)(2,1)S(1)}, u32[]{:S(2)}, u32[]{:S(2)}) collective-permute-start(bf16[384,512]{1,0:T(8,128)(2,1)S(1)} %pair_y.1.refs_0_), channel_id=1, source_target_pairs={{0,6},{2,0},{4,2},{6,4},{1,7},{3,1},{5,3},{7,5},{8,14},{10,8},{12,... | collective-permute-start | bytes 1179656 | tf_op jit(solution)/shard_map/ppermute | solution.py:426
  74.7 6.3 %collective-permute-start.22 = (bf16[64,512]{1,0:T(8,128)(2,1)S(1)}, bf16[64,512]{1,0:T(8,128)(2,1)S(1)}, u32[]{:S(2)}, u32[]{:S(2)}) collective-permute-start(bf16[64,512]{1,0:T(8,128)(2,1)S(1)} %get-tuple-element.100), channel_id=1, source_target_pairs={{0,32},{16,48},{32,0},{48,16},{1,33},{17,49},{33,1},{49,17},{2,34}... | collective-permute-start | bytes 196616 | tf_op jit(solution)/shard_map/ppermute | solution.py:346
  78.9 5.5 %collective-permute-start.23 = (bf16[64,512]{1,0:T(8,128)(2,1)S(1)}, bf16[64,512]{1,0:T(8,128)(2,1)S(1)}, u32[]{:S(2)}, u32[]{:S(2)}) collective-permute-start(bf16[64,512]{1,0:T(8,128)(2,1)S(1)} %get-tuple-element.101), channel_id=1, source_target_pairs={{0,48},{16,32},{32,16},{48,0},{1,49},{17,33},{33,17},{49,1},{2,50}... | collective-permute-start | bytes 196616 | tf_op jit(solution)/shard_map/ppermute | solution.py:346
  84.5 5.6 %collective-permute-start.26 = (bf16[64,512]{1,0:T(8,128)(2,1)S(1)}, bf16[64,512]{1,0:T(8,128)(2,1)S(1)}, u32[]{:S(2)}, u32[]{:S(2)}) collective-permute-start(bf16[64,512]{1,0:T(8,128)(2,1)S(1)} %sum_z.1.a), channel_id=1, source_target_pairs={{0,72},{8,64},{64,8},{72,0},{1,73},{9,65},{65,9},{73,1},{2,74},{10... | collective-permute-start | bytes 196616 | tf_op jit(solution)/shard_map/ppermute | solution.py:346
  85.3 5.2 %collective-permute-start.25 = (bf16[64,512]{1,0:T(8,128)(2,1)S(1)}, bf16[64,512]{1,0:T(8,128)(2,1)S(1)}, u32[]{:S(2)}, u32[]{:S(2)}) collective-permute-start(bf16[64,512]{1,0:T(8,128)(2,1)S(1)} %sum_z.1.a), channel_id=1, source_target_pairs={{0,64},{8,72},{64,0},{72,8},{1,65},{9,73},{65,1},{73,9},{2,66},{10... | collective-permute-start | bytes 196616 | tf_op jit(solution)/shard_map/ppermute | solution.py:346
  90.0 5.8 %collective-permute-start.24 = (bf16[64,512]{1,0:T(8,128)(2,1)S(1)}, bf16[64,512]{1,0:T(8,128)(2,1)S(1)}, u32[]{:S(2)}, u32[]{:S(2)}) collective-permute-start(bf16[64,512]{1,0:T(8,128)(2,1)S(1)} %sum_z.1.a), channel_id=1, source_target_pairs={{0,8},{8,0},{64,72},{72,64},{1,9},{9,1},{65,73},{73,65},{2,10},{10... | collective-permute-start | bytes 196616 | tf_op jit(solution)/shard_map/ppermute | solution.py:346
  100.4 7.5 %collective-permute-start.29 = (bf16[128,512]{1,0:T(8,128)(2,1)S(1)}, bf16[128,512]{1,0:T(8,128)(2,1)S(1)}, u32[]{:S(2)}, u32[]{:S(2)}) collective-permute-start(bf16[128,512]{1,0:T(8,128)(2,1)S(1)} %double.1.low), channel_id=1, source_target_pairs={{0,32},{16,48},{32,0},{48,16},{1,33},{17,49},{33,1},{49,17},{2,34}... | collective-permute-start | bytes 393224 | tf_op jit(solution)/shard_map/ppermute | solution.py:346
  107.9 24.5 %all-to-all-start = ((bf16[8,192,512]{2,1,0:T(8,128)(2,1)}), bf16[8,192,512]{2,1,0:T(8,128)(2,1)S(1)}, u32[]{:S(2)}, u32[]{:S(2)}) async-start(bf16[8,192,512]{2,1,0:T(8,128)(2,1)} %up_far.1), calls=%async_computation | async-start | bytes 3145728 | tf_op jit(solution)/shard_map/all_to_all | solution.py:342
  111.5 5.5 %collective-permute-start.30 = (bf16[256,128]{1,0:T(8,128)(2,1)S(1)}, bf16[256,128]{1,0:T(8,128)(2,1)S(1)}, u32[]{:S(2)}, u32[]{:S(2)}) collective-permute-start(bf16[256,128]{1,0:T(8,128)(2,1)S(1)} %get-tuple-element.111), channel_id=1, source_target_pairs={{0,2},{2,4},{4,6},{6,0},{1,3},{3,5},{5,7},{7,1},{8,10},{10,12},{12... | collective-permute-start | bytes 196616 | tf_op jit(solution)/shard_map/ppermute | solution.py:376
  113.8 5.8 %collective-permute-start.31 = (bf16[256,128]{1,0:T(8,128)(2,1)S(1)}, bf16[256,128]{1,0:T(8,128)(2,1)S(1)}, u32[]{:S(2)}, u32[]{:S(2)}) collective-permute-start(bf16[256,128]{1,0:T(8,128)(2,1)S(1)} %get-tuple-element.112), channel_id=1, source_target_pairs={{0,4},{2,6},{4,0},{6,2},{1,5},{3,7},{5,1},{7,3},{8,12},{10,14},{12... | collective-permute-start | bytes 196616 | tf_op jit(solution)/shard_map/ppermute | solution.py:376
  114.1 5.4 %collective-permute-start.32 = (bf16[256,128]{1,0:T(8,128)(2,1)S(1)}, bf16[256,128]{1,0:T(8,128)(2,1)S(1)}, u32[]{:S(2)}, u32[]{:S(2)}) collective-permute-start(bf16[256,128]{1,0:T(8,128)(2,1)S(1)} %get-tuple-element.113), channel_id=1, source_target_pairs={{0,6},{2,0},{4,2},{6,4},{1,7},{3,1},{5,3},{7,5},{8,14},{10,8},{12,... | collective-permute-start | bytes 196616 | tf_op jit(solution)/shard_map/ppermute | solution.py:376
  119.6 6.2 %collective-permute-start.35 = (bf16[256,128]{1,0:T(8,128)(2,1)S(1)}, bf16[256,128]{1,0:T(8,128)(2,1)S(1)}, u32[]{:S(2)}, u32[]{:S(2)}) collective-permute-start(bf16[256,128]{1,0:T(8,128)(2,1)S(1)} %sum_x.1.refs_0_), channel_id=1, source_target_pairs={{0,2},{2,4},{4,6},{6,0},{1,3},{3,5},{5,7},{7,1},{8,10},{10,12},{12... | collective-permute-start | bytes 196616 | tf_op jit(solution)/shard_map/ppermute | solution.py:383
  120.8 5.9 %collective-permute-start.34 = (bf16[256,128]{1,0:T(8,128)(2,1)S(1)}, bf16[256,128]{1,0:T(8,128)(2,1)S(1)}, u32[]{:S(2)}, u32[]{:S(2)}) collective-permute-start(bf16[256,128]{1,0:T(8,128)(2,1)S(1)} %sum_x.1.refs_0_), channel_id=1, source_target_pairs={{0,4},{2,6},{4,0},{6,2},{1,5},{3,7},{5,1},{7,3},{8,12},{10,14},{12... | collective-permute-start | bytes 196616 | tf_op jit(solution)/shard_map/ppermute | solution.py:383
  (10 other events, 80.2 us)

commit v15 on v12

--- a/solution.py
+++ b/solution.py
@@ -332,10 +332,11 @@
 
 
 def turn_kernel(low, high, *outs):
-    rows = low.shape[0]
     for g, out in enumerate(outs):
-        for n, part in enumerate((low, high)):
-            out[n * rows : (n + 1) * rows] = part[:, g * LANES : (g + 1) * LANES]
+        for k in range(RING):
+            part = (low, high)[k & 1]
+            rows = slice((k >> 1) * PIECE, ((k >> 1) + 1) * PIECE)
+            out[k * PIECE : (k + 1) * PIECE] = part[rows, g * LANES : (g + 1) * LANES]
 
 
 def join_kernel(*refs):
@@ -460,7 +461,7 @@
         cost_estimate=pl.CostEstimate(flops=work, bytes_accessed=12 << 20, transcendentals=0),
         name="up_near",
     )(dense, mine)
-    next_piece, own = lax.optimization_barrier((trade(summed, "z", 1), own))
+    next_piece, own = lax.optimization_barrier((trade(summed, "z", 2), own))
     pair = vmem_call(double_kernel, bf16(2 * PIECE, WIDTH), "double")(summed, next_piece)
     partial_grad = pl.pallas_call(
         up_add_kernel,
@@ -476,7 +477,7 @@
         cost_estimate=pl.CostEstimate(flops=work, bytes_accessed=12 << 20, transcendentals=0),
         name="up_far",
     )(far, theirs, own)
-    pairs = (pair, trade(pair, "z", 2))
+    pairs = (pair, trade(pair, "z", 1))
     partial_grad, *pairs = lax.optimization_barrier((partial_grad, *pairs))
     received = exchange(partial_grad, ROW)
 

time: 126 us -> 125 us (level)
  waiting for transfers between devices: 43.1 us -> 45.4 us
  starting transfers between devices: 54.4 us -> 52.3 us
  Pallas kernels: 23.1 us -> 21.7 us
    ppermute x17, starting transfers between devices: 20.9 us -> 18.6 us  [trade(): lax.ppermute(array, axes, [(i, i ^ bits) for i in range(lax.axis_size(axe...]
    ppermute x17, waiting for transfers between devices: 22 us -> 24 us  [trade(): lax.ppermute(array, axes, [(i, i ^ bits) for i in range(lax.axis_size(axe...]
    pallas_call x2, Pallas kernels: 3.43 us -> 2.09 us  [build(): pl.pallas_call(functools.partial(build_kernel, part), out_shape=bf16(2 *...]
  transfers between devices with their start and end apart: 35 -> 35, of which waited for: 24 -> 25; matrix products, arithmetic and copies ran while one was open for 1% -> 1% of each run, Pallas kernels for 15% -> 14%
where the time goes in v15:
time: 125 us; the launch traced here: 124 us
  starting transfers between devices  52.3 us (42%)
  waiting for transfers between devices  45.4 us (36%)
  Pallas kernels  21.7 us (17%)
  local copies, waits for them, and re-layouts  1.68 us (1%)
  other arithmetic  1.6 us (1%)
  between operations  1.52 us (1%)
    ppermute x17, waiting for transfers between devices, trade(): lax.ppermute(array, axes, [(i, i ^ bits) for i in range(lax.axis_size(axe...  24 us
    ppermute x17, starting transfers between devices, trade(): lax.ppermute(array, axes, [(i, i ^ bits) for i in range(lax.axis_size(axe...  18.6 us
    pallas_call x18, Pallas kernels, call(): pl.pallas_call(kernel, out_shape=outs, in_specs=[vmem] * len(args), out_s...  11.4 us
    ppermute x5, starting transfers between devices, ahead(): lax.ppermute(array, fast, [(i, (i - step) % RING) for i in range(RING)])  8.79 us
    all_to_all x2, starting transfers between devices, exchange(): return lax.all_to_all(parts, axes, 0, 0)  8.39 us
    ppermute x5, waiting for transfers between devices, pass_on(): lax.ppermute(array, fast, [(i, (i + step) % RING) for i in range(RING)])  7.67 us
    ppermute x5, starting transfers between devices, pass_on(): lax.ppermute(array, fast, [(i, (i + step) % RING) for i in range(RING)])  7.64 us
    ppermute x5, waiting for transfers between devices, ahead(): lax.ppermute(array, fast, [(i, (i - step) % RING) for i in range(RING)])  5.56 us
  transfers between devices with their start and end apart: 35, of which 25 were waited for; matrix products, arithmetic and copies ran while one was open for 1% of the time, Pallas kernels for 14%

profile of v15, /device:TPU:0, one launch (start us, length us, event | category | flops | bytes accessed | tf_op | source)
XLA Modules:
  0.0 124.2 jit_solution(7015544454703159973)
XLA Ops:
  0.6 2.1 %collective-permute-start.1 = (bf16[192,512]{1,0:T(8,128)(2,1)}, bf16[192,512]{1,0:T(8,128)(2,1)S(1)}, u32[]{:S(2)}, u32[]{:S(2)}) collective-permute-start(bf16[192,512]{1,0:T(8,128)(2,1)} %refs_1_.1), channel_id=1, source_target_pairs={{0,16},{16,32},{32,48},{48,0},{1,17},{17,33},{33,49},{49,1},{2,18}... | collective-permute-start | bytes 589832 | tf_op jit(solution)/shard_map/ppermute | solution.py:375
  4.3 2.2 %collective-permute-start.2 = (bf16[192,512]{1,0:T(8,128)(2,1)}, bf16[192,512]{1,0:T(8,128)(2,1)S(1)}, u32[]{:S(2)}, u32[]{:S(2)}) collective-permute-start(bf16[192,512]{1,0:T(8,128)(2,1)} %refs_1_.1), channel_id=1, source_target_pairs={{0,48},{16,0},{32,16},{48,32},{1,49},{17,1},{33,17},{49,33},{2,50}... | collective-permute-start | bytes 589832 | tf_op jit(solution)/shard_map/ppermute | solution.py:375
  8.8 1.7 %copy-done.1 = bf16[1,1,288,4096]{3,2,1,0:T(8,128)(2,1)S(1)} copy-done((bf16[1,1,288,4096]{3,2,1,0:T(8,128)(2,1)S(1)}, bf16[1,1,288,4096]{3,2,1,0:T(8,128)(2,1)}, u32[]{:S(2)}) %copy-start.1) | copy-done | bytes 2359320
  11.8 2.5 %collective-permute-start.4 = (bf16[192,512]{1,0:T(8,128)(2,1)S(1)}, bf16[192,512]{1,0:T(8,128)(2,1)S(1)}, u32[]{:S(2)}, u32[]{:S(2)}) collective-permute-start(bf16[192,512]{1,0:T(8,128)(2,1)S(1)} %collective-permute-done.refs_5_), channel_id=1, source_target_pairs={{0,48},{16,0},{32,16},{48,32},{1,49},{17,1},{33,17},{49,33},{2,50}... | collective-permute-start | bytes 589832 | tf_op jit(solution)/shard_map/ppermute | solution.py:375
  15.6 2.7 %collective-permute-done.4.refs_6_ = bf16[192,512]{1,0:T(8,128)(2,1)S(1)} collective-permute-done((bf16[192,512]{1,0:T(8,128)(2,1)S(1)}, bf16[192,512]{1,0:T(8,128)(2,1)S(1)}, u32[]{:S(2)}, u32[]{:S(2)}) %collective-permute-start.4) | collective-permute-done | bytes 196640 | tf_op jit(solution)/shard_map/ppermute | solution.py:375
  18.3 2.8 %collective-permute-done.5.refs_4_ = bf16[192,512]{1,0:T(8,128)(2,1)S(1)} collective-permute-done((bf16[192,512]{1,0:T(8,128)(2,1)S(1)}, bf16[192,512]{1,0:T(8,128)(2,1)S(1)}, u32[]{:S(2)}, u32[]{:S(2)}) %collective-permute-start.5) | collective-permute-done | bytes 196640 | tf_op jit(solution)/shard_map/ppermute | solution.py:375
  21.2 2.0 %collective-permute-start.6 = (bf16[192,512]{1,0:T(8,128)(2,1)S(1)}, bf16[192,512]{1,0:T(8,128)(2,1)S(1)}, u32[]{:S(2)}, u32[]{:S(2)}) collective-permute-start(bf16[192,512]{1,0:T(8,128)(2,1)S(1)} %collective-permute-done.4.refs_6_), channel_id=1, source_target_pairs={{0,48},{16,0},{32,16},{48,32},{1,49},{17,1},{33,17},{49,33},{2,50}... | collective-permute-start | bytes 589832 | tf_op jit(solution)/shard_map/ppermute | solution.py:375
  23.2 5.0 %down_most.1.most = f32[3072,512]{1,0:T(8,128)S(1)} custom-call(bf16[3072,1536]{1,0:T(8,128)(2,1)S(1)} %build_1.1.refs_0_.dense, bf16[192,512]{1,0:T(8,128)(2,1)S(1)} %copy-done.4, bf16[192,512]{1,0:T(8,128)(2,1)S(1)} %collective-permute-done.2.refs_2_, bf16[192,512]{1,0:T(8,128)(2,1)S(1)} %collective-permute-done.1.refs_3_, ...), custom_call_target="tpu_custom_call" | custom-call | flops 4831838208 | bytes 1048576 | tf_op jit(solution)/shard_map/down_most/pallas_call | solution.py:33
  28.7 2.0 %collective-permute-done.7.other = bf16[576,512]{1,0:T(8,128)(2,1)S(1)} collective-permute-done((bf16[576,512]{1,0:T(8,128)(2,1)S(1)}, bf16[576,512]{1,0:T(8,128)(2,1)S(1)}, u32[]{:S(2)}, u32[]{:S(2)}) %collective-permute-start.7) | collective-permute-done | bytes 589856 | tf_op jit(solution)/shard_map/ppermute | solution.py:364
  31.6 2.4 %collective-permute-start.8 = (bf16[192,512]{1,0:T(8,128)(2,1)S(1)}, bf16[192,512]{1,0:T(8,128)(2,1)S(1)}, u32[]{:S(2)}, u32[]{:S(2)}) collective-permute-start(bf16[192,512]{1,0:T(8,128)(2,1)S(1)} %get-tuple-element.72), channel_id=1, source_target_pairs={{0,2},{2,4},{4,6},{6,0},{1,3},{3,5},{5,7},{7,1},{8,10},{10,12},{12... | collective-permute-start | bytes 589832 | tf_op jit(solution)/shard_map/ppermute | solution.py:248
  34.0 2.1 %collective-permute-start.9 = (bf16[192,512]{1,0:T(8,128)(2,1)S(1)}, bf16[192,512]{1,0:T(8,128)(2,1)S(1)}, u32[]{:S(2)}, u32[]{:S(2)}) collective-permute-start(bf16[192,512]{1,0:T(8,128)(2,1)S(1)} %get-tuple-element.73), channel_id=1, source_target_pairs={{0,8},{8,0},{1,9},{9,1},{2,10},{10,2},{3,11},{11,3},{4,12},{12,4},... | collective-permute-start | bytes 589832 | tf_op jit(solution)/shard_map/ppermute | solution.py:364
  36.1 1.7 %collective-permute-start.10 = (bf16[192,512]{1,0:T(8,128)(2,1)S(1)}, bf16[192,512]{1,0:T(8,128)(2,1)S(1)}, u32[]{:S(2)}, u32[]{:S(2)}) collective-permute-start(bf16[192,512]{1,0:T(8,128)(2,1)S(1)} %get-tuple-element.74), channel_id=1, source_target_pairs={{0,6},{2,0},{4,2},{6,4},{1,7},{3,1},{5,3},{7,5},{8,14},{10,8},{12,... | collective-permute-start | bytes 589832 | tf_op jit(solution)/shard_map/ppermute | solution.py:248
  38.3 1.9 %collective-permute-done.8.b = bf16[192,512]{1,0:T(8,128)(2,1)S(1)} collective-permute-done((bf16[192,512]{1,0:T(8,128)(2,1)S(1)}, bf16[192,512]{1,0:T(8,128)(2,1)S(1)}, u32[]{:S(2)}, u32[]{:S(2)}) %collective-permute-start.8) | collective-permute-done | bytes 196640 | tf_op jit(solution)/shard_map/ppermute | solution.py:248
  40.2 2.2 %collective-permute-done.9.d = bf16[192,512]{1,0:T(8,128)(2,1)S(1)} collective-permute-done((bf16[192,512]{1,0:T(8,128)(2,1)S(1)}, bf16[192,512]{1,0:T(8,128)(2,1)S(1)}, u32[]{:S(2)}, u32[]{:S(2)}) %collective-permute-start.9) | collective-permute-done | bytes 196640 | tf_op jit(solution)/shard_map/ppermute | solution.py:364
  44.4 1.8 %collective-permute-start.13 = (bf16[192,512]{1,0:T(8,128)(2,1)S(1)}, bf16[192,512]{1,0:T(8,128)(2,1)S(1)}, u32[]{:S(2)}, u32[]{:S(2)}) collective-permute-start(bf16[192,512]{1,0:T(8,128)(2,1)S(1)} %get-tuple-element.87), channel_id=1, source_target_pairs={{0,6},{2,0},{4,2},{6,4},{1,7},{3,1},{5,3},{7,5},{8,14},{10,8},{12,... | collective-permute-start | bytes 589832 | tf_op jit(solution)/shard_map/ppermute | solution.py:248
  46.4 5.0 %collective-permute-done.12.refs_1_ = bf16[192,512]{1,0:T(8,128)(2,1)S(1)} collective-permute-done((bf16[192,512]{1,0:T(8,128)(2,1)S(1)}, bf16[192,512]{1,0:T(8,128)(2,1)S(1)}, u32[]{:S(2)}, u32[]{:S(2)}) %collective-permute-start.12) | collective-permute-done | bytes 196640 | tf_op jit(solution)/shard_map/ppermute | solution.py:248
  51.5 2.2 %collective-permute-start.14 = (bf16[192,512]{1,0:T(8,128)(2,1)S(1)}, bf16[192,512]{1,0:T(8,128)(2,1)S(1)}, u32[]{:S(2)}, u32[]{:S(2)}) collective-permute-start(bf16[192,512]{1,0:T(8,128)(2,1)S(1)} %sum_across.1), channel_id=1, source_target_pairs={{0,8},{8,0},{1,9},{9,1},{2,10},{10,2},{3,11},{11,3},{4,12},{12,4},... | collective-permute-start | bytes 589832 | tf_op jit(solution)/shard_map/ppermute | solution.py:364
  54.1 4.6 %collective-permute-done.14.c = bf16[192,512]{1,0:T(8,128)(2,1)S(1)} collective-permute-done((bf16[192,512]{1,0:T(8,128)(2,1)S(1)}, bf16[192,512]{1,0:T(8,128)(2,1)S(1)}, u32[]{:S(2)}, u32[]{:S(2)}) %collective-permute-start.14) | collective-permute-done | bytes 196640 | tf_op jit(solution)/shard_map/ppermute | solution.py:364
  58.7 2.0 %middle.1 = (bf16[192,512]{1,0:T(8,128)(2,1)}, bf16[8,192,512]{2,1,0:T(8,128)(2,1)}, bf16[192,512]{1,0:T(8,128)(2,1)S(1)}, bf16[192,512]{1,0:T(8,128)(2,1)S(1)}) custom-call(bf16[192,512]{1,0:T(8,128)(2,1)S(1)} %get-tuple-element.80.a, bf16[192,512]{1,0:T(8,128)(2,1)S(1)} %collective-permute-done.13.b, bf16[192,512]{1,0:T(8,128)(2,1)S(1)} %collective-permute-done.14.c, ...), custom_call_target="tpu_custom_call" | custom-call | flops 201326592 | bytes 1048576 | tf_op jit(solution)/shard_map/middle/pallas_call | solution.py:33
  60.7 4.5 %all-to-all-start = ((bf16[8,192,512]{2,1,0:T(8,128)(2,1)}), bf16[8,192,512]{2,1,0:T(8,128)(2,1)S(1)}, u32[]{:S(2)}, u32[]{:S(2)}) async-start(bf16[8,192,512]{2,1,0:T(8,128)(2,1)} %get-tuple-element.101), calls=%async_computation | async-start | bytes 3145728 | tf_op jit(solution)/shard_map/all_to_all | solution.py:360
  67.7 3.3 %collective-permute-start.18 = (bf16[64,512]{1,0:T(8,128)(2,1)S(1)}, bf16[64,512]{1,0:T(8,128)(2,1)S(1)}, u32[]{:S(2)}, u32[]{:S(2)}) collective-permute-start(bf16[64,512]{1,0:T(8,128)(2,1)S(1)} %get-tuple-element.99), channel_id=1, source_target_pairs={{0,32},{16,48},{32,0},{48,16},{1,33},{17,49},{33,1},{49,17},{2,34}... | collective-permute-start | bytes 196616 | tf_op jit(solution)/shard_map/ppermute | solution.py:364
  72.5 1.9 %collective-permute-done.18.refs_2_ = bf16[64,512]{1,0:T(8,128)(2,1)S(1)} collective-permute-done((bf16[64,512]{1,0:T(8,128)(2,1)S(1)}, bf16[64,512]{1,0:T(8,128)(2,1)S(1)}, u32[]{:S(2)}, u32[]{:S(2)}) %collective-permute-start.18) | collective-permute-done | bytes 65568 | tf_op jit(solution)/shard_map/ppermute | solution.py:364
  74.5 2.0 %collective-permute-done.19.refs_3_ = bf16[64,512]{1,0:T(8,128)(2,1)S(1)} collective-permute-done((bf16[64,512]{1,0:T(8,128)(2,1)S(1)}, bf16[64,512]{1,0:T(8,128)(2,1)S(1)}, u32[]{:S(2)}, u32[]{:S(2)}) %collective-permute-start.19) | collective-permute-done | bytes 65568 | tf_op jit(solution)/shard_map/ppermute | solution.py:364
  76.5 3.0 %collective-permute-start.22 = (bf16[64,512]{1,0:T(8,128)(2,1)S(1)}, bf16[64,512]{1,0:T(8,128)(2,1)S(1)}, u32[]{:S(2)}, u32[]{:S(2)}) collective-permute-start(bf16[64,512]{1,0:T(8,128)(2,1)S(1)} %sum_z.1.a), channel_id=1, source_target_pairs={{0,72},{8,64},{64,8},{72,0},{1,73},{9,65},{65,9},{73,1},{2,74},{10... | collective-permute-start | bytes 196616 | tf_op jit(solution)/shard_map/ppermute | solution.py:364
  81.2 5.2 %collective-permute-done.22.d = bf16[64,512]{1,0:T(8,128)(2,1)S(1)} collective-permute-done((bf16[64,512]{1,0:T(8,128)(2,1)S(1)}, bf16[64,512]{1,0:T(8,128)(2,1)S(1)}, u32[]{:S(2)}, u32[]{:S(2)}) %collective-permute-start.22) | collective-permute-done | bytes 65568 | tf_op jit(solution)/shard_map/ppermute | solution.py:364
  88.1 4.8 %up_near.1 = (f32[1536,512]{1,0:T(8,128)S(1)}, bf16[1536,1536]{1,0:T(8,128)(2,1)S(1)}) custom-call(bf16[3072,1536]{1,0:T(8,128)(2,1)} %copy-done, bf16[8,192,512]{2,1,0:T(8,128)(2,1)S(1)} %all-to-all-done.rows), custom_call_target="tpu_custom_call" | custom-call | flops 2415919104 | bytes 12582912 | tf_op jit(solution)/shard_map/up_near/pallas_call | solution.py:450
  93.9 1.7 %collective-permute-start.25 = (bf16[128,512]{1,0:T(8,128)(2,1)S(1)}, bf16[128,512]{1,0:T(8,128)(2,1)S(1)}, u32[]{:S(2)}, u32[]{:S(2)}) collective-permute-start(bf16[128,512]{1,0:T(8,128)(2,1)S(1)} %double.1.low), channel_id=1, source_target_pairs={{0,16},{16,0},{32,48},{48,32},{1,17},{17,1},{33,49},{49,33},{2,18}... | collective-permute-start | bytes 393224 | tf_op jit(solution)/shard_map/ppermute | solution.py:364
  95.7 3.4 %up_far.1 = bf16[8,192,512]{2,1,0:T(8,128)(2,1)} custom-call(bf16[1536,1536]{1,0:T(8,128)(2,1)S(1)} %get-tuple-element.103.tile, bf16[8,192,512]{2,1,0:T(8,128)(2,1)S(1)} %collective-permute-done.23.rows, f32[1536,512]{1,0:T(8,128)S(1)} %get-tuple-element.106.other), custom_call_target="tpu_custom_call" | custom-call | flops 2415919104 | bytes 12582912 | tf_op jit(solution)/shard_map/up_far/pallas_call | solution.py:466
  99.5 3.8 %all-to-all-start.1 = ((bf16[8,192,512]{2,1,0:T(8,128)(2,1)}), bf16[8,192,512]{2,1,0:T(8,128)(2,1)S(1)}, u32[]{:S(2)}, u32[]{:S(2)}) async-start(bf16[8,192,512]{2,1,0:T(8,128)(2,1)} %up_far.1), calls=%async_computation.1 | async-start | bytes 3145728 | tf_op jit(solution)/shard_map/all_to_all | solution.py:360
  104.0 2.5 %collective-permute-start.27 = (bf16[256,128]{1,0:T(8,128)(2,1)S(1)}, bf16[256,128]{1,0:T(8,128)(2,1)S(1)}, u32[]{:S(2)}, u32[]{:S(2)}) collective-permute-start(bf16[256,128]{1,0:T(8,128)(2,1)S(1)} %get-tuple-element.112), channel_id=1, source_target_pairs={{0,4},{2,6},{4,0},{6,2},{1,5},{3,7},{5,1},{7,3},{8,12},{10,14},{12... | collective-permute-start | bytes 196616 | tf_op jit(solution)/shard_map/ppermute | solution.py:394
  111.9 3.1 %collective-permute-start.30 = (bf16[256,128]{1,0:T(8,128)(2,1)S(1)}, bf16[256,128]{1,0:T(8,128)(2,1)S(1)}, u32[]{:S(2)}, u32[]{:S(2)}) collective-permute-start(bf16[256,128]{1,0:T(8,128)(2,1)S(1)} %sum_x.1.refs_0_), channel_id=1, source_target_pairs={{0,4},{2,6},{4,0},{6,2},{1,5},{3,7},{5,1},{7,3},{8,12},{10,14},{12... | collective-permute-start | bytes 196616 | tf_op jit(solution)/shard_map/ppermute | solution.py:401
  116.3 1.6 %collective-permute-done.30.refs_2_ = bf16[256,128]{1,0:T(8,128)(2,1)S(1)} collective-permute-done((bf16[256,128]{1,0:T(8,128)(2,1)S(1)}, bf16[256,128]{1,0:T(8,128)(2,1)S(1)}, u32[]{:S(2)}, u32[]{:S(2)}) %collective-permute-start.30) | collective-permute-done | bytes 65568 | tf_op jit(solution)/shard_map/ppermute | solution.py:401
  (73 shorter events, 32.9 us)
Async XLA Ops:
  0.6 11.1 %collective-permute-start.1 = (bf16[192,512]{1,0:T(8,128)(2,1)}, bf16[192,512]{1,0:T(8,128)(2,1)S(1)}, u32[]{:S(2)}, u32[]{:S(2)}) collective-permute-start(bf16[192,512]{1,0:T(8,128)(2,1)} %refs_1_.1), channel_id=1, source_target_pairs={{0,16},{16,32},{32,48},{48,0},{1,17},{17,33},{33,49},{49,1},{2,18}... | collective-permute-start | bytes 589832 | tf_op jit(solution)/shard_map/ppermute | solution.py:375
  2.7 9.1 %collective-permute-start = (bf16[192,512]{1,0:T(8,128)(2,1)}, bf16[192,512]{1,0:T(8,128)(2,1)S(1)}, u32[]{:S(2)}, u32[]{:S(2)}) collective-permute-start(bf16[192,512]{1,0:T(8,128)(2,1)} %refs_1_.1), channel_id=1, source_target_pairs={{0,64},{64,0},{1,65},{65,1},{2,66},{66,2},{3,67},{67,3},{4,68},{68... | collective-permute-start | bytes 589832 | tf_op jit(solution)/shard_map/ppermute | solution.py:364
  4.3 7.5 %collective-permute-start.2 = (bf16[192,512]{1,0:T(8,128)(2,1)}, bf16[192,512]{1,0:T(8,128)(2,1)S(1)}, u32[]{:S(2)}, u32[]{:S(2)}) collective-permute-start(bf16[192,512]{1,0:T(8,128)(2,1)} %refs_1_.1), channel_id=1, source_target_pairs={{0,48},{16,0},{32,16},{48,32},{1,49},{17,1},{33,17},{49,33},{2,50}... | collective-permute-start | bytes 589832 | tf_op jit(solution)/shard_map/ppermute | solution.py:375
  11.8 6.5 %collective-permute-start.4 = (bf16[192,512]{1,0:T(8,128)(2,1)S(1)}, bf16[192,512]{1,0:T(8,128)(2,1)S(1)}, u32[]{:S(2)}, u32[]{:S(2)}) collective-permute-start(bf16[192,512]{1,0:T(8,128)(2,1)S(1)} %collective-permute-done.refs_5_), channel_id=1, source_target_pairs={{0,48},{16,0},{32,16},{48,32},{1,49},{17,1},{33,17},{49,33},{2,50}... | collective-permute-start | bytes 589832 | tf_op jit(solution)/shard_map/ppermute | solution.py:375
  14.3 6.9 %collective-permute-start.5 = (bf16[192,512]{1,0:T(8,128)(2,1)S(1)}, bf16[192,512]{1,0:T(8,128)(2,1)S(1)}, u32[]{:S(2)}, u32[]{:S(2)}) collective-permute-start(bf16[192,512]{1,0:T(8,128)(2,1)S(1)} %collective-permute-done.1.refs_3_), channel_id=1, source_target_pairs={{0,16},{16,32},{32,48},{48,0},{1,17},{17,33},{33,49},{49,1},{2,18}... | collective-permute-start | bytes 589832 | tf_op jit(solution)/shard_map/ppermute | solution.py:375
  14.3 6.9 %collective-permute-start.3 = (bf16[192,512]{1,0:T(8,128)(2,1)S(1)}, bf16[192,512]{1,0:T(8,128)(2,1)S(1)}, u32[]{:S(2)}, u32[]{:S(2)}) collective-permute-start(bf16[192,512]{1,0:T(8,128)(2,1)S(1)} %collective-permute-done.1.refs_3_), channel_id=1, source_target_pairs={{0,64},{64,0},{1,65},{65,1},{2,66},{66,2},{3,67},{67,3},{4,68},{68... | collective-permute-start | bytes 589832 | tf_op jit(solution)/shard_map/ppermute | solution.py:364
  21.2 7.1 %collective-permute-start.6 = (bf16[192,512]{1,0:T(8,128)(2,1)S(1)}, bf16[192,512]{1,0:T(8,128)(2,1)S(1)}, u32[]{:S(2)}, u32[]{:S(2)}) collective-permute-start(bf16[192,512]{1,0:T(8,128)(2,1)S(1)} %collective-permute-done.4.refs_6_), channel_id=1, source_target_pairs={{0,48},{16,0},{32,16},{48,32},{1,49},{17,1},{33,17},{49,33},{2,50}... | collective-permute-start | bytes 589832 | tf_op jit(solution)/shard_map/ppermute | solution.py:375
  31.1 6.8 %collective-permute-start.11 = (bf16[960,512]{1,0:T(8,128)(2,1)S(1)}, bf16[960,512]{1,0:T(8,128)(2,1)S(1)}, u32[]{:S(2)}, u32[]{:S(2)}) collective-permute-start(bf16[960,512]{1,0:T(8,128)(2,1)S(1)} %down_far_1.1), channel_id=1, source_target_pairs={{0,1},{1,0},{2,3},{3,2},{4,5},{5,4},{6,7},{7,6},{8,9},{9,8},{10,11... | collective-permute-start | bytes 2949128 | tf_op jit(solution)/shard_map/ppermute | solution.py:364
  31.6 8.6 %collective-permute-start.8 = (bf16[192,512]{1,0:T(8,128)(2,1)S(1)}, bf16[192,512]{1,0:T(8,128)(2,1)S(1)}, u32[]{:S(2)}, u32[]{:S(2)}) collective-permute-start(bf16[192,512]{1,0:T(8,128)(2,1)S(1)} %get-tuple-element.72), channel_id=1, source_target_pairs={{0,2},{2,4},{4,6},{6,0},{1,3},{3,5},{5,7},{7,1},{8,10},{10,12},{12... | collective-permute-start | bytes 589832 | tf_op jit(solution)/shard_map/ppermute | solution.py:248
  34.0 8.4 %collective-permute-start.9 = (bf16[192,512]{1,0:T(8,128)(2,1)S(1)}, bf16[192,512]{1,0:T(8,128)(2,1)S(1)}, u32[]{:S(2)}, u32[]{:S(2)}) collective-permute-start(bf16[192,512]{1,0:T(8,128)(2,1)S(1)} %get-tuple-element.73), channel_id=1, source_target_pairs={{0,8},{8,0},{1,9},{9,1},{2,10},{10,2},{3,11},{11,3},{4,12},{12,4},... | collective-permute-start | bytes 589832 | tf_op jit(solution)/shard_map/ppermute | solution.py:364
  36.1 6.6 %collective-permute-start.10 = (bf16[192,512]{1,0:T(8,128)(2,1)S(1)}, bf16[192,512]{1,0:T(8,128)(2,1)S(1)}, u32[]{:S(2)}, u32[]{:S(2)}) collective-permute-start(bf16[192,512]{1,0:T(8,128)(2,1)S(1)} %get-tuple-element.74), channel_id=1, source_target_pairs={{0,6},{2,0},{4,2},{6,4},{1,7},{3,1},{5,3},{7,5},{8,14},{10,8},{12,... | collective-permute-start | bytes 589832 | tf_op jit(solution)/shard_map/ppermute | solution.py:248
  42.9 8.5 %collective-permute-start.12 = (bf16[192,512]{1,0:T(8,128)(2,1)S(1)}, bf16[192,512]{1,0:T(8,128)(2,1)S(1)}, u32[]{:S(2)}, u32[]{:S(2)}) collective-permute-start(bf16[192,512]{1,0:T(8,128)(2,1)S(1)} %get-tuple-element.86), channel_id=1, source_target_pairs={{0,2},{2,4},{4,6},{6,0},{1,3},{3,5},{5,7},{7,1},{8,10},{10,12},{12... | collective-permute-start | bytes 589832 | tf_op jit(solution)/shard_map/ppermute | solution.py:248
  44.4 7.0 %collective-permute-start.13 = (bf16[192,512]{1,0:T(8,128)(2,1)S(1)}, bf16[192,512]{1,0:T(8,128)(2,1)S(1)}, u32[]{:S(2)}, u32[]{:S(2)}) collective-permute-start(bf16[192,512]{1,0:T(8,128)(2,1)S(1)} %get-tuple-element.87), channel_id=1, source_target_pairs={{0,6},{2,0},{4,2},{6,4},{1,7},{3,1},{5,3},{7,5},{8,14},{10,8},{12,... | collective-permute-start | bytes 589832 | tf_op jit(solution)/shard_map/ppermute | solution.py:248
  46.2 7.9 %collective-permute-start.15 = (bf16[192,512]{1,0:T(8,128)(2,1)S(1)}, bf16[192,512]{1,0:T(8,128)(2,1)S(1)}, u32[]{:S(2)}, u32[]{:S(2)}) collective-permute-start(bf16[192,512]{1,0:T(8,128)(2,1)S(1)} %get-tuple-element.91), channel_id=1, source_target_pairs={{0,2},{2,4},{4,6},{6,0},{1,3},{3,5},{5,7},{7,1},{8,10},{10,12},{12... | collective-permute-start | bytes 589832 | tf_op jit(solution)/shard_map/ppermute | solution.py:248
  51.5 7.3 %collective-permute-start.14 = (bf16[192,512]{1,0:T(8,128)(2,1)S(1)}, bf16[192,512]{1,0:T(8,128)(2,1)S(1)}, u32[]{:S(2)}, u32[]{:S(2)}) collective-permute-start(bf16[192,512]{1,0:T(8,128)(2,1)S(1)} %sum_across.1), channel_id=1, source_target_pairs={{0,8},{8,0},{1,9},{9,1},{2,10},{10,2},{3,11},{11,3},{4,12},{12,4},... | collective-permute-start | bytes 589832 | tf_op jit(solution)/shard_map/ppermute | solution.py:364
  60.7 27.1 %all-to-all-start = ((bf16[8,192,512]{2,1,0:T(8,128)(2,1)}), bf16[8,192,512]{2,1,0:T(8,128)(2,1)S(1)}, u32[]{:S(2)}, u32[]{:S(2)}) async-start(bf16[8,192,512]{2,1,0:T(8,128)(2,1)} %get-tuple-element.101), calls=%async_computation | async-start | bytes 3145728 | tf_op jit(solution)/shard_map/all_to_all | solution.py:360
  67.6 5.0 %collective-permute-start.17 = (bf16[64,512]{1,0:T(8,128)(2,1)S(1)}, bf16[64,512]{1,0:T(8,128)(2,1)S(1)}, u32[]{:S(2)}, u32[]{:S(2)}) collective-permute-start(bf16[64,512]{1,0:T(8,128)(2,1)S(1)} %get-tuple-element.98), channel_id=1, source_target_pairs={{0,16},{16,0},{32,48},{48,32},{1,17},{17,1},{33,49},{49,33},{2,18}... | collective-permute-start | bytes 196616 | tf_op jit(solution)/shard_map/ppermute | solution.py:364
  67.7 6.8 %collective-permute-start.18 = (bf16[64,512]{1,0:T(8,128)(2,1)S(1)}, bf16[64,512]{1,0:T(8,128)(2,1)S(1)}, u32[]{:S(2)}, u32[]{:S(2)}) collective-permute-start(bf16[64,512]{1,0:T(8,128)(2,1)S(1)} %get-tuple-element.99), channel_id=1, source_target_pairs={{0,32},{16,48},{32,0},{48,16},{1,33},{17,49},{33,1},{49,17},{2,34}... | collective-permute-start | bytes 196616 | tf_op jit(solution)/shard_map/ppermute | solution.py:364
  70.9 5.5 %collective-permute-start.19 = (bf16[64,512]{1,0:T(8,128)(2,1)S(1)}, bf16[64,512]{1,0:T(8,128)(2,1)S(1)}, u32[]{:S(2)}, u32[]{:S(2)}) collective-permute-start(bf16[64,512]{1,0:T(8,128)(2,1)S(1)} %get-tuple-element.100), channel_id=1, source_target_pairs={{0,48},{16,32},{32,16},{48,0},{1,49},{17,33},{33,17},{49,1},{2,50}... | collective-permute-start | bytes 196616 | tf_op jit(solution)/shard_map/ppermute | solution.py:364
  76.5 10.0 %collective-permute-start.22 = (bf16[64,512]{1,0:T(8,128)(2,1)S(1)}, bf16[64,512]{1,0:T(8,128)(2,1)S(1)}, u32[]{:S(2)}, u32[]{:S(2)}) collective-permute-start(bf16[64,512]{1,0:T(8,128)(2,1)S(1)} %sum_z.1.a), channel_id=1, source_target_pairs={{0,72},{8,64},{64,8},{72,0},{1,73},{9,65},{65,9},{73,1},{2,74},{10... | collective-permute-start | bytes 196616 | tf_op jit(solution)/shard_map/ppermute | solution.py:364
  79.4 7.0 %collective-permute-start.21 = (bf16[64,512]{1,0:T(8,128)(2,1)S(1)}, bf16[64,512]{1,0:T(8,128)(2,1)S(1)}, u32[]{:S(2)}, u32[]{:S(2)}) collective-permute-start(bf16[64,512]{1,0:T(8,128)(2,1)S(1)} %sum_z.1.a), channel_id=1, source_target_pairs={{0,64},{8,72},{64,0},{72,8},{1,65},{9,73},{65,1},{73,9},{2,66},{10... | collective-permute-start | bytes 196616 | tf_op jit(solution)/shard_map/ppermute | solution.py:364
  80.0 7.8 %collective-permute-start.20 = (bf16[64,512]{1,0:T(8,128)(2,1)S(1)}, bf16[64,512]{1,0:T(8,128)(2,1)S(1)}, u32[]{:S(2)}, u32[]{:S(2)}) collective-permute-start(bf16[64,512]{1,0:T(8,128)(2,1)S(1)} %sum_z.1.a), channel_id=1, source_target_pairs={{0,8},{8,0},{64,72},{72,64},{1,9},{9,1},{65,73},{73,65},{2,10},{10... | collective-permute-start | bytes 196616 | tf_op jit(solution)/shard_map/ppermute | solution.py:364
  87.8 7.8 %collective-permute-start.23 = (bf16[8,192,512]{2,1,0:T(8,128)(2,1)S(1)}, bf16[8,192,512]{2,1,0:T(8,128)(2,1)S(1)}, u32[]{:S(2)}, u32[]{:S(2)}) collective-permute-start(bf16[8,192,512]{2,1,0:T(8,128)(2,1)S(1)} %all-to-all-done.rows), channel_id=1, source_target_pairs={{0,1},{1,0},{2,3},{3,2},{4,5},{5,4},{6,7},{7,6},{8,9},{9,8},{10,11... | collective-permute-start | bytes 4718600 | tf_op jit(solution)/shard_map/ppermute | solution.py:364
  87.9 6.0 %collective-permute-start.24 = (bf16[64,512]{1,0:T(8,128)(2,1)S(1)}, bf16[64,512]{1,0:T(8,128)(2,1)S(1)}, u32[]{:S(2)}, u32[]{:S(2)}) collective-permute-start(bf16[64,512]{1,0:T(8,128)(2,1)S(1)} %sum_y.1.first), channel_id=1, source_target_pairs={{0,32},{16,48},{32,0},{48,16},{1,33},{17,49},{33,1},{49,17},{2,34}... | collective-permute-start | bytes 196616 | tf_op jit(solution)/shard_map/ppermute | solution.py:364
  93.9 5.5 %collective-permute-start.25 = (bf16[128,512]{1,0:T(8,128)(2,1)S(1)}, bf16[128,512]{1,0:T(8,128)(2,1)S(1)}, u32[]{:S(2)}, u32[]{:S(2)}) collective-permute-start(bf16[128,512]{1,0:T(8,128)(2,1)S(1)} %double.1.low), channel_id=1, source_target_pairs={{0,16},{16,0},{32,48},{48,32},{1,17},{17,1},{33,49},{49,33},{2,18}... | collective-permute-start | bytes 393224 | tf_op jit(solution)/shard_map/ppermute | solution.py:364
  99.5 23.8 %all-to-all-start.1 = ((bf16[8,192,512]{2,1,0:T(8,128)(2,1)}), bf16[8,192,512]{2,1,0:T(8,128)(2,1)S(1)}, u32[]{:S(2)}, u32[]{:S(2)}) async-start(bf16[8,192,512]{2,1,0:T(8,128)(2,1)} %up_far.1), calls=%async_computation.1 | async-start | bytes 3145728 | tf_op jit(solution)/shard_map/all_to_all | solution.py:360
  103.4 5.5 %collective-permute-start.26 = (bf16[256,128]{1,0:T(8,128)(2,1)S(1)}, bf16[256,128]{1,0:T(8,128)(2,1)S(1)}, u32[]{:S(2)}, u32[]{:S(2)}) collective-permute-start(bf16[256,128]{1,0:T(8,128)(2,1)S(1)} %get-tuple-element.111), channel_id=1, source_target_pairs={{0,2},{2,4},{4,6},{6,0},{1,3},{3,5},{5,7},{7,1},{8,10},{10,12},{12... | collective-permute-start | bytes 196616 | tf_op jit(solution)/shard_map/ppermute | solution.py:394
  104.0 5.8 %collective-permute-start.27 = (bf16[256,128]{1,0:T(8,128)(2,1)S(1)}, bf16[256,128]{1,0:T(8,128)(2,1)S(1)}, u32[]{:S(2)}, u32[]{:S(2)}) collective-permute-start(bf16[256,128]{1,0:T(8,128)(2,1)S(1)} %get-tuple-element.112), channel_id=1, source_target_pairs={{0,4},{2,6},{4,0},{6,2},{1,5},{3,7},{5,1},{7,3},{8,12},{10,14},{12... | collective-permute-start | bytes 196616 | tf_op jit(solution)/shard_map/ppermute | solution.py:394
  106.5 4.3 %collective-permute-start.28 = (bf16[256,128]{1,0:T(8,128)(2,1)S(1)}, bf16[256,128]{1,0:T(8,128)(2,1)S(1)}, u32[]{:S(2)}, u32[]{:S(2)}) collective-permute-start(bf16[256,128]{1,0:T(8,128)(2,1)S(1)} %get-tuple-element.113), channel_id=1, source_target_pairs={{0,6},{2,0},{4,2},{6,4},{1,7},{3,1},{5,3},{7,5},{8,14},{10,8},{12,... | collective-permute-start | bytes 196616 | tf_op jit(solution)/shard_map/ppermute | solution.py:394
  110.8 5.5 %collective-permute-start.31 = (bf16[256,128]{1,0:T(8,128)(2,1)S(1)}, bf16[256,128]{1,0:T(8,128)(2,1)S(1)}, u32[]{:S(2)}, u32[]{:S(2)}) collective-permute-start(bf16[256,128]{1,0:T(8,128)(2,1)S(1)} %sum_x.1.refs_0_), channel_id=1, source_target_pairs={{0,2},{2,4},{4,6},{6,0},{1,3},{3,5},{5,7},{7,1},{8,10},{10,12},{12... | collective-permute-start | bytes 196616 | tf_op jit(solution)/shard_map/ppermute | solution.py:401
  111.9 6.0 %collective-permute-start.30 = (bf16[256,128]{1,0:T(8,128)(2,1)S(1)}, bf16[256,128]{1,0:T(8,128)(2,1)S(1)}, u32[]{:S(2)}, u32[]{:S(2)}) collective-permute-start(bf16[256,128]{1,0:T(8,128)(2,1)S(1)} %sum_x.1.refs_0_), channel_id=1, source_target_pairs={{0,4},{2,6},{4,0},{6,2},{1,5},{3,7},{5,1},{7,3},{8,12},{10,14},{12... | collective-permute-start | bytes 196616 | tf_op jit(solution)/shard_map/ppermute | solution.py:401
  115.0 4.3 %collective-permute-start.29 = (bf16[256,128]{1,0:T(8,128)(2,1)S(1)}, bf16[256,128]{1,0:T(8,128)(2,1)S(1)}, u32[]{:S(2)}, u32[]{:S(2)}) collective-permute-start(bf16[256,128]{1,0:T(8,128)(2,1)S(1)} %sum_x.1.refs_0_), channel_id=1, source_target_pairs={{0,6},{2,0},{4,2},{6,4},{1,7},{3,1},{5,3},{7,5},{8,14},{10,8},{12,... | collective-permute-start | bytes 196616 | tf_op jit(solution)/shard_map/ppermute | solution.py:401
  (8 other events, 86.0 us)
